TPU v7x, 32 devices: a whole 2x2x4 slice. The times are simulated.
32 devices in a mesh: pts: 8 (over y, x, core), cols: 4 (over z).
Axes of the slice: x: 2, y: 2, z: 4, core: 2. Of those that a mesh axis runs over, the one named last changes fastest.
Arguments:
- snapshot: float32 [1024, 2048], P('pts', 'cols'), may hold values from -18 to 18
- weights: float32 [1024], P('pts'), may hold values from 0.25 to 9
- damping: int32 [3, 2], replicated, may hold values from 1 to 8
Outputs:
- rotated: float32 [1024, 2048], P('pts', 'cols')
All inputs are finite; a program needn't handle non-finite values.
Results may differ from a plain program's by a relative error of at most 0.0003.
Values sent between devices are 32-bit elements; how exact they have to be, the bound alone decides.
No kernel may reach another device: no remote copies, remote signals or barrier semaphores. Data moves between devices by JAX's collectives and lax.ppermute only.
A program may use at most 64 MiB of HBM per device.

v0:
```python
import jax
import jax.numpy as jnp
from jax import lax
from jax.sharding import PartitionSpec as P

STEPS = 3
NS_ITERS = 3


EPSILON = 1e-06


def shifted(value, axis, steps):
    count = lax.axis_size(axis)
    pairs = [(source, (source + steps) % count) for source in range(count)]
    return lax.ppermute(value, axis, pairs)


def dot_full(left, right):
    return jnp.dot(left, right, precision=lax.Precision.HIGHEST, preferred_element_type=jnp.float32)


def inner_full(left, right):
    return lax.dot_general(
        left,
        right,
        (((0,), (0,)), ((), ())),
        precision=lax.Precision.HIGHEST,
        preferred_element_type=jnp.float32,
    )


def inverse_root(square, scale):
    identity = jnp.eye(square.shape[0], dtype=jnp.float32)
    current = square / scale
    factor = identity
    for turn_index in range(NS_ITERS):
        if turn_index == 0:
            middle = 1.5 * identity - 0.5 * current
            factor = middle
        else:
            middle = 1.5 * identity - 0.5 * dot_full(factor, current)
            factor = dot_full(middle, factor)
        if turn_index + 1 < NS_ITERS:
            current = dot_full(current, middle)
    return factor / jnp.sqrt(scale)


def side_factors(coupling, scale):
    identity = jnp.eye(coupling.shape[0], dtype=jnp.float32)
    square = identity + dot_full(coupling, coupling.T)
    factor = inverse_root(square, scale)
    return (factor, dot_full(coupling.T, factor))


def move_lower(block):
    return shifted(block, "cols", 1)


def body(snapshot, weights, damping):
    width = snapshot.shape[1] // 2
    upper_block = snapshot[:, :width]
    lower_block = snapshot[:, width:]
    point_weight = weights[:, None]
    for step_index in range(STEPS):
        weighted = point_weight * lower_block
        pair_gram = inner_full(upper_block, weighted)
        norm_upper = jnp.sum(point_weight * upper_block * upper_block, axis=0)
        norm_lower = jnp.sum(weighted * lower_block, axis=0)
        pair_gram, norm_upper, norm_lower = lax.psum((pair_gram, norm_upper, norm_lower), "pts")
        numer = damping[step_index, 0].astype(jnp.float32)
        denom = damping[step_index, 1].astype(jnp.float32)
        damping_now = numer / (numer + denom)
        coupling = (
            damping_now
            * pair_gram
            / jnp.sqrt((norm_upper[:, None] + EPSILON) * (norm_lower[None, :] + EPSILON))
        )
        scale = 1.0 + jnp.sum(coupling * coupling)
        upper_factor, upper_cross = side_factors(coupling, scale)
        lower_factor, lower_cross = side_factors(coupling.T, scale)
        new_upper = dot_full(upper_block, upper_factor) - dot_full(lower_block, upper_cross)
        new_lower = dot_full(upper_block, lower_cross) + dot_full(lower_block, lower_factor)
        upper_block, lower_block = (new_upper, new_lower)
        if step_index + 1 < STEPS:
            lower_block = move_lower(lower_block)
    lower_back = STEPS - 1
    lower_block = shifted(lower_block, "cols", -lower_back)
    return jnp.concatenate([upper_block, lower_block], axis=1)


def solution(mesh):
    placed = (P("pts", "cols"), P("pts"), P())
    return jax.shard_map(
        body, mesh=mesh, in_specs=placed, out_specs=P("pts", "cols"), check_vma=False
    )
```

profile of v0, /device:TPU:0, one launch (start us, length us, event | category | flops | bytes accessed | tf_op | source)
XLA Modules:
  0.0 251.6 jit_solution(10224633029720659895)
XLA Ops:
  6.5 2.2 convolution_bitcast_fusion
  8.8 0.9 copy-done
  14.9 15.2 %all-reduce.2 = (f32[256]{0:T(256)S(1)}, f32[256]{0:T(256)S(1)}) all-reduce(f32[256]{0:T(256)S(1)} %get-tuple-element.6, f32[256]{0:T(256)S(1)} %get-tuple-element.5), channel_id=1, replica_groups=mesh['pts'=8,'cols'=4] {'pts'}, use_global_device_ids=true, to_apply=%region_4.0 | all-reduce | flops 512 | bytes 4096 | tf_op jit(solution)/shard_map/psum | solution.py:70
  30.0 36.6 %all-reduce.7.cloned.1.call-done = f32[256,256]{0,1:T(8,128)} async-done(((f32[256,256]{0,1:T(8,128)}), f32[256,256]{0,1:T(8,128)}) %all-reduce.7.cloned.1.call-update) | async-done | bytes 262160 | tf_op jit(solution)/shard_map/psum | solution.py:70
  66.7 1.8 multiply_reduce_fusion.2
  71.3 0.7 fusion.5
  74.4 0.7 fusion.149
  75.7 1.5 collective-permute-start
  78.7 3.8 %collective-permute-done = f32[128,256]{1,0:T(8,128)S(1)} collective-permute-done((f32[128,256]{1,0:T(8,128)S(1)}, f32[128,256]{1,0:T(8,128)S(1)}, u32[]{:S(2)}, u32[]{:S(2)}) %collective-permute-start) | collective-permute-done | bytes 131104 | tf_op jit(solution)/shard_map/ppermute | solution.py:16
  82.8 11.8 %all-reduce.1 = (f32[256]{0:T(256)S(1)}, f32[256]{0:T(256)S(1)}) all-reduce(f32[256]{0:T(256)S(1)} %get-tuple-element.10, f32[256]{0:T(256)S(1)} %get-tuple-element.9), channel_id=1, replica_groups=mesh['pts'=8,'cols'=4] {'pts'}, use_global_device_ids=true, to_apply=%region_10.0 | all-reduce | flops 512 | bytes 4096 | tf_op jit(solution)/shard_map/psum | solution.py:70
  94.6 1.2 fusion.21
  96.1 51.0 %all-reduce.9.cloned.1.call-done = f32[256,256]{1,0:T(8,128)} async-done(((f32[256,256]{1,0:T(8,128)}), f32[256,256]{1,0:T(8,128)}) %all-reduce.9.cloned.1.call-update) | async-done | bytes 262160 | tf_op jit(solution)/shard_map/psum | solution.py:70
  147.1 1.8 multiply_reduce_fusion.1
  149.5 0.7 fusion.2
  155.8 1.5 collective-permute-start.1
  159.1 3.5 %collective-permute-done.1 = f32[128,256]{1,0:T(8,128)S(1)} collective-permute-done((f32[128,256]{1,0:T(8,128)S(1)}, f32[128,256]{1,0:T(8,128)S(1)}, u32[]{:S(2)}, u32[]{:S(2)}) %collective-permute-start.1) | collective-permute-done | bytes 131104 | tf_op jit(solution)/shard_map/ppermute | solution.py:16
  162.9 12.0 %all-reduce = (f32[256]{0:T(256)S(1)}, f32[256]{0:T(256)S(1)}) all-reduce(f32[256]{0:T(256)S(1)} %get-tuple-element.8, f32[256]{0:T(256)S(1)} %get-tuple-element.7), channel_id=1, replica_groups=mesh['pts'=8,'cols'=4] {'pts'}, use_global_device_ids=true, to_apply=%region_16.0 | all-reduce | flops 512 | bytes 4096 | tf_op jit(solution)/shard_map/psum | solution.py:70
  175.0 1.2 fusion.19
  176.2 51.2 %all-reduce.11.cloned.1.call-done = f32[256,256]{1,0:T(8,128)} async-done(((f32[256,256]{1,0:T(8,128)}), f32[256,256]{1,0:T(8,128)}) %all-reduce.11.cloned.1.call-update) | async-done | bytes 262160 | tf_op jit(solution)/shard_map/psum | solution.py:70
  227.4 1.8 multiply_reduce_fusion
  229.8 0.7 fusion
  236.1 2.5 collective-permute-start.2
  240.6 3.7 %collective-permute-done.2 = f32[128,256]{1,0:T(8,128)S(1)} collective-permute-done((f32[128,256]{1,0:T(8,128)S(1)}, f32[128,256]{1,0:T(8,128)S(1)}, u32[]{:S(2)}, u32[]{:S(2)}) %collective-permute-start.2) | collective-permute-done | bytes 131104 | tf_op jit(solution)/shard_map/ppermute | solution.py:16
  244.3 0.7 pad_maximum_fusion
  (80 shorter events, 23.4 us)
Async XLA Ops:
  6.5 60.1 %all-reduce.7.cloned.1.call-start = ((), (), s32[]{:S(2)}) async-start(), calls=%async_computation | async-start | bytes 524288 | tf_op jit(solution)/shard_map/psum | solution.py:70
  8.7 0.9 copy-start
  8.7 1.0 copy-start.4
  8.7 138.4 %all-reduce.9.cloned.1.call-start = ((), (), s32[]{:S(2)}) async-start(), calls=%async_computation.1 | async-start | bytes 524288 | tf_op jit(solution)/shard_map/psum | solution.py:70
  9.7 0.7 copy-start.5
  66.7 2.4 copy-start.1
  75.7 6.8 %collective-permute-start = (f32[128,256]{1,0:T(8,128)S(1)}, f32[128,256]{1,0:T(8,128)S(1)}, u32[]{:S(2)}, u32[]{:S(2)}) collective-permute-start(f32[128,256]{1,0:T(8,128)S(1)} %fusion.6), channel_id=1, source_target_pairs={{0,1},{1,2},{2,3},{3,0},{4,5},{5,6},{6,7},{7,4},{8,9},{9,10},{10,1... | collective-permute-start | bytes 393224 | tf_op jit(solution)/shard_map/ppermute | solution.py:16
  95.8 131.6 %all-reduce.11.cloned.1.call-start = ((), (), s32[]{:S(2)}) async-start(), calls=%async_computation.2 | async-start | bytes 524288 | tf_op jit(solution)/shard_map/psum | solution.py:70
  147.1 2.4 copy-start.3
  155.8 6.8 %collective-permute-start.1 = (f32[128,256]{1,0:T(8,128)S(1)}, f32[128,256]{1,0:T(8,128)S(1)}, u32[]{:S(2)}, u32[]{:S(2)}) collective-permute-start(f32[128,256]{1,0:T(8,128)S(1)} %convolution_add_fusion.7), channel_id=1, source_target_pairs={{0,1},{1,2},{2,3},{3,0},{4,5},{5,6},{6,7},{7,4},{8,9},{9,10},{10,1... | collective-permute-start | bytes 393224 | tf_op jit(solution)/shard_map/ppermute | solution.py:16
  227.4 2.4 copy-start.2
  236.1 8.2 %collective-permute-start.2 = (f32[128,256]{1,0:T(8,128)S(1)}, f32[128,256]{1,0:T(8,128)S(1)}, u32[]{:S(2)}, u32[]{:S(2)}) collective-permute-start(f32[128,256]{1,0:T(8,128)S(1)} %convolution_add_fusion.6), channel_id=1, source_target_pairs={{0,2},{1,3},{2,0},{3,1},{4,6},{5,7},{6,4},{7,5},{8,10},{9,11},{10,... | collective-permute-start | bytes 393224 | tf_op jit(solution)/shard_map/ppermute | solution.py:16
Sparse Core Ops, SparseCore 0:
  10.4 56.2 all-reduce.6
  95.9 51.1 all-reduce.8
  176.3 51.0 all-reduce.10
where the time goes:
time: 252 us
  waiting for transfers between devices  150 us (60%)
  blocking collectives  39 us (15%)
  matrix products  29 us (12%)
  between operations  19.6 us (8%)
  other arithmetic  6.17 us (2%)
  starting transfers between devices  5.82 us (2%)
    psum x3, waiting for transfers between devices, body(): lax.psum((pair_gram, norm_upper, norm_lower), 'pts')  139 us
    psum x3, blocking collectives, body(): lax.psum((pair_gram, norm_upper, norm_lower), 'pts')  39 us
    dot_general x60, matrix products, dot_full(): jnp.dot(left, right, precision=lax.Precision.HIGHEST, preferred_element_t...  24.5 us
    ppermute x3, waiting for transfers between devices, shifted(): return lax.ppermute(value, axis, pairs)  11 us
    ppermute x3, starting transfers between devices, shifted(): return lax.ppermute(value, axis, pairs)  5.55 us
    reduce_sum x3, other arithmetic, body(): scale = 1.0 + jnp.sum(coupling * coupling)  5.31 us
  transfers between devices with their start and end apart: 6, of which 6 were waited for; matrix products, arithmetic and copies ran while one was open for 2% of the time, Pallas kernels for 0%

commit v1 on v0

v1 whole, which is shorter than its diff:
```python
import jax
import jax.numpy as jnp
from jax import lax
from jax.sharding import PartitionSpec as P

STEPS = 3
EPSILON = 1e-06


def shifted(value, axis, steps):
    count = lax.axis_size(axis)
    pairs = [(source, (source + steps) % count) for source in range(count)]
    return lax.ppermute(value, axis, pairs)


def swapped(value, bits):
    count = lax.axis_size("pts")
    return lax.ppermute(value, "pts", [(source, source ^ bits) for source in range(count)])


def chip_sum(value):
    count = lax.axis_size("pts")
    bit = 2
    while bit < count:
        if 2 * bit < count:
            parts = [swapped(value, bits) for bits in (3 * bit, 2 * bit, bit)]
            bit *= 4
        else:
            parts = [swapped(value, bit)]
            bit *= 2
        value = sum(parts, value)
    return value


def dot_high(left, right, dims=((1,), (0,))):
    return lax.dot_general(
        left, right, (dims, ((), ())), precision=lax.Precision.HIGH, preferred_element_type=jnp.float32
    )


def rows_swapped(value):
    half = value.shape[0] // 2
    return jnp.concatenate([value[half:], value[:half]], axis=0)


def inverse_root(square, scale):
    identity = jnp.eye(square.shape[0], dtype=jnp.float32)
    base = (identity + square) / scale
    second = dot_high(base, base)
    first = 1.5 * identity - 0.5 * base
    first_square = 2.25 * identity - 1.5 * base + 0.25 * second
    both = 1.5 * first - 0.5 * dot_high(1.5 * base - 0.5 * second, first_square)
    cubic = dot_high(dot_high(base, both), dot_high(both, both))
    return (1.5 * both - 0.5 * cubic) / jnp.sqrt(scale)


def body(snapshot, weights, damping):
    rows, columns = snapshot.shape
    width = columns // 2
    half = width // 2
    first_core = lax.axis_index("pts") % 2 == 0

    def own_first(block):
        left, right = block[:, :half], block[:, half:]
        return jnp.concatenate(
            [jnp.where(first_core, left, right), jnp.where(first_core, right, left)], axis=1
        )

    point_weight = jnp.concatenate([weights, swapped(weights, 1)])[:, None]
    other = swapped(snapshot, 1)
    upper = own_first(jnp.concatenate([snapshot[:, :width], other[:, :width]], axis=0))
    lower = own_first(jnp.concatenate([snapshot[:, width:], other[:, width:]], axis=0))
    own = lower[:, :half]
    for step in range(STEPS):
        weighted = point_weight * own
        gram = dot_high(upper, weighted, ((0,), (0,)))
        norm_lower = jnp.sum(weighted * own, axis=0)
        norm_upper = jnp.sum(point_weight * upper[:, :half] * upper[:, :half], axis=0)
        norms = jnp.concatenate([norm_lower[None], norm_upper[None], jnp.zeros((6, half), jnp.float32)])
        payload = chip_sum(jnp.concatenate([gram, norms], axis=0))
        remote = swapped(payload, 1)
        if step > 0:
            lower = jnp.concatenate([own, rows_swapped(swapped(own, 1))], axis=1)
        gram = jnp.concatenate([payload[:width], rows_swapped(remote[:width])], axis=1)
        norm_lower = jnp.concatenate([payload[width], remote[width]])
        norm_upper = jnp.concatenate([payload[width + 1], remote[width + 1]])
        numer = damping[step, 0].astype(jnp.float32)
        denom = damping[step, 1].astype(jnp.float32)
        coupling = (
            numer
            / (numer + denom)
            * gram
            * lax.rsqrt(norm_upper + EPSILON)[:, None]
            * lax.rsqrt(norm_lower + EPSILON)[None, :]
        )
        scale = 1.0 + jnp.sum(coupling * coupling)
        upper_factor = inverse_root(dot_high(coupling, coupling, ((1,), (1,))), scale)
        lower_factor = inverse_root(dot_high(coupling, coupling, ((0,), (0,))), scale)
        cross = dot_high(upper_factor, coupling)
        if step + 1 < STEPS:
            own = dot_high(upper, cross[:, :half]) + dot_high(lower, lower_factor[:, :half])
            own = shifted(own, "cols", 1)
            upper = dot_high(upper, upper_factor) - dot_high(lower, cross, ((1,), (1,)))
        else:
            upper, lower = upper[:rows], lower[:rows]
            moved = dot_high(upper, cross) + dot_high(lower, lower_factor)
            moved = shifted(own_first(moved), "cols", 1 - STEPS)
            upper = own_first(dot_high(upper, upper_factor) - dot_high(lower, cross, ((1,), (1,))))
    return jnp.concatenate([upper, moved], axis=1)


def solution(mesh):
    placed = (P("pts", "cols"), P("pts"), P())
    return jax.shard_map(
        body, mesh=mesh, in_specs=placed, out_specs=P("pts", "cols"), check_vma=False
    )
```

time: 252 us -> 83.3 us (0.33)
  waiting for transfers between devices: 150 us -> 38.2 us
  blocking collectives: 39 us -> 0 us
  between operations: 19.6 us -> 6.74 us
  matrix products: 29 us -> 17 us
  starting transfers between devices: 5.82 us -> 14.6 us
    psum x3 -> x0, waiting for transfers between devices: 139 us -> none  [body(): lax.psum((pair_gram, norm_upper, norm_lower), 'pts')]
    psum x3 -> x0, blocking collectives: 39 us -> none  [body(): lax.psum((pair_gram, norm_upper, norm_lower), 'pts')]
    ppermute x0 -> x16, waiting for transfers between devices: none -> 18.9 us  [swapped(): lax.ppermute(value, 'pts', [(source, source ^ bits) for source in range(c...]
    ppermute x0 -> x16, starting transfers between devices: none -> 12.5 us  [swapped(): lax.ppermute(value, 'pts', [(source, source ^ bits) for source in range(c...]
    dot_general x63 -> x54, matrix products: 29 us -> 17 us  [dot_high(): lax.dot_general(left, right, (dims, ((), ())), precision=lax.Precision.HI...]
    ppermute x3, waiting for transfers between devices: 11 us -> 19.3 us  [shifted(): return lax.ppermute(value, axis, pairs)]
    ppermute x3, starting transfers between devices: 5.55 us -> 2.08 us  [shifted(): return lax.ppermute(value, axis, pairs)]
    reduce_sum x3, other arithmetic: 5.31 us -> 2.22 us  [body(): scale = 1.0 + jnp.sum(coupling * coupling)]
  transfers between devices with their start and end apart: 6 -> 19, of which waited for: 6 -> 14; matrix products, arithmetic and copies ran while one was open for 2% -> 4% of each run, Pallas kernels for 0% -> 0%
where the time goes in v1:
time: 83.3 us; the launch traced here: 83 us
  waiting for transfers between devices  38.2 us (46%)
  matrix products  17 us (20%)
  starting transfers between devices  14.6 us (18%)
  between operations  6.74 us (8%)
  other arithmetic  4.03 us (5%)
  local copies, waits for them, and re-layouts  2.44 us (3%)
    ppermute x3, waiting for transfers between devices, shifted(): return lax.ppermute(value, axis, pairs)  19.3 us
    ppermute x16, waiting for transfers between devices, swapped(): lax.ppermute(value, 'pts', [(source, source ^ bits) for source in range(c...  18.9 us
    dot_general x54, matrix products, dot_high(): lax.dot_general(left, right, (dims, ((), ())), precision=lax.Precision.HI...  17 us
    ppermute x16, starting transfers between devices, swapped(): lax.ppermute(value, 'pts', [(source, source ^ bits) for source in range(c...  12.5 us
    reduce_sum x3, other arithmetic, body(): scale = 1.0 + jnp.sum(coupling * coupling)  2.22 us
    ppermute x3, starting transfers between devices, shifted(): return lax.ppermute(value, axis, pairs)  2.08 us
  transfers between devices with their start and end apart: 19, of which 14 were waited for; matrix products, arithmetic and copies ran while one was open for 4% of the time, Pallas kernels for 0%

profile of v1, /device:TPU:0, one launch (start us, length us, event | category | flops | bytes accessed | tf_op | source)
XLA Modules:
  0.0 83.0 jit_solution(13690741896817428847)
XLA Ops:
  0.5 1.0 %fusion.197 = (f32[128,256]{1,0:T(8,128)S(1)}, f32[128,256]{1,0:T(8,128)S(1)}) fusion(f32[128,512]{1,0:T(8,128)} %param.3), kind=kLoop, calls=%fused_computation.277 | loop fusion | bytes 524288 | tf_op jit(solution)/shard_map/slice | solution.py:72
  2.9 3.0 %collective-permute-start.3 = (f32[264,128]{1,0:T(8,128)S(1)}, f32[264,128]{1,0:T(8,128)S(1)}, u32[]{:S(2)}, u32[]{:S(2)}) collective-permute-start(f32[264,128]{1,0:T(8,128)S(1)} %maximum_maximum_fusion.3), channel_id=1, source_target_pairs={{0,16},{4,20},{8,24},{12,28},{16,0},{20,4},{24,8},{28,12},{1,17},{... | collective-permute-start | bytes 405512 | tf_op jit(solution)/shard_map/ppermute | solution.py:18
  5.9 1.5 %collective-permute-start.4 = (f32[264,128]{1,0:T(8,128)S(1)}, f32[264,128]{1,0:T(8,128)S(1)}, u32[]{:S(2)}, u32[]{:S(2)}) collective-permute-start(f32[264,128]{1,0:T(8,128)S(1)} %maximum_maximum_fusion.3), channel_id=1, source_target_pairs={{0,8},{4,12},{8,0},{12,4},{16,24},{20,28},{24,16},{28,20},{1,9},{5... | collective-permute-start | bytes 405512 | tf_op jit(solution)/shard_map/ppermute | solution.py:18
  12.4 1.5 %collective-permute-done.2 = f32[264,128]{1,0:T(8,128)S(1)} collective-permute-done((f32[264,128]{1,0:T(8,128)S(1)}, f32[264,128]{1,0:T(8,128)S(1)}, u32[]{:S(2)}, u32[]{:S(2)}) %collective-permute-start.2) | collective-permute-done | bytes 135200 | tf_op jit(solution)/shard_map/ppermute | solution.py:18
  14.1 1.3 %collective-permute-done.5 = f32[264,128]{1,0:T(8,128)S(1)} collective-permute-done((f32[264,128]{1,0:T(8,128)S(1)}, f32[264,128]{1,0:T(8,128)S(1)}, u32[]{:S(2)}, u32[]{:S(2)}) %collective-permute-start.5) | collective-permute-done | bytes 135200 | tf_op jit(solution)/shard_map/ppermute | solution.py:18
  15.5 0.7 multiply_reduce_fusion.2
  22.0 1.8 %collective-permute-start.6 = (f32[256,128]{1,0:T(8,128)S(1)}, f32[256,128]{1,0:T(8,128)S(1)}, u32[]{:S(2)}, u32[]{:S(2)}) collective-permute-start(f32[256,128]{1,0:T(8,128)S(1)} %convolution_add_fusion.8), channel_id=1, source_target_pairs={{0,1},{1,2},{2,3},{3,0},{4,5},{5,6},{6,7},{7,4},{8,9},{9,10},{10,1... | collective-permute-start | bytes 393224 | tf_op jit(solution)/shard_map/ppermute | solution.py:13
  24.1 5.5 %collective-permute-done.6 = f32[256,128]{1,0:T(8,128)S(1)} collective-permute-done((f32[256,128]{1,0:T(8,128)S(1)}, f32[256,128]{1,0:T(8,128)S(1)}, u32[]{:S(2)}, u32[]{:S(2)}) %collective-permute-start.6) | collective-permute-done | bytes 131104 | tf_op jit(solution)/shard_map/ppermute | solution.py:13
  30.4 1.6 %collective-permute-start.8 = (f32[264,128]{1,0:T(8,128)S(1)}, f32[264,128]{1,0:T(8,128)S(1)}, u32[]{:S(2)}, u32[]{:S(2)}) collective-permute-start(f32[264,128]{1,0:T(8,128)S(1)} %maximum_maximum_fusion.4), channel_id=1, source_target_pairs={{0,16},{4,20},{8,24},{12,28},{16,0},{20,4},{24,8},{28,12},{1,17},{... | collective-permute-start | bytes 405512 | tf_op jit(solution)/shard_map/ppermute | solution.py:18
  32.0 1.5 %collective-permute-start.9 = (f32[264,128]{1,0:T(8,128)S(1)}, f32[264,128]{1,0:T(8,128)S(1)}, u32[]{:S(2)}, u32[]{:S(2)}) collective-permute-start(f32[264,128]{1,0:T(8,128)S(1)} %maximum_maximum_fusion.4), channel_id=1, source_target_pairs={{0,8},{4,12},{8,0},{12,4},{16,24},{20,28},{24,16},{28,20},{1,9},{5... | collective-permute-start | bytes 405512 | tf_op jit(solution)/shard_map/ppermute | solution.py:18
  33.9 2.5 %collective-permute-done.8 = f32[264,128]{1,0:T(8,128)S(1)} collective-permute-done((f32[264,128]{1,0:T(8,128)S(1)}, f32[264,128]{1,0:T(8,128)S(1)}, u32[]{:S(2)}, u32[]{:S(2)}) %collective-permute-start.8) | collective-permute-done | bytes 135200 | tf_op jit(solution)/shard_map/ppermute | solution.py:18
  36.4 2.0 %collective-permute-done.9 = f32[264,128]{1,0:T(8,128)S(1)} collective-permute-done((f32[264,128]{1,0:T(8,128)S(1)}, f32[264,128]{1,0:T(8,128)S(1)}, u32[]{:S(2)}, u32[]{:S(2)}) %collective-permute-start.9) | collective-permute-done | bytes 135200 | tf_op jit(solution)/shard_map/ppermute | solution.py:18
  38.4 2.1 %collective-permute-done.7 = f32[264,128]{1,0:T(8,128)S(1)} collective-permute-done((f32[264,128]{1,0:T(8,128)S(1)}, f32[264,128]{1,0:T(8,128)S(1)}, u32[]{:S(2)}, u32[]{:S(2)}) %collective-permute-start.7) | collective-permute-done | bytes 135200 | tf_op jit(solution)/shard_map/ppermute | solution.py:18
  40.7 1.3 %collective-permute-done.10 = f32[264,128]{1,0:T(8,128)S(1)} collective-permute-done((f32[264,128]{1,0:T(8,128)S(1)}, f32[264,128]{1,0:T(8,128)S(1)}, u32[]{:S(2)}, u32[]{:S(2)}) %collective-permute-start.10) | collective-permute-done | bytes 135200 | tf_op jit(solution)/shard_map/ppermute | solution.py:18
  42.1 0.7 multiply_reduce_fusion.1
  49.2 7.0 %collective-permute-done.12 = f32[256,128]{1,0:T(8,128)S(1)} collective-permute-done((f32[256,128]{1,0:T(8,128)S(1)}, f32[256,128]{1,0:T(8,128)S(1)}, u32[]{:S(2)}, u32[]{:S(2)}) %collective-permute-start.12) | collective-permute-done | bytes 131104 | tf_op jit(solution)/shard_map/ppermute | solution.py:13
  56.9 1.6 %collective-permute-start.14 = (f32[264,128]{1,0:T(8,128)S(1)}, f32[264,128]{1,0:T(8,128)S(1)}, u32[]{:S(2)}, u32[]{:S(2)}) collective-permute-start(f32[264,128]{1,0:T(8,128)S(1)} %maximum_maximum_fusion.5), channel_id=1, source_target_pairs={{0,16},{4,20},{8,24},{12,28},{16,0},{20,4},{24,8},{28,12},{1,17},{... | collective-permute-start | bytes 405512 | tf_op jit(solution)/shard_map/ppermute | solution.py:18
  58.5 1.5 %collective-permute-start.15 = (f32[264,128]{1,0:T(8,128)S(1)}, f32[264,128]{1,0:T(8,128)S(1)}, u32[]{:S(2)}, u32[]{:S(2)}) collective-permute-start(f32[264,128]{1,0:T(8,128)S(1)} %maximum_maximum_fusion.5), channel_id=1, source_target_pairs={{0,8},{4,12},{8,0},{12,4},{16,24},{20,28},{24,16},{28,20},{1,9},{5... | collective-permute-start | bytes 405512 | tf_op jit(solution)/shard_map/ppermute | solution.py:18
  60.5 2.5 %collective-permute-done.14 = f32[264,128]{1,0:T(8,128)S(1)} collective-permute-done((f32[264,128]{1,0:T(8,128)S(1)}, f32[264,128]{1,0:T(8,128)S(1)}, u32[]{:S(2)}, u32[]{:S(2)}) %collective-permute-start.14) | collective-permute-done | bytes 135200 | tf_op jit(solution)/shard_map/ppermute | solution.py:18
  63.0 2.0 %collective-permute-done.15 = f32[264,128]{1,0:T(8,128)S(1)} collective-permute-done((f32[264,128]{1,0:T(8,128)S(1)}, f32[264,128]{1,0:T(8,128)S(1)}, u32[]{:S(2)}, u32[]{:S(2)}) %collective-permute-start.15) | collective-permute-done | bytes 135200 | tf_op jit(solution)/shard_map/ppermute | solution.py:18
  64.9 2.1 %collective-permute-done.13 = f32[264,128]{1,0:T(8,128)S(1)} collective-permute-done((f32[264,128]{1,0:T(8,128)S(1)}, f32[264,128]{1,0:T(8,128)S(1)}, u32[]{:S(2)}, u32[]{:S(2)}) %collective-permute-start.13) | collective-permute-done | bytes 135200 | tf_op jit(solution)/shard_map/ppermute | solution.py:18
  67.3 1.3 %collective-permute-done.16 = f32[264,128]{1,0:T(8,128)S(1)} collective-permute-done((f32[264,128]{1,0:T(8,128)S(1)}, f32[264,128]{1,0:T(8,128)S(1)}, u32[]{:S(2)}, u32[]{:S(2)}) %collective-permute-start.16) | collective-permute-done | bytes 135200 | tf_op jit(solution)/shard_map/ppermute | solution.py:18
  68.7 0.7 multiply_reduce_fusion
  75.5 6.8 %collective-permute-done.18 = f32[128,256]{1,0:T(8,128)S(1)} collective-permute-done((f32[128,256]{1,0:T(8,128)S(1)}, f32[128,256]{1,0:T(8,128)S(1)}, u32[]{:S(2)}, u32[]{:S(2)}) %collective-permute-start.18) | collective-permute-done | bytes 131104 | tf_op jit(solution)/shard_map/ppermute | solution.py:13
  (113 shorter events, 22.8 us)
Async XLA Ops:
  0.0 1.6 %collective-permute-start.1 = (f32[128]{0:T(128)}, f32[128]{0:T(128)S(1)}, u32[]{:S(2)}, u32[]{:S(2)}) collective-permute-start(f32[128]{0:T(128)} %param.4), channel_id=1, source_target_pairs={{0,4},{4,0},{8,12},{12,8},{16,20},{20,16},{24,28},{28,24},{1,5},{5... | collective-permute-start | bytes 1544 | tf_op jit(solution)/shard_map/ppermute | solution.py:18
  0.5 1.7 %collective-permute-start = (f32[128,512]{1,0:T(8,128)}, f32[128,512]{1,0:T(8,128)S(1)}, u32[]{:S(2)}, u32[]{:S(2)}) collective-permute-start(f32[128,512]{1,0:T(8,128)} %param.3), channel_id=1, source_target_pairs={{0,4},{4,0},{8,12},{12,8},{16,20},{20,16},{24,28},{28,24},{1,5},{5... | collective-permute-start | bytes 786440 | tf_op jit(solution)/shard_map/ppermute | solution.py:18
  1.5 0.7 copy-start.1
  2.8 4.7 %copy-start = (s32[3,2]{0,1:T(2,128)S(1)}, s32[3,2]{0,1:T(2,128)}, u32[]{:S(2)}) copy-start(s32[3,2]{0,1:T(2,128)} %param.5) | copy-start | bytes 76
  2.9 9.2 %collective-permute-start.3 = (f32[264,128]{1,0:T(8,128)S(1)}, f32[264,128]{1,0:T(8,128)S(1)}, u32[]{:S(2)}, u32[]{:S(2)}) collective-permute-start(f32[264,128]{1,0:T(8,128)S(1)} %maximum_maximum_fusion.3), channel_id=1, source_target_pairs={{0,16},{4,20},{8,24},{12,28},{16,0},{20,4},{24,8},{28,12},{1,17},{... | collective-permute-start | bytes 405512 | tf_op jit(solution)/shard_map/ppermute | solution.py:18
  5.9 6.5 %collective-permute-start.4 = (f32[264,128]{1,0:T(8,128)S(1)}, f32[264,128]{1,0:T(8,128)S(1)}, u32[]{:S(2)}, u32[]{:S(2)}) collective-permute-start(f32[264,128]{1,0:T(8,128)S(1)} %maximum_maximum_fusion.3), channel_id=1, source_target_pairs={{0,8},{4,12},{8,0},{12,4},{16,24},{20,28},{24,16},{28,20},{1,9},{5... | collective-permute-start | bytes 405512 | tf_op jit(solution)/shard_map/ppermute | solution.py:18
  7.4 6.5 %collective-permute-start.2 = (f32[264,128]{1,0:T(8,128)S(1)}, f32[264,128]{1,0:T(8,128)S(1)}, u32[]{:S(2)}, u32[]{:S(2)}) collective-permute-start(f32[264,128]{1,0:T(8,128)S(1)} %maximum_maximum_fusion.3), channel_id=1, source_target_pairs={{0,24},{4,28},{8,16},{12,20},{16,8},{20,12},{24,0},{28,4},{1,25},{... | collective-permute-start | bytes 405512 | tf_op jit(solution)/shard_map/ppermute | solution.py:18
  14.0 1.4 %collective-permute-start.5 = (f32[264,128]{1,0:T(8,128)S(1)}, f32[264,128]{1,0:T(8,128)S(1)}, u32[]{:S(2)}, u32[]{:S(2)}) collective-permute-start(f32[264,128]{1,0:T(8,128)S(1)} %add_add_fusion.2), channel_id=1, source_target_pairs={{0,4},{4,0},{8,12},{12,8},{16,20},{20,16},{24,28},{28,24},{1,5},{5... | collective-permute-start | bytes 405512 | tf_op jit(solution)/shard_map/ppermute | solution.py:18
  22.0 7.6 %collective-permute-start.6 = (f32[256,128]{1,0:T(8,128)S(1)}, f32[256,128]{1,0:T(8,128)S(1)}, u32[]{:S(2)}, u32[]{:S(2)}) collective-permute-start(f32[256,128]{1,0:T(8,128)S(1)} %convolution_add_fusion.8), channel_id=1, source_target_pairs={{0,1},{1,2},{2,3},{3,0},{4,5},{5,6},{6,7},{7,4},{8,9},{9,10},{10,1... | collective-permute-start | bytes 393224 | tf_op jit(solution)/shard_map/ppermute | solution.py:13
  30.2 3.7 %collective-permute-start.11 = (f32[256,128]{1,0:T(8,128)S(1)}, f32[256,128]{1,0:T(8,128)S(1)}, u32[]{:S(2)}, u32[]{:S(2)}) collective-permute-start(f32[256,128]{1,0:T(8,128)S(1)} %collective-permute-done.6), channel_id=1, source_target_pairs={{0,4},{4,0},{8,12},{12,8},{16,20},{20,16},{24,28},{28,24},{1,5},{5... | collective-permute-start | bytes 393224 | tf_op jit(solution)/shard_map/ppermute | solution.py:18
  30.4 6.0 %collective-permute-start.8 = (f32[264,128]{1,0:T(8,128)S(1)}, f32[264,128]{1,0:T(8,128)S(1)}, u32[]{:S(2)}, u32[]{:S(2)}) collective-permute-start(f32[264,128]{1,0:T(8,128)S(1)} %maximum_maximum_fusion.4), channel_id=1, source_target_pairs={{0,16},{4,20},{8,24},{12,28},{16,0},{20,4},{24,8},{28,12},{1,17},{... | collective-permute-start | bytes 405512 | tf_op jit(solution)/shard_map/ppermute | solution.py:18
  32.0 6.4 %collective-permute-start.9 = (f32[264,128]{1,0:T(8,128)S(1)}, f32[264,128]{1,0:T(8,128)S(1)}, u32[]{:S(2)}, u32[]{:S(2)}) collective-permute-start(f32[264,128]{1,0:T(8,128)S(1)} %maximum_maximum_fusion.4), channel_id=1, source_target_pairs={{0,8},{4,12},{8,0},{12,4},{16,24},{20,28},{24,16},{28,20},{1,9},{5... | collective-permute-start | bytes 405512 | tf_op jit(solution)/shard_map/ppermute | solution.py:18
  33.4 7.1 %collective-permute-start.7 = (f32[264,128]{1,0:T(8,128)S(1)}, f32[264,128]{1,0:T(8,128)S(1)}, u32[]{:S(2)}, u32[]{:S(2)}) collective-permute-start(f32[264,128]{1,0:T(8,128)S(1)} %maximum_maximum_fusion.4), channel_id=1, source_target_pairs={{0,24},{4,28},{8,16},{12,20},{16,8},{20,12},{24,0},{28,4},{1,25},{... | collective-permute-start | bytes 405512 | tf_op jit(solution)/shard_map/ppermute | solution.py:18
  40.6 1.4 %collective-permute-start.10 = (f32[264,128]{1,0:T(8,128)S(1)}, f32[264,128]{1,0:T(8,128)S(1)}, u32[]{:S(2)}, u32[]{:S(2)}) collective-permute-start(f32[264,128]{1,0:T(8,128)S(1)} %add_add_fusion.1), channel_id=1, source_target_pairs={{0,4},{4,0},{8,12},{12,8},{16,20},{20,16},{24,28},{28,24},{1,5},{5... | collective-permute-start | bytes 405512 | tf_op jit(solution)/shard_map/ppermute | solution.py:18
  48.6 7.6 %collective-permute-start.12 = (f32[256,128]{1,0:T(8,128)S(1)}, f32[256,128]{1,0:T(8,128)S(1)}, u32[]{:S(2)}, u32[]{:S(2)}) collective-permute-start(f32[256,128]{1,0:T(8,128)S(1)} %convolution_add_fusion.7), channel_id=1, source_target_pairs={{0,1},{1,2},{2,3},{3,0},{4,5},{5,6},{6,7},{7,4},{8,9},{9,10},{10,1... | collective-permute-start | bytes 393224 | tf_op jit(solution)/shard_map/ppermute | solution.py:13
  56.7 3.7 %collective-permute-start.17 = (f32[256,128]{1,0:T(8,128)S(1)}, f32[256,128]{1,0:T(8,128)S(1)}, u32[]{:S(2)}, u32[]{:S(2)}) collective-permute-start(f32[256,128]{1,0:T(8,128)S(1)} %collective-permute-done.12), channel_id=1, source_target_pairs={{0,4},{4,0},{8,12},{12,8},{16,20},{20,16},{24,28},{28,24},{1,5},{5... | collective-permute-start | bytes 393224 | tf_op jit(solution)/shard_map/ppermute | solution.py:18
  56.9 6.0 %collective-permute-start.14 = (f32[264,128]{1,0:T(8,128)S(1)}, f32[264,128]{1,0:T(8,128)S(1)}, u32[]{:S(2)}, u32[]{:S(2)}) collective-permute-start(f32[264,128]{1,0:T(8,128)S(1)} %maximum_maximum_fusion.5), channel_id=1, source_target_pairs={{0,16},{4,20},{8,24},{12,28},{16,0},{20,4},{24,8},{28,12},{1,17},{... | collective-permute-start | bytes 405512 | tf_op jit(solution)/shard_map/ppermute | solution.py:18
  58.5 6.4 %collective-permute-start.15 = (f32[264,128]{1,0:T(8,128)S(1)}, f32[264,128]{1,0:T(8,128)S(1)}, u32[]{:S(2)}, u32[]{:S(2)}) collective-permute-start(f32[264,128]{1,0:T(8,128)S(1)} %maximum_maximum_fusion.5), channel_id=1, source_target_pairs={{0,8},{4,12},{8,0},{12,4},{16,24},{20,28},{24,16},{28,20},{1,9},{5... | collective-permute-start | bytes 405512 | tf_op jit(solution)/shard_map/ppermute | solution.py:18
  60.0 7.0 %collective-permute-start.13 = (f32[264,128]{1,0:T(8,128)S(1)}, f32[264,128]{1,0:T(8,128)S(1)}, u32[]{:S(2)}, u32[]{:S(2)}) collective-permute-start(f32[264,128]{1,0:T(8,128)S(1)} %maximum_maximum_fusion.5), channel_id=1, source_target_pairs={{0,24},{4,28},{8,16},{12,20},{16,8},{20,12},{24,0},{28,4},{1,25},{... | collective-permute-start | bytes 405512 | tf_op jit(solution)/shard_map/ppermute | solution.py:18
  67.2 1.4 %collective-permute-start.16 = (f32[264,128]{1,0:T(8,128)S(1)}, f32[264,128]{1,0:T(8,128)S(1)}, u32[]{:S(2)}, u32[]{:S(2)}) collective-permute-start(f32[264,128]{1,0:T(8,128)S(1)} %add_add_fusion), channel_id=1, source_target_pairs={{0,4},{4,0},{8,12},{12,8},{16,20},{20,16},{24,28},{28,24},{1,5},{5... | collective-permute-start | bytes 405512 | tf_op jit(solution)/shard_map/ppermute | solution.py:18
  75.1 7.3 %collective-permute-start.18 = (f32[128,256]{1,0:T(8,128)S(1)}, f32[128,256]{1,0:T(8,128)S(1)}, u32[]{:S(2)}, u32[]{:S(2)}) collective-permute-start(f32[128,256]{1,0:T(8,128)S(1)} %pad_maximum_fusion.12), channel_id=1, source_target_pairs={{0,2},{1,3},{2,0},{3,1},{4,6},{5,7},{6,4},{7,5},{8,10},{9,11},{10,... | collective-permute-start | bytes 393224 | tf_op jit(solution)/shard_map/ppermute | solution.py:13

commit v2 on v1

v2 whole, which is shorter than its diff:
```python
import functools

import jax
import jax.numpy as jnp
from jax import lax
from jax.experimental import pallas as pl
from jax.experimental.pallas import tpu as pltpu
from jax.sharding import PartitionSpec as P

STEPS = 3
EPSILON = 1e-06
F32 = jnp.float32


def shifted(value, axis, steps):
    count = lax.axis_size(axis)
    pairs = [(source, (source + steps) % count) for source in range(count)]
    return lax.ppermute(value, axis, pairs)


def swapped(value, even_bits, odd_bits):
    count = lax.axis_size("pts")
    pairs = [(source, source ^ (odd_bits if source % 2 else even_bits)) for source in range(count)]
    return lax.ppermute(value, "pts", pairs)


def chip_sum(value):
    count = lax.axis_size("pts")
    bit = 2
    while bit < count:
        if 2 * bit < count:
            rounds = [(bit, 2 * bit), (2 * bit, bit)]
        else:
            rounds = [(bit, bit)]
        for even_bits, odd_bits in rounds:
            value = value + swapped(value, even_bits, odd_bits)
        bit *= 2 ** len(rounds)
    return value


def dot_high(left, right, dims=((1,), (0,))):
    return lax.dot_general(
        left, right, (dims, ((), ())), precision=lax.Precision.HIGH, preferred_element_type=F32
    )


def two_parts(value):
    high = value.astype(jnp.bfloat16)
    return high, (value - high.astype(F32)).astype(jnp.bfloat16)


def as_left(value):
    high, low = two_parts(value)
    return jnp.concatenate([high, high, low], axis=1)


def as_right(value):
    high, low = two_parts(value)
    return jnp.concatenate([high, low, high], axis=0)


def product(left, right):
    return jnp.dot(left, right, preferred_element_type=F32)


def product_bt(left, right):
    high, low = two_parts(right)
    return lax.dot_general(
        as_left(left),
        jnp.concatenate([high, low, high], axis=1),
        (((1,), (1,)), ((), ())),
        preferred_element_type=F32,
    )


def halves_swapped(value):
    half = value.shape[0] // 2
    return jnp.concatenate([value[half:], value[:half]], axis=0)


def inverse_root(square, inverse_scale, columns):
    width = square.shape[0]
    rows = lax.broadcasted_iota(jnp.int32, (width, width), 0)
    cols = lax.broadcasted_iota(jnp.int32, (width, width), 1)
    identity = jnp.where(rows == cols, 1.0, 0.0).astype(F32)
    base = (identity + square) * inverse_scale
    base_left = as_left(base)
    second = product(base_left, as_right(base))
    first = 1.5 * identity - 0.5 * base
    first_square = 2.25 * identity - 1.5 * base + 0.25 * second
    both = 1.5 * first - 0.5 * product(as_left(1.5 * base - 0.5 * second), as_right(first_square))
    both_right = as_right(both)
    cubic_left = product(base_left, both_right)
    cubic_right = product(as_left(both), both_right[:, :columns])
    cubic = product(as_left(cubic_left), as_right(cubic_right))
    return 1.5 * both[:, :columns] - 0.5 * cubic


def joined(own, other):
    return jnp.concatenate([own, halves_swapped(other)], axis=1)


def lower_kernel(rows, columns, damp, own_sum, other_sum, upper, own, other, moved, coupling_out, scale_out):
    width = upper.shape[0]
    gram = joined(own_sum[:width], other_sum[:width])
    norms = jnp.concatenate([own_sum[width:], other_sum[width:]], axis=1)
    inverse = lax.rsqrt(norms + EPSILON)
    coupling = gram * (damp[0] * inverse.T[:, 1:2]) * inverse[0:1]
    scale = 1.0 + jnp.sum(coupling * coupling, keepdims=True)
    coupling_out[...] = coupling
    scale_out[...] = jnp.broadcast_to(scale, scale_out.shape)
    coupling_right = as_right(coupling)
    square = product(as_left(coupling.T), coupling_right)
    factor = inverse_root(square, 1.0 / scale, columns) * lax.rsqrt(scale)
    lower = joined(own[...], other[...])[:rows]
    mixed = lower + product(as_left(upper[:rows]), coupling_right)
    moved[...] = product(as_left(mixed), as_right(factor))


def upper_kernel(coupling_ref, scale_ref, upper, own, other, *rest):
    coupling = coupling_ref[...]
    scale = scale_ref[0:1, 0:1]
    factor = inverse_root(product_bt(coupling, coupling), 1.0 / scale, coupling.shape[1])
    factor = factor * lax.rsqrt(scale)
    rows = rest[-1].shape[0]
    lower = joined(own[...], other[...])[:rows]
    mixed = upper[:rows] - product_bt(lower, coupling)
    upper = product(as_left(mixed), as_right(factor))
    if len(rest) == 1:
        rest[0][...] = upper
        return
    weight, gram_left, norm_out, upper_out = rest
    upper_out[...] = upper
    weighted = weight[...] * upper
    norm_out[...] = jnp.sum(weighted * upper, axis=0, keepdims=True)[:, : norm_out.shape[1]]
    gram_left[...] = as_left(weighted.T)


def gram_kernel(gram_left, norm_upper, weight, own_ref, payload):
    width = gram_left.shape[0]
    own = own_ref[...]
    payload[:width] = product(gram_left[...], as_right(own))
    norm_lower = jnp.sum(weight[...] * own * own, axis=0, keepdims=True)
    rows = lax.broadcasted_iota(jnp.int32, (8, own.shape[1]), 0)
    payload[width:] = jnp.where(rows == 0, norm_lower, jnp.where(rows == 1, norm_upper[...], 0.0))


def in_vmem(kernel, outs, *args, scalars=0):
    specs = [pl.BlockSpec(memory_space=pltpu.SMEM)] * scalars
    specs += [pl.BlockSpec(memory_space=pltpu.VMEM)] * (len(args) - scalars)
    return pl.pallas_call(
        kernel,
        out_shape=[jax.ShapeDtypeStruct(shape, dtype) for shape, dtype in outs],
        in_specs=specs,
        out_specs=[pl.BlockSpec(memory_space=pltpu.VMEM)] * len(outs),
        compiler_params=pltpu.CompilerParams(vmem_limit_bytes=24 << 20),
    )(*args)


def body(snapshot, weights, damping):
    rows, columns = snapshot.shape
    width = columns // 2
    half = width // 2
    first_core = lax.axis_index("pts") % 2 == 0

    def own_first(block):
        left, right = block[:, :half], block[:, half:]
        return jnp.concatenate(
            [jnp.where(first_core, left, right), jnp.where(first_core, right, left)], axis=1
        )

    weight = jnp.concatenate([weights, swapped(weights, 1, 1)])[:, None]
    far = swapped(snapshot, 1, 1)
    upper = own_first(jnp.concatenate([snapshot[:, :width], far[:, :width]], axis=0))
    lower = own_first(jnp.concatenate([snapshot[:, width:], far[:, width:]], axis=0))
    own, other = lower[:, :half], halves_swapped(lower[:, half:])
    weighted = weight * upper
    gram = dot_high(weighted, own, ((0,), (0,)))
    norm_lower = jnp.sum(weight * own * own, axis=0)
    norm_upper = jnp.sum(weighted[:, :half] * upper[:, :half], axis=0)
    norms = jnp.concatenate([norm_lower[None], norm_upper[None], jnp.zeros((6, half), F32)])
    payload = jnp.concatenate([gram, norms], axis=0)
    damps = damping[:, 0].astype(F32) / (damping[:, 0] + damping[:, 1]).astype(F32)
    whole = (2 * rows, width)
    for step in range(STEPS):
        last = step + 1 == STEPS
        payload = chip_sum(payload)
        remote = swapped(payload, 1, 1)
        if step > 0:
            other = swapped(own, 1, 1)
        shape = (rows, width) if last else (2 * rows, half)
        moved, coupling, scale = in_vmem(
            functools.partial(lower_kernel, *shape),
            [(shape, F32), ((width, width), F32), ((8, 128), F32)],
            damps[step : step + 1],
            payload,
            remote,
            upper,
            own,
            other,
            scalars=1,
        )
        if last:
            moved = shifted(own_first(moved), "cols", 1 - STEPS)
            (upper,) = in_vmem(upper_kernel, [(shape, F32)], coupling, scale, upper, own, other)
            return jnp.concatenate([own_first(upper), moved], axis=1)
        gram_left, norm_upper, upper = in_vmem(
            upper_kernel,
            [((width, 6 * rows), jnp.bfloat16), ((1, half), F32), (whole, F32)],
            coupling,
            scale,
            upper,
            own,
            other,
            weight,
        )
        own = shifted(moved, "cols", 1)
        (payload,) = in_vmem(
            gram_kernel, [((width + 8, half), F32)], gram_left, norm_upper, weight, own
        )


def solution(mesh):
    placed = (P("pts", "cols"), P("pts"), P())
    return jax.shard_map(
        body, mesh=mesh, in_specs=placed, out_specs=P("pts", "cols"), check_vma=False
    )
```

time: 83.3 us -> 72.6 us (0.87)
  matrix products: 17 us -> 0.39 us
  Pallas kernels: 0 us -> 15.4 us
  between operations: 6.74 us -> 0.25 us
  other arithmetic: 4.03 us -> 1.36 us
  waiting for transfers between devices: 38.2 us -> 37.1 us
    dot_general x54 -> x1, matrix products: 17 us -> 0.39 us  [dot_high(): lax.dot_general(left, right, (dims, ((), ())), precision=lax.Precision.HI...]
    pallas_call x0 -> x8, Pallas kernels: none -> 15.4 us  [in_vmem(): pl.pallas_call(kernel, out_shape=[jax.ShapeDtypeStruct(shape, dtype) for...]
    ppermute x3, waiting for transfers between devices: 19.3 us -> 14.4 us  [shifted(): return lax.ppermute(value, axis, pairs)]
    ppermute x16 -> x13, waiting for transfers between devices: 18.9 us -> 22.7 us  [swapped(): return lax.ppermute(value, 'pts', pairs)]
    reduce_sum x6 -> x2, other arithmetic: 2.57 us -> 0.16 us  [the longest x1 0.11 us: body(): norm_lower = jnp.sum(weight * own * own, axis=0)]
    ppermute x16 -> x13, starting transfers between devices: 12.5 us -> 13.1 us  [swapped(): return lax.ppermute(value, 'pts', pairs)]
  transfers between devices with their start and end apart: 19 -> 16, of which waited for: 14 -> 12; matrix products, arithmetic and copies ran while one was open for 4% -> 3% of each run, Pallas kernels for 0% -> 8%
where the time goes in v2:
time: 72.6 us; the launch traced here: 72.4 us
  waiting for transfers between devices  37.1 us (51%)
  starting transfers between devices  15.4 us (21%)
  Pallas kernels  15.4 us (21%)
  local copies, waits for them, and re-layouts  2.57 us (4%)
  other arithmetic  1.36 us (2%)
    ppermute x13, waiting for transfers between devices, swapped(): return lax.ppermute(value, 'pts', pairs)  22.7 us
    pallas_call x8, Pallas kernels, in_vmem(): pl.pallas_call(kernel, out_shape=[jax.ShapeDtypeStruct(shape, dtype) for...  15.4 us
    ppermute x3, waiting for transfers between devices, shifted(): return lax.ppermute(value, axis, pairs)  14.4 us
    ppermute x13, starting transfers between devices, swapped(): return lax.ppermute(value, 'pts', pairs)  13.1 us
    ppermute x3, starting transfers between devices, shifted(): return lax.ppermute(value, axis, pairs)  2.25 us
  transfers between devices with their start and end apart: 16, of which 12 were waited for; matrix products, arithmetic and copies ran while one was open for 3% of the time, Pallas kernels for 8%

profile of v2, /device:TPU:0, one launch (start us, length us, event | category | flops | bytes accessed | tf_op | source)
XLA Modules:
  0.0 72.4 jit_solution(4485498825381313771)
XLA Ops:
  3.1 3.0 %collective-permute-start.2 = (f32[264,128]{1,0:T(8,128)S(1)}, f32[264,128]{1,0:T(8,128)S(1)}, u32[]{:S(2)}, u32[]{:S(2)}) collective-permute-start(f32[264,128]{1,0:T(8,128)S(1)} %maximum_maximum_fusion), channel_id=1, source_target_pairs={{0,8},{4,20},{8,0},{12,28},{16,24},{20,4},{24,16},{28,12},{1,9},{5... | collective-permute-start | bytes 405512 | tf_op jit(solution)/shard_map/ppermute | solution.py:24
  6.1 3.0 %collective-permute-done.2 = f32[264,128]{1,0:T(8,128)S(1)} collective-permute-done((f32[264,128]{1,0:T(8,128)S(1)}, f32[264,128]{1,0:T(8,128)S(1)}, u32[]{:S(2)}, u32[]{:S(2)}) %collective-permute-start.2) | collective-permute-done | bytes 135200 | tf_op jit(solution)/shard_map/ppermute | solution.py:24
  9.2 2.1 %collective-permute-start.3 = (f32[264,128]{1,0:T(8,128)S(1)}, f32[264,128]{1,0:T(8,128)S(1)}, u32[]{:S(2)}, u32[]{:S(2)}) collective-permute-start(f32[264,128]{1,0:T(8,128)S(1)} %fusion.4), channel_id=1, source_target_pairs={{0,16},{4,12},{8,24},{12,4},{16,0},{20,28},{24,8},{28,20},{1,17},{... | collective-permute-start | bytes 405512 | tf_op jit(solution)/shard_map/ppermute | solution.py:24
  12.0 2.3 %collective-permute-done.3 = f32[264,128]{1,0:T(8,128)S(1)} collective-permute-done((f32[264,128]{1,0:T(8,128)S(1)}, f32[264,128]{1,0:T(8,128)S(1)}, u32[]{:S(2)}, u32[]{:S(2)}) %collective-permute-start.3) | collective-permute-done | bytes 135200 | tf_op jit(solution)/shard_map/ppermute | solution.py:24
  14.5 1.3 %collective-permute-done.4.other_sum = f32[264,128]{1,0:T(8,128)S(1)} collective-permute-done((f32[264,128]{1,0:T(8,128)S(1)}, f32[264,128]{1,0:T(8,128)S(1)}, u32[]{:S(2)}, u32[]{:S(2)}) %collective-permute-start.4) | collective-permute-done | bytes 135200 | tf_op jit(solution)/shard_map/ppermute | solution.py:24
  15.8 3.0 %shard_map.37 = (f32[256,128]{1,0:T(8,128)S(1)}, f32[256,256]{1,0:T(8,128)S(1)}, f32[8,128]{1,0:T(8,128)S(1)}) custom-call(f32[1]{0:T(128)} %bitcast.2.damp, f32[264,128]{1,0:T(8,128)S(1)} %add.29.own_sum, f32[264,128]{1,0:T(8,128)S(1)} %collective-permute-done.4.other_sum, f32[256,256]{1,0:T(8,128)S(1)} %get-tuple-element.38.upper, ...), custom_call_target="tpu_custom_call" | custom-call | tf_op jit(solution)/shard_map/pallas_call | solution.py:151
  18.8 2.1 %collective-permute-start.5 = (f32[256,128]{1,0:T(8,128)S(1)}, f32[256,128]{1,0:T(8,128)S(1)}, u32[]{:S(2)}, u32[]{:S(2)}) collective-permute-start(f32[256,128]{1,0:T(8,128)S(1)} %get-tuple-element.24), channel_id=1, source_target_pairs={{0,1},{1,2},{2,3},{3,0},{4,5},{5,6},{6,7},{7,4},{8,9},{9,10},{10,1... | collective-permute-start | bytes 393224 | tf_op jit(solution)/shard_map/ppermute | solution.py:18
  21.1 2.1 %shard_map.38 = (bf16[256,768]{1,0:T(8,128)(2,1)S(1)}, f32[1,128]{1,0:T(1,128)S(1)}, f32[256,256]{1,0:T(8,128)S(1)}) custom-call(f32[256,256]{1,0:T(8,128)S(1)} %get-tuple-element.20.coupling_ref, f32[8,128]{1,0:T(8,128)S(1)} %get-tuple-element.21.scale_ref, f32[256,256]{1,0:T(8,128)S(1)} %get-tuple-element.38.upper, f32[256,128]{1,0:T(8,128)S(1)} %get-tuple-element.36.own, ...), custom_call_target="tpu_custom_call" | custom-call | tf_op jit(solution)/shard_map/pallas_call | solution.py:151
  23.2 3.6 %collective-permute-done.5.own_ref.own = f32[256,128]{1,0:T(8,128)S(1)} collective-permute-done((f32[256,128]{1,0:T(8,128)S(1)}, f32[256,128]{1,0:T(8,128)S(1)}, u32[]{:S(2)}, u32[]{:S(2)}) %collective-permute-start.5) | collective-permute-done | bytes 131104 | tf_op jit(solution)/shard_map/ppermute | solution.py:18
  27.0 1.6 %collective-permute-start.6 = (f32[264,128]{1,0:T(8,128)S(1)}, f32[264,128]{1,0:T(8,128)S(1)}, u32[]{:S(2)}, u32[]{:S(2)}) collective-permute-start(f32[264,128]{1,0:T(8,128)S(1)} %shard_map.39), channel_id=1, source_target_pairs={{0,8},{4,20},{8,0},{12,28},{16,24},{20,4},{24,16},{28,12},{1,9},{5... | collective-permute-start | bytes 405512 | tf_op jit(solution)/shard_map/ppermute | solution.py:24
  28.6 3.5 %collective-permute-done.6 = f32[264,128]{1,0:T(8,128)S(1)} collective-permute-done((f32[264,128]{1,0:T(8,128)S(1)}, f32[264,128]{1,0:T(8,128)S(1)}, u32[]{:S(2)}, u32[]{:S(2)}) %collective-permute-start.6) | collective-permute-done | bytes 135200 | tf_op jit(solution)/shard_map/ppermute | solution.py:24
  32.1 1.6 %collective-permute-start.7 = (f32[264,128]{1,0:T(8,128)S(1)}, f32[264,128]{1,0:T(8,128)S(1)}, u32[]{:S(2)}, u32[]{:S(2)}) collective-permute-start(f32[264,128]{1,0:T(8,128)S(1)} %add.30), channel_id=1, source_target_pairs={{0,16},{4,12},{8,24},{12,4},{16,0},{20,28},{24,8},{28,20},{1,17},{... | collective-permute-start | bytes 405512 | tf_op jit(solution)/shard_map/ppermute | solution.py:24
  33.7 3.5 %collective-permute-done.7 = f32[264,128]{1,0:T(8,128)S(1)} collective-permute-done((f32[264,128]{1,0:T(8,128)S(1)}, f32[264,128]{1,0:T(8,128)S(1)}, u32[]{:S(2)}, u32[]{:S(2)}) %collective-permute-start.7) | collective-permute-done | bytes 135200 | tf_op jit(solution)/shard_map/ppermute | solution.py:24
  37.8 1.0 %collective-permute-done.9.other = f32[256,128]{1,0:T(8,128)S(1)} collective-permute-done((f32[256,128]{1,0:T(8,128)S(1)}, f32[256,128]{1,0:T(8,128)S(1)}, u32[]{:S(2)}, u32[]{:S(2)}) %collective-permute-start.9) | collective-permute-done | bytes 131104 | tf_op jit(solution)/shard_map/ppermute | solution.py:24
  38.8 2.9 %shard_map.40 = (f32[256,128]{1,0:T(8,128)S(1)}, f32[256,256]{1,0:T(8,128)S(1)}, f32[8,128]{1,0:T(8,128)S(1)}) custom-call(f32[1]{0:T(128)} %bitcast.1.damp, f32[264,128]{1,0:T(8,128)S(1)} %add.31.own_sum, f32[264,128]{1,0:T(8,128)S(1)} %collective-permute-done.8.other_sum, f32[256,256]{1,0:T(8,128)S(1)} %get-tuple-element.25.upper, ...), custom_call_target="tpu_custom_call" | custom-call | tf_op jit(solution)/shard_map/pallas_call | solution.py:151
  41.8 2.1 %shard_map.41 = (bf16[256,768]{1,0:T(8,128)(2,1)S(1)}, f32[1,128]{1,0:T(1,128)S(1)}, f32[256,256]{1,0:T(8,128)S(1)}) custom-call(f32[256,256]{1,0:T(8,128)S(1)} %get-tuple-element.26.coupling_ref, f32[8,128]{1,0:T(8,128)S(1)} %get-tuple-element.27.scale_ref, f32[256,256]{1,0:T(8,128)S(1)} %get-tuple-element.25.upper, ...), custom_call_target="tpu_custom_call" | custom-call | tf_op jit(solution)/shard_map/pallas_call | solution.py:151
  43.9 5.4 %collective-permute-done.10.own_ref.own = f32[256,128]{1,0:T(8,128)S(1)} collective-permute-done((f32[256,128]{1,0:T(8,128)S(1)}, f32[256,128]{1,0:T(8,128)S(1)}, u32[]{:S(2)}, u32[]{:S(2)}) %collective-permute-start.10) | collective-permute-done | bytes 131104 | tf_op jit(solution)/shard_map/ppermute | solution.py:18
  49.6 1.6 %collective-permute-start.11 = (f32[264,128]{1,0:T(8,128)S(1)}, f32[264,128]{1,0:T(8,128)S(1)}, u32[]{:S(2)}, u32[]{:S(2)}) collective-permute-start(f32[264,128]{1,0:T(8,128)S(1)} %shard_map.42), channel_id=1, source_target_pairs={{0,8},{4,20},{8,0},{12,28},{16,24},{20,4},{24,16},{28,12},{1,9},{5... | collective-permute-start | bytes 405512 | tf_op jit(solution)/shard_map/ppermute | solution.py:24
  51.1 3.5 %collective-permute-done.11 = f32[264,128]{1,0:T(8,128)S(1)} collective-permute-done((f32[264,128]{1,0:T(8,128)S(1)}, f32[264,128]{1,0:T(8,128)S(1)}, u32[]{:S(2)}, u32[]{:S(2)}) %collective-permute-start.11) | collective-permute-done | bytes 135200 | tf_op jit(solution)/shard_map/ppermute | solution.py:24
  54.7 1.6 %collective-permute-start.12 = (f32[264,128]{1,0:T(8,128)S(1)}, f32[264,128]{1,0:T(8,128)S(1)}, u32[]{:S(2)}, u32[]{:S(2)}) collective-permute-start(f32[264,128]{1,0:T(8,128)S(1)} %add.32), channel_id=1, source_target_pairs={{0,16},{4,12},{8,24},{12,4},{16,0},{20,28},{24,8},{28,20},{1,17},{... | collective-permute-start | bytes 405512 | tf_op jit(solution)/shard_map/ppermute | solution.py:24
  56.3 3.5 %collective-permute-done.12 = f32[264,128]{1,0:T(8,128)S(1)} collective-permute-done((f32[264,128]{1,0:T(8,128)S(1)}, f32[264,128]{1,0:T(8,128)S(1)}, u32[]{:S(2)}, u32[]{:S(2)}) %collective-permute-start.12) | collective-permute-done | bytes 135200 | tf_op jit(solution)/shard_map/ppermute | solution.py:24
  61.4 2.8 %shard_map.43 = (f32[128,256]{1,0:T(8,128)S(1)}, f32[256,256]{1,0:T(8,128)S(1)}, f32[8,128]{1,0:T(8,128)S(1)}) custom-call(f32[1]{0:T(128)} %bitcast.damp, f32[264,128]{1,0:T(8,128)S(1)} %add.33.own_sum, f32[264,128]{1,0:T(8,128)S(1)} %collective-permute-done.13.other_sum, f32[256,256]{1,0:T(8,128)S(1)} %get-tuple-element.31.upper, ...), custom_call_target="tpu_custom_call" | custom-call | tf_op jit(solution)/shard_map/pallas_call | solution.py:151
  64.3 1.9 %shard_map.44 = f32[128,256]{1,0:T(8,128)S(1)} custom-call(f32[256,256]{1,0:T(8,128)S(1)} %get-tuple-element.32.coupling_ref, f32[8,128]{1,0:T(8,128)S(1)} %get-tuple-element.33.scale_ref, f32[256,256]{1,0:T(8,128)S(1)} %get-tuple-element.31.upper, f32[256,128]{1,0:T(8,128)S(1)} %collective-permute-done.10.own_ref.own, ...), custom_call_target="tpu_custom_call" | custom-call | tf_op jit(solution)/shard_map/pallas_call | solution.py:151
  66.3 5.4 %collective-permute-done.15 = f32[128,256]{1,0:T(8,128)S(1)} collective-permute-done((f32[128,256]{1,0:T(8,128)S(1)}, f32[128,256]{1,0:T(8,128)S(1)}, u32[]{:S(2)}, u32[]{:S(2)}) %collective-permute-start.15) | collective-permute-done | bytes 131104 | tf_op jit(solution)/shard_map/ppermute | solution.py:18
  (48 shorter events, 7.7 us)
Async XLA Ops:
  0.0 2.3 %collective-permute-start = (f32[128]{0:T(128)}, f32[128]{0:T(128)S(1)}, u32[]{:S(2)}, u32[]{:S(2)}) collective-permute-start(f32[128]{0:T(128)} %param.4), channel_id=1, source_target_pairs={{0,4},{4,0},{8,12},{12,8},{16,20},{20,16},{24,28},{28,24},{1,5},{5... | collective-permute-start | bytes 1544 | tf_op jit(solution)/shard_map/ppermute | solution.py:24
  0.5 1.8 %collective-permute-start.1 = (f32[128,512]{1,0:T(8,128)}, f32[128,512]{1,0:T(8,128)S(1)}, u32[]{:S(2)}, u32[]{:S(2)}) collective-permute-start(f32[128,512]{1,0:T(8,128)} %param.3), channel_id=1, source_target_pairs={{0,4},{4,0},{8,12},{12,8},{16,20},{20,16},{24,28},{28,24},{1,5},{5... | collective-permute-start | bytes 786440 | tf_op jit(solution)/shard_map/ppermute | solution.py:24
  1.5 0.7 copy-start.1
  3.1 8.2 %copy-start = (s32[3,2]{0,1:T(2,128)S(1)}, s32[3,2]{0,1:T(2,128)}, u32[]{:S(2)}) copy-start(s32[3,2]{0,1:T(2,128)} %param.5) | copy-start | bytes 76
  3.1 6.0 %collective-permute-start.2 = (f32[264,128]{1,0:T(8,128)S(1)}, f32[264,128]{1,0:T(8,128)S(1)}, u32[]{:S(2)}, u32[]{:S(2)}) collective-permute-start(f32[264,128]{1,0:T(8,128)S(1)} %maximum_maximum_fusion), channel_id=1, source_target_pairs={{0,8},{4,20},{8,0},{12,28},{16,24},{20,4},{24,16},{28,12},{1,9},{5... | collective-permute-start | bytes 405512 | tf_op jit(solution)/shard_map/ppermute | solution.py:24
  9.2 5.1 %collective-permute-start.3 = (f32[264,128]{1,0:T(8,128)S(1)}, f32[264,128]{1,0:T(8,128)S(1)}, u32[]{:S(2)}, u32[]{:S(2)}) collective-permute-start(f32[264,128]{1,0:T(8,128)S(1)} %fusion.4), channel_id=1, source_target_pairs={{0,16},{4,12},{8,24},{12,4},{16,0},{20,28},{24,8},{28,20},{1,17},{... | collective-permute-start | bytes 405512 | tf_op jit(solution)/shard_map/ppermute | solution.py:24
  14.4 1.4 %collective-permute-start.4 = (f32[264,128]{1,0:T(8,128)S(1)}, f32[264,128]{1,0:T(8,128)S(1)}, u32[]{:S(2)}, u32[]{:S(2)}) collective-permute-start(f32[264,128]{1,0:T(8,128)S(1)} %add.29.own_sum), channel_id=1, source_target_pairs={{0,4},{4,0},{8,12},{12,8},{16,20},{20,16},{24,28},{28,24},{1,5},{5... | collective-permute-start | bytes 405512 | tf_op jit(solution)/shard_map/ppermute | solution.py:24
  18.8 8.0 %collective-permute-start.5 = (f32[256,128]{1,0:T(8,128)S(1)}, f32[256,128]{1,0:T(8,128)S(1)}, u32[]{:S(2)}, u32[]{:S(2)}) collective-permute-start(f32[256,128]{1,0:T(8,128)S(1)} %get-tuple-element.24), channel_id=1, source_target_pairs={{0,1},{1,2},{2,3},{3,0},{4,5},{5,6},{6,7},{7,4},{8,9},{9,10},{10,1... | collective-permute-start | bytes 393224 | tf_op jit(solution)/shard_map/ppermute | solution.py:18
  27.0 5.1 %collective-permute-start.6 = (f32[264,128]{1,0:T(8,128)S(1)}, f32[264,128]{1,0:T(8,128)S(1)}, u32[]{:S(2)}, u32[]{:S(2)}) collective-permute-start(f32[264,128]{1,0:T(8,128)S(1)} %shard_map.39), channel_id=1, source_target_pairs={{0,8},{4,20},{8,0},{12,28},{16,24},{20,4},{24,16},{28,12},{1,9},{5... | collective-permute-start | bytes 405512 | tf_op jit(solution)/shard_map/ppermute | solution.py:24
  32.1 5.1 %collective-permute-start.7 = (f32[264,128]{1,0:T(8,128)S(1)}, f32[264,128]{1,0:T(8,128)S(1)}, u32[]{:S(2)}, u32[]{:S(2)}) collective-permute-start(f32[264,128]{1,0:T(8,128)S(1)} %add.30), channel_id=1, source_target_pairs={{0,16},{4,12},{8,24},{12,4},{16,0},{20,28},{24,8},{28,20},{1,17},{... | collective-permute-start | bytes 405512 | tf_op jit(solution)/shard_map/ppermute | solution.py:24
  37.2 1.6 %collective-permute-start.8 = (f32[264,128]{1,0:T(8,128)S(1)}, f32[264,128]{1,0:T(8,128)S(1)}, u32[]{:S(2)}, u32[]{:S(2)}) collective-permute-start(f32[264,128]{1,0:T(8,128)S(1)} %add.31.own_sum), channel_id=1, source_target_pairs={{0,4},{4,0},{8,12},{12,8},{16,20},{20,16},{24,28},{28,24},{1,5},{5... | collective-permute-start | bytes 405512 | tf_op jit(solution)/shard_map/ppermute | solution.py:24
  37.3 1.5 %collective-permute-start.9 = (f32[256,128]{1,0:T(8,128)S(1)}, f32[256,128]{1,0:T(8,128)S(1)}, u32[]{:S(2)}, u32[]{:S(2)}) collective-permute-start(f32[256,128]{1,0:T(8,128)S(1)} %collective-permute-done.5.own_ref.own), channel_id=1, source_target_pairs={{0,4},{4,0},{8,12},{12,8},{16,20},{20,16},{24,28},{28,24},{1,5},{5... | collective-permute-start | bytes 393224 | tf_op jit(solution)/shard_map/ppermute | solution.py:24
  41.8 7.6 %collective-permute-start.10 = (f32[256,128]{1,0:T(8,128)S(1)}, f32[256,128]{1,0:T(8,128)S(1)}, u32[]{:S(2)}, u32[]{:S(2)}) collective-permute-start(f32[256,128]{1,0:T(8,128)S(1)} %get-tuple-element.30), channel_id=1, source_target_pairs={{0,1},{1,2},{2,3},{3,0},{4,5},{5,6},{6,7},{7,4},{8,9},{9,10},{10,1... | collective-permute-start | bytes 393224 | tf_op jit(solution)/shard_map/ppermute | solution.py:18
  49.6 5.1 %collective-permute-start.11 = (f32[264,128]{1,0:T(8,128)S(1)}, f32[264,128]{1,0:T(8,128)S(1)}, u32[]{:S(2)}, u32[]{:S(2)}) collective-permute-start(f32[264,128]{1,0:T(8,128)S(1)} %shard_map.42), channel_id=1, source_target_pairs={{0,8},{4,20},{8,0},{12,28},{16,24},{20,4},{24,16},{28,12},{1,9},{5... | collective-permute-start | bytes 405512 | tf_op jit(solution)/shard_map/ppermute | solution.py:24
  54.7 5.1 %collective-permute-start.12 = (f32[264,128]{1,0:T(8,128)S(1)}, f32[264,128]{1,0:T(8,128)S(1)}, u32[]{:S(2)}, u32[]{:S(2)}) collective-permute-start(f32[264,128]{1,0:T(8,128)S(1)} %add.32), channel_id=1, source_target_pairs={{0,16},{4,12},{8,24},{12,4},{16,0},{20,28},{24,8},{28,20},{1,17},{... | collective-permute-start | bytes 405512 | tf_op jit(solution)/shard_map/ppermute | solution.py:24
  59.8 1.6 %collective-permute-start.13 = (f32[264,128]{1,0:T(8,128)S(1)}, f32[264,128]{1,0:T(8,128)S(1)}, u32[]{:S(2)}, u32[]{:S(2)}) collective-permute-start(f32[264,128]{1,0:T(8,128)S(1)} %add.33.own_sum), channel_id=1, source_target_pairs={{0,4},{4,0},{8,12},{12,8},{16,20},{20,16},{24,28},{28,24},{1,5},{5... | collective-permute-start | bytes 405512 | tf_op jit(solution)/shard_map/ppermute | solution.py:24
  59.9 1.5 %collective-permute-start.14 = (f32[256,128]{1,0:T(8,128)S(1)}, f32[256,128]{1,0:T(8,128)S(1)}, u32[]{:S(2)}, u32[]{:S(2)}) collective-permute-start(f32[256,128]{1,0:T(8,128)S(1)} %collective-permute-done.10.own_ref.own), channel_id=1, source_target_pairs={{0,4},{4,0},{8,12},{12,8},{16,20},{20,16},{24,28},{28,24},{1,5},{5... | collective-permute-start | bytes 393224 | tf_op jit(solution)/shard_map/ppermute | solution.py:24
  64.3 7.4 %collective-permute-start.15 = (f32[128,256]{1,0:T(8,128)S(1)}, f32[128,256]{1,0:T(8,128)S(1)}, u32[]{:S(2)}, u32[]{:S(2)}) collective-permute-start(f32[128,256]{1,0:T(8,128)S(1)} %pad_maximum_fusion.5), channel_id=1, source_target_pairs={{0,2},{1,3},{2,0},{3,1},{4,6},{5,7},{6,4},{7,5},{8,10},{9,11},{10,... | collective-permute-start | bytes 393224 | tf_op jit(solution)/shard_map/ppermute | solution.py:18

commit v3 on v2

v3 whole, which is shorter than its diff:
```python
import functools

import jax
import jax.numpy as jnp
from jax import lax
from jax.experimental import pallas as pl
from jax.experimental.pallas import tpu as pltpu
from jax.sharding import PartitionSpec as P

STEPS = 3
EPSILON = 1e-06
F32 = jnp.float32


def shifted(value, axis, steps):
    count = lax.axis_size(axis)
    pairs = [(source, (source + steps) % count) for source in range(count)]
    return lax.ppermute(value, axis, pairs)


def swapped(value, even_bits, odd_bits):
    count = lax.axis_size("pts")
    pairs = [(source, source ^ (odd_bits if source % 2 else even_bits)) for source in range(count)]
    return lax.ppermute(value, "pts", pairs)


def chip_sum(value, beside=None):
    count = lax.axis_size("pts")
    bit = 2
    while bit < count:
        if 2 * bit < count:
            rounds = [(bit, 2 * bit), (2 * bit, bit)]
        else:
            rounds = [(bit, bit)]
        for even_bits, odd_bits in rounds:
            value = value + swapped(value, even_bits, odd_bits)
            if beside is not None:
                value, beside = lax.optimization_barrier((value, beside))
        bit *= 2 ** len(rounds)
    return value, beside


def two_parts(value):
    high = value.astype(jnp.bfloat16)
    return high, (value - high.astype(F32)).astype(jnp.bfloat16)


def as_left(value):
    high, low = two_parts(value)
    return jnp.concatenate([high, high, low], axis=1)


def as_right(value):
    high, low = two_parts(value)
    return jnp.concatenate([high, low, high], axis=0)


def product(left, right):
    return jnp.dot(left, right, preferred_element_type=F32)


def product_tl(left, right):
    high, low = two_parts(left)
    return lax.dot_general(
        jnp.concatenate([high, high, low], axis=0),
        right,
        (((0,), (0,)), ((), ())),
        preferred_element_type=F32,
    )


def product_bt(left, right):
    high, low = two_parts(right)
    return lax.dot_general(
        as_left(left),
        jnp.concatenate([high, low, high], axis=1),
        (((1,), (1,)), ((), ())),
        preferred_element_type=F32,
    )


def halves_swapped(value):
    half = value.shape[0] // 2
    return jnp.concatenate([value[half:], value[:half]], axis=0)


def unit(width):
    rows = lax.broadcasted_iota(jnp.int32, (width, width), 0)
    columns = lax.broadcasted_iota(jnp.int32, (width, width), 1)
    return jnp.where(rows == columns, 1.0, 0.0).astype(F32)


def times_inverse_root(left, square, scale, columns):
    identity = unit(square.shape[0])
    base = (identity + square) * (1.0 / scale)
    base_right = as_right(base)
    left_parts = as_left(left)
    second = product(as_left(base), base_right)
    left_base = product(left_parts, base_right)
    first_square = 2.25 * identity - 1.5 * base + 0.25 * second
    both = 2.25 * identity - 0.75 * base
    both = both - 0.5 * product(as_left(1.5 * base - 0.5 * second), as_right(first_square))
    both_right = as_right(both)
    both_square = product(as_left(both), both_right[:, :columns])
    left_both = product(left_parts, both_right[:, :columns])
    left_cubic = product(as_left(product(as_left(left_base), both_right)), as_right(both_square))
    return (1.5 * left_both - 0.5 * left_cubic) * lax.rsqrt(scale)


def joined(own, other):
    return jnp.concatenate([own, halves_swapped(other)], axis=1)


def own_half(half):
    own = (lax.axis_index("pts") % 2) * half
    return pl.multiple_of(own, half), pl.multiple_of(half - own, half)


def start_blocks(near, far):
    width = near.shape[1] // 2
    own, other = own_half(width // 2)

    def taken(start):
        piece = (slice(None), pl.ds(start, width // 2))
        return jnp.concatenate([near[piece], far[piece]], axis=0)

    upper = jnp.concatenate([taken(own), taken(other)], axis=1)
    return upper, jnp.concatenate([taken(width + own), taken(width + other)], axis=1)


def later_blocks(upper, own, other):
    return upper[...], joined(own[...], other[...])


def stored(ref, value):
    half = ref.shape[1] // 2
    own, other = own_half(half)
    ref[:, pl.ds(own, half)] = value[:, :half]
    ref[:, pl.ds(other, half)] = value[:, half:]


def start_kernel(near, weight, own_part, other_part):
    width = near.shape[1] // 2
    half = width // 2
    own, other = own_half(half)
    point_weight = jnp.broadcast_to(weight[...], (8, weight.shape[1])).T[:, 0:1]
    upper_own, upper_other = near[:, pl.ds(own, half)], near[:, pl.ds(other, half)]
    upper = jnp.concatenate([upper_own, upper_other], axis=1)
    rows = lax.broadcasted_iota(jnp.int32, (8, half), 0)
    for start, norm_of, out in ((own, upper_own, own_part), (other, upper_other, other_part)):
        lower = near[:, pl.ds(width + start, half)]
        weighted = point_weight * lower
        gram = product_tl(upper, as_right(weighted))
        out[:width] = gram if out is own_part else halves_swapped(gram)
        norm_lower = jnp.sum(weighted * lower, axis=0, keepdims=True)
        norm_upper = jnp.sum(point_weight * norm_of * norm_of, axis=0, keepdims=True)
        out[width:] = jnp.where(rows == 0, norm_lower, jnp.where(rows == 1, norm_upper, 0.0))


def lower_kernel(blocks, last, damp, own_sum, other_sum, *refs):
    *block_refs, moved, coupling_out, scale_out = refs
    width = coupling_out.shape[0]
    upper, lower = blocks(*block_refs)
    gram = joined(own_sum[:width], other_sum[:width])
    norms = jnp.concatenate([own_sum[width:], other_sum[width:]], axis=1)
    inverse = lax.rsqrt(norms + EPSILON)
    coupling = gram * (damp[0:1, 0:1] * inverse.T[:, 1:2]) * inverse[0:1]
    scale = 1.0 + jnp.sum(coupling * coupling, keepdims=True)
    coupling_out[...] = coupling
    scale_out[...] = jnp.broadcast_to(scale, scale_out.shape)
    coupling_right = as_right(coupling)
    square = product_tl(coupling, coupling_right)
    rows, columns = moved.shape
    mixed = lower[:rows] + product(as_left(upper[:rows]), coupling_right)
    result = times_inverse_root(mixed, square, scale, columns)
    if last:
        stored(moved, result)
    else:
        moved[...] = result


def rotated_upper(blocks, rows, coupling_ref, scale_ref, *block_refs):
    coupling = coupling_ref[...]
    upper, lower = blocks(*block_refs)
    mixed = upper[:rows] - product_bt(lower[:rows], coupling)
    square = product_bt(coupling, coupling)
    return times_inverse_root(mixed, square, scale_ref[0:1, 0:1], coupling.shape[1])


def upper_kernel(blocks, weight, *refs):
    *ins, gram_left, norm_out, upper_out = refs
    upper = rotated_upper(blocks, upper_out.shape[0], *ins)
    upper_out[...] = upper
    weighted = weight[...] * upper
    norm_out[...] = jnp.sum(weighted * upper, axis=0, keepdims=True)[:, : norm_out.shape[1]]
    gram_left[...] = as_left(weighted.T)


def last_upper_kernel(blocks, *refs):
    *ins, out, held, sent = refs
    stored(held, rotated_upper(blocks, held.shape[0], *ins))
    copy = pltpu.make_async_copy(held, out.at[:, pl.ds(0, held.shape[1])], sent)
    copy.start()
    copy.wait()


def last_lower_kernel(lower, filled, out, sent):
    del filled
    width = lower.shape[1]
    copy = pltpu.make_async_copy(lower, out.at[:, pl.ds(width, width)], sent)
    copy.start()
    copy.wait()


def gram_kernel(gram_left, norm_upper, weight, own_ref, payload):
    width = gram_left.shape[0]
    own = own_ref[...]
    payload[:width] = product(gram_left[...], as_right(own))
    norm_lower = jnp.sum(weight[...] * own * own, axis=0, keepdims=True)
    rows = lax.broadcasted_iota(jnp.int32, (8, own.shape[1]), 0)
    payload[width:] = jnp.where(rows == 0, norm_lower, jnp.where(rows == 1, norm_upper[...], 0.0))


ON_CHIP = pl.BlockSpec(memory_space=pltpu.VMEM)
ANYWHERE = pl.BlockSpec(memory_space=pl.ANY)
GRANT = pltpu.CompilerParams(vmem_limit_bytes=24 << 20)


def in_vmem(kernel, outs, *args):
    return pl.pallas_call(
        kernel,
        out_shape=[jax.ShapeDtypeStruct(shape, dtype) for shape, dtype in outs],
        in_specs=[ON_CHIP] * len(args),
        out_specs=[ON_CHIP] * len(outs),
        compiler_params=GRANT,
    )(*args)


def body(snapshot, weights, damping):
    rows, columns = snapshot.shape
    width = columns // 2
    half = width // 2
    whole = (2 * rows, width)
    own_part, other_part = in_vmem(start_kernel, [((width + 8, half), F32)] * 2, snapshot, weights[None])
    payload = own_part + swapped(other_part, 1, 1)
    weight = jnp.concatenate([weights, swapped(weights, 1, 1)])[:, None]
    blocks, held, arriving = start_blocks, (snapshot,), swapped(snapshot, 1, 1)
    damps = damping[:, 0].astype(F32) / (damping[:, 0] + damping[:, 1]).astype(F32)
    damps = jnp.broadcast_to(damps[:, None], (STEPS, 128))
    for step in range(STEPS):
        last = step + 1 == STEPS
        payload, arriving = chip_sum(payload, arriving)
        held = held + (arriving,)
        moved, coupling, scale = in_vmem(
            functools.partial(lower_kernel, blocks, last),
            [((rows, width) if last else (2 * rows, half), F32), ((width, width), F32), ((8, 128), F32)],
            damps[step : step + 1],
            payload,
            swapped(payload, 1, 1),
            *held,
        )
        if last:
            break
        moved = shifted(moved, "cols", 1)
        gram_left, norm_upper, upper = in_vmem(
            functools.partial(upper_kernel, blocks),
            [((width, 6 * rows), jnp.bfloat16), ((1, half), F32), (whole, F32)],
            weight,
            coupling,
            scale,
            *held,
        )
        blocks, held, arriving = later_blocks, (upper, moved), swapped(moved, 1, 1)
        (payload,) = in_vmem(gram_kernel, [((width + 8, half), F32)], gram_left, norm_upper, weight, moved)
    moved = shifted(moved, "cols", 1 - STEPS)
    out_shape = jax.ShapeDtypeStruct((rows, columns), F32)
    rotated = pl.pallas_call(
        functools.partial(last_upper_kernel, blocks),
        out_shape=out_shape,
        in_specs=[ON_CHIP] * (2 + len(held)),
        out_specs=ANYWHERE,
        scratch_shapes=[pltpu.VMEM((rows, width), F32), pltpu.SemaphoreType.DMA(())],
        compiler_params=GRANT,
    )(coupling, scale, *held)
    return pl.pallas_call(
        last_lower_kernel,
        out_shape=out_shape,
        in_specs=[ON_CHIP, ANYWHERE],
        out_specs=ANYWHERE,
        scratch_shapes=[pltpu.SemaphoreType.DMA(())],
        input_output_aliases={1: 0},
        compiler_params=GRANT,
    )(moved, rotated)


def solution(mesh):
    placed = (P("pts", "cols"), P("pts"), P())
    return jax.shard_map(
        body, mesh=mesh, in_specs=placed, out_specs=P("pts", "cols"), check_vma=False
    )
```

time: 72.6 us -> 71.7 us (0.988)
  local copies, waits for them, and re-layouts: 2.57 us -> 4.43 us
  other arithmetic: 1.36 us -> 0.16 us
  Pallas kernels: 15.4 us -> 14.3 us
  starting transfers between devices: 15.4 us -> 14.4 us
  waiting for transfers between devices: 37.1 us -> 38 us
    pallas_call x8, Pallas kernels: 15.4 us -> 11.3 us  [in_vmem(): pl.pallas_call(kernel, out_shape=[jax.ShapeDtypeStruct(shape, dtype) for...]
    pallas_call x0 -> x2, Pallas kernels: none -> 3.06 us  [the longest x1 2.39 us: body(): pl.pallas_call(functools.partial(last_upper_kernel, blocks), out_shape=ou...]
    ppermute x13 -> x14, waiting for transfers between devices: 22.7 us -> 25.4 us  [swapped(): return lax.ppermute(value, 'pts', pairs)]
    broadcast_in_dim x1 -> x3, local copies, waits for them, and re-layouts: 0.01 us -> 2.01 us  [body(): damps = jnp.broadcast_to(damps[:, None], (STEPS, 128))]
    ppermute x3, waiting for transfers between devices: 14.4 us -> 12.6 us  [shifted(): return lax.ppermute(value, axis, pairs)]
    slice x3 -> x0, local copies, waits for them, and re-layouts: 1.02 us -> none  [the longest x1 0.99 us: body(): snapshot[:, width:]]
    ppermute x13 -> x14, starting transfers between devices: 13.1 us -> 12.1 us  [swapped(): return lax.ppermute(value, 'pts', pairs)]
    unnamed x5 -> x8, local copies, waits for them, and re-layouts: 0.67 us -> 1.62 us
  transfers between devices with their start and end apart: 16 -> 17, of which waited for: 12 -> 14; matrix products, arithmetic and copies ran while one was open for 3% -> 1% of each run, Pallas kernels for 8% -> 9%
where the time goes in v3:
time: 71.7 us; the launch traced here: 71.5 us
  waiting for transfers between devices  38 us (53%)
  starting transfers between devices  14.4 us (20%)
  Pallas kernels  14.3 us (20%)
  local copies, waits for them, and re-layouts  4.43 us (6%)
    ppermute x14, waiting for transfers between devices, swapped(): return lax.ppermute(value, 'pts', pairs)  25.4 us
    ppermute x3, waiting for transfers between devices, shifted(): return lax.ppermute(value, axis, pairs)  12.6 us
    ppermute x14, starting transfers between devices, swapped(): return lax.ppermute(value, 'pts', pairs)  12.1 us
    pallas_call x8, Pallas kernels, in_vmem(): pl.pallas_call(kernel, out_shape=[jax.ShapeDtypeStruct(shape, dtype) for...  11.3 us
    pallas_call x1, Pallas kernels, body(): pl.pallas_call(functools.partial(last_upper_kernel, blocks), out_shape=ou...  2.39 us
    ppermute x3, starting transfers between devices, shifted(): return lax.ppermute(value, axis, pairs)  2.26 us
    broadcast_in_dim x3, local copies, waits for them, and re-layouts, body(): damps = jnp.broadcast_to(damps[:, None], (STEPS, 128))  2.01 us
    unnamed x8, local copies, waits for them, and re-layouts  1.62 us
  transfers between devices with their start and end apart: 17, of which 14 were waited for; matrix products, arithmetic and copies ran while one was open for 1% of the time, Pallas kernels for 9%

profile of v3, /device:TPU:0, one launch (start us, length us, event | category | flops | bytes accessed | tf_op | source)
XLA Modules:
  0.0 71.5 jit_solution(8905724636481091336)
XLA Ops:
  3.5 2.9 %collective-permute-start.2 = (f32[264,128]{1,0:T(8,128)S(1)}, f32[264,128]{1,0:T(8,128)S(1)}, u32[]{:S(2)}, u32[]{:S(2)}) collective-permute-start(f32[264,128]{1,0:T(8,128)S(1)} %add.26), channel_id=1, source_target_pairs={{0,8},{4,20},{8,0},{12,28},{16,24},{20,4},{24,16},{28,12},{1,9},{5... | collective-permute-start | bytes 405512 | tf_op jit(solution)/shard_map/ppermute | solution.py:24
  6.5 3.0 %collective-permute-done.2 = f32[264,128]{1,0:T(8,128)S(1)} collective-permute-done((f32[264,128]{1,0:T(8,128)S(1)}, f32[264,128]{1,0:T(8,128)S(1)}, u32[]{:S(2)}, u32[]{:S(2)}) %collective-permute-start.2) | collective-permute-done | bytes 135200 | tf_op jit(solution)/shard_map/ppermute | solution.py:24
  9.5 2.1 %collective-permute-start.4 = (f32[264,128]{1,0:T(8,128)S(1)}, f32[264,128]{1,0:T(8,128)S(1)}, u32[]{:S(2)}, u32[]{:S(2)}) collective-permute-start(f32[264,128]{1,0:T(8,128)S(1)} %add.27), channel_id=1, source_target_pairs={{0,16},{4,12},{8,24},{12,4},{16,0},{20,28},{24,8},{28,20},{1,17},{... | collective-permute-start | bytes 405512 | tf_op jit(solution)/shard_map/ppermute | solution.py:24
  11.6 3.0 %collective-permute-done.4 = f32[264,128]{1,0:T(8,128)S(1)} collective-permute-done((f32[264,128]{1,0:T(8,128)S(1)}, f32[264,128]{1,0:T(8,128)S(1)}, u32[]{:S(2)}, u32[]{:S(2)}) %collective-permute-start.4) | collective-permute-done | bytes 135200 | tf_op jit(solution)/shard_map/ppermute | solution.py:24
  16.7 2.2 %shard_map.38 = (f32[256,128]{1,0:T(8,128)S(1)}, f32[256,256]{1,0:T(8,128)S(1)}, f32[8,128]{1,0:T(8,128)S(1)}) custom-call(f32[1,128]{1,0:T(1,128)S(1)} %broadcast_in_dim.19.damp, f32[264,128]{1,0:T(8,128)S(1)} %add.28.own_sum, f32[264,128]{1,0:T(8,128)S(1)} %collective-permute-done.5.other_sum, f32[128,512]{1,0:T(8,128)S(1)} %copy-done, ...), custom_call_target="tpu_custom_call" | custom-call | tf_op jit(solution)/shard_map/pallas_call | solution.py:230
  18.9 2.1 %collective-permute-start.6 = (f32[256,128]{1,0:T(8,128)S(1)}, f32[256,128]{1,0:T(8,128)S(1)}, u32[]{:S(2)}, u32[]{:S(2)}) collective-permute-start(f32[256,128]{1,0:T(8,128)S(1)} %get-tuple-element.44), channel_id=1, source_target_pairs={{0,1},{1,2},{2,3},{3,0},{4,5},{5,6},{6,7},{7,4},{8,9},{9,10},{10,1... | collective-permute-start | bytes 393224 | tf_op jit(solution)/shard_map/ppermute | solution.py:18
  22.3 2.0 %shard_map.39 = (bf16[256,768]{1,0:T(8,128)(2,1)S(1)}, f32[1,128]{1,0:T(1,128)S(1)}, f32[256,256]{1,0:T(8,128)S(1)}) custom-call(f32[256,1]{1,0:T(8,128)S(1)} %copy.7.weight, f32[256,256]{1,0:T(8,128)S(1)} %get-tuple-element.40.refs_0_, f32[8,128]{1,0:T(8,128)S(1)} %get-tuple-element.41.refs_1_, f32[128,512]{1,0:T(8,128)S(1)} %copy-done.1, ...), custom_call_target="tpu_custom_call" | custom-call | tf_op jit(solution)/shard_map/pallas_call | solution.py:230
  24.4 2.5 %collective-permute-done.6.own_ref.refs_1_.refs_3_ = f32[256,128]{1,0:T(8,128)S(1)} collective-permute-done((f32[256,128]{1,0:T(8,128)S(1)}, f32[256,128]{1,0:T(8,128)S(1)}, u32[]{:S(2)}, u32[]{:S(2)}) %collective-permute-start.6) | collective-permute-done | bytes 131104 | tf_op jit(solution)/shard_map/ppermute | solution.py:18
  27.2 1.6 %collective-permute-start.7 = (f32[264,128]{1,0:T(8,128)S(1)}, f32[264,128]{1,0:T(8,128)S(1)}, u32[]{:S(2)}, u32[]{:S(2)}) collective-permute-start(f32[264,128]{1,0:T(8,128)S(1)} %shard_map.40), channel_id=1, source_target_pairs={{0,8},{4,20},{8,0},{12,28},{16,24},{20,4},{24,16},{28,12},{1,9},{5... | collective-permute-start | bytes 405512 | tf_op jit(solution)/shard_map/ppermute | solution.py:24
  28.7 3.5 %collective-permute-done.7 = f32[264,128]{1,0:T(8,128)S(1)} collective-permute-done((f32[264,128]{1,0:T(8,128)S(1)}, f32[264,128]{1,0:T(8,128)S(1)}, u32[]{:S(2)}, u32[]{:S(2)}) %collective-permute-start.7) | collective-permute-done | bytes 135200 | tf_op jit(solution)/shard_map/ppermute | solution.py:24
  32.3 1.6 %collective-permute-start.9 = (f32[264,128]{1,0:T(8,128)S(1)}, f32[264,128]{1,0:T(8,128)S(1)}, u32[]{:S(2)}, u32[]{:S(2)}) collective-permute-start(f32[264,128]{1,0:T(8,128)S(1)} %add.29), channel_id=1, source_target_pairs={{0,16},{4,12},{8,24},{12,4},{16,0},{20,28},{24,8},{28,20},{1,17},{... | collective-permute-start | bytes 405512 | tf_op jit(solution)/shard_map/ppermute | solution.py:24
  33.8 3.5 %collective-permute-done.9 = f32[264,128]{1,0:T(8,128)S(1)} collective-permute-done((f32[264,128]{1,0:T(8,128)S(1)}, f32[264,128]{1,0:T(8,128)S(1)}, u32[]{:S(2)}, u32[]{:S(2)}) %collective-permute-start.9) | collective-permute-done | bytes 135200 | tf_op jit(solution)/shard_map/ppermute | solution.py:24
  37.4 1.3 %collective-permute-done.10.other_sum = f32[264,128]{1,0:T(8,128)S(1)} collective-permute-done((f32[264,128]{1,0:T(8,128)S(1)}, f32[264,128]{1,0:T(8,128)S(1)}, u32[]{:S(2)}, u32[]{:S(2)}) %collective-permute-start.10) | collective-permute-done | bytes 135200 | tf_op jit(solution)/shard_map/ppermute | solution.py:24
  39.5 2.2 %shard_map.41 = (f32[256,128]{1,0:T(8,128)S(1)}, f32[256,256]{1,0:T(8,128)S(1)}, f32[8,128]{1,0:T(8,128)S(1)}) custom-call(f32[1,128]{1,0:T(1,128)S(1)} %broadcast_in_dim.18.damp, f32[264,128]{1,0:T(8,128)S(1)} %add.30.own_sum, f32[264,128]{1,0:T(8,128)S(1)} %collective-permute-done.10.other_sum, f32[256,256]{1,0:T(8,128)S(1)} %get-tuple-element.48.refs_0_.refs_2_, ...), custom_call_target="tpu_custom_call" | custom-call | tf_op jit(solution)/shard_map/pallas_call | solution.py:230
  41.7 2.0 %shard_map.42 = (bf16[256,768]{1,0:T(8,128)(2,1)S(1)}, f32[1,128]{1,0:T(1,128)S(1)}, f32[256,256]{1,0:T(8,128)S(1)}) custom-call(f32[256,1]{1,0:T(8,128)S(1)} %copy.7.weight, f32[256,256]{1,0:T(8,128)S(1)} %get-tuple-element.50.refs_0_, f32[8,128]{1,0:T(8,128)S(1)} %get-tuple-element.51.refs_1_, f32[256,256]{1,0:T(8,128)S(1)} %get-tuple-element.48.refs_0_.refs_2_, ...), custom_call_target="tpu_custom_call" | custom-call | tf_op jit(solution)/shard_map/pallas_call | solution.py:230
  43.7 5.3 %collective-permute-done.11.own_ref.refs_1_.refs_3_ = f32[256,128]{1,0:T(8,128)S(1)} collective-permute-done((f32[256,128]{1,0:T(8,128)S(1)}, f32[256,128]{1,0:T(8,128)S(1)}, u32[]{:S(2)}, u32[]{:S(2)}) %collective-permute-start.11) | collective-permute-done | bytes 131104 | tf_op jit(solution)/shard_map/ppermute | solution.py:18
  49.3 1.6 %collective-permute-start.12 = (f32[264,128]{1,0:T(8,128)S(1)}, f32[264,128]{1,0:T(8,128)S(1)}, u32[]{:S(2)}, u32[]{:S(2)}) collective-permute-start(f32[264,128]{1,0:T(8,128)S(1)} %shard_map.43), channel_id=1, source_target_pairs={{0,8},{4,20},{8,0},{12,28},{16,24},{20,4},{24,16},{28,12},{1,9},{5... | collective-permute-start | bytes 405512 | tf_op jit(solution)/shard_map/ppermute | solution.py:24
  50.9 3.5 %collective-permute-done.12 = f32[264,128]{1,0:T(8,128)S(1)} collective-permute-done((f32[264,128]{1,0:T(8,128)S(1)}, f32[264,128]{1,0:T(8,128)S(1)}, u32[]{:S(2)}, u32[]{:S(2)}) %collective-permute-start.12) | collective-permute-done | bytes 135200 | tf_op jit(solution)/shard_map/ppermute | solution.py:24
  54.4 1.6 %collective-permute-start.14 = (f32[264,128]{1,0:T(8,128)S(1)}, f32[264,128]{1,0:T(8,128)S(1)}, u32[]{:S(2)}, u32[]{:S(2)}) collective-permute-start(f32[264,128]{1,0:T(8,128)S(1)} %add.31), channel_id=1, source_target_pairs={{0,16},{4,12},{8,24},{12,4},{16,0},{20,28},{24,8},{28,20},{1,17},{... | collective-permute-start | bytes 405512 | tf_op jit(solution)/shard_map/ppermute | solution.py:24
  56.0 3.5 %collective-permute-done.14 = f32[264,128]{1,0:T(8,128)S(1)} collective-permute-done((f32[264,128]{1,0:T(8,128)S(1)}, f32[264,128]{1,0:T(8,128)S(1)}, u32[]{:S(2)}, u32[]{:S(2)}) %collective-permute-start.14) | collective-permute-done | bytes 135200 | tf_op jit(solution)/shard_map/ppermute | solution.py:24
  59.6 1.3 %collective-permute-done.15.other_sum = f32[264,128]{1,0:T(8,128)S(1)} collective-permute-done((f32[264,128]{1,0:T(8,128)S(1)}, f32[264,128]{1,0:T(8,128)S(1)}, u32[]{:S(2)}, u32[]{:S(2)}) %collective-permute-start.15) | collective-permute-done | bytes 135200 | tf_op jit(solution)/shard_map/ppermute | solution.py:24
  61.7 2.0 %shard_map.44 = (f32[128,256]{1,0:T(8,128)S(1)}, f32[256,256]{1,0:T(8,128)S(1)}, f32[8,128]{1,0:T(8,128)S(1)}) custom-call(f32[1,128]{1,0:T(1,128)S(1)} %broadcast_in_dim.16.damp, f32[264,128]{1,0:T(8,128)S(1)} %add.32.own_sum, f32[264,128]{1,0:T(8,128)S(1)} %collective-permute-done.15.other_sum, f32[256,256]{1,0:T(8,128)S(1)} %get-tuple-element.58.refs_0_.refs_2_, ...), custom_call_target="tpu_custom_call" | custom-call | tf_op jit(solution)/shard_map/pallas_call | solution.py:230
  63.7 2.4 %shard_map.45.filled = f32[128,512]{1,0:T(8,128)} custom-call(f32[256,256]{1,0:T(8,128)S(1)} %get-tuple-element.61.refs_0_, f32[8,128]{1,0:T(8,128)S(1)} %get-tuple-element.62.refs_1_, f32[256,256]{1,0:T(8,128)S(1)} %get-tuple-element.58.refs_0_.refs_2_, f32[256,128]{1,0:T(8,128)S(1)} %collective-permute-done.11.own_ref.refs_1_.refs_3_, ...), custom_call_target="tpu_custom_call" | custom-call | tf_op jit(solution)/shard_map/pallas_call | solution.py:277
  66.1 4.8 %collective-permute-done.16.lower = f32[128,256]{1,0:T(8,128)S(1)} collective-permute-done((f32[128,256]{1,0:T(8,128)S(1)}, f32[128,256]{1,0:T(8,128)S(1)}, u32[]{:S(2)}, u32[]{:S(2)}) %collective-permute-start.16) | collective-permute-done | bytes 131104 | tf_op jit(solution)/shard_map/ppermute | solution.py:18
  (42 shorter events, 9.8 us)
Async XLA Ops:
  0.0 0.7 copy-start.2
  0.7 0.9 %copy-start = (f32[128,512]{1,0:T(8,128)S(1)}, f32[128,512]{1,0:T(8,128)}, u32[]{:S(2)}) copy-start(f32[128,512]{1,0:T(8,128)} %refs_2_.1) | copy-start | bytes 786436
  2.0 1.5 %collective-permute-start.1 = (f32[264,128]{1,0:T(8,128)S(1)}, f32[264,128]{1,0:T(8,128)S(1)}, u32[]{:S(2)}, u32[]{:S(2)}) collective-permute-start(f32[264,128]{1,0:T(8,128)S(1)} %get-tuple-element.35), channel_id=1, source_target_pairs={{0,4},{4,0},{8,12},{12,8},{16,20},{20,16},{24,28},{28,24},{1,5},{5... | collective-permute-start | bytes 405512 | tf_op jit(solution)/shard_map/ppermute | solution.py:24
  2.5 7.0 %collective-permute-start.3 = (f32[128,512]{1,0:T(8,128)S(1)}, f32[128,512]{1,0:T(8,128)S(1)}, u32[]{:S(2)}, u32[]{:S(2)}) collective-permute-start(f32[128,512]{1,0:T(8,128)S(1)} %copy-done), channel_id=1, source_target_pairs={{0,4},{4,0},{8,12},{12,8},{16,20},{20,16},{24,28},{28,24},{1,5},{5... | collective-permute-start | bytes 786440 | tf_op jit(solution)/shard_map/ppermute | solution.py:24
  3.5 5.9 %collective-permute-start.2 = (f32[264,128]{1,0:T(8,128)S(1)}, f32[264,128]{1,0:T(8,128)S(1)}, u32[]{:S(2)}, u32[]{:S(2)}) collective-permute-start(f32[264,128]{1,0:T(8,128)S(1)} %add.26), channel_id=1, source_target_pairs={{0,8},{4,20},{8,0},{12,28},{16,24},{20,4},{24,16},{28,12},{1,9},{5... | collective-permute-start | bytes 405512 | tf_op jit(solution)/shard_map/ppermute | solution.py:24
  9.5 5.2 %copy-start.3 = (s32[3,2]{0,1:T(2,128)S(1)}, s32[3,2]{0,1:T(2,128)}, u32[]{:S(2)}) copy-start(s32[3,2]{0,1:T(2,128)} %param.5) | copy-start | bytes 76
  9.5 5.1 %collective-permute-start.4 = (f32[264,128]{1,0:T(8,128)S(1)}, f32[264,128]{1,0:T(8,128)S(1)}, u32[]{:S(2)}, u32[]{:S(2)}) collective-permute-start(f32[264,128]{1,0:T(8,128)S(1)} %add.27), channel_id=1, source_target_pairs={{0,16},{4,12},{8,24},{12,4},{16,0},{20,28},{24,8},{28,20},{1,17},{... | collective-permute-start | bytes 405512 | tf_op jit(solution)/shard_map/ppermute | solution.py:24
  14.6 1.4 %collective-permute-start.5 = (f32[264,128]{1,0:T(8,128)S(1)}, f32[264,128]{1,0:T(8,128)S(1)}, u32[]{:S(2)}, u32[]{:S(2)}) collective-permute-start(f32[264,128]{1,0:T(8,128)S(1)} %add.28.own_sum), channel_id=1, source_target_pairs={{0,4},{4,0},{8,12},{12,8},{16,20},{20,16},{24,28},{28,24},{1,5},{5... | collective-permute-start | bytes 405512 | tf_op jit(solution)/shard_map/ppermute | solution.py:24
  16.7 5.6 %copy-start.1 = (f32[128,512]{1,0:T(8,128)S(1)}, f32[128,512]{1,0:T(8,128)}, u32[]{:S(2)}) copy-start(f32[128,512]{1,0:T(8,128)} %refs_2_.1) | copy-start | bytes 786436
  18.9 8.0 %collective-permute-start.6 = (f32[256,128]{1,0:T(8,128)S(1)}, f32[256,128]{1,0:T(8,128)S(1)}, u32[]{:S(2)}, u32[]{:S(2)}) collective-permute-start(f32[256,128]{1,0:T(8,128)S(1)} %get-tuple-element.44), channel_id=1, source_target_pairs={{0,1},{1,2},{2,3},{3,0},{4,5},{5,6},{6,7},{7,4},{8,9},{9,10},{10,1... | collective-permute-start | bytes 393224 | tf_op jit(solution)/shard_map/ppermute | solution.py:18
  21.1 1.1 %collective-permute-start = (f32[128]{0:T(128)S(1)}, f32[128]{0:T(128)S(1)}, u32[]{:S(2)}, u32[]{:S(2)}) collective-permute-start(f32[128]{0:T(128)S(1)} %copy-done.2), channel_id=1, source_target_pairs={{0,4},{4,0},{8,12},{12,8},{16,20},{20,16},{24,28},{28,24},{1,5},{5... | collective-permute-start | bytes 1544 | tf_op jit(solution)/shard_map/ppermute | solution.py:24
  27.2 5.1 %collective-permute-start.7 = (f32[264,128]{1,0:T(8,128)S(1)}, f32[264,128]{1,0:T(8,128)S(1)}, u32[]{:S(2)}, u32[]{:S(2)}) collective-permute-start(f32[264,128]{1,0:T(8,128)S(1)} %shard_map.40), channel_id=1, source_target_pairs={{0,8},{4,20},{8,0},{12,28},{16,24},{20,4},{24,16},{28,12},{1,9},{5... | collective-permute-start | bytes 405512 | tf_op jit(solution)/shard_map/ppermute | solution.py:24
  28.7 3.5 %collective-permute-start.8 = (f32[256,128]{1,0:T(8,128)S(1)}, f32[256,128]{1,0:T(8,128)S(1)}, u32[]{:S(2)}, u32[]{:S(2)}) collective-permute-start(f32[256,128]{1,0:T(8,128)S(1)} %collective-permute-done.6.own_ref.refs_1_.refs_3_), channel_id=1, source_target_pairs={{0,4},{4,0},{8,12},{12,8},{16,20},{20,16},{24,28},{28,24},{1,5},{5... | collective-permute-start | bytes 393224 | tf_op jit(solution)/shard_map/ppermute | solution.py:24
  32.3 5.1 %collective-permute-start.9 = (f32[264,128]{1,0:T(8,128)S(1)}, f32[264,128]{1,0:T(8,128)S(1)}, u32[]{:S(2)}, u32[]{:S(2)}) collective-permute-start(f32[264,128]{1,0:T(8,128)S(1)} %add.29), channel_id=1, source_target_pairs={{0,16},{4,12},{8,24},{12,4},{16,0},{20,28},{24,8},{28,20},{1,17},{... | collective-permute-start | bytes 405512 | tf_op jit(solution)/shard_map/ppermute | solution.py:24
  37.4 1.4 %collective-permute-start.10 = (f32[264,128]{1,0:T(8,128)S(1)}, f32[264,128]{1,0:T(8,128)S(1)}, u32[]{:S(2)}, u32[]{:S(2)}) collective-permute-start(f32[264,128]{1,0:T(8,128)S(1)} %add.30.own_sum), channel_id=1, source_target_pairs={{0,4},{4,0},{8,12},{12,8},{16,20},{20,16},{24,28},{28,24},{1,5},{5... | collective-permute-start | bytes 405512 | tf_op jit(solution)/shard_map/ppermute | solution.py:24
  41.7 7.4 %collective-permute-start.11 = (f32[256,128]{1,0:T(8,128)S(1)}, f32[256,128]{1,0:T(8,128)S(1)}, u32[]{:S(2)}, u32[]{:S(2)}) collective-permute-start(f32[256,128]{1,0:T(8,128)S(1)} %get-tuple-element.54), channel_id=1, source_target_pairs={{0,1},{1,2},{2,3},{3,0},{4,5},{5,6},{6,7},{7,4},{8,9},{9,10},{10,1... | collective-permute-start | bytes 393224 | tf_op jit(solution)/shard_map/ppermute | solution.py:18
  49.3 5.1 %collective-permute-start.12 = (f32[264,128]{1,0:T(8,128)S(1)}, f32[264,128]{1,0:T(8,128)S(1)}, u32[]{:S(2)}, u32[]{:S(2)}) collective-permute-start(f32[264,128]{1,0:T(8,128)S(1)} %shard_map.43), channel_id=1, source_target_pairs={{0,8},{4,20},{8,0},{12,28},{16,24},{20,4},{24,16},{28,12},{1,9},{5... | collective-permute-start | bytes 405512 | tf_op jit(solution)/shard_map/ppermute | solution.py:24
  50.9 3.5 %collective-permute-start.13 = (f32[256,128]{1,0:T(8,128)S(1)}, f32[256,128]{1,0:T(8,128)S(1)}, u32[]{:S(2)}, u32[]{:S(2)}) collective-permute-start(f32[256,128]{1,0:T(8,128)S(1)} %collective-permute-done.11.own_ref.refs_1_.refs_3_), channel_id=1, source_target_pairs={{0,4},{4,0},{8,12},{12,8},{16,20},{20,16},{24,28},{28,24},{1,5},{5... | collective-permute-start | bytes 393224 | tf_op jit(solution)/shard_map/ppermute | solution.py:24
  54.4 5.1 %collective-permute-start.14 = (f32[264,128]{1,0:T(8,128)S(1)}, f32[264,128]{1,0:T(8,128)S(1)}, u32[]{:S(2)}, u32[]{:S(2)}) collective-permute-start(f32[264,128]{1,0:T(8,128)S(1)} %add.31), channel_id=1, source_target_pairs={{0,16},{4,12},{8,24},{12,4},{16,0},{20,28},{24,8},{28,20},{1,17},{... | collective-permute-start | bytes 405512 | tf_op jit(solution)/shard_map/ppermute | solution.py:24
  59.5 1.4 %collective-permute-start.15 = (f32[264,128]{1,0:T(8,128)S(1)}, f32[264,128]{1,0:T(8,128)S(1)}, u32[]{:S(2)}, u32[]{:S(2)}) collective-permute-start(f32[264,128]{1,0:T(8,128)S(1)} %add.32.own_sum), channel_id=1, source_target_pairs={{0,4},{4,0},{8,12},{12,8},{16,20},{20,16},{24,28},{28,24},{1,5},{5... | collective-permute-start | bytes 405512 | tf_op jit(solution)/shard_map/ppermute | solution.py:24
  63.6 7.2 %collective-permute-start.16 = (f32[128,256]{1,0:T(8,128)S(1)}, f32[128,256]{1,0:T(8,128)S(1)}, u32[]{:S(2)}, u32[]{:S(2)}) collective-permute-start(f32[128,256]{1,0:T(8,128)S(1)} %get-tuple-element.60), channel_id=1, source_target_pairs={{0,2},{1,3},{2,0},{3,1},{4,6},{5,7},{6,4},{7,5},{8,10},{9,11},{10,... | collective-permute-start | bytes 393224 | tf_op jit(solution)/shard_map/ppermute | solution.py:18

commit v4 on v3

--- a/solution.py
+++ b/solution.py
@@ -139,7 +139,15 @@
     ref[:, pl.ds(other, half)] = value[:, half:]
 
 
-def start_kernel(near, weight, own_part, other_part):
+def start_kernel(near_ref, weight_ref, own_part, other_part, near, weight, near_sent, weight_sent):
+    copies = [
+        pltpu.make_async_copy(near_ref, near, near_sent),
+        pltpu.make_async_copy(weight_ref, weight, weight_sent),
+    ]
+    for copy in copies:
+        copy.start()
+    for copy in copies:
+        copy.wait()
     width = near.shape[1] // 2
     half = width // 2
     own, other = own_half(half)
@@ -157,14 +165,14 @@
         out[width:] = jnp.where(rows == 0, norm_lower, jnp.where(rows == 1, norm_upper, 0.0))
 
 
-def lower_kernel(blocks, last, damp, own_sum, other_sum, *refs):
+def lower_kernel(blocks, step, last, damps, own_sum, other_sum, *refs):
     *block_refs, moved, coupling_out, scale_out = refs
     width = coupling_out.shape[0]
     upper, lower = blocks(*block_refs)
     gram = joined(own_sum[:width], other_sum[:width])
     norms = jnp.concatenate([own_sum[width:], other_sum[width:]], axis=1)
     inverse = lax.rsqrt(norms + EPSILON)
-    coupling = gram * (damp[0:1, 0:1] * inverse.T[:, 1:2]) * inverse[0:1]
+    coupling = gram * (damps[step : step + 1, 0:1] * inverse.T[:, 1:2]) * inverse[0:1]
     scale = 1.0 + jnp.sum(coupling * coupling, keepdims=True)
     coupling_out[...] = coupling
     scale_out[...] = jnp.broadcast_to(scale, scale_out.shape)
@@ -241,20 +249,32 @@
     width = columns // 2
     half = width // 2
     whole = (2 * rows, width)
-    own_part, other_part = in_vmem(start_kernel, [((width + 8, half), F32)] * 2, snapshot, weights[None])
+    own_part, other_part = pl.pallas_call(
+        start_kernel,
+        out_shape=[jax.ShapeDtypeStruct((width + 8, half), F32)] * 2,
+        in_specs=[ANYWHERE] * 2,
+        out_specs=[ON_CHIP] * 2,
+        scratch_shapes=[
+            pltpu.VMEM((rows, columns), F32),
+            pltpu.VMEM((1, rows), F32),
+            pltpu.SemaphoreType.DMA(()),
+            pltpu.SemaphoreType.DMA(()),
+        ],
+        compiler_params=GRANT,
+    )(snapshot, weights[None])
     payload = own_part + swapped(other_part, 1, 1)
     weight = jnp.concatenate([weights, swapped(weights, 1, 1)])[:, None]
     blocks, held, arriving = start_blocks, (snapshot,), swapped(snapshot, 1, 1)
     damps = damping[:, 0].astype(F32) / (damping[:, 0] + damping[:, 1]).astype(F32)
-    damps = jnp.broadcast_to(damps[:, None], (STEPS, 128))
+    damps = lax.optimization_barrier(jnp.broadcast_to(damps[:, None], (STEPS, 128)))
     for step in range(STEPS):
         last = step + 1 == STEPS
         payload, arriving = chip_sum(payload, arriving)
         held = held + (arriving,)
         moved, coupling, scale = in_vmem(
-            functools.partial(lower_kernel, blocks, last),
+            functools.partial(lower_kernel, blocks, step, last),
             [((rows, width) if last else (2 * rows, half), F32), ((width, width), F32), ((8, 128), F32)],
-            damps[step : step + 1],
+            damps,
             payload,
             swapped(payload, 1, 1),
             *held,

time: 71.7 us -> 69.7 us (0.972)
  local copies, waits for them, and re-layouts: 4.43 us -> 1.82 us
    broadcast_in_dim x3 -> x1, local copies, waits for them, and re-layouts: 2.01 us -> 0.07 us  [body(): jnp.broadcast_to(damps[:, None], (STEPS, 128))]
    pallas_call x8 -> x7, Pallas kernels: 11.3 us -> 10.9 us  [in_vmem(): pl.pallas_call(kernel, out_shape=[jax.ShapeDtypeStruct(shape, dtype) for...]
  transfers between devices with their start and end apart: 17 -> 17, of which waited for: 14 -> 14; matrix products, arithmetic and copies ran while one was open for 1% -> 0% of each run, Pallas kernels for 9% -> 9%
where the time goes in v4:
time: 69.7 us; the launch traced here: 69.5 us
  waiting for transfers between devices  38.6 us (55%)
  Pallas kernels  14.4 us (21%)
  starting transfers between devices  14.4 us (21%)
  local copies, waits for them, and re-layouts  1.82 us (3%)
    ppermute x14, waiting for transfers between devices, swapped(): return lax.ppermute(value, 'pts', pairs)  26 us
    ppermute x3, waiting for transfers between devices, shifted(): return lax.ppermute(value, axis, pairs)  12.6 us
    ppermute x14, starting transfers between devices, swapped(): return lax.ppermute(value, 'pts', pairs)  12.1 us
    pallas_call x7, Pallas kernels, in_vmem(): pl.pallas_call(kernel, out_shape=[jax.ShapeDtypeStruct(shape, dtype) for...  10.9 us
    pallas_call x1, Pallas kernels, body(): pl.pallas_call(functools.partial(last_upper_kernel, blocks), out_shape=ou...  2.39 us
    ppermute x3, starting transfers between devices, shifted(): return lax.ppermute(value, axis, pairs)  2.26 us
    unnamed x8, local copies, waits for them, and re-layouts  1.61 us
  transfers between devices with their start and end apart: 17, of which 14 were waited for; matrix products, arithmetic and copies ran while one was open for 0% of the time, Pallas kernels for 9%

profile of v4, /device:TPU:0, one launch (start us, length us, event | category | flops | bytes accessed | tf_op | source)
XLA Modules:
  0.0 69.5 jit_solution(13763520671435871525)
XLA Ops:
  3.6 2.9 %collective-permute-start.2 = (f32[264,128]{1,0:T(8,128)S(1)}, f32[264,128]{1,0:T(8,128)S(1)}, u32[]{:S(2)}, u32[]{:S(2)}) collective-permute-start(f32[264,128]{1,0:T(8,128)S(1)} %add.26), channel_id=1, source_target_pairs={{0,8},{4,20},{8,0},{12,28},{16,24},{20,4},{24,16},{28,12},{1,9},{5... | collective-permute-start | bytes 405512 | tf_op jit(solution)/shard_map/ppermute | solution.py:24
  6.5 3.0 %collective-permute-done.2 = f32[264,128]{1,0:T(8,128)S(1)} collective-permute-done((f32[264,128]{1,0:T(8,128)S(1)}, f32[264,128]{1,0:T(8,128)S(1)}, u32[]{:S(2)}, u32[]{:S(2)}) %collective-permute-start.2) | collective-permute-done | bytes 135200 | tf_op jit(solution)/shard_map/ppermute | solution.py:24
  9.5 2.1 %collective-permute-start.4 = (f32[264,128]{1,0:T(8,128)S(1)}, f32[264,128]{1,0:T(8,128)S(1)}, u32[]{:S(2)}, u32[]{:S(2)}) collective-permute-start(f32[264,128]{1,0:T(8,128)S(1)} %add.27), channel_id=1, source_target_pairs={{0,16},{4,12},{8,24},{12,4},{16,0},{20,28},{24,8},{28,20},{1,17},{... | collective-permute-start | bytes 405512 | tf_op jit(solution)/shard_map/ppermute | solution.py:24
  11.7 3.0 %collective-permute-done.4 = f32[264,128]{1,0:T(8,128)S(1)} collective-permute-done((f32[264,128]{1,0:T(8,128)S(1)}, f32[264,128]{1,0:T(8,128)S(1)}, u32[]{:S(2)}, u32[]{:S(2)}) %collective-permute-start.4) | collective-permute-done | bytes 135200 | tf_op jit(solution)/shard_map/ppermute | solution.py:24
  16.1 2.2 %shard_map.38 = (f32[256,128]{1,0:T(8,128)S(1)}, f32[256,256]{1,0:T(8,128)S(1)}, f32[8,128]{1,0:T(8,128)S(1)}) custom-call(f32[3,128]{1,0:T(4,128)S(1)} %broadcast_in_dim.15.damps, f32[264,128]{1,0:T(8,128)S(1)} %add.28.own_sum, f32[264,128]{1,0:T(8,128)S(1)} %collective-permute-done.5.other_sum, f32[128,512]{1,0:T(8,128)S(1)} %copy-done, ...), custom_call_target="tpu_custom_call" | custom-call | tf_op jit(solution)/shard_map/pallas_call | solution.py:238
  18.3 2.1 %collective-permute-start.6 = (f32[256,128]{1,0:T(8,128)S(1)}, f32[256,128]{1,0:T(8,128)S(1)}, u32[]{:S(2)}, u32[]{:S(2)}) collective-permute-start(f32[256,128]{1,0:T(8,128)S(1)} %get-tuple-element.44), channel_id=1, source_target_pairs={{0,1},{1,2},{2,3},{3,0},{4,5},{5,6},{6,7},{7,4},{8,9},{9,10},{10,1... | collective-permute-start | bytes 393224 | tf_op jit(solution)/shard_map/ppermute | solution.py:18
  21.7 2.0 %shard_map.39 = (bf16[256,768]{1,0:T(8,128)(2,1)S(1)}, f32[1,128]{1,0:T(1,128)S(1)}, f32[256,256]{1,0:T(8,128)S(1)}) custom-call(f32[256,1]{1,0:T(8,128)S(1)} %copy.7.weight, f32[256,256]{1,0:T(8,128)S(1)} %get-tuple-element.40.refs_0_, f32[8,128]{1,0:T(8,128)S(1)} %get-tuple-element.41.refs_1_, f32[128,512]{1,0:T(8,128)S(1)} %copy-done.1, ...), custom_call_target="tpu_custom_call" | custom-call | tf_op jit(solution)/shard_map/pallas_call | solution.py:238
  23.7 2.6 %collective-permute-done.6.own_ref.refs_1_.refs_3_ = f32[256,128]{1,0:T(8,128)S(1)} collective-permute-done((f32[256,128]{1,0:T(8,128)S(1)}, f32[256,128]{1,0:T(8,128)S(1)}, u32[]{:S(2)}, u32[]{:S(2)}) %collective-permute-start.6) | collective-permute-done | bytes 131104 | tf_op jit(solution)/shard_map/ppermute | solution.py:18
  26.5 1.6 %collective-permute-start.7 = (f32[264,128]{1,0:T(8,128)S(1)}, f32[264,128]{1,0:T(8,128)S(1)}, u32[]{:S(2)}, u32[]{:S(2)}) collective-permute-start(f32[264,128]{1,0:T(8,128)S(1)} %shard_map.40), channel_id=1, source_target_pairs={{0,8},{4,20},{8,0},{12,28},{16,24},{20,4},{24,16},{28,12},{1,9},{5... | collective-permute-start | bytes 405512 | tf_op jit(solution)/shard_map/ppermute | solution.py:24
  28.1 3.5 %collective-permute-done.7 = f32[264,128]{1,0:T(8,128)S(1)} collective-permute-done((f32[264,128]{1,0:T(8,128)S(1)}, f32[264,128]{1,0:T(8,128)S(1)}, u32[]{:S(2)}, u32[]{:S(2)}) %collective-permute-start.7) | collective-permute-done | bytes 135200 | tf_op jit(solution)/shard_map/ppermute | solution.py:24
  31.6 1.6 %collective-permute-start.9 = (f32[264,128]{1,0:T(8,128)S(1)}, f32[264,128]{1,0:T(8,128)S(1)}, u32[]{:S(2)}, u32[]{:S(2)}) collective-permute-start(f32[264,128]{1,0:T(8,128)S(1)} %add.29), channel_id=1, source_target_pairs={{0,16},{4,12},{8,24},{12,4},{16,0},{20,28},{24,8},{28,20},{1,17},{... | collective-permute-start | bytes 405512 | tf_op jit(solution)/shard_map/ppermute | solution.py:24
  33.2 3.5 %collective-permute-done.9 = f32[264,128]{1,0:T(8,128)S(1)} collective-permute-done((f32[264,128]{1,0:T(8,128)S(1)}, f32[264,128]{1,0:T(8,128)S(1)}, u32[]{:S(2)}, u32[]{:S(2)}) %collective-permute-start.9) | collective-permute-done | bytes 135200 | tf_op jit(solution)/shard_map/ppermute | solution.py:24
  36.8 1.3 %collective-permute-done.10.other_sum = f32[264,128]{1,0:T(8,128)S(1)} collective-permute-done((f32[264,128]{1,0:T(8,128)S(1)}, f32[264,128]{1,0:T(8,128)S(1)}, u32[]{:S(2)}, u32[]{:S(2)}) %collective-permute-start.10) | collective-permute-done | bytes 135200 | tf_op jit(solution)/shard_map/ppermute | solution.py:24
  38.2 2.2 %shard_map.41 = (f32[256,128]{1,0:T(8,128)S(1)}, f32[256,256]{1,0:T(8,128)S(1)}, f32[8,128]{1,0:T(8,128)S(1)}) custom-call(f32[3,128]{1,0:T(4,128)S(1)} %broadcast_in_dim.15.damps, f32[264,128]{1,0:T(8,128)S(1)} %add.30.own_sum, f32[264,128]{1,0:T(8,128)S(1)} %collective-permute-done.10.other_sum, f32[256,256]{1,0:T(8,128)S(1)} %get-tuple-element.48.refs_0_.refs_2_, ...), custom_call_target="tpu_custom_call" | custom-call | tf_op jit(solution)/shard_map/pallas_call | solution.py:238
  40.5 2.0 %shard_map.42 = (bf16[256,768]{1,0:T(8,128)(2,1)S(1)}, f32[1,128]{1,0:T(1,128)S(1)}, f32[256,256]{1,0:T(8,128)S(1)}) custom-call(f32[256,1]{1,0:T(8,128)S(1)} %copy.7.weight, f32[256,256]{1,0:T(8,128)S(1)} %get-tuple-element.50.refs_0_, f32[8,128]{1,0:T(8,128)S(1)} %get-tuple-element.51.refs_1_, f32[256,256]{1,0:T(8,128)S(1)} %get-tuple-element.48.refs_0_.refs_2_, ...), custom_call_target="tpu_custom_call" | custom-call | tf_op jit(solution)/shard_map/pallas_call | solution.py:238
  42.5 5.3 %collective-permute-done.11.own_ref.refs_1_.refs_3_ = f32[256,128]{1,0:T(8,128)S(1)} collective-permute-done((f32[256,128]{1,0:T(8,128)S(1)}, f32[256,128]{1,0:T(8,128)S(1)}, u32[]{:S(2)}, u32[]{:S(2)}) %collective-permute-start.11) | collective-permute-done | bytes 131104 | tf_op jit(solution)/shard_map/ppermute | solution.py:18
  48.0 1.6 %collective-permute-start.12 = (f32[264,128]{1,0:T(8,128)S(1)}, f32[264,128]{1,0:T(8,128)S(1)}, u32[]{:S(2)}, u32[]{:S(2)}) collective-permute-start(f32[264,128]{1,0:T(8,128)S(1)} %shard_map.43), channel_id=1, source_target_pairs={{0,8},{4,20},{8,0},{12,28},{16,24},{20,4},{24,16},{28,12},{1,9},{5... | collective-permute-start | bytes 405512 | tf_op jit(solution)/shard_map/ppermute | solution.py:24
  49.6 3.5 %collective-permute-done.12 = f32[264,128]{1,0:T(8,128)S(1)} collective-permute-done((f32[264,128]{1,0:T(8,128)S(1)}, f32[264,128]{1,0:T(8,128)S(1)}, u32[]{:S(2)}, u32[]{:S(2)}) %collective-permute-start.12) | collective-permute-done | bytes 135200 | tf_op jit(solution)/shard_map/ppermute | solution.py:24
  53.1 1.6 %collective-permute-start.14 = (f32[264,128]{1,0:T(8,128)S(1)}, f32[264,128]{1,0:T(8,128)S(1)}, u32[]{:S(2)}, u32[]{:S(2)}) collective-permute-start(f32[264,128]{1,0:T(8,128)S(1)} %add.31), channel_id=1, source_target_pairs={{0,16},{4,12},{8,24},{12,4},{16,0},{20,28},{24,8},{28,20},{1,17},{... | collective-permute-start | bytes 405512 | tf_op jit(solution)/shard_map/ppermute | solution.py:24
  54.7 3.5 %collective-permute-done.14 = f32[264,128]{1,0:T(8,128)S(1)} collective-permute-done((f32[264,128]{1,0:T(8,128)S(1)}, f32[264,128]{1,0:T(8,128)S(1)}, u32[]{:S(2)}, u32[]{:S(2)}) %collective-permute-start.14) | collective-permute-done | bytes 135200 | tf_op jit(solution)/shard_map/ppermute | solution.py:24
  58.3 1.3 %collective-permute-done.15.other_sum = f32[264,128]{1,0:T(8,128)S(1)} collective-permute-done((f32[264,128]{1,0:T(8,128)S(1)}, f32[264,128]{1,0:T(8,128)S(1)}, u32[]{:S(2)}, u32[]{:S(2)}) %collective-permute-start.15) | collective-permute-done | bytes 135200 | tf_op jit(solution)/shard_map/ppermute | solution.py:24
  59.7 2.0 %shard_map.44 = (f32[128,256]{1,0:T(8,128)S(1)}, f32[256,256]{1,0:T(8,128)S(1)}, f32[8,128]{1,0:T(8,128)S(1)}) custom-call(f32[3,128]{1,0:T(4,128)S(1)} %broadcast_in_dim.15.damps, f32[264,128]{1,0:T(8,128)S(1)} %add.32.own_sum, f32[264,128]{1,0:T(8,128)S(1)} %collective-permute-done.15.other_sum, f32[256,256]{1,0:T(8,128)S(1)} %get-tuple-element.58.refs_0_.refs_2_, ...), custom_call_target="tpu_custom_call" | custom-call | tf_op jit(solution)/shard_map/pallas_call | solution.py:238
  61.7 2.4 %shard_map.45.filled = f32[128,512]{1,0:T(8,128)} custom-call(f32[256,256]{1,0:T(8,128)S(1)} %get-tuple-element.61.refs_0_, f32[8,128]{1,0:T(8,128)S(1)} %get-tuple-element.62.refs_1_, f32[256,256]{1,0:T(8,128)S(1)} %get-tuple-element.58.refs_0_.refs_2_, f32[256,128]{1,0:T(8,128)S(1)} %collective-permute-done.11.own_ref.refs_1_.refs_3_, ...), custom_call_target="tpu_custom_call" | custom-call | tf_op jit(solution)/shard_map/pallas_call | solution.py:297
  64.1 4.8 %collective-permute-done.16.lower = f32[128,256]{1,0:T(8,128)S(1)} collective-permute-done((f32[128,256]{1,0:T(8,128)S(1)}, f32[128,256]{1,0:T(8,128)S(1)}, u32[]{:S(2)}, u32[]{:S(2)}) %collective-permute-start.16) | collective-permute-done | bytes 131104 | tf_op jit(solution)/shard_map/ppermute | solution.py:18
  (39 shorter events, 7.8 us)
Async XLA Ops:
  0.0 0.7 copy-start.2
  0.7 0.9 %copy-start = (f32[128,512]{1,0:T(8,128)S(1)}, f32[128,512]{1,0:T(8,128)}, u32[]{:S(2)}) copy-start(f32[128,512]{1,0:T(8,128)} %refs_2_.1) | copy-start | bytes 786436
  2.1 1.5 %collective-permute-start.1 = (f32[264,128]{1,0:T(8,128)S(1)}, f32[264,128]{1,0:T(8,128)S(1)}, u32[]{:S(2)}, u32[]{:S(2)}) collective-permute-start(f32[264,128]{1,0:T(8,128)S(1)} %get-tuple-element.35), channel_id=1, source_target_pairs={{0,4},{4,0},{8,12},{12,8},{16,20},{20,16},{24,28},{28,24},{1,5},{5... | collective-permute-start | bytes 405512 | tf_op jit(solution)/shard_map/ppermute | solution.py:24
  2.6 7.0 %collective-permute-start.3 = (f32[128,512]{1,0:T(8,128)S(1)}, f32[128,512]{1,0:T(8,128)S(1)}, u32[]{:S(2)}, u32[]{:S(2)}) collective-permute-start(f32[128,512]{1,0:T(8,128)S(1)} %copy-done), channel_id=1, source_target_pairs={{0,4},{4,0},{8,12},{12,8},{16,20},{20,16},{24,28},{28,24},{1,5},{5... | collective-permute-start | bytes 786440 | tf_op jit(solution)/shard_map/ppermute | solution.py:24
  3.6 5.9 %collective-permute-start.2 = (f32[264,128]{1,0:T(8,128)S(1)}, f32[264,128]{1,0:T(8,128)S(1)}, u32[]{:S(2)}, u32[]{:S(2)}) collective-permute-start(f32[264,128]{1,0:T(8,128)S(1)} %add.26), channel_id=1, source_target_pairs={{0,8},{4,20},{8,0},{12,28},{16,24},{20,4},{24,16},{28,12},{1,9},{5... | collective-permute-start | bytes 405512 | tf_op jit(solution)/shard_map/ppermute | solution.py:24
  9.5 5.2 %copy-start.3 = (s32[3,2]{0,1:T(2,128)S(1)}, s32[3,2]{0,1:T(2,128)}, u32[]{:S(2)}) copy-start(s32[3,2]{0,1:T(2,128)} %param.5) | copy-start | bytes 76
  9.5 5.1 %collective-permute-start.4 = (f32[264,128]{1,0:T(8,128)S(1)}, f32[264,128]{1,0:T(8,128)S(1)}, u32[]{:S(2)}, u32[]{:S(2)}) collective-permute-start(f32[264,128]{1,0:T(8,128)S(1)} %add.27), channel_id=1, source_target_pairs={{0,16},{4,12},{8,24},{12,4},{16,0},{20,28},{24,8},{28,20},{1,17},{... | collective-permute-start | bytes 405512 | tf_op jit(solution)/shard_map/ppermute | solution.py:24
  14.7 1.4 %collective-permute-start.5 = (f32[264,128]{1,0:T(8,128)S(1)}, f32[264,128]{1,0:T(8,128)S(1)}, u32[]{:S(2)}, u32[]{:S(2)}) collective-permute-start(f32[264,128]{1,0:T(8,128)S(1)} %add.28.own_sum), channel_id=1, source_target_pairs={{0,4},{4,0},{8,12},{12,8},{16,20},{20,16},{24,28},{28,24},{1,5},{5... | collective-permute-start | bytes 405512 | tf_op jit(solution)/shard_map/ppermute | solution.py:24
  16.1 5.6 %copy-start.1 = (f32[128,512]{1,0:T(8,128)S(1)}, f32[128,512]{1,0:T(8,128)}, u32[]{:S(2)}) copy-start(f32[128,512]{1,0:T(8,128)} %refs_2_.1) | copy-start | bytes 786436
  18.3 8.0 %collective-permute-start.6 = (f32[256,128]{1,0:T(8,128)S(1)}, f32[256,128]{1,0:T(8,128)S(1)}, u32[]{:S(2)}, u32[]{:S(2)}) collective-permute-start(f32[256,128]{1,0:T(8,128)S(1)} %get-tuple-element.44), channel_id=1, source_target_pairs={{0,1},{1,2},{2,3},{3,0},{4,5},{5,6},{6,7},{7,4},{8,9},{9,10},{10,1... | collective-permute-start | bytes 393224 | tf_op jit(solution)/shard_map/ppermute | solution.py:18
  20.4 1.1 %collective-permute-start = (f32[128]{0:T(128)S(1)}, f32[128]{0:T(128)S(1)}, u32[]{:S(2)}, u32[]{:S(2)}) collective-permute-start(f32[128]{0:T(128)S(1)} %copy-done.2), channel_id=1, source_target_pairs={{0,4},{4,0},{8,12},{12,8},{16,20},{20,16},{24,28},{28,24},{1,5},{5... | collective-permute-start | bytes 1544 | tf_op jit(solution)/shard_map/ppermute | solution.py:24
  26.5 5.1 %collective-permute-start.7 = (f32[264,128]{1,0:T(8,128)S(1)}, f32[264,128]{1,0:T(8,128)S(1)}, u32[]{:S(2)}, u32[]{:S(2)}) collective-permute-start(f32[264,128]{1,0:T(8,128)S(1)} %shard_map.40), channel_id=1, source_target_pairs={{0,8},{4,20},{8,0},{12,28},{16,24},{20,4},{24,16},{28,12},{1,9},{5... | collective-permute-start | bytes 405512 | tf_op jit(solution)/shard_map/ppermute | solution.py:24
  28.1 3.5 %collective-permute-start.8 = (f32[256,128]{1,0:T(8,128)S(1)}, f32[256,128]{1,0:T(8,128)S(1)}, u32[]{:S(2)}, u32[]{:S(2)}) collective-permute-start(f32[256,128]{1,0:T(8,128)S(1)} %collective-permute-done.6.own_ref.refs_1_.refs_3_), channel_id=1, source_target_pairs={{0,4},{4,0},{8,12},{12,8},{16,20},{20,16},{24,28},{28,24},{1,5},{5... | collective-permute-start | bytes 393224 | tf_op jit(solution)/shard_map/ppermute | solution.py:24
  31.6 5.1 %collective-permute-start.9 = (f32[264,128]{1,0:T(8,128)S(1)}, f32[264,128]{1,0:T(8,128)S(1)}, u32[]{:S(2)}, u32[]{:S(2)}) collective-permute-start(f32[264,128]{1,0:T(8,128)S(1)} %add.29), channel_id=1, source_target_pairs={{0,16},{4,12},{8,24},{12,4},{16,0},{20,28},{24,8},{28,20},{1,17},{... | collective-permute-start | bytes 405512 | tf_op jit(solution)/shard_map/ppermute | solution.py:24
  36.7 1.4 %collective-permute-start.10 = (f32[264,128]{1,0:T(8,128)S(1)}, f32[264,128]{1,0:T(8,128)S(1)}, u32[]{:S(2)}, u32[]{:S(2)}) collective-permute-start(f32[264,128]{1,0:T(8,128)S(1)} %add.30.own_sum), channel_id=1, source_target_pairs={{0,4},{4,0},{8,12},{12,8},{16,20},{20,16},{24,28},{28,24},{1,5},{5... | collective-permute-start | bytes 405512 | tf_op jit(solution)/shard_map/ppermute | solution.py:24
  40.4 7.4 %collective-permute-start.11 = (f32[256,128]{1,0:T(8,128)S(1)}, f32[256,128]{1,0:T(8,128)S(1)}, u32[]{:S(2)}, u32[]{:S(2)}) collective-permute-start(f32[256,128]{1,0:T(8,128)S(1)} %get-tuple-element.54), channel_id=1, source_target_pairs={{0,1},{1,2},{2,3},{3,0},{4,5},{5,6},{6,7},{7,4},{8,9},{9,10},{10,1... | collective-permute-start | bytes 393224 | tf_op jit(solution)/shard_map/ppermute | solution.py:18
  48.0 5.1 %collective-permute-start.12 = (f32[264,128]{1,0:T(8,128)S(1)}, f32[264,128]{1,0:T(8,128)S(1)}, u32[]{:S(2)}, u32[]{:S(2)}) collective-permute-start(f32[264,128]{1,0:T(8,128)S(1)} %shard_map.43), channel_id=1, source_target_pairs={{0,8},{4,20},{8,0},{12,28},{16,24},{20,4},{24,16},{28,12},{1,9},{5... | collective-permute-start | bytes 405512 | tf_op jit(solution)/shard_map/ppermute | solution.py:24
  49.6 3.5 %collective-permute-start.13 = (f32[256,128]{1,0:T(8,128)S(1)}, f32[256,128]{1,0:T(8,128)S(1)}, u32[]{:S(2)}, u32[]{:S(2)}) collective-permute-start(f32[256,128]{1,0:T(8,128)S(1)} %collective-permute-done.11.own_ref.refs_1_.refs_3_), channel_id=1, source_target_pairs={{0,4},{4,0},{8,12},{12,8},{16,20},{20,16},{24,28},{28,24},{1,5},{5... | collective-permute-start | bytes 393224 | tf_op jit(solution)/shard_map/ppermute | solution.py:24
  53.1 5.1 %collective-permute-start.14 = (f32[264,128]{1,0:T(8,128)S(1)}, f32[264,128]{1,0:T(8,128)S(1)}, u32[]{:S(2)}, u32[]{:S(2)}) collective-permute-start(f32[264,128]{1,0:T(8,128)S(1)} %add.31), channel_id=1, source_target_pairs={{0,16},{4,12},{8,24},{12,4},{16,0},{20,28},{24,8},{28,20},{1,17},{... | collective-permute-start | bytes 405512 | tf_op jit(solution)/shard_map/ppermute | solution.py:24
  58.2 1.4 %collective-permute-start.15 = (f32[264,128]{1,0:T(8,128)S(1)}, f32[264,128]{1,0:T(8,128)S(1)}, u32[]{:S(2)}, u32[]{:S(2)}) collective-permute-start(f32[264,128]{1,0:T(8,128)S(1)} %add.32.own_sum), channel_id=1, source_target_pairs={{0,4},{4,0},{8,12},{12,8},{16,20},{20,16},{24,28},{28,24},{1,5},{5... | collective-permute-start | bytes 405512 | tf_op jit(solution)/shard_map/ppermute | solution.py:24
  61.6 7.2 %collective-permute-start.16 = (f32[128,256]{1,0:T(8,128)S(1)}, f32[128,256]{1,0:T(8,128)S(1)}, u32[]{:S(2)}, u32[]{:S(2)}) collective-permute-start(f32[128,256]{1,0:T(8,128)S(1)} %get-tuple-element.60), channel_id=1, source_target_pairs={{0,2},{1,3},{2,0},{3,1},{4,6},{5,7},{6,4},{7,5},{8,10},{9,11},{10,... | collective-permute-start | bytes 393224 | tf_op jit(solution)/shard_map/ppermute | solution.py:18

commit v5 on v4

--- a/solution.py
+++ b/solution.py
@@ -252,7 +252,7 @@
     own_part, other_part = pl.pallas_call(
         start_kernel,
         out_shape=[jax.ShapeDtypeStruct((width + 8, half), F32)] * 2,
-        in_specs=[ANYWHERE] * 2,
+        in_specs=[pl.BlockSpec(memory_space=pltpu.HBM)] * 2,
         out_specs=[ON_CHIP] * 2,
         scratch_shapes=[
             pltpu.VMEM((rows, columns), F32),
@@ -260,7 +260,7 @@
             pltpu.SemaphoreType.DMA(()),
             pltpu.SemaphoreType.DMA(()),
         ],
-        compiler_params=GRANT,
+        compiler_params=pltpu.CompilerParams(vmem_limit_bytes=(64 << 20) - (10752 << 10)),
     )(snapshot, weights[None])
     payload = own_part + swapped(other_part, 1, 1)
     weight = jnp.concatenate([weights, swapped(weights, 1, 1)])[:, None]

time: 69.7 us -> 69.7 us (level)
  local copies, waits for them, and re-layouts: 1.82 us -> 0.91 us
  Pallas kernels: 14.4 us -> 15.3 us
    pallas_call x1, Pallas kernels: 0.45 us -> 1.38 us  [body(): pl.pallas_call(start_kernel, out_shape=[jax.ShapeDtypeStruct((width + 8,...]
    unnamed x8 -> x6, local copies, waits for them, and re-layouts: 1.61 us -> 0.71 us
where the time goes in v5:
time: 69.7 us; the launch traced here: 69.6 us
  waiting for transfers between devices  38.6 us (55%)
  Pallas kernels  15.3 us (22%)
  starting transfers between devices  14.4 us (21%)
  local copies, waits for them, and re-layouts  0.91 us (1%)
    ppermute x14, waiting for transfers between devices, swapped(): return lax.ppermute(value, 'pts', pairs)  25.9 us
    ppermute x3, waiting for transfers between devices, shifted(): return lax.ppermute(value, axis, pairs)  12.7 us
    ppermute x14, starting transfers between devices, swapped(): return lax.ppermute(value, 'pts', pairs)  12.1 us
    pallas_call x7, Pallas kernels, in_vmem(): pl.pallas_call(kernel, out_shape=[jax.ShapeDtypeStruct(shape, dtype) for...  10.9 us
    pallas_call x1, Pallas kernels, body(): pl.pallas_call(functools.partial(last_upper_kernel, blocks), out_shape=ou...  2.39 us
    ppermute x3, starting transfers between devices, shifted(): return lax.ppermute(value, axis, pairs)  2.26 us
  transfers between devices with their start and end apart: 17, of which 14 were waited for; matrix products, arithmetic and copies ran while one was open for 0% of the time, Pallas kernels for 9%

profile of v5, /device:TPU:0, one launch (start us, length us, event | category | flops | bytes accessed | tf_op | source)
XLA Modules:
  0.0 69.6 jit_solution(11317459604729031820)
XLA Ops:
  0.7 1.4 %shard_map.37 = (f32[264,128]{1,0:T(8,128)S(1)}, f32[264,128]{1,0:T(8,128)S(1)}) custom-call(f32[128,512]{1,0:T(8,128)} %refs_2_.1, f32[1,128]{1,0:T(1,128)S(1)} %bitcast.4), custom_call_target="tpu_custom_call" | custom-call | tf_op jit(solution)/shard_map/pallas_call | solution.py:252
  3.6 2.9 %collective-permute-start.2 = (f32[264,128]{1,0:T(8,128)S(1)}, f32[264,128]{1,0:T(8,128)S(1)}, u32[]{:S(2)}, u32[]{:S(2)}) collective-permute-start(f32[264,128]{1,0:T(8,128)S(1)} %add.26), channel_id=1, source_target_pairs={{0,8},{4,20},{8,0},{12,28},{16,24},{20,4},{24,16},{28,12},{1,9},{5... | collective-permute-start | bytes 405512 | tf_op jit(solution)/shard_map/ppermute | solution.py:24
  6.5 3.0 %collective-permute-done.2 = f32[264,128]{1,0:T(8,128)S(1)} collective-permute-done((f32[264,128]{1,0:T(8,128)S(1)}, f32[264,128]{1,0:T(8,128)S(1)}, u32[]{:S(2)}, u32[]{:S(2)}) %collective-permute-start.2) | collective-permute-done | bytes 135200 | tf_op jit(solution)/shard_map/ppermute | solution.py:24
  9.6 2.1 %collective-permute-start.4 = (f32[264,128]{1,0:T(8,128)S(1)}, f32[264,128]{1,0:T(8,128)S(1)}, u32[]{:S(2)}, u32[]{:S(2)}) collective-permute-start(f32[264,128]{1,0:T(8,128)S(1)} %add.27), channel_id=1, source_target_pairs={{0,16},{4,12},{8,24},{12,4},{16,0},{20,28},{24,8},{28,20},{1,17},{... | collective-permute-start | bytes 405512 | tf_op jit(solution)/shard_map/ppermute | solution.py:24
  11.7 3.0 %collective-permute-done.4 = f32[264,128]{1,0:T(8,128)S(1)} collective-permute-done((f32[264,128]{1,0:T(8,128)S(1)}, f32[264,128]{1,0:T(8,128)S(1)}, u32[]{:S(2)}, u32[]{:S(2)}) %collective-permute-start.4) | collective-permute-done | bytes 135200 | tf_op jit(solution)/shard_map/ppermute | solution.py:24
  16.1 2.2 %shard_map.38 = (f32[256,128]{1,0:T(8,128)S(1)}, f32[256,256]{1,0:T(8,128)S(1)}, f32[8,128]{1,0:T(8,128)S(1)}) custom-call(f32[3,128]{1,0:T(4,128)S(1)} %broadcast_in_dim.15.damps, f32[264,128]{1,0:T(8,128)S(1)} %add.28.own_sum, f32[264,128]{1,0:T(8,128)S(1)} %collective-permute-done.5.other_sum, f32[128,512]{1,0:T(8,128)S(1)} %copy-done, ...), custom_call_target="tpu_custom_call" | custom-call | tf_op jit(solution)/shard_map/pallas_call | solution.py:238
  18.3 2.1 %collective-permute-start.6 = (f32[256,128]{1,0:T(8,128)S(1)}, f32[256,128]{1,0:T(8,128)S(1)}, u32[]{:S(2)}, u32[]{:S(2)}) collective-permute-start(f32[256,128]{1,0:T(8,128)S(1)} %get-tuple-element.44), channel_id=1, source_target_pairs={{0,1},{1,2},{2,3},{3,0},{4,5},{5,6},{6,7},{7,4},{8,9},{9,10},{10,1... | collective-permute-start | bytes 393224 | tf_op jit(solution)/shard_map/ppermute | solution.py:18
  21.7 2.0 %shard_map.39 = (bf16[256,768]{1,0:T(8,128)(2,1)S(1)}, f32[1,128]{1,0:T(1,128)S(1)}, f32[256,256]{1,0:T(8,128)S(1)}) custom-call(f32[256,1]{1,0:T(8,128)S(1)} %copy.7.weight, f32[256,256]{1,0:T(8,128)S(1)} %get-tuple-element.40.refs_0_, f32[8,128]{1,0:T(8,128)S(1)} %get-tuple-element.41.refs_1_, f32[128,512]{1,0:T(8,128)S(1)} %copy-done, ...), custom_call_target="tpu_custom_call" | custom-call | tf_op jit(solution)/shard_map/pallas_call | solution.py:238
  23.7 2.6 %collective-permute-done.6.own_ref.refs_1_.refs_3_ = f32[256,128]{1,0:T(8,128)S(1)} collective-permute-done((f32[256,128]{1,0:T(8,128)S(1)}, f32[256,128]{1,0:T(8,128)S(1)}, u32[]{:S(2)}, u32[]{:S(2)}) %collective-permute-start.6) | collective-permute-done | bytes 131104 | tf_op jit(solution)/shard_map/ppermute | solution.py:18
  26.6 1.6 %collective-permute-start.7 = (f32[264,128]{1,0:T(8,128)S(1)}, f32[264,128]{1,0:T(8,128)S(1)}, u32[]{:S(2)}, u32[]{:S(2)}) collective-permute-start(f32[264,128]{1,0:T(8,128)S(1)} %shard_map.40), channel_id=1, source_target_pairs={{0,8},{4,20},{8,0},{12,28},{16,24},{20,4},{24,16},{28,12},{1,9},{5... | collective-permute-start | bytes 405512 | tf_op jit(solution)/shard_map/ppermute | solution.py:24
  28.1 3.5 %collective-permute-done.7 = f32[264,128]{1,0:T(8,128)S(1)} collective-permute-done((f32[264,128]{1,0:T(8,128)S(1)}, f32[264,128]{1,0:T(8,128)S(1)}, u32[]{:S(2)}, u32[]{:S(2)}) %collective-permute-start.7) | collective-permute-done | bytes 135200 | tf_op jit(solution)/shard_map/ppermute | solution.py:24
  31.7 1.6 %collective-permute-start.9 = (f32[264,128]{1,0:T(8,128)S(1)}, f32[264,128]{1,0:T(8,128)S(1)}, u32[]{:S(2)}, u32[]{:S(2)}) collective-permute-start(f32[264,128]{1,0:T(8,128)S(1)} %add.29), channel_id=1, source_target_pairs={{0,16},{4,12},{8,24},{12,4},{16,0},{20,28},{24,8},{28,20},{1,17},{... | collective-permute-start | bytes 405512 | tf_op jit(solution)/shard_map/ppermute | solution.py:24
  33.2 3.5 %collective-permute-done.9 = f32[264,128]{1,0:T(8,128)S(1)} collective-permute-done((f32[264,128]{1,0:T(8,128)S(1)}, f32[264,128]{1,0:T(8,128)S(1)}, u32[]{:S(2)}, u32[]{:S(2)}) %collective-permute-start.9) | collective-permute-done | bytes 135200 | tf_op jit(solution)/shard_map/ppermute | solution.py:24
  36.8 1.3 %collective-permute-done.10.other_sum = f32[264,128]{1,0:T(8,128)S(1)} collective-permute-done((f32[264,128]{1,0:T(8,128)S(1)}, f32[264,128]{1,0:T(8,128)S(1)}, u32[]{:S(2)}, u32[]{:S(2)}) %collective-permute-start.10) | collective-permute-done | bytes 135200 | tf_op jit(solution)/shard_map/ppermute | solution.py:24
  38.2 2.2 %shard_map.41 = (f32[256,128]{1,0:T(8,128)S(1)}, f32[256,256]{1,0:T(8,128)S(1)}, f32[8,128]{1,0:T(8,128)S(1)}) custom-call(f32[3,128]{1,0:T(4,128)S(1)} %broadcast_in_dim.15.damps, f32[264,128]{1,0:T(8,128)S(1)} %add.30.own_sum, f32[264,128]{1,0:T(8,128)S(1)} %collective-permute-done.10.other_sum, f32[256,256]{1,0:T(8,128)S(1)} %get-tuple-element.48.refs_0_.refs_2_, ...), custom_call_target="tpu_custom_call" | custom-call | tf_op jit(solution)/shard_map/pallas_call | solution.py:238
  40.5 2.0 %shard_map.42 = (bf16[256,768]{1,0:T(8,128)(2,1)S(1)}, f32[1,128]{1,0:T(1,128)S(1)}, f32[256,256]{1,0:T(8,128)S(1)}) custom-call(f32[256,1]{1,0:T(8,128)S(1)} %copy.7.weight, f32[256,256]{1,0:T(8,128)S(1)} %get-tuple-element.50.refs_0_, f32[8,128]{1,0:T(8,128)S(1)} %get-tuple-element.51.refs_1_, f32[256,256]{1,0:T(8,128)S(1)} %get-tuple-element.48.refs_0_.refs_2_, ...), custom_call_target="tpu_custom_call" | custom-call | tf_op jit(solution)/shard_map/pallas_call | solution.py:238
  42.5 5.3 %collective-permute-done.11.own_ref.refs_1_.refs_3_ = f32[256,128]{1,0:T(8,128)S(1)} collective-permute-done((f32[256,128]{1,0:T(8,128)S(1)}, f32[256,128]{1,0:T(8,128)S(1)}, u32[]{:S(2)}, u32[]{:S(2)}) %collective-permute-start.11) | collective-permute-done | bytes 131104 | tf_op jit(solution)/shard_map/ppermute | solution.py:18
  48.1 1.6 %collective-permute-start.12 = (f32[264,128]{1,0:T(8,128)S(1)}, f32[264,128]{1,0:T(8,128)S(1)}, u32[]{:S(2)}, u32[]{:S(2)}) collective-permute-start(f32[264,128]{1,0:T(8,128)S(1)} %shard_map.43), channel_id=1, source_target_pairs={{0,8},{4,20},{8,0},{12,28},{16,24},{20,4},{24,16},{28,12},{1,9},{5... | collective-permute-start | bytes 405512 | tf_op jit(solution)/shard_map/ppermute | solution.py:24
  49.6 3.5 %collective-permute-done.12 = f32[264,128]{1,0:T(8,128)S(1)} collective-permute-done((f32[264,128]{1,0:T(8,128)S(1)}, f32[264,128]{1,0:T(8,128)S(1)}, u32[]{:S(2)}, u32[]{:S(2)}) %collective-permute-start.12) | collective-permute-done | bytes 135200 | tf_op jit(solution)/shard_map/ppermute | solution.py:24
  53.2 1.6 %collective-permute-start.14 = (f32[264,128]{1,0:T(8,128)S(1)}, f32[264,128]{1,0:T(8,128)S(1)}, u32[]{:S(2)}, u32[]{:S(2)}) collective-permute-start(f32[264,128]{1,0:T(8,128)S(1)} %add.31), channel_id=1, source_target_pairs={{0,16},{4,12},{8,24},{12,4},{16,0},{20,28},{24,8},{28,20},{1,17},{... | collective-permute-start | bytes 405512 | tf_op jit(solution)/shard_map/ppermute | solution.py:24
  54.8 3.5 %collective-permute-done.14 = f32[264,128]{1,0:T(8,128)S(1)} collective-permute-done((f32[264,128]{1,0:T(8,128)S(1)}, f32[264,128]{1,0:T(8,128)S(1)}, u32[]{:S(2)}, u32[]{:S(2)}) %collective-permute-start.14) | collective-permute-done | bytes 135200 | tf_op jit(solution)/shard_map/ppermute | solution.py:24
  59.7 2.0 %shard_map.44 = (f32[128,256]{1,0:T(8,128)S(1)}, f32[256,256]{1,0:T(8,128)S(1)}, f32[8,128]{1,0:T(8,128)S(1)}) custom-call(f32[3,128]{1,0:T(4,128)S(1)} %broadcast_in_dim.15.damps, f32[264,128]{1,0:T(8,128)S(1)} %add.32.own_sum, f32[264,128]{1,0:T(8,128)S(1)} %collective-permute-done.15.other_sum, f32[256,256]{1,0:T(8,128)S(1)} %get-tuple-element.58.refs_0_.refs_2_, ...), custom_call_target="tpu_custom_call" | custom-call | tf_op jit(solution)/shard_map/pallas_call | solution.py:238
  61.7 2.4 %shard_map.45.filled = f32[128,512]{1,0:T(8,128)} custom-call(f32[256,256]{1,0:T(8,128)S(1)} %get-tuple-element.61.refs_0_, f32[8,128]{1,0:T(8,128)S(1)} %get-tuple-element.62.refs_1_, f32[256,256]{1,0:T(8,128)S(1)} %get-tuple-element.58.refs_0_.refs_2_, f32[256,128]{1,0:T(8,128)S(1)} %collective-permute-done.11.own_ref.refs_1_.refs_3_, ...), custom_call_target="tpu_custom_call" | custom-call | tf_op jit(solution)/shard_map/pallas_call | solution.py:297
  64.1 4.8 %collective-permute-done.16.lower = f32[128,256]{1,0:T(8,128)S(1)} collective-permute-done((f32[128,256]{1,0:T(8,128)S(1)}, f32[128,256]{1,0:T(8,128)S(1)}, u32[]{:S(2)}, u32[]{:S(2)}) %collective-permute-start.16) | collective-permute-done | bytes 131104 | tf_op jit(solution)/shard_map/ppermute | solution.py:18
  (37 shorter events, 7.8 us)
Async XLA Ops:
  0.0 2.6 %copy-start = (f32[128,512]{1,0:T(8,128)S(1)}, f32[128,512]{1,0:T(8,128)}, u32[]{:S(2)}) copy-start(f32[128,512]{1,0:T(8,128)} %refs_2_.1) | copy-start | bytes 786436
  0.0 0.7 %copy-start.1 = (f32[128]{0:T(128)S(1)}, f32[128]{0:T(128)}, u32[]{:S(2)}) copy-start(f32[128]{0:T(128)} %param.4) | copy-start | bytes 1540
  2.1 1.5 %collective-permute-start.1 = (f32[264,128]{1,0:T(8,128)S(1)}, f32[264,128]{1,0:T(8,128)S(1)}, u32[]{:S(2)}, u32[]{:S(2)}) collective-permute-start(f32[264,128]{1,0:T(8,128)S(1)} %get-tuple-element.35), channel_id=1, source_target_pairs={{0,4},{4,0},{8,12},{12,8},{16,20},{20,16},{24,28},{28,24},{1,5},{5... | collective-permute-start | bytes 405512 | tf_op jit(solution)/shard_map/ppermute | solution.py:24
  2.6 7.0 %collective-permute-start.3 = (f32[128,512]{1,0:T(8,128)S(1)}, f32[128,512]{1,0:T(8,128)S(1)}, u32[]{:S(2)}, u32[]{:S(2)}) collective-permute-start(f32[128,512]{1,0:T(8,128)S(1)} %copy-done), channel_id=1, source_target_pairs={{0,4},{4,0},{8,12},{12,8},{16,20},{20,16},{24,28},{28,24},{1,5},{5... | collective-permute-start | bytes 786440 | tf_op jit(solution)/shard_map/ppermute | solution.py:24
  3.6 5.9 %collective-permute-start.2 = (f32[264,128]{1,0:T(8,128)S(1)}, f32[264,128]{1,0:T(8,128)S(1)}, u32[]{:S(2)}, u32[]{:S(2)}) collective-permute-start(f32[264,128]{1,0:T(8,128)S(1)} %add.26), channel_id=1, source_target_pairs={{0,8},{4,20},{8,0},{12,28},{16,24},{20,4},{24,16},{28,12},{1,9},{5... | collective-permute-start | bytes 405512 | tf_op jit(solution)/shard_map/ppermute | solution.py:24
  9.5 5.2 %copy-start.2 = (s32[3,2]{0,1:T(2,128)S(1)}, s32[3,2]{0,1:T(2,128)}, u32[]{:S(2)}) copy-start(s32[3,2]{0,1:T(2,128)} %param.5) | copy-start | bytes 76
  9.6 5.1 %collective-permute-start.4 = (f32[264,128]{1,0:T(8,128)S(1)}, f32[264,128]{1,0:T(8,128)S(1)}, u32[]{:S(2)}, u32[]{:S(2)}) collective-permute-start(f32[264,128]{1,0:T(8,128)S(1)} %add.27), channel_id=1, source_target_pairs={{0,16},{4,12},{8,24},{12,4},{16,0},{20,28},{24,8},{28,20},{1,17},{... | collective-permute-start | bytes 405512 | tf_op jit(solution)/shard_map/ppermute | solution.py:24
  14.7 1.4 %collective-permute-start.5 = (f32[264,128]{1,0:T(8,128)S(1)}, f32[264,128]{1,0:T(8,128)S(1)}, u32[]{:S(2)}, u32[]{:S(2)}) collective-permute-start(f32[264,128]{1,0:T(8,128)S(1)} %add.28.own_sum), channel_id=1, source_target_pairs={{0,4},{4,0},{8,12},{12,8},{16,20},{20,16},{24,28},{28,24},{1,5},{5... | collective-permute-start | bytes 405512 | tf_op jit(solution)/shard_map/ppermute | solution.py:24
  18.3 8.0 %collective-permute-start.6 = (f32[256,128]{1,0:T(8,128)S(1)}, f32[256,128]{1,0:T(8,128)S(1)}, u32[]{:S(2)}, u32[]{:S(2)}) collective-permute-start(f32[256,128]{1,0:T(8,128)S(1)} %get-tuple-element.44), channel_id=1, source_target_pairs={{0,1},{1,2},{2,3},{3,0},{4,5},{5,6},{6,7},{7,4},{8,9},{9,10},{10,1... | collective-permute-start | bytes 393224 | tf_op jit(solution)/shard_map/ppermute | solution.py:18
  20.5 1.1 %collective-permute-start = (f32[128]{0:T(128)S(1)}, f32[128]{0:T(128)S(1)}, u32[]{:S(2)}, u32[]{:S(2)}) collective-permute-start(f32[128]{0:T(128)S(1)} %copy-done.1), channel_id=1, source_target_pairs={{0,4},{4,0},{8,12},{12,8},{16,20},{20,16},{24,28},{28,24},{1,5},{5... | collective-permute-start | bytes 1544 | tf_op jit(solution)/shard_map/ppermute | solution.py:24
  26.6 5.1 %collective-permute-start.7 = (f32[264,128]{1,0:T(8,128)S(1)}, f32[264,128]{1,0:T(8,128)S(1)}, u32[]{:S(2)}, u32[]{:S(2)}) collective-permute-start(f32[264,128]{1,0:T(8,128)S(1)} %shard_map.40), channel_id=1, source_target_pairs={{0,8},{4,20},{8,0},{12,28},{16,24},{20,4},{24,16},{28,12},{1,9},{5... | collective-permute-start | bytes 405512 | tf_op jit(solution)/shard_map/ppermute | solution.py:24
  28.1 3.5 %collective-permute-start.8 = (f32[256,128]{1,0:T(8,128)S(1)}, f32[256,128]{1,0:T(8,128)S(1)}, u32[]{:S(2)}, u32[]{:S(2)}) collective-permute-start(f32[256,128]{1,0:T(8,128)S(1)} %collective-permute-done.6.own_ref.refs_1_.refs_3_), channel_id=1, source_target_pairs={{0,4},{4,0},{8,12},{12,8},{16,20},{20,16},{24,28},{28,24},{1,5},{5... | collective-permute-start | bytes 393224 | tf_op jit(solution)/shard_map/ppermute | solution.py:24
  31.7 5.1 %collective-permute-start.9 = (f32[264,128]{1,0:T(8,128)S(1)}, f32[264,128]{1,0:T(8,128)S(1)}, u32[]{:S(2)}, u32[]{:S(2)}) collective-permute-start(f32[264,128]{1,0:T(8,128)S(1)} %add.29), channel_id=1, source_target_pairs={{0,16},{4,12},{8,24},{12,4},{16,0},{20,28},{24,8},{28,20},{1,17},{... | collective-permute-start | bytes 405512 | tf_op jit(solution)/shard_map/ppermute | solution.py:24
  36.8 1.4 %collective-permute-start.10 = (f32[264,128]{1,0:T(8,128)S(1)}, f32[264,128]{1,0:T(8,128)S(1)}, u32[]{:S(2)}, u32[]{:S(2)}) collective-permute-start(f32[264,128]{1,0:T(8,128)S(1)} %add.30.own_sum), channel_id=1, source_target_pairs={{0,4},{4,0},{8,12},{12,8},{16,20},{20,16},{24,28},{28,24},{1,5},{5... | collective-permute-start | bytes 405512 | tf_op jit(solution)/shard_map/ppermute | solution.py:24
  40.4 7.4 %collective-permute-start.11 = (f32[256,128]{1,0:T(8,128)S(1)}, f32[256,128]{1,0:T(8,128)S(1)}, u32[]{:S(2)}, u32[]{:S(2)}) collective-permute-start(f32[256,128]{1,0:T(8,128)S(1)} %get-tuple-element.54), channel_id=1, source_target_pairs={{0,1},{1,2},{2,3},{3,0},{4,5},{5,6},{6,7},{7,4},{8,9},{9,10},{10,1... | collective-permute-start | bytes 393224 | tf_op jit(solution)/shard_map/ppermute | solution.py:18
  48.1 5.1 %collective-permute-start.12 = (f32[264,128]{1,0:T(8,128)S(1)}, f32[264,128]{1,0:T(8,128)S(1)}, u32[]{:S(2)}, u32[]{:S(2)}) collective-permute-start(f32[264,128]{1,0:T(8,128)S(1)} %shard_map.43), channel_id=1, source_target_pairs={{0,8},{4,20},{8,0},{12,28},{16,24},{20,4},{24,16},{28,12},{1,9},{5... | collective-permute-start | bytes 405512 | tf_op jit(solution)/shard_map/ppermute | solution.py:24
  49.6 3.5 %collective-permute-start.13 = (f32[256,128]{1,0:T(8,128)S(1)}, f32[256,128]{1,0:T(8,128)S(1)}, u32[]{:S(2)}, u32[]{:S(2)}) collective-permute-start(f32[256,128]{1,0:T(8,128)S(1)} %collective-permute-done.11.own_ref.refs_1_.refs_3_), channel_id=1, source_target_pairs={{0,4},{4,0},{8,12},{12,8},{16,20},{20,16},{24,28},{28,24},{1,5},{5... | collective-permute-start | bytes 393224 | tf_op jit(solution)/shard_map/ppermute | solution.py:24
  53.2 5.1 %collective-permute-start.14 = (f32[264,128]{1,0:T(8,128)S(1)}, f32[264,128]{1,0:T(8,128)S(1)}, u32[]{:S(2)}, u32[]{:S(2)}) collective-permute-start(f32[264,128]{1,0:T(8,128)S(1)} %add.31), channel_id=1, source_target_pairs={{0,16},{4,12},{8,24},{12,4},{16,0},{20,28},{24,8},{28,20},{1,17},{... | collective-permute-start | bytes 405512 | tf_op jit(solution)/shard_map/ppermute | solution.py:24
  58.3 1.4 %collective-permute-start.15 = (f32[264,128]{1,0:T(8,128)S(1)}, f32[264,128]{1,0:T(8,128)S(1)}, u32[]{:S(2)}, u32[]{:S(2)}) collective-permute-start(f32[264,128]{1,0:T(8,128)S(1)} %add.32.own_sum), channel_id=1, source_target_pairs={{0,4},{4,0},{8,12},{12,8},{16,20},{20,16},{24,28},{28,24},{1,5},{5... | collective-permute-start | bytes 405512 | tf_op jit(solution)/shard_map/ppermute | solution.py:24
  61.7 7.2 %collective-permute-start.16 = (f32[128,256]{1,0:T(8,128)S(1)}, f32[128,256]{1,0:T(8,128)S(1)}, u32[]{:S(2)}, u32[]{:S(2)}) collective-permute-start(f32[128,256]{1,0:T(8,128)S(1)} %get-tuple-element.60), channel_id=1, source_target_pairs={{0,2},{1,3},{2,0},{3,1},{4,6},{5,7},{6,4},{7,5},{8,10},{9,11},{10,... | collective-permute-start | bytes 393224 | tf_op jit(solution)/shard_map/ppermute | solution.py:18

commit v6 on v5

--- a/solution.py
+++ b/solution.py
@@ -45,36 +45,15 @@
     return high, (value - high.astype(F32)).astype(jnp.bfloat16)
 
 
-def as_left(value):
-    high, low = two_parts(value)
-    return jnp.concatenate([high, high, low], axis=1)
-
-
-def as_right(value):
-    high, low = two_parts(value)
-    return jnp.concatenate([high, low, high], axis=0)
-
-
-def product(left, right):
-    return jnp.dot(left, right, preferred_element_type=F32)
-
-
-def product_tl(left, right):
-    high, low = two_parts(left)
+def first_columns(parts, columns):
+    return parts[0][:, :columns], parts[1][:, :columns]
+
+
+def product(left, right, left_axis=1, right_axis=0):
     return lax.dot_general(
-        jnp.concatenate([high, high, low], axis=0),
-        right,
-        (((0,), (0,)), ((), ())),
-        preferred_element_type=F32,
-    )
-
-
-def product_bt(left, right):
-    high, low = two_parts(right)
-    return lax.dot_general(
-        as_left(left),
-        jnp.concatenate([high, low, high], axis=1),
-        (((1,), (1,)), ((), ())),
+        jnp.concatenate([left[0], left[0], left[1]], axis=left_axis),
+        jnp.concatenate([right[0], right[1], right[0]], axis=right_axis),
+        (((left_axis,), (right_axis,)), ((), ())),
         preferred_element_type=F32,
     )
 
@@ -84,27 +63,23 @@
     return jnp.concatenate([value[half:], value[:half]], axis=0)
 
 
-def unit(width):
-    rows = lax.broadcasted_iota(jnp.int32, (width, width), 0)
-    columns = lax.broadcasted_iota(jnp.int32, (width, width), 1)
-    return jnp.where(rows == columns, 1.0, 0.0).astype(F32)
-
-
 def times_inverse_root(left, square, scale, columns):
-    identity = unit(square.shape[0])
+    rows = lax.broadcasted_iota(jnp.int32, square.shape, 0)
+    identity = jnp.where(rows == lax.broadcasted_iota(jnp.int32, square.shape, 1), 1.0, 0.0)
     base = (identity + square) * (1.0 / scale)
-    base_right = as_right(base)
-    left_parts = as_left(left)
-    second = product(as_left(base), base_right)
-    left_base = product(left_parts, base_right)
-    first_square = 2.25 * identity - 1.5 * base + 0.25 * second
-    both = 2.25 * identity - 0.75 * base
-    both = both - 0.5 * product(as_left(1.5 * base - 0.5 * second), as_right(first_square))
-    both_right = as_right(both)
-    both_square = product(as_left(both), both_right[:, :columns])
-    left_both = product(left_parts, both_right[:, :columns])
-    left_cubic = product(as_left(product(as_left(left_base), both_right)), as_right(both_square))
-    return (1.5 * left_both - 0.5 * left_cubic) * lax.rsqrt(scale)
+    base_parts = two_parts(base)
+    left_parts = two_parts(left)
+    second = product(base_parts, base_parts)
+    left_base = product(left_parts, base_parts)
+    first_square = two_parts(2.25 * identity - 1.5 * base + 0.25 * second)
+    cubic = product(two_parts(1.5 * base - 0.5 * second), first_square)
+    both = two_parts(2.25 * identity - 0.75 * base - 0.5 * cubic)
+    both_first = first_columns(both, columns)
+    both_square = product(both, both_first)
+    left_cubic = product(two_parts(left_base), both)
+    left_both = product(left_parts, both_first)
+    left_last = product(two_parts(left_cubic), two_parts(both_square))
+    return (1.5 * left_both - 0.5 * left_last) * lax.rsqrt(scale)
 
 
 def joined(own, other):
@@ -153,12 +128,12 @@
     own, other = own_half(half)
     point_weight = jnp.broadcast_to(weight[...], (8, weight.shape[1])).T[:, 0:1]
     upper_own, upper_other = near[:, pl.ds(own, half)], near[:, pl.ds(other, half)]
-    upper = jnp.concatenate([upper_own, upper_other], axis=1)
+    upper_parts = two_parts(jnp.concatenate([upper_own, upper_other], axis=1))
     rows = lax.broadcasted_iota(jnp.int32, (8, half), 0)
     for start, norm_of, out in ((own, upper_own, own_part), (other, upper_other, other_part)):
         lower = near[:, pl.ds(width + start, half)]
         weighted = point_weight * lower
-        gram = product_tl(upper, as_right(weighted))
+        gram = product(upper_parts, two_parts(weighted), 0, 0)
         out[:width] = gram if out is own_part else halves_swapped(gram)
         norm_lower = jnp.sum(weighted * lower, axis=0, keepdims=True)
         norm_upper = jnp.sum(point_weight * norm_of * norm_of, axis=0, keepdims=True)
@@ -176,10 +151,10 @@
     scale = 1.0 + jnp.sum(coupling * coupling, keepdims=True)
     coupling_out[...] = coupling
     scale_out[...] = jnp.broadcast_to(scale, scale_out.shape)
-    coupling_right = as_right(coupling)
-    square = product_tl(coupling, coupling_right)
+    parts = two_parts(coupling)
+    square = product(parts, parts, 0, 0)
     rows, columns = moved.shape
-    mixed = lower[:rows] + product(as_left(upper[:rows]), coupling_right)
+    mixed = lower[:rows] + product(two_parts(upper[:rows]), parts)
     result = times_inverse_root(mixed, square, scale, columns)
     if last:
         stored(moved, result)
@@ -190,8 +165,9 @@
 def rotated_upper(blocks, rows, coupling_ref, scale_ref, *block_refs):
     coupling = coupling_ref[...]
     upper, lower = blocks(*block_refs)
-    mixed = upper[:rows] - product_bt(lower[:rows], coupling)
-    square = product_bt(coupling, coupling)
+    parts = two_parts(coupling)
+    mixed = upper[:rows] - product(two_parts(lower[:rows]), parts, 1, 1)
+    square = product(parts, parts, 1, 1)
     return times_inverse_root(mixed, square, scale_ref[0:1, 0:1], coupling.shape[1])
 
 
@@ -201,7 +177,8 @@
     upper_out[...] = upper
     weighted = weight[...] * upper
     norm_out[...] = jnp.sum(weighted * upper, axis=0, keepdims=True)[:, : norm_out.shape[1]]
-    gram_left[...] = as_left(weighted.T)
+    high, low = two_parts(weighted.T)
+    gram_left[...] = jnp.concatenate([high, high, low], axis=1)
 
 
 def last_upper_kernel(blocks, *refs):
@@ -223,7 +200,9 @@
 def gram_kernel(gram_left, norm_upper, weight, own_ref, payload):
     width = gram_left.shape[0]
     own = own_ref[...]
-    payload[:width] = product(gram_left[...], as_right(own))
+    high, low = two_parts(own)
+    right = jnp.concatenate([high, low, high], axis=0)
+    payload[:width] = jnp.dot(gram_left[...], right, preferred_element_type=F32)
     norm_lower = jnp.sum(weight[...] * own * own, axis=0, keepdims=True)
     rows = lax.broadcasted_iota(jnp.int32, (8, own.shape[1]), 0)
     payload[width:] = jnp.where(rows == 0, norm_lower, jnp.where(rows == 1, norm_upper[...], 0.0))
@@ -262,6 +241,7 @@
         ],
         compiler_params=pltpu.CompilerParams(vmem_limit_bytes=(64 << 20) - (10752 << 10)),
     )(snapshot, weights[None])
+    own_part, other_part, damping = lax.optimization_barrier((own_part, other_part, damping))
     payload = own_part + swapped(other_part, 1, 1)
     weight = jnp.concatenate([weights, swapped(weights, 1, 1)])[:, None]
     blocks, held, arriving = start_blocks, (snapshot,), swapped(snapshot, 1, 1)

time: 69.7 us -> 69.1 us (level)
  Pallas kernels: 15.3 us -> 14.4 us
    pallas_call x7, Pallas kernels: 10.9 us -> 10 us  [in_vmem(): pl.pallas_call(kernel, out_shape=[jax.ShapeDtypeStruct(shape, dtype) for...]
where the time goes in v6:
time: 69.1 us; the launch traced here: 69 us
  waiting for transfers between devices  38.9 us (56%)
  Pallas kernels  14.4 us (21%)
  starting transfers between devices  14.4 us (21%)
  local copies, waits for them, and re-layouts  0.91 us (1%)
    ppermute x14, waiting for transfers between devices, swapped(): return lax.ppermute(value, 'pts', pairs)  25.9 us
    ppermute x3, waiting for transfers between devices, shifted(): return lax.ppermute(value, axis, pairs)  13 us
    ppermute x14, starting transfers between devices, swapped(): return lax.ppermute(value, 'pts', pairs)  12.2 us
    pallas_call x7, Pallas kernels, in_vmem(): pl.pallas_call(kernel, out_shape=[jax.ShapeDtypeStruct(shape, dtype) for...  10 us
    pallas_call x1, Pallas kernels, body(): pl.pallas_call(functools.partial(last_upper_kernel, blocks), out_shape=ou...  2.33 us
    ppermute x3, starting transfers between devices, shifted(): return lax.ppermute(value, axis, pairs)  2.26 us
  transfers between devices with their start and end apart: 17, of which 14 were waited for; matrix products, arithmetic and copies ran while one was open for 0% of the time, Pallas kernels for 9%

profile of v6, /device:TPU:0, one launch (start us, length us, event | category | flops | bytes accessed | tf_op | source)
XLA Modules:
  0.0 69.0 jit_solution(14894251431781046263)
XLA Ops:
  0.7 1.4 %shard_map.37 = (f32[264,128]{1,0:T(8,128)S(1)}, f32[264,128]{1,0:T(8,128)S(1)}) custom-call(f32[128,512]{1,0:T(8,128)} %refs_2_.1, f32[1,128]{1,0:T(1,128)S(1)} %bitcast.4), custom_call_target="tpu_custom_call" | custom-call | tf_op jit(solution)/shard_map/pallas_call | solution.py:231
  3.6 2.9 %collective-permute-start.2 = (f32[264,128]{1,0:T(8,128)S(1)}, f32[264,128]{1,0:T(8,128)S(1)}, u32[]{:S(2)}, u32[]{:S(2)}) collective-permute-start(f32[264,128]{1,0:T(8,128)S(1)} %add.26), channel_id=1, source_target_pairs={{0,8},{4,20},{8,0},{12,28},{16,24},{20,4},{24,16},{28,12},{1,9},{5... | collective-permute-start | bytes 405512 | tf_op jit(solution)/shard_map/ppermute | solution.py:24
  6.5 3.0 %collective-permute-done.2 = f32[264,128]{1,0:T(8,128)S(1)} collective-permute-done((f32[264,128]{1,0:T(8,128)S(1)}, f32[264,128]{1,0:T(8,128)S(1)}, u32[]{:S(2)}, u32[]{:S(2)}) %collective-permute-start.2) | collective-permute-done | bytes 135200 | tf_op jit(solution)/shard_map/ppermute | solution.py:24
  9.6 2.1 %collective-permute-start.4 = (f32[264,128]{1,0:T(8,128)S(1)}, f32[264,128]{1,0:T(8,128)S(1)}, u32[]{:S(2)}, u32[]{:S(2)}) collective-permute-start(f32[264,128]{1,0:T(8,128)S(1)} %add.27), channel_id=1, source_target_pairs={{0,16},{4,12},{8,24},{12,4},{16,0},{20,28},{24,8},{28,20},{1,17},{... | collective-permute-start | bytes 405512 | tf_op jit(solution)/shard_map/ppermute | solution.py:24
  11.7 3.0 %collective-permute-done.4 = f32[264,128]{1,0:T(8,128)S(1)} collective-permute-done((f32[264,128]{1,0:T(8,128)S(1)}, f32[264,128]{1,0:T(8,128)S(1)}, u32[]{:S(2)}, u32[]{:S(2)}) %collective-permute-start.4) | collective-permute-done | bytes 135200 | tf_op jit(solution)/shard_map/ppermute | solution.py:24
  16.1 2.0 %shard_map.38 = (f32[256,128]{1,0:T(8,128)S(1)}, f32[256,256]{1,0:T(8,128)S(1)}, f32[8,128]{1,0:T(8,128)S(1)}) custom-call(f32[3,128]{1,0:T(4,128)S(1)} %broadcast_in_dim.16.damps, f32[264,128]{1,0:T(8,128)S(1)} %add.28.own_sum, f32[264,128]{1,0:T(8,128)S(1)} %collective-permute-done.5.other_sum, f32[128,512]{1,0:T(8,128)S(1)} %copy-done, ...), custom_call_target="tpu_custom_call" | custom-call | tf_op jit(solution)/shard_map/pallas_call | solution.py:217
  18.1 2.1 %collective-permute-start.6 = (f32[256,128]{1,0:T(8,128)S(1)}, f32[256,128]{1,0:T(8,128)S(1)}, u32[]{:S(2)}, u32[]{:S(2)}) collective-permute-start(f32[256,128]{1,0:T(8,128)S(1)} %get-tuple-element.50), channel_id=1, source_target_pairs={{0,1},{1,2},{2,3},{3,0},{4,5},{5,6},{6,7},{7,4},{8,9},{9,10},{10,1... | collective-permute-start | bytes 393224 | tf_op jit(solution)/shard_map/ppermute | solution.py:18
  21.5 1.9 %shard_map.39 = (bf16[256,768]{1,0:T(8,128)(2,1)S(1)}, f32[1,128]{1,0:T(1,128)S(1)}, f32[256,256]{1,0:T(8,128)S(1)}) custom-call(f32[256,1]{1,0:T(8,128)S(1)} %copy.7.weight, f32[256,256]{1,0:T(8,128)S(1)} %get-tuple-element.46.refs_0_, f32[8,128]{1,0:T(8,128)S(1)} %get-tuple-element.47.refs_1_, f32[128,512]{1,0:T(8,128)S(1)} %copy-done, ...), custom_call_target="tpu_custom_call" | custom-call | tf_op jit(solution)/shard_map/pallas_call | solution.py:217
  23.4 2.7 %collective-permute-done.6.own_ref.refs_1_.refs_3_ = f32[256,128]{1,0:T(8,128)S(1)} collective-permute-done((f32[256,128]{1,0:T(8,128)S(1)}, f32[256,128]{1,0:T(8,128)S(1)}, u32[]{:S(2)}, u32[]{:S(2)}) %collective-permute-start.6) | collective-permute-done | bytes 131104 | tf_op jit(solution)/shard_map/ppermute | solution.py:18
  26.3 1.6 %collective-permute-start.7 = (f32[264,128]{1,0:T(8,128)S(1)}, f32[264,128]{1,0:T(8,128)S(1)}, u32[]{:S(2)}, u32[]{:S(2)}) collective-permute-start(f32[264,128]{1,0:T(8,128)S(1)} %shard_map.40), channel_id=1, source_target_pairs={{0,8},{4,20},{8,0},{12,28},{16,24},{20,4},{24,16},{28,12},{1,9},{5... | collective-permute-start | bytes 405512 | tf_op jit(solution)/shard_map/ppermute | solution.py:24
  27.9 3.5 %collective-permute-done.7 = f32[264,128]{1,0:T(8,128)S(1)} collective-permute-done((f32[264,128]{1,0:T(8,128)S(1)}, f32[264,128]{1,0:T(8,128)S(1)}, u32[]{:S(2)}, u32[]{:S(2)}) %collective-permute-start.7) | collective-permute-done | bytes 135200 | tf_op jit(solution)/shard_map/ppermute | solution.py:24
  31.4 1.6 %collective-permute-start.9 = (f32[264,128]{1,0:T(8,128)S(1)}, f32[264,128]{1,0:T(8,128)S(1)}, u32[]{:S(2)}, u32[]{:S(2)}) collective-permute-start(f32[264,128]{1,0:T(8,128)S(1)} %add.29), channel_id=1, source_target_pairs={{0,16},{4,12},{8,24},{12,4},{16,0},{20,28},{24,8},{28,20},{1,17},{... | collective-permute-start | bytes 405512 | tf_op jit(solution)/shard_map/ppermute | solution.py:24
  33.0 3.5 %collective-permute-done.9 = f32[264,128]{1,0:T(8,128)S(1)} collective-permute-done((f32[264,128]{1,0:T(8,128)S(1)}, f32[264,128]{1,0:T(8,128)S(1)}, u32[]{:S(2)}, u32[]{:S(2)}) %collective-permute-start.9) | collective-permute-done | bytes 135200 | tf_op jit(solution)/shard_map/ppermute | solution.py:24
  36.6 1.3 %collective-permute-done.10.other_sum = f32[264,128]{1,0:T(8,128)S(1)} collective-permute-done((f32[264,128]{1,0:T(8,128)S(1)}, f32[264,128]{1,0:T(8,128)S(1)}, u32[]{:S(2)}, u32[]{:S(2)}) %collective-permute-start.10) | collective-permute-done | bytes 135200 | tf_op jit(solution)/shard_map/ppermute | solution.py:24
  37.9 2.0 %shard_map.41 = (f32[256,128]{1,0:T(8,128)S(1)}, f32[256,256]{1,0:T(8,128)S(1)}, f32[8,128]{1,0:T(8,128)S(1)}) custom-call(f32[3,128]{1,0:T(4,128)S(1)} %broadcast_in_dim.16.damps, f32[264,128]{1,0:T(8,128)S(1)} %add.30.own_sum, f32[264,128]{1,0:T(8,128)S(1)} %collective-permute-done.10.other_sum, f32[256,256]{1,0:T(8,128)S(1)} %get-tuple-element.54.refs_0_.refs_2_, ...), custom_call_target="tpu_custom_call" | custom-call | tf_op jit(solution)/shard_map/pallas_call | solution.py:217
  40.0 1.9 %shard_map.42 = (bf16[256,768]{1,0:T(8,128)(2,1)S(1)}, f32[1,128]{1,0:T(1,128)S(1)}, f32[256,256]{1,0:T(8,128)S(1)}) custom-call(f32[256,1]{1,0:T(8,128)S(1)} %copy.7.weight, f32[256,256]{1,0:T(8,128)S(1)} %get-tuple-element.56.refs_0_, f32[8,128]{1,0:T(8,128)S(1)} %get-tuple-element.57.refs_1_, f32[256,256]{1,0:T(8,128)S(1)} %get-tuple-element.54.refs_0_.refs_2_, ...), custom_call_target="tpu_custom_call" | custom-call | tf_op jit(solution)/shard_map/pallas_call | solution.py:217
  41.8 5.5 %collective-permute-done.11.own_ref.refs_1_.refs_3_ = f32[256,128]{1,0:T(8,128)S(1)} collective-permute-done((f32[256,128]{1,0:T(8,128)S(1)}, f32[256,128]{1,0:T(8,128)S(1)}, u32[]{:S(2)}, u32[]{:S(2)}) %collective-permute-start.11) | collective-permute-done | bytes 131104 | tf_op jit(solution)/shard_map/ppermute | solution.py:18
  47.6 1.6 %collective-permute-start.12 = (f32[264,128]{1,0:T(8,128)S(1)}, f32[264,128]{1,0:T(8,128)S(1)}, u32[]{:S(2)}, u32[]{:S(2)}) collective-permute-start(f32[264,128]{1,0:T(8,128)S(1)} %shard_map.43), channel_id=1, source_target_pairs={{0,8},{4,20},{8,0},{12,28},{16,24},{20,4},{24,16},{28,12},{1,9},{5... | collective-permute-start | bytes 405512 | tf_op jit(solution)/shard_map/ppermute | solution.py:24
  49.1 3.5 %collective-permute-done.12 = f32[264,128]{1,0:T(8,128)S(1)} collective-permute-done((f32[264,128]{1,0:T(8,128)S(1)}, f32[264,128]{1,0:T(8,128)S(1)}, u32[]{:S(2)}, u32[]{:S(2)}) %collective-permute-start.12) | collective-permute-done | bytes 135200 | tf_op jit(solution)/shard_map/ppermute | solution.py:24
  52.7 1.6 %collective-permute-start.14 = (f32[264,128]{1,0:T(8,128)S(1)}, f32[264,128]{1,0:T(8,128)S(1)}, u32[]{:S(2)}, u32[]{:S(2)}) collective-permute-start(f32[264,128]{1,0:T(8,128)S(1)} %add.31), channel_id=1, source_target_pairs={{0,16},{4,12},{8,24},{12,4},{16,0},{20,28},{24,8},{28,20},{1,17},{... | collective-permute-start | bytes 405512 | tf_op jit(solution)/shard_map/ppermute | solution.py:24
  54.3 3.5 %collective-permute-done.14 = f32[264,128]{1,0:T(8,128)S(1)} collective-permute-done((f32[264,128]{1,0:T(8,128)S(1)}, f32[264,128]{1,0:T(8,128)S(1)}, u32[]{:S(2)}, u32[]{:S(2)}) %collective-permute-start.14) | collective-permute-done | bytes 135200 | tf_op jit(solution)/shard_map/ppermute | solution.py:24
  59.2 1.9 %shard_map.44 = (f32[128,256]{1,0:T(8,128)S(1)}, f32[256,256]{1,0:T(8,128)S(1)}, f32[8,128]{1,0:T(8,128)S(1)}) custom-call(f32[3,128]{1,0:T(4,128)S(1)} %broadcast_in_dim.16.damps, f32[264,128]{1,0:T(8,128)S(1)} %add.32.own_sum, f32[264,128]{1,0:T(8,128)S(1)} %collective-permute-done.15.other_sum, f32[256,256]{1,0:T(8,128)S(1)} %get-tuple-element.64.refs_0_.refs_2_, ...), custom_call_target="tpu_custom_call" | custom-call | tf_op jit(solution)/shard_map/pallas_call | solution.py:217
  61.2 2.3 %shard_map.45.filled = f32[128,512]{1,0:T(8,128)} custom-call(f32[256,256]{1,0:T(8,128)S(1)} %get-tuple-element.67.refs_0_, f32[8,128]{1,0:T(8,128)S(1)} %get-tuple-element.68.refs_1_, f32[256,256]{1,0:T(8,128)S(1)} %get-tuple-element.64.refs_0_.refs_2_, f32[256,128]{1,0:T(8,128)S(1)} %collective-permute-done.11.own_ref.refs_1_.refs_3_, ...), custom_call_target="tpu_custom_call" | custom-call | tf_op jit(solution)/shard_map/pallas_call | solution.py:277
  63.5 4.8 %collective-permute-done.16.lower = f32[128,256]{1,0:T(8,128)S(1)} collective-permute-done((f32[128,256]{1,0:T(8,128)S(1)}, f32[128,256]{1,0:T(8,128)S(1)}, u32[]{:S(2)}, u32[]{:S(2)}) %collective-permute-start.16) | collective-permute-done | bytes 131104 | tf_op jit(solution)/shard_map/ppermute | solution.py:18
  (37 shorter events, 7.8 us)
Async XLA Ops:
  0.0 2.6 %copy-start = (f32[128,512]{1,0:T(8,128)S(1)}, f32[128,512]{1,0:T(8,128)}, u32[]{:S(2)}) copy-start(f32[128,512]{1,0:T(8,128)} %refs_2_.1) | copy-start | bytes 786436
  0.0 0.7 %copy-start.1 = (f32[128]{0:T(128)S(1)}, f32[128]{0:T(128)}, u32[]{:S(2)}) copy-start(f32[128]{0:T(128)} %param.4) | copy-start | bytes 1540
  2.1 1.5 %collective-permute-start.1 = (f32[264,128]{1,0:T(8,128)S(1)}, f32[264,128]{1,0:T(8,128)S(1)}, u32[]{:S(2)}, u32[]{:S(2)}) collective-permute-start(f32[264,128]{1,0:T(8,128)S(1)} %get-tuple-element.41), channel_id=1, source_target_pairs={{0,4},{4,0},{8,12},{12,8},{16,20},{20,16},{24,28},{28,24},{1,5},{5... | collective-permute-start | bytes 405512 | tf_op jit(solution)/shard_map/ppermute | solution.py:24
  2.6 7.0 %collective-permute-start.3 = (f32[128,512]{1,0:T(8,128)S(1)}, f32[128,512]{1,0:T(8,128)S(1)}, u32[]{:S(2)}, u32[]{:S(2)}) collective-permute-start(f32[128,512]{1,0:T(8,128)S(1)} %copy-done), channel_id=1, source_target_pairs={{0,4},{4,0},{8,12},{12,8},{16,20},{20,16},{24,28},{28,24},{1,5},{5... | collective-permute-start | bytes 786440 | tf_op jit(solution)/shard_map/ppermute | solution.py:24
  3.6 5.9 %collective-permute-start.2 = (f32[264,128]{1,0:T(8,128)S(1)}, f32[264,128]{1,0:T(8,128)S(1)}, u32[]{:S(2)}, u32[]{:S(2)}) collective-permute-start(f32[264,128]{1,0:T(8,128)S(1)} %add.26), channel_id=1, source_target_pairs={{0,8},{4,20},{8,0},{12,28},{16,24},{20,4},{24,16},{28,12},{1,9},{5... | collective-permute-start | bytes 405512 | tf_op jit(solution)/shard_map/ppermute | solution.py:24
  9.5 5.2 %copy-start.2 = (s32[3,2]{0,1:T(2,128)S(1)}, s32[3,2]{0,1:T(2,128)}, u32[]{:S(2)}) copy-start(s32[3,2]{0,1:T(2,128)} %param.5) | copy-start | bytes 76
  9.6 5.1 %collective-permute-start.4 = (f32[264,128]{1,0:T(8,128)S(1)}, f32[264,128]{1,0:T(8,128)S(1)}, u32[]{:S(2)}, u32[]{:S(2)}) collective-permute-start(f32[264,128]{1,0:T(8,128)S(1)} %add.27), channel_id=1, source_target_pairs={{0,16},{4,12},{8,24},{12,4},{16,0},{20,28},{24,8},{28,20},{1,17},{... | collective-permute-start | bytes 405512 | tf_op jit(solution)/shard_map/ppermute | solution.py:24
  14.7 1.4 %collective-permute-start.5 = (f32[264,128]{1,0:T(8,128)S(1)}, f32[264,128]{1,0:T(8,128)S(1)}, u32[]{:S(2)}, u32[]{:S(2)}) collective-permute-start(f32[264,128]{1,0:T(8,128)S(1)} %add.28.own_sum), channel_id=1, source_target_pairs={{0,4},{4,0},{8,12},{12,8},{16,20},{20,16},{24,28},{28,24},{1,5},{5... | collective-permute-start | bytes 405512 | tf_op jit(solution)/shard_map/ppermute | solution.py:24
  18.1 8.0 %collective-permute-start.6 = (f32[256,128]{1,0:T(8,128)S(1)}, f32[256,128]{1,0:T(8,128)S(1)}, u32[]{:S(2)}, u32[]{:S(2)}) collective-permute-start(f32[256,128]{1,0:T(8,128)S(1)} %get-tuple-element.50), channel_id=1, source_target_pairs={{0,1},{1,2},{2,3},{3,0},{4,5},{5,6},{6,7},{7,4},{8,9},{9,10},{10,1... | collective-permute-start | bytes 393224 | tf_op jit(solution)/shard_map/ppermute | solution.py:18
  20.2 1.1 %collective-permute-start = (f32[128]{0:T(128)S(1)}, f32[128]{0:T(128)S(1)}, u32[]{:S(2)}, u32[]{:S(2)}) collective-permute-start(f32[128]{0:T(128)S(1)} %copy-done.1), channel_id=1, source_target_pairs={{0,4},{4,0},{8,12},{12,8},{16,20},{20,16},{24,28},{28,24},{1,5},{5... | collective-permute-start | bytes 1544 | tf_op jit(solution)/shard_map/ppermute | solution.py:24
  26.3 5.1 %collective-permute-start.7 = (f32[264,128]{1,0:T(8,128)S(1)}, f32[264,128]{1,0:T(8,128)S(1)}, u32[]{:S(2)}, u32[]{:S(2)}) collective-permute-start(f32[264,128]{1,0:T(8,128)S(1)} %shard_map.40), channel_id=1, source_target_pairs={{0,8},{4,20},{8,0},{12,28},{16,24},{20,4},{24,16},{28,12},{1,9},{5... | collective-permute-start | bytes 405512 | tf_op jit(solution)/shard_map/ppermute | solution.py:24
  27.9 3.5 %collective-permute-start.8 = (f32[256,128]{1,0:T(8,128)S(1)}, f32[256,128]{1,0:T(8,128)S(1)}, u32[]{:S(2)}, u32[]{:S(2)}) collective-permute-start(f32[256,128]{1,0:T(8,128)S(1)} %collective-permute-done.6.own_ref.refs_1_.refs_3_), channel_id=1, source_target_pairs={{0,4},{4,0},{8,12},{12,8},{16,20},{20,16},{24,28},{28,24},{1,5},{5... | collective-permute-start | bytes 393224 | tf_op jit(solution)/shard_map/ppermute | solution.py:24
  31.4 5.1 %collective-permute-start.9 = (f32[264,128]{1,0:T(8,128)S(1)}, f32[264,128]{1,0:T(8,128)S(1)}, u32[]{:S(2)}, u32[]{:S(2)}) collective-permute-start(f32[264,128]{1,0:T(8,128)S(1)} %add.29), channel_id=1, source_target_pairs={{0,16},{4,12},{8,24},{12,4},{16,0},{20,28},{24,8},{28,20},{1,17},{... | collective-permute-start | bytes 405512 | tf_op jit(solution)/shard_map/ppermute | solution.py:24
  36.5 1.4 %collective-permute-start.10 = (f32[264,128]{1,0:T(8,128)S(1)}, f32[264,128]{1,0:T(8,128)S(1)}, u32[]{:S(2)}, u32[]{:S(2)}) collective-permute-start(f32[264,128]{1,0:T(8,128)S(1)} %add.30.own_sum), channel_id=1, source_target_pairs={{0,4},{4,0},{8,12},{12,8},{16,20},{20,16},{24,28},{28,24},{1,5},{5... | collective-permute-start | bytes 405512 | tf_op jit(solution)/shard_map/ppermute | solution.py:24
  39.9 7.4 %collective-permute-start.11 = (f32[256,128]{1,0:T(8,128)S(1)}, f32[256,128]{1,0:T(8,128)S(1)}, u32[]{:S(2)}, u32[]{:S(2)}) collective-permute-start(f32[256,128]{1,0:T(8,128)S(1)} %get-tuple-element.60), channel_id=1, source_target_pairs={{0,1},{1,2},{2,3},{3,0},{4,5},{5,6},{6,7},{7,4},{8,9},{9,10},{10,1... | collective-permute-start | bytes 393224 | tf_op jit(solution)/shard_map/ppermute | solution.py:18
  47.6 5.1 %collective-permute-start.12 = (f32[264,128]{1,0:T(8,128)S(1)}, f32[264,128]{1,0:T(8,128)S(1)}, u32[]{:S(2)}, u32[]{:S(2)}) collective-permute-start(f32[264,128]{1,0:T(8,128)S(1)} %shard_map.43), channel_id=1, source_target_pairs={{0,8},{4,20},{8,0},{12,28},{16,24},{20,4},{24,16},{28,12},{1,9},{5... | collective-permute-start | bytes 405512 | tf_op jit(solution)/shard_map/ppermute | solution.py:24
  49.1 3.5 %collective-permute-start.13 = (f32[256,128]{1,0:T(8,128)S(1)}, f32[256,128]{1,0:T(8,128)S(1)}, u32[]{:S(2)}, u32[]{:S(2)}) collective-permute-start(f32[256,128]{1,0:T(8,128)S(1)} %collective-permute-done.11.own_ref.refs_1_.refs_3_), channel_id=1, source_target_pairs={{0,4},{4,0},{8,12},{12,8},{16,20},{20,16},{24,28},{28,24},{1,5},{5... | collective-permute-start | bytes 393224 | tf_op jit(solution)/shard_map/ppermute | solution.py:24
  52.7 5.1 %collective-permute-start.14 = (f32[264,128]{1,0:T(8,128)S(1)}, f32[264,128]{1,0:T(8,128)S(1)}, u32[]{:S(2)}, u32[]{:S(2)}) collective-permute-start(f32[264,128]{1,0:T(8,128)S(1)} %add.31), channel_id=1, source_target_pairs={{0,16},{4,12},{8,24},{12,4},{16,0},{20,28},{24,8},{28,20},{1,17},{... | collective-permute-start | bytes 405512 | tf_op jit(solution)/shard_map/ppermute | solution.py:24
  57.8 1.4 %collective-permute-start.15 = (f32[264,128]{1,0:T(8,128)S(1)}, f32[264,128]{1,0:T(8,128)S(1)}, u32[]{:S(2)}, u32[]{:S(2)}) collective-permute-start(f32[264,128]{1,0:T(8,128)S(1)} %add.32.own_sum), channel_id=1, source_target_pairs={{0,4},{4,0},{8,12},{12,8},{16,20},{20,16},{24,28},{28,24},{1,5},{5... | collective-permute-start | bytes 405512 | tf_op jit(solution)/shard_map/ppermute | solution.py:24
  61.1 7.2 %collective-permute-start.16 = (f32[128,256]{1,0:T(8,128)S(1)}, f32[128,256]{1,0:T(8,128)S(1)}, u32[]{:S(2)}, u32[]{:S(2)}) collective-permute-start(f32[128,256]{1,0:T(8,128)S(1)} %get-tuple-element.66), channel_id=1, source_target_pairs={{0,2},{1,3},{2,0},{3,1},{4,6},{5,7},{6,4},{7,5},{8,10},{9,11},{10,... | collective-permute-start | bytes 393224 | tf_op jit(solution)/shard_map/ppermute | solution.py:18

commit v7 on v6

--- a/solution.py
+++ b/solution.py
@@ -24,9 +24,8 @@
     return lax.ppermute(value, "pts", pairs)
 
 
-def chip_sum(value, beside=None):
+def chip_sum(value, bit, beside):
     count = lax.axis_size("pts")
-    bit = 2
     while bit < count:
         if 2 * bit < count:
             rounds = [(bit, 2 * bit), (2 * bit, bit)]
@@ -34,8 +33,7 @@
             rounds = [(bit, bit)]
         for even_bits, odd_bits in rounds:
             value = value + swapped(value, even_bits, odd_bits)
-            if beside is not None:
-                value, beside = lax.optimization_barrier((value, beside))
+            value, beside = lax.optimization_barrier((value, beside))
         bit *= 2 ** len(rounds)
     return value, beside
 
@@ -58,9 +56,9 @@
     )
 
 
-def halves_swapped(value):
-    half = value.shape[0] // 2
-    return jnp.concatenate([value[half:], value[:half]], axis=0)
+def neighbours_swapped(value, block):
+    count = value.shape[0] // block
+    return jnp.concatenate([value[(i ^ 1) * block : ((i ^ 1) + 1) * block] for i in range(count)], axis=0)
 
 
 def times_inverse_root(left, square, scale, columns):
@@ -82,8 +80,8 @@
     return (1.5 * left_both - 0.5 * left_last) * lax.rsqrt(scale)
 
 
-def joined(own, other):
-    return jnp.concatenate([own, halves_swapped(other)], axis=1)
+def joined(own, other, block):
+    return jnp.concatenate([own, neighbours_swapped(other, block)], axis=1)
 
 
 def own_half(half):
@@ -91,20 +89,20 @@
     return pl.multiple_of(own, half), pl.multiple_of(half - own, half)
 
 
-def start_blocks(near, far):
-    width = near.shape[1] // 2
+def start_blocks(*pieces):
+    width = pieces[0].shape[1] // 2
     own, other = own_half(width // 2)
 
     def taken(start):
         piece = (slice(None), pl.ds(start, width // 2))
-        return jnp.concatenate([near[piece], far[piece]], axis=0)
+        return jnp.concatenate([ref[piece] for ref in pieces], axis=0)
 
     upper = jnp.concatenate([taken(own), taken(other)], axis=1)
     return upper, jnp.concatenate([taken(width + own), taken(width + other)], axis=1)
 
 
-def later_blocks(upper, own, other):
-    return upper[...], joined(own[...], other[...])
+def later_blocks(block, upper, own, other):
+    return upper[...], joined(own[...], other[...], block)
 
 
 def stored(ref, value):
@@ -134,7 +132,7 @@
         lower = near[:, pl.ds(width + start, half)]
         weighted = point_weight * lower
         gram = product(upper_parts, two_parts(weighted), 0, 0)
-        out[:width] = gram if out is own_part else halves_swapped(gram)
+        out[:width] = gram if out is own_part else neighbours_swapped(gram, half)
         norm_lower = jnp.sum(weighted * lower, axis=0, keepdims=True)
         norm_upper = jnp.sum(point_weight * norm_of * norm_of, axis=0, keepdims=True)
         out[width:] = jnp.where(rows == 0, norm_lower, jnp.where(rows == 1, norm_upper, 0.0))
@@ -144,7 +142,7 @@
     *block_refs, moved, coupling_out, scale_out = refs
     width = coupling_out.shape[0]
     upper, lower = blocks(*block_refs)
-    gram = joined(own_sum[:width], other_sum[:width])
+    gram = joined(own_sum[:width], other_sum[:width], width // 2)
     norms = jnp.concatenate([own_sum[width:], other_sum[width:]], axis=1)
     inverse = lax.rsqrt(norms + EPSILON)
     coupling = gram * (damps[step : step + 1, 0:1] * inverse.T[:, 1:2]) * inverse[0:1]
@@ -227,7 +225,7 @@
     rows, columns = snapshot.shape
     width = columns // 2
     half = width // 2
-    whole = (2 * rows, width)
+    held_rows = 4 * rows
     own_part, other_part = pl.pallas_call(
         start_kernel,
         out_shape=[jax.ShapeDtypeStruct((width + 8, half), F32)] * 2,
@@ -243,17 +241,23 @@
     )(snapshot, weights[None])
     own_part, other_part, damping = lax.optimization_barrier((own_part, other_part, damping))
     payload = own_part + swapped(other_part, 1, 1)
-    weight = jnp.concatenate([weights, swapped(weights, 1, 1)])[:, None]
-    blocks, held, arriving = start_blocks, (snapshot,), swapped(snapshot, 1, 1)
+    weight = jnp.concatenate([weights, swapped(weights, 1, 1)])
+    weight = jnp.concatenate([weight, swapped(weight, 2, 2)])[:, None]
+    across = swapped(snapshot, 2, 2)
+    blocks, held, arriving = start_blocks, (snapshot,), (swapped(snapshot, 1, 1), across, swapped(across, 1, 1))
     damps = damping[:, 0].astype(F32) / (damping[:, 0] + damping[:, 1]).astype(F32)
     damps = lax.optimization_barrier(jnp.broadcast_to(damps[:, None], (STEPS, 128)))
     for step in range(STEPS):
         last = step + 1 == STEPS
-        payload, arriving = chip_sum(payload, arriving)
-        held = held + (arriving,)
+        if step == 0:
+            payload, first = chip_sum(payload, 2, arriving[:1])
+            held = held + first + arriving[1:]
+        else:
+            payload, arriving = chip_sum(payload, 4, arriving)
+            held = held + arriving
         moved, coupling, scale = in_vmem(
             functools.partial(lower_kernel, blocks, step, last),
-            [((rows, width) if last else (2 * rows, half), F32), ((width, width), F32), ((8, 128), F32)],
+            [((rows, width) if last else (held_rows, half), F32), ((width, width), F32), ((8, 128), F32)],
             damps,
             payload,
             swapped(payload, 1, 1),
@@ -264,13 +268,15 @@
         moved = shifted(moved, "cols", 1)
         gram_left, norm_upper, upper = in_vmem(
             functools.partial(upper_kernel, blocks),
-            [((width, 6 * rows), jnp.bfloat16), ((1, half), F32), (whole, F32)],
+            [((width, 3 * held_rows), jnp.bfloat16), ((1, half), F32), ((held_rows, width), F32)],
             weight,
             coupling,
             scale,
             *held,
         )
-        blocks, held, arriving = later_blocks, (upper, moved), swapped(moved, 1, 1)
+        gram_left, norm_upper, upper, moved = lax.optimization_barrier((gram_left, norm_upper, upper, moved))
+        blocks = functools.partial(later_blocks, rows)
+        held, arriving = (upper, moved), (swapped(moved, 1, 1),)
         (payload,) = in_vmem(gram_kernel, [((width + 8, half), F32)], gram_left, norm_upper, weight, moved)
     moved = shifted(moved, "cols", 1 - STEPS)
     out_shape = jax.ShapeDtypeStruct((rows, columns), F32)

time: 69.1 us -> 73 us (1.056)
  waiting for transfers between devices: 38.9 us -> 41.2 us
  Pallas kernels: 14.4 us -> 16.3 us
    pallas_call x7, Pallas kernels: 10 us -> 11.9 us  [in_vmem(): pl.pallas_call(kernel, out_shape=[jax.ShapeDtypeStruct(shape, dtype) for...]
    ppermute x14 -> x15, waiting for transfers between devices: 25.9 us -> 27.3 us  [swapped(): return lax.ppermute(value, 'pts', pairs)]
    ppermute x3, waiting for transfers between devices: 13 us -> 13.9 us  [shifted(): return lax.ppermute(value, axis, pairs)]
    ppermute x14 -> x15, starting transfers between devices: 12.2 us -> 11.4 us  [swapped(): return lax.ppermute(value, 'pts', pairs)]
  transfers between devices with their start and end apart: 17 -> 18, of which waited for: 14 -> 12; matrix products, arithmetic and copies ran while one was open for 0% -> 0% of each run, Pallas kernels for 9% -> 11%
where the time goes in v7:
time: 73 us; the launch traced here: 72.9 us
  waiting for transfers between devices  41.2 us (56%)
  Pallas kernels  16.3 us (22%)
  starting transfers between devices  14 us (19%)
  local copies, waits for them, and re-layouts  0.93 us (1%)
    ppermute x15, waiting for transfers between devices, swapped(): return lax.ppermute(value, 'pts', pairs)  27.3 us
    ppermute x3, waiting for transfers between devices, shifted(): return lax.ppermute(value, axis, pairs)  13.9 us
    pallas_call x7, Pallas kernels, in_vmem(): pl.pallas_call(kernel, out_shape=[jax.ShapeDtypeStruct(shape, dtype) for...  11.9 us
    ppermute x15, starting transfers between devices, swapped(): return lax.ppermute(value, 'pts', pairs)  11.4 us
    ppermute x3, starting transfers between devices, shifted(): return lax.ppermute(value, axis, pairs)  2.63 us
    pallas_call x1, Pallas kernels, body(): pl.pallas_call(functools.partial(last_upper_kernel, blocks), out_shape=ou...  2.33 us
  transfers between devices with their start and end apart: 18, of which 12 were waited for; matrix products, arithmetic and copies ran while one was open for 0% of the time, Pallas kernels for 11%

profile of v7, /device:TPU:0, one launch (start us, length us, event | category | flops | bytes accessed | tf_op | source)
XLA Modules:
  0.0 72.9 jit_solution(5896266324630703729)
XLA Ops:
  0.7 1.4 %shard_map.37 = (f32[264,128]{1,0:T(8,128)S(1)}, f32[264,128]{1,0:T(8,128)S(1)}) custom-call(f32[128,512]{1,0:T(8,128)} %refs_2_.1, f32[1,128]{1,0:T(1,128)S(1)} %bitcast.4), custom_call_target="tpu_custom_call" | custom-call | tf_op jit(solution)/shard_map/pallas_call | solution.py:229
  2.7 2.9 %collective-permute-start.7 = (f32[128,512]{1,0:T(8,128)S(1)}, f32[128,512]{1,0:T(8,128)S(1)}, u32[]{:S(2)}, u32[]{:S(2)}) collective-permute-start(f32[128,512]{1,0:T(8,128)S(1)} %copy-done), channel_id=1, source_target_pairs={{0,8},{4,12},{8,0},{12,4},{16,24},{20,28},{24,16},{28,20},{1,9},{5... | collective-permute-start | bytes 786440 | tf_op jit(solution)/shard_map/ppermute | solution.py:24
  6.5 8.3 %collective-permute-done.3 = f32[264,128]{1,0:T(8,128)S(1)} collective-permute-done((f32[264,128]{1,0:T(8,128)S(1)}, f32[264,128]{1,0:T(8,128)S(1)}, u32[]{:S(2)}, u32[]{:S(2)}) %collective-permute-start.3) | collective-permute-done | bytes 135200 | tf_op jit(solution)/shard_map/ppermute | solution.py:24
  14.8 2.1 %collective-permute-start.5 = (f32[264,128]{1,0:T(8,128)S(1)}, f32[264,128]{1,0:T(8,128)S(1)}, u32[]{:S(2)}, u32[]{:S(2)}) collective-permute-start(f32[264,128]{1,0:T(8,128)S(1)} %add.21), channel_id=1, source_target_pairs={{0,16},{4,12},{8,24},{12,4},{16,0},{20,28},{24,8},{28,20},{1,17},{... | collective-permute-start | bytes 405512 | tf_op jit(solution)/shard_map/ppermute | solution.py:24
  16.9 3.0 %collective-permute-done.5 = f32[264,128]{1,0:T(8,128)S(1)} collective-permute-done((f32[264,128]{1,0:T(8,128)S(1)}, f32[264,128]{1,0:T(8,128)S(1)}, u32[]{:S(2)}, u32[]{:S(2)}) %collective-permute-start.5) | collective-permute-done | bytes 135200 | tf_op jit(solution)/shard_map/ppermute | solution.py:24
  20.1 1.2 %collective-permute-done.6.other_sum = f32[264,128]{1,0:T(8,128)S(1)} collective-permute-done((f32[264,128]{1,0:T(8,128)S(1)}, f32[264,128]{1,0:T(8,128)S(1)}, u32[]{:S(2)}, u32[]{:S(2)}) %collective-permute-start.6) | collective-permute-done | bytes 135200 | tf_op jit(solution)/shard_map/ppermute | solution.py:24
  21.4 2.3 %shard_map.38 = (f32[512,128]{1,0:T(8,128)S(1)}, f32[256,256]{1,0:T(8,128)S(1)}, f32[8,128]{1,0:T(8,128)S(1)}) custom-call(f32[3,128]{1,0:T(4,128)S(1)} %broadcast_in_dim.16.damps, f32[264,128]{1,0:T(8,128)S(1)} %add.22.own_sum, f32[264,128]{1,0:T(8,128)S(1)} %collective-permute-done.6.other_sum, f32[128,512]{1,0:T(8,128)S(1)} %copy-done, ...), custom_call_target="tpu_custom_call" | custom-call | tf_op jit(solution)/shard_map/pallas_call | solution.py:215
  23.7 2.1 %collective-permute-start.9 = (f32[512,128]{1,0:T(8,128)S(1)}, f32[512,128]{1,0:T(8,128)S(1)}, u32[]{:S(2)}, u32[]{:S(2)}) collective-permute-start(f32[512,128]{1,0:T(8,128)S(1)} %get-tuple-element.55), channel_id=1, source_target_pairs={{0,1},{1,2},{2,3},{3,0},{4,5},{5,6},{6,7},{7,4},{8,9},{9,10},{10,1... | collective-permute-start | bytes 786440 | tf_op jit(solution)/shard_map/ppermute | solution.py:18
  26.9 1.5 %collective-permute-start.1 = (f32[256]{0:T(256)S(1)}, f32[256]{0:T(256)S(1)}, u32[]{:S(2)}, u32[]{:S(2)}) collective-permute-start(f32[256]{0:T(256)S(1)} %pad_maximum_fusion.1), channel_id=1, source_target_pairs={{0,8},{4,12},{8,0},{12,4},{16,24},{20,28},{24,16},{28,20},{1,9},{5... | collective-permute-start | bytes 3080 | tf_op jit(solution)/shard_map/ppermute | solution.py:24
  28.4 2.1 %collective-permute-done.1 = f32[256]{0:T(256)S(1)} collective-permute-done((f32[256]{0:T(256)S(1)}, f32[256]{0:T(256)S(1)}, u32[]{:S(2)}, u32[]{:S(2)}) %collective-permute-start.1) | collective-permute-done | bytes 1056 | tf_op jit(solution)/shard_map/ppermute | solution.py:24
  30.7 2.3 %shard_map.39 = (bf16[256,1536]{1,0:T(8,128)(2,1)S(1)}, f32[1,128]{1,0:T(1,128)S(1)}, f32[512,256]{1,0:T(8,128)S(1)}) custom-call(f32[512,1]{1,0:T(8,128)S(1)} %copy.7.weight, f32[256,256]{1,0:T(8,128)S(1)} %get-tuple-element.50.refs_0_, f32[8,128]{1,0:T(8,128)S(1)} %get-tuple-element.51.refs_1_, f32[128,512]{1,0:T(8,128)S(1)} %copy-done, ...), custom_call_target="tpu_custom_call" | custom-call | tf_op jit(solution)/shard_map/pallas_call | solution.py:215
  33.0 1.4 %collective-permute-done.9.own_ref.refs_1_.refs_3_ = f32[512,128]{1,0:T(8,128)S(1)} collective-permute-done((f32[512,128]{1,0:T(8,128)S(1)}, f32[512,128]{1,0:T(8,128)S(1)}, u32[]{:S(2)}, u32[]{:S(2)}) %collective-permute-start.9) | collective-permute-done | bytes 262176 | tf_op jit(solution)/shard_map/ppermute | solution.py:18
  34.8 1.6 %collective-permute-start.10 = (f32[264,128]{1,0:T(8,128)S(1)}, f32[264,128]{1,0:T(8,128)S(1)}, u32[]{:S(2)}, u32[]{:S(2)}) collective-permute-start(f32[264,128]{1,0:T(8,128)S(1)} %shard_map.40), channel_id=1, source_target_pairs={{0,16},{4,20},{8,24},{12,28},{16,0},{20,4},{24,8},{28,12},{1,17},{... | collective-permute-start | bytes 405512 | tf_op jit(solution)/shard_map/ppermute | solution.py:24
  36.4 4.5 %collective-permute-done.10 = f32[264,128]{1,0:T(8,128)S(1)} collective-permute-done((f32[264,128]{1,0:T(8,128)S(1)}, f32[264,128]{1,0:T(8,128)S(1)}, u32[]{:S(2)}, u32[]{:S(2)}) %collective-permute-start.10) | collective-permute-done | bytes 135200 | tf_op jit(solution)/shard_map/ppermute | solution.py:24
  41.0 1.3 %collective-permute-done.12.other_sum = f32[264,128]{1,0:T(8,128)S(1)} collective-permute-done((f32[264,128]{1,0:T(8,128)S(1)}, f32[264,128]{1,0:T(8,128)S(1)}, u32[]{:S(2)}, u32[]{:S(2)}) %collective-permute-start.12) | collective-permute-done | bytes 135200 | tf_op jit(solution)/shard_map/ppermute | solution.py:24
  42.3 2.3 %shard_map.41 = (f32[512,128]{1,0:T(8,128)S(1)}, f32[256,256]{1,0:T(8,128)S(1)}, f32[8,128]{1,0:T(8,128)S(1)}) custom-call(f32[3,128]{1,0:T(4,128)S(1)} %broadcast_in_dim.16.damps, f32[264,128]{1,0:T(8,128)S(1)} %add.23.own_sum, f32[264,128]{1,0:T(8,128)S(1)} %collective-permute-done.12.other_sum, f32[512,256]{1,0:T(8,128)S(1)} %get-tuple-element.60.refs_0_.refs_2_, ...), custom_call_target="tpu_custom_call" | custom-call | tf_op jit(solution)/shard_map/pallas_call | solution.py:215
  45.1 2.3 %shard_map.42 = (bf16[256,1536]{1,0:T(8,128)(2,1)S(1)}, f32[1,128]{1,0:T(1,128)S(1)}, f32[512,256]{1,0:T(8,128)S(1)}) custom-call(f32[512,1]{1,0:T(8,128)S(1)} %copy.7.weight, f32[256,256]{1,0:T(8,128)S(1)} %get-tuple-element.62.refs_0_, f32[8,128]{1,0:T(8,128)S(1)} %get-tuple-element.63.refs_1_, f32[512,256]{1,0:T(8,128)S(1)} %get-tuple-element.60.refs_0_.refs_2_, ...), custom_call_target="tpu_custom_call" | custom-call | tf_op jit(solution)/shard_map/pallas_call | solution.py:215
  47.4 7.6 %collective-permute-done.13.own_ref.refs_1_.refs_3_ = f32[512,128]{1,0:T(8,128)S(1)} collective-permute-done((f32[512,128]{1,0:T(8,128)S(1)}, f32[512,128]{1,0:T(8,128)S(1)}, u32[]{:S(2)}, u32[]{:S(2)}) %collective-permute-start.13) | collective-permute-done | bytes 262176 | tf_op jit(solution)/shard_map/ppermute | solution.py:18
  55.4 1.6 %collective-permute-start.14 = (f32[264,128]{1,0:T(8,128)S(1)}, f32[264,128]{1,0:T(8,128)S(1)}, u32[]{:S(2)}, u32[]{:S(2)}) collective-permute-start(f32[264,128]{1,0:T(8,128)S(1)} %shard_map.43), channel_id=1, source_target_pairs={{0,16},{4,20},{8,24},{12,28},{16,0},{20,4},{24,8},{28,12},{1,17},{... | collective-permute-start | bytes 405512 | tf_op jit(solution)/shard_map/ppermute | solution.py:24
  57.0 4.5 %collective-permute-done.14 = f32[264,128]{1,0:T(8,128)S(1)} collective-permute-done((f32[264,128]{1,0:T(8,128)S(1)}, f32[264,128]{1,0:T(8,128)S(1)}, u32[]{:S(2)}, u32[]{:S(2)}) %collective-permute-start.14) | collective-permute-done | bytes 135200 | tf_op jit(solution)/shard_map/ppermute | solution.py:24
  61.6 1.3 %collective-permute-done.16.other_sum = f32[264,128]{1,0:T(8,128)S(1)} collective-permute-done((f32[264,128]{1,0:T(8,128)S(1)}, f32[264,128]{1,0:T(8,128)S(1)}, u32[]{:S(2)}, u32[]{:S(2)}) %collective-permute-start.16) | collective-permute-done | bytes 135200 | tf_op jit(solution)/shard_map/ppermute | solution.py:24
  62.9 1.9 %shard_map.44 = (f32[128,256]{1,0:T(8,128)S(1)}, f32[256,256]{1,0:T(8,128)S(1)}, f32[8,128]{1,0:T(8,128)S(1)}) custom-call(f32[3,128]{1,0:T(4,128)S(1)} %broadcast_in_dim.16.damps, f32[264,128]{1,0:T(8,128)S(1)} %add.24.own_sum, f32[264,128]{1,0:T(8,128)S(1)} %collective-permute-done.16.other_sum, f32[512,256]{1,0:T(8,128)S(1)} %get-tuple-element.72.refs_0_.refs_2_, ...), custom_call_target="tpu_custom_call" | custom-call | tf_op jit(solution)/shard_map/pallas_call | solution.py:215
  64.9 2.3 %shard_map.45.filled = f32[128,512]{1,0:T(8,128)} custom-call(f32[256,256]{1,0:T(8,128)S(1)} %get-tuple-element.75.refs_0_, f32[8,128]{1,0:T(8,128)S(1)} %get-tuple-element.76.refs_1_, f32[512,256]{1,0:T(8,128)S(1)} %get-tuple-element.72.refs_0_.refs_2_, f32[512,128]{1,0:T(8,128)S(1)} %collective-permute-done.13.own_ref.refs_1_.refs_3_, ...), custom_call_target="tpu_custom_call" | custom-call | tf_op jit(solution)/shard_map/pallas_call | solution.py:283
  67.2 4.8 %collective-permute-done.17.lower = f32[128,256]{1,0:T(8,128)S(1)} collective-permute-done((f32[128,256]{1,0:T(8,128)S(1)}, f32[128,256]{1,0:T(8,128)S(1)}, u32[]{:S(2)}, u32[]{:S(2)}) %collective-permute-start.17) | collective-permute-done | bytes 131104 | tf_op jit(solution)/shard_map/ppermute | solution.py:18
  (38 shorter events, 5.8 us)
Async XLA Ops:
  0.0 2.6 %copy-start = (f32[128,512]{1,0:T(8,128)S(1)}, f32[128,512]{1,0:T(8,128)}, u32[]{:S(2)}) copy-start(f32[128,512]{1,0:T(8,128)} %refs_2_.1) | copy-start | bytes 786436
  0.0 0.7 copy-start.1
  2.1 3.5 %collective-permute-start.2 = (f32[264,128]{1,0:T(8,128)S(1)}, f32[264,128]{1,0:T(8,128)S(1)}, u32[]{:S(2)}, u32[]{:S(2)}) collective-permute-start(f32[264,128]{1,0:T(8,128)S(1)} %get-tuple-element.45), channel_id=1, source_target_pairs={{0,4},{4,0},{8,12},{12,8},{16,20},{20,16},{24,28},{28,24},{1,5},{5... | collective-permute-start | bytes 405512 | tf_op jit(solution)/shard_map/ppermute | solution.py:24
  2.6 12.2 %collective-permute-start.4 = (f32[128,512]{1,0:T(8,128)S(1)}, f32[128,512]{1,0:T(8,128)S(1)}, u32[]{:S(2)}, u32[]{:S(2)}) collective-permute-start(f32[128,512]{1,0:T(8,128)S(1)} %copy-done), channel_id=1, source_target_pairs={{0,4},{4,0},{8,12},{12,8},{16,20},{20,16},{24,28},{28,24},{1,5},{5... | collective-permute-start | bytes 786440 | tf_op jit(solution)/shard_map/ppermute | solution.py:24
  2.7 14.2 %collective-permute-start.7 = (f32[128,512]{1,0:T(8,128)S(1)}, f32[128,512]{1,0:T(8,128)S(1)}, u32[]{:S(2)}, u32[]{:S(2)}) collective-permute-start(f32[128,512]{1,0:T(8,128)S(1)} %copy-done), channel_id=1, source_target_pairs={{0,8},{4,12},{8,0},{12,4},{16,24},{20,28},{24,16},{28,20},{1,9},{5... | collective-permute-start | bytes 786440 | tf_op jit(solution)/shard_map/ppermute | solution.py:24
  5.6 9.2 %collective-permute-start.3 = (f32[264,128]{1,0:T(8,128)S(1)}, f32[264,128]{1,0:T(8,128)S(1)}, u32[]{:S(2)}, u32[]{:S(2)}) collective-permute-start(f32[264,128]{1,0:T(8,128)S(1)} %add.20), channel_id=1, source_target_pairs={{0,8},{4,20},{8,0},{12,28},{16,24},{20,4},{24,16},{28,12},{1,9},{5... | collective-permute-start | bytes 405512 | tf_op jit(solution)/shard_map/ppermute | solution.py:24
  14.8 5.2 %copy-start.2 = (s32[3,2]{0,1:T(2,128)S(1)}, s32[3,2]{0,1:T(2,128)}, u32[]{:S(2)}) copy-start(s32[3,2]{0,1:T(2,128)} %param.5) | copy-start | bytes 76
  14.8 5.1 %collective-permute-start.5 = (f32[264,128]{1,0:T(8,128)S(1)}, f32[264,128]{1,0:T(8,128)S(1)}, u32[]{:S(2)}, u32[]{:S(2)}) collective-permute-start(f32[264,128]{1,0:T(8,128)S(1)} %add.21), channel_id=1, source_target_pairs={{0,16},{4,12},{8,24},{12,4},{16,0},{20,28},{24,8},{28,20},{1,17},{... | collective-permute-start | bytes 405512 | tf_op jit(solution)/shard_map/ppermute | solution.py:24
  16.9 3.2 %collective-permute-start.8 = (f32[128,512]{1,0:T(8,128)S(1)}, f32[128,512]{1,0:T(8,128)S(1)}, u32[]{:S(2)}, u32[]{:S(2)}) collective-permute-start(f32[128,512]{1,0:T(8,128)S(1)} %collective-permute-done.7.refs_2_.refs_4_), channel_id=1, source_target_pairs={{0,4},{4,0},{8,12},{12,8},{16,20},{20,16},{24,28},{28,24},{1,5},{5... | collective-permute-start | bytes 786440 | tf_op jit(solution)/shard_map/ppermute | solution.py:24
  19.9 1.4 %collective-permute-start.6 = (f32[264,128]{1,0:T(8,128)S(1)}, f32[264,128]{1,0:T(8,128)S(1)}, u32[]{:S(2)}, u32[]{:S(2)}) collective-permute-start(f32[264,128]{1,0:T(8,128)S(1)} %add.22.own_sum), channel_id=1, source_target_pairs={{0,4},{4,0},{8,12},{12,8},{16,20},{20,16},{24,28},{28,24},{1,5},{5... | collective-permute-start | bytes 405512 | tf_op jit(solution)/shard_map/ppermute | solution.py:24
  23.7 10.8 %collective-permute-start.9 = (f32[512,128]{1,0:T(8,128)S(1)}, f32[512,128]{1,0:T(8,128)S(1)}, u32[]{:S(2)}, u32[]{:S(2)}) collective-permute-start(f32[512,128]{1,0:T(8,128)S(1)} %get-tuple-element.55), channel_id=1, source_target_pairs={{0,1},{1,2},{2,3},{3,0},{4,5},{5,6},{6,7},{7,4},{8,9},{9,10},{10,1... | collective-permute-start | bytes 786440 | tf_op jit(solution)/shard_map/ppermute | solution.py:18
  25.8 1.1 %collective-permute-start = (f32[128]{0:T(128)S(1)}, f32[128]{0:T(128)S(1)}, u32[]{:S(2)}, u32[]{:S(2)}) collective-permute-start(f32[128]{0:T(128)S(1)} %copy-done.1), channel_id=1, source_target_pairs={{0,4},{4,0},{8,12},{12,8},{16,20},{20,16},{24,28},{28,24},{1,5},{5... | collective-permute-start | bytes 1544 | tf_op jit(solution)/shard_map/ppermute | solution.py:24
  26.9 3.6 %collective-permute-start.1 = (f32[256]{0:T(256)S(1)}, f32[256]{0:T(256)S(1)}, u32[]{:S(2)}, u32[]{:S(2)}) collective-permute-start(f32[256]{0:T(256)S(1)} %pad_maximum_fusion.1), channel_id=1, source_target_pairs={{0,8},{4,12},{8,0},{12,4},{16,24},{20,28},{24,16},{28,20},{1,9},{5... | collective-permute-start | bytes 3080 | tf_op jit(solution)/shard_map/ppermute | solution.py:24
  34.5 6.5 %collective-permute-start.11 = (f32[512,128]{1,0:T(8,128)S(1)}, f32[512,128]{1,0:T(8,128)S(1)}, u32[]{:S(2)}, u32[]{:S(2)}) collective-permute-start(f32[512,128]{1,0:T(8,128)S(1)} %collective-permute-done.9.own_ref.refs_1_.refs_3_), channel_id=1, source_target_pairs={{0,4},{4,0},{8,12},{12,8},{16,20},{20,16},{24,28},{28,24},{1,5},{5... | collective-permute-start | bytes 786440 | tf_op jit(solution)/shard_map/ppermute | solution.py:24
  34.8 6.1 %collective-permute-start.10 = (f32[264,128]{1,0:T(8,128)S(1)}, f32[264,128]{1,0:T(8,128)S(1)}, u32[]{:S(2)}, u32[]{:S(2)}) collective-permute-start(f32[264,128]{1,0:T(8,128)S(1)} %shard_map.40), channel_id=1, source_target_pairs={{0,16},{4,20},{8,24},{12,28},{16,0},{20,4},{24,8},{28,12},{1,17},{... | collective-permute-start | bytes 405512 | tf_op jit(solution)/shard_map/ppermute | solution.py:24
  40.9 1.4 %collective-permute-start.12 = (f32[264,128]{1,0:T(8,128)S(1)}, f32[264,128]{1,0:T(8,128)S(1)}, u32[]{:S(2)}, u32[]{:S(2)}) collective-permute-start(f32[264,128]{1,0:T(8,128)S(1)} %add.23.own_sum), channel_id=1, source_target_pairs={{0,4},{4,0},{8,12},{12,8},{16,20},{20,16},{24,28},{28,24},{1,5},{5... | collective-permute-start | bytes 405512 | tf_op jit(solution)/shard_map/ppermute | solution.py:24
  44.6 10.4 %collective-permute-start.13 = (f32[512,128]{1,0:T(8,128)S(1)}, f32[512,128]{1,0:T(8,128)S(1)}, u32[]{:S(2)}, u32[]{:S(2)}) collective-permute-start(f32[512,128]{1,0:T(8,128)S(1)} %get-tuple-element.67), channel_id=1, source_target_pairs={{0,1},{1,2},{2,3},{3,0},{4,5},{5,6},{6,7},{7,4},{8,9},{9,10},{10,1... | collective-permute-start | bytes 786440 | tf_op jit(solution)/shard_map/ppermute | solution.py:18
  55.0 6.5 %collective-permute-start.15 = (f32[512,128]{1,0:T(8,128)S(1)}, f32[512,128]{1,0:T(8,128)S(1)}, u32[]{:S(2)}, u32[]{:S(2)}) collective-permute-start(f32[512,128]{1,0:T(8,128)S(1)} %collective-permute-done.13.own_ref.refs_1_.refs_3_), channel_id=1, source_target_pairs={{0,4},{4,0},{8,12},{12,8},{16,20},{20,16},{24,28},{28,24},{1,5},{5... | collective-permute-start | bytes 786440 | tf_op jit(solution)/shard_map/ppermute | solution.py:24
  55.4 6.1 %collective-permute-start.14 = (f32[264,128]{1,0:T(8,128)S(1)}, f32[264,128]{1,0:T(8,128)S(1)}, u32[]{:S(2)}, u32[]{:S(2)}) collective-permute-start(f32[264,128]{1,0:T(8,128)S(1)} %shard_map.43), channel_id=1, source_target_pairs={{0,16},{4,20},{8,24},{12,28},{16,0},{20,4},{24,8},{28,12},{1,17},{... | collective-permute-start | bytes 405512 | tf_op jit(solution)/shard_map/ppermute | solution.py:24
  61.5 1.4 %collective-permute-start.16 = (f32[264,128]{1,0:T(8,128)S(1)}, f32[264,128]{1,0:T(8,128)S(1)}, u32[]{:S(2)}, u32[]{:S(2)}) collective-permute-start(f32[264,128]{1,0:T(8,128)S(1)} %add.24.own_sum), channel_id=1, source_target_pairs={{0,4},{4,0},{8,12},{12,8},{16,20},{20,16},{24,28},{28,24},{1,5},{5... | collective-permute-start | bytes 405512 | tf_op jit(solution)/shard_map/ppermute | solution.py:24
  64.8 7.2 %collective-permute-start.17 = (f32[128,256]{1,0:T(8,128)S(1)}, f32[128,256]{1,0:T(8,128)S(1)}, u32[]{:S(2)}, u32[]{:S(2)}) collective-permute-start(f32[128,256]{1,0:T(8,128)S(1)} %get-tuple-element.74), channel_id=1, source_target_pairs={{0,2},{1,3},{2,0},{3,1},{4,6},{5,7},{6,4},{7,5},{8,10},{9,11},{10,... | collective-permute-start | bytes 393224 | tf_op jit(solution)/shard_map/ppermute | solution.py:18

commit v8 on v6

--- a/solution.py
+++ b/solution.py
@@ -38,6 +38,13 @@
                 value, beside = lax.optimization_barrier((value, beside))
         bit *= 2 ** len(rounds)
     return value, beside
+
+
+def chip_sum_at_once(value, copies):
+    count = lax.axis_size("pts")
+    groups = [list(range(core, count, 2)) for core in range(2)]
+    parts = lax.all_to_all(value, "pts", 0, 0, axis_index_groups=groups, tiled=True)
+    return jnp.sum(parts.reshape(copies, -1, value.shape[1]), axis=0)
 
 
 def two_parts(value):
@@ -197,15 +204,19 @@
     copy.wait()
 
 
-def gram_kernel(gram_left, norm_upper, weight, own_ref, payload):
+def gram_kernel(copies, gram_left, norm_upper, weight, own_ref, payload):
     width = gram_left.shape[0]
     own = own_ref[...]
     high, low = two_parts(own)
     right = jnp.concatenate([high, low, high], axis=0)
-    payload[:width] = jnp.dot(gram_left[...], right, preferred_element_type=F32)
+    gram = jnp.dot(gram_left[...], right, preferred_element_type=F32)
     norm_lower = jnp.sum(weight[...] * own * own, axis=0, keepdims=True)
     rows = lax.broadcasted_iota(jnp.int32, (8, own.shape[1]), 0)
-    payload[width:] = jnp.where(rows == 0, norm_lower, jnp.where(rows == 1, norm_upper[...], 0.0))
+    norms = jnp.where(rows == 0, norm_lower, jnp.where(rows == 1, norm_upper[...], 0.0))
+    for copy in range(copies):
+        start = copy * (width + 8)
+        payload[start : start + width] = gram
+        payload[start + width : start + width + 8] = norms
 
 
 ON_CHIP = pl.BlockSpec(memory_space=pltpu.VMEM)
@@ -227,6 +238,7 @@
     rows, columns = snapshot.shape
     width = columns // 2
     half = width // 2
+    copies = lax.axis_size("pts") // 2
     whole = (2 * rows, width)
     own_part, other_part = pl.pallas_call(
         start_kernel,
@@ -249,7 +261,10 @@
     damps = lax.optimization_barrier(jnp.broadcast_to(damps[:, None], (STEPS, 128)))
     for step in range(STEPS):
         last = step + 1 == STEPS
-        payload, arriving = chip_sum(payload, arriving)
+        if step == 0:
+            payload, arriving = chip_sum(payload, arriving)
+        else:
+            payload = chip_sum_at_once(payload, copies)
         held = held + (arriving,)
         moved, coupling, scale = in_vmem(
             functools.partial(lower_kernel, blocks, step, last),
@@ -271,7 +286,8 @@
             *held,
         )
         blocks, held, arriving = later_blocks, (upper, moved), swapped(moved, 1, 1)
-        (payload,) = in_vmem(gram_kernel, [((width + 8, half), F32)], gram_left, norm_upper, weight, moved)
+        (payload,) = in_vmem(
+            functools.partial(gram_kernel, copies), [((copies * (width + 8), half), F32)], gram_left, norm_upper, weight, moved)
     moved = shifted(moved, "cols", 1 - STEPS)
     out_shape = jax.ShapeDtypeStruct((rows, columns), F32)
     rotated = pl.pallas_call(

time: 69.1 us -> 73.3 us (1.061)
  blocking collectives: 0 us -> 23.4 us
  waiting for transfers between devices: 38.9 us -> 25 us
  starting transfers between devices: 14.4 us -> 9.09 us
    all_to_all x0 -> x2, blocking collectives: none -> 23.4 us  [chip_sum_at_once(): lax.all_to_all(value, 'pts', 0, 0, axis_index_groups=groups, tiled=True)]
    ppermute x14 -> x10, waiting for transfers between devices: 25.9 us -> 11.3 us  [swapped(): return lax.ppermute(value, 'pts', pairs)]
    ppermute x14 -> x10, starting transfers between devices: 12.2 us -> 6.84 us  [swapped(): return lax.ppermute(value, 'pts', pairs)]
  transfers between devices with their start and end apart: 17 -> 13, of which waited for: 14 -> 10; matrix products, arithmetic and copies ran while one was open for 0% -> 0% of each run, Pallas kernels for 9% -> 8%
where the time goes in v8:
time: 73.3 us; the launch traced here: 73.1 us
  waiting for transfers between devices  25 us (34%)
  blocking collectives  23.4 us (32%)
  Pallas kernels  14.4 us (20%)
  starting transfers between devices  9.09 us (12%)
  local copies, waits for them, and re-layouts  0.87 us (1%)
    all_to_all x2, blocking collectives, chip_sum_at_once(): lax.all_to_all(value, 'pts', 0, 0, axis_index_groups=groups, tiled=True)  23.4 us
    ppermute x3, waiting for transfers between devices, shifted(): return lax.ppermute(value, axis, pairs)  13.7 us
    ppermute x10, waiting for transfers between devices, swapped(): return lax.ppermute(value, 'pts', pairs)  11.3 us
    pallas_call x7, Pallas kernels, in_vmem(): pl.pallas_call(kernel, out_shape=[jax.ShapeDtypeStruct(shape, dtype) for...  10 us
    ppermute x10, starting transfers between devices, swapped(): return lax.ppermute(value, 'pts', pairs)  6.84 us
    pallas_call x1, Pallas kernels, body(): pl.pallas_call(functools.partial(last_upper_kernel, blocks), out_shape=ou...  2.33 us
    ppermute x3, starting transfers between devices, shifted(): return lax.ppermute(value, axis, pairs)  2.25 us
  transfers between devices with their start and end apart: 13, of which 10 were waited for; matrix products, arithmetic and copies ran while one was open for 0% of the time, Pallas kernels for 8%

profile of v8, /device:TPU:0, one launch (start us, length us, event | category | flops | bytes accessed | tf_op | source)
XLA Modules:
  0.0 73.1 jit_solution(8471071722269365449)
XLA Ops:
  0.0 0.7 copy-done.1
  0.7 1.4 %shard_map.37 = (f32[264,128]{1,0:T(8,128)S(1)}, f32[264,128]{1,0:T(8,128)S(1)}) custom-call(f32[128,512]{1,0:T(8,128)} %refs_2_.1, f32[1,128]{1,0:T(1,128)S(1)} %bitcast.8), custom_call_target="tpu_custom_call" | custom-call | tf_op jit(solution)/shard_map/pallas_call | solution.py:243
  2.7 0.9 %collective-permute-done.1 = f32[264,128]{1,0:T(8,128)S(1)} collective-permute-done((f32[264,128]{1,0:T(8,128)S(1)}, f32[264,128]{1,0:T(8,128)S(1)}, u32[]{:S(2)}, u32[]{:S(2)}) %collective-permute-start.1) | collective-permute-done | bytes 135200 | tf_op jit(solution)/shard_map/ppermute | solution.py:24
  3.6 2.9 %collective-permute-start.2 = (f32[264,128]{1,0:T(8,128)S(1)}, f32[264,128]{1,0:T(8,128)S(1)}, u32[]{:S(2)}, u32[]{:S(2)}) collective-permute-start(f32[264,128]{1,0:T(8,128)S(1)} %add.14), channel_id=1, source_target_pairs={{0,8},{4,20},{8,0},{12,28},{16,24},{20,4},{24,16},{28,12},{1,9},{5... | collective-permute-start | bytes 405512 | tf_op jit(solution)/shard_map/ppermute | solution.py:24
  6.5 3.0 %collective-permute-done.2 = f32[264,128]{1,0:T(8,128)S(1)} collective-permute-done((f32[264,128]{1,0:T(8,128)S(1)}, f32[264,128]{1,0:T(8,128)S(1)}, u32[]{:S(2)}, u32[]{:S(2)}) %collective-permute-start.2) | collective-permute-done | bytes 135200 | tf_op jit(solution)/shard_map/ppermute | solution.py:24
  9.5 2.1 %collective-permute-start.4 = (f32[264,128]{1,0:T(8,128)S(1)}, f32[264,128]{1,0:T(8,128)S(1)}, u32[]{:S(2)}, u32[]{:S(2)}) collective-permute-start(f32[264,128]{1,0:T(8,128)S(1)} %add.15), channel_id=1, source_target_pairs={{0,16},{4,12},{8,24},{12,4},{16,0},{20,28},{24,8},{28,20},{1,17},{... | collective-permute-start | bytes 405512 | tf_op jit(solution)/shard_map/ppermute | solution.py:24
  11.6 3.0 %collective-permute-done.4 = f32[264,128]{1,0:T(8,128)S(1)} collective-permute-done((f32[264,128]{1,0:T(8,128)S(1)}, f32[264,128]{1,0:T(8,128)S(1)}, u32[]{:S(2)}, u32[]{:S(2)}) %collective-permute-start.4) | collective-permute-done | bytes 135200 | tf_op jit(solution)/shard_map/ppermute | solution.py:24
  14.8 1.2 %collective-permute-done.5.other_sum = f32[264,128]{1,0:T(8,128)S(1)} collective-permute-done((f32[264,128]{1,0:T(8,128)S(1)}, f32[264,128]{1,0:T(8,128)S(1)}, u32[]{:S(2)}, u32[]{:S(2)}) %collective-permute-start.5) | collective-permute-done | bytes 135200 | tf_op jit(solution)/shard_map/ppermute | solution.py:24
  16.1 2.0 %shard_map.38 = (f32[256,128]{1,0:T(8,128)S(1)}, f32[256,256]{1,0:T(8,128)S(1)}, f32[8,128]{1,0:T(8,128)S(1)}) custom-call(f32[3,128]{1,0:T(4,128)S(1)} %broadcast_in_dim.16.damps, f32[264,128]{1,0:T(8,128)S(1)} %add.16.own_sum, f32[264,128]{1,0:T(8,128)S(1)} %collective-permute-done.5.other_sum, f32[128,512]{1,0:T(8,128)S(1)} %copy-done, ...), custom_call_target="tpu_custom_call" | custom-call | tf_op jit(solution)/shard_map/pallas_call | solution.py:228
  18.0 2.1 %collective-permute-start.6 = (f32[256,128]{1,0:T(8,128)S(1)}, f32[256,128]{1,0:T(8,128)S(1)}, u32[]{:S(2)}, u32[]{:S(2)}) collective-permute-start(f32[256,128]{1,0:T(8,128)S(1)} %get-tuple-element.42), channel_id=1, source_target_pairs={{0,1},{1,2},{2,3},{3,0},{4,5},{5,6},{6,7},{7,4},{8,9},{9,10},{10,1... | collective-permute-start | bytes 393224 | tf_op jit(solution)/shard_map/ppermute | solution.py:18
  20.2 1.1 %collective-permute-done = f32[128]{0:T(128)S(1)} collective-permute-done((f32[128]{0:T(128)S(1)}, f32[128]{0:T(128)S(1)}, u32[]{:S(2)}, u32[]{:S(2)}) %collective-permute-start) | collective-permute-done | bytes 544 | tf_op jit(solution)/shard_map/ppermute | solution.py:24
  21.4 1.9 %shard_map.39 = (bf16[256,768]{1,0:T(8,128)(2,1)S(1)}, f32[1,128]{1,0:T(1,128)S(1)}, f32[256,256]{1,0:T(8,128)S(1)}) custom-call(f32[256,1]{1,0:T(8,128)S(1)} %copy.7.weight, f32[256,256]{1,0:T(8,128)S(1)} %get-tuple-element.38.refs_0_, f32[8,128]{1,0:T(8,128)S(1)} %get-tuple-element.39.refs_1_, f32[128,512]{1,0:T(8,128)S(1)} %copy-done, ...), custom_call_target="tpu_custom_call" | custom-call | tf_op jit(solution)/shard_map/pallas_call | solution.py:228
  23.3 2.7 %collective-permute-done.6.own_ref.refs_1_.refs_3_ = f32[256,128]{1,0:T(8,128)S(1)} collective-permute-done((f32[256,128]{1,0:T(8,128)S(1)}, f32[256,128]{1,0:T(8,128)S(1)}, u32[]{:S(2)}, u32[]{:S(2)}) %collective-permute-start.6) | collective-permute-done | bytes 131104 | tf_op jit(solution)/shard_map/ppermute | solution.py:18
  26.3 12.1 %all_to_all.18 = f32[4,264,128]{2,1,0:T(8,128)S(1)} all-to-all(f32[4,264,128]{2,1,0:T(8,128)S(1)} %bitcast.7), channel_id=1, replica_groups={{0,8,16,24},{4,12,20,28},{1,9,17,25},{5,13,21,29},{2,10,18,26},{6,14,22..., dimensions={0} | all-to-all | bytes 1081344 | tf_op jit(solution)/shard_map/all_to_all | solution.py:46
  38.9 1.0 %collective-permute-done.8.refs_2_.refs_4_ = f32[256,128]{1,0:T(8,128)S(1)} collective-permute-done((f32[256,128]{1,0:T(8,128)S(1)}, f32[256,128]{1,0:T(8,128)S(1)}, u32[]{:S(2)}, u32[]{:S(2)}) %collective-permute-start.8) | collective-permute-done | bytes 131104 | tf_op jit(solution)/shard_map/ppermute | solution.py:24
  40.0 2.0 %shard_map.41 = (f32[256,128]{1,0:T(8,128)S(1)}, f32[256,256]{1,0:T(8,128)S(1)}, f32[8,128]{1,0:T(8,128)S(1)}) custom-call(f32[3,128]{1,0:T(4,128)S(1)} %broadcast_in_dim.16.damps, f32[264,128]{1,0:T(8,128)S(1)} %reduce_sum.18.own_sum, f32[264,128]{1,0:T(8,128)S(1)} %collective-permute-done.7.other_sum, f32[256,256]{1,0:T(8,128)S(1)} %get-tuple-element.43.refs_0_.refs_2_, ...), custom_call_target="tpu_custom_call" | custom-call | tf_op jit(solution)/shard_map/pallas_call | solution.py:228
  42.0 1.8 %shard_map.42 = (bf16[256,768]{1,0:T(8,128)(2,1)S(1)}, f32[1,128]{1,0:T(1,128)S(1)}, f32[256,256]{1,0:T(8,128)S(1)}) custom-call(f32[256,1]{1,0:T(8,128)S(1)} %copy.7.weight, f32[256,256]{1,0:T(8,128)S(1)} %get-tuple-element.44.refs_0_, f32[8,128]{1,0:T(8,128)S(1)} %get-tuple-element.45.refs_1_, f32[256,256]{1,0:T(8,128)S(1)} %get-tuple-element.43.refs_0_.refs_2_, ...), custom_call_target="tpu_custom_call" | custom-call | tf_op jit(solution)/shard_map/pallas_call | solution.py:228
  43.9 5.6 %collective-permute-done.9.own_ref.refs_1_.refs_3_ = f32[256,128]{1,0:T(8,128)S(1)} collective-permute-done((f32[256,128]{1,0:T(8,128)S(1)}, f32[256,128]{1,0:T(8,128)S(1)}, u32[]{:S(2)}, u32[]{:S(2)}) %collective-permute-start.9) | collective-permute-done | bytes 131104 | tf_op jit(solution)/shard_map/ppermute | solution.py:18
  49.8 11.3 %all_to_all.19 = f32[4,264,128]{2,1,0:T(8,128)S(1)} all-to-all(f32[4,264,128]{2,1,0:T(8,128)S(1)} %bitcast.6), channel_id=1, replica_groups={{0,8,16,24},{4,12,20,28},{1,9,17,25},{5,13,21,29},{2,10,18,26},{6,14,22..., dimensions={0} | all-to-all | bytes 1081344 | tf_op jit(solution)/shard_map/all_to_all | solution.py:46
  61.7 1.0 %collective-permute-done.11.refs_2_.refs_4_ = f32[256,128]{1,0:T(8,128)S(1)} collective-permute-done((f32[256,128]{1,0:T(8,128)S(1)}, f32[256,128]{1,0:T(8,128)S(1)}, u32[]{:S(2)}, u32[]{:S(2)}) %collective-permute-start.11) | collective-permute-done | bytes 131104 | tf_op jit(solution)/shard_map/ppermute | solution.py:24
  62.8 1.9 %shard_map.44 = (f32[128,256]{1,0:T(8,128)S(1)}, f32[256,256]{1,0:T(8,128)S(1)}, f32[8,128]{1,0:T(8,128)S(1)}) custom-call(f32[3,128]{1,0:T(4,128)S(1)} %broadcast_in_dim.16.damps, f32[264,128]{1,0:T(8,128)S(1)} %reduce_sum.19.own_sum, f32[264,128]{1,0:T(8,128)S(1)} %collective-permute-done.10.other_sum, f32[256,256]{1,0:T(8,128)S(1)} %get-tuple-element.49.refs_0_.refs_2_, ...), custom_call_target="tpu_custom_call" | custom-call | tf_op jit(solution)/shard_map/pallas_call | solution.py:228
  64.7 2.3 %shard_map.45.filled = f32[128,512]{1,0:T(8,128)} custom-call(f32[256,256]{1,0:T(8,128)S(1)} %get-tuple-element.51.refs_0_, f32[8,128]{1,0:T(8,128)S(1)} %get-tuple-element.52.refs_1_, f32[256,256]{1,0:T(8,128)S(1)} %get-tuple-element.49.refs_0_.refs_2_, f32[256,128]{1,0:T(8,128)S(1)} %collective-permute-done.9.own_ref.refs_1_.refs_3_, ...), custom_call_target="tpu_custom_call" | custom-call | tf_op jit(solution)/shard_map/pallas_call | solution.py:293
  67.1 5.3 %collective-permute-done.12.lower = f32[128,256]{1,0:T(8,128)S(1)} collective-permute-done((f32[128,256]{1,0:T(8,128)S(1)}, f32[128,256]{1,0:T(8,128)S(1)}, u32[]{:S(2)}, u32[]{:S(2)}) %collective-permute-start.12) | collective-permute-done | bytes 131104 | tf_op jit(solution)/shard_map/ppermute | solution.py:18
  72.4 0.7 shard_map.46
  (29 shorter events, 2.8 us)
Async XLA Ops:
  0.0 0.7 copy-start.1
  0.0 2.6 %copy-start = (f32[128,512]{1,0:T(8,128)S(1)}, f32[128,512]{1,0:T(8,128)}, u32[]{:S(2)}) copy-start(f32[128,512]{1,0:T(8,128)} %refs_2_.1) | copy-start | bytes 786436
  2.0 1.5 %collective-permute-start.1 = (f32[264,128]{1,0:T(8,128)S(1)}, f32[264,128]{1,0:T(8,128)S(1)}, u32[]{:S(2)}, u32[]{:S(2)}) collective-permute-start(f32[264,128]{1,0:T(8,128)S(1)} %get-tuple-element.33), channel_id=1, source_target_pairs={{0,4},{4,0},{8,12},{12,8},{16,20},{20,16},{24,28},{28,24},{1,5},{5... | collective-permute-start | bytes 405512 | tf_op jit(solution)/shard_map/ppermute | solution.py:24
  2.6 7.0 %collective-permute-start.3 = (f32[128,512]{1,0:T(8,128)S(1)}, f32[128,512]{1,0:T(8,128)S(1)}, u32[]{:S(2)}, u32[]{:S(2)}) collective-permute-start(f32[128,512]{1,0:T(8,128)S(1)} %copy-done), channel_id=1, source_target_pairs={{0,4},{4,0},{8,12},{12,8},{16,20},{20,16},{24,28},{28,24},{1,5},{5... | collective-permute-start | bytes 786440 | tf_op jit(solution)/shard_map/ppermute | solution.py:24
  3.6 5.9 %collective-permute-start.2 = (f32[264,128]{1,0:T(8,128)S(1)}, f32[264,128]{1,0:T(8,128)S(1)}, u32[]{:S(2)}, u32[]{:S(2)}) collective-permute-start(f32[264,128]{1,0:T(8,128)S(1)} %add.14), channel_id=1, source_target_pairs={{0,8},{4,20},{8,0},{12,28},{16,24},{20,4},{24,16},{28,12},{1,9},{5... | collective-permute-start | bytes 405512 | tf_op jit(solution)/shard_map/ppermute | solution.py:24
  9.5 5.2 %copy-start.2 = (s32[3,2]{0,1:T(2,128)S(1)}, s32[3,2]{0,1:T(2,128)}, u32[]{:S(2)}) copy-start(s32[3,2]{0,1:T(2,128)} %param.5) | copy-start | bytes 76
  9.5 5.1 %collective-permute-start.4 = (f32[264,128]{1,0:T(8,128)S(1)}, f32[264,128]{1,0:T(8,128)S(1)}, u32[]{:S(2)}, u32[]{:S(2)}) collective-permute-start(f32[264,128]{1,0:T(8,128)S(1)} %add.15), channel_id=1, source_target_pairs={{0,16},{4,12},{8,24},{12,4},{16,0},{20,28},{24,8},{28,20},{1,17},{... | collective-permute-start | bytes 405512 | tf_op jit(solution)/shard_map/ppermute | solution.py:24
  14.6 1.4 %collective-permute-start.5 = (f32[264,128]{1,0:T(8,128)S(1)}, f32[264,128]{1,0:T(8,128)S(1)}, u32[]{:S(2)}, u32[]{:S(2)}) collective-permute-start(f32[264,128]{1,0:T(8,128)S(1)} %add.16.own_sum), channel_id=1, source_target_pairs={{0,4},{4,0},{8,12},{12,8},{16,20},{20,16},{24,28},{28,24},{1,5},{5... | collective-permute-start | bytes 405512 | tf_op jit(solution)/shard_map/ppermute | solution.py:24
  18.0 8.0 %collective-permute-start.6 = (f32[256,128]{1,0:T(8,128)S(1)}, f32[256,128]{1,0:T(8,128)S(1)}, u32[]{:S(2)}, u32[]{:S(2)}) collective-permute-start(f32[256,128]{1,0:T(8,128)S(1)} %get-tuple-element.42), channel_id=1, source_target_pairs={{0,1},{1,2},{2,3},{3,0},{4,5},{5,6},{6,7},{7,4},{8,9},{9,10},{10,1... | collective-permute-start | bytes 393224 | tf_op jit(solution)/shard_map/ppermute | solution.py:18
  20.2 1.1 %collective-permute-start = (f32[128]{0:T(128)S(1)}, f32[128]{0:T(128)S(1)}, u32[]{:S(2)}, u32[]{:S(2)}) collective-permute-start(f32[128]{0:T(128)S(1)} %copy-done.1), channel_id=1, source_target_pairs={{0,4},{4,0},{8,12},{12,8},{16,20},{20,16},{24,28},{28,24},{1,5},{5... | collective-permute-start | bytes 1544 | tf_op jit(solution)/shard_map/ppermute | solution.py:24
  38.4 1.6 %collective-permute-start.7 = (f32[264,128]{1,0:T(8,128)S(1)}, f32[264,128]{1,0:T(8,128)S(1)}, u32[]{:S(2)}, u32[]{:S(2)}) collective-permute-start(f32[264,128]{1,0:T(8,128)S(1)} %reduce_sum.18.own_sum), channel_id=1, source_target_pairs={{0,4},{4,0},{8,12},{12,8},{16,20},{20,16},{24,28},{28,24},{1,5},{5... | collective-permute-start | bytes 405512 | tf_op jit(solution)/shard_map/ppermute | solution.py:24
  38.4 1.5 %collective-permute-start.8 = (f32[256,128]{1,0:T(8,128)S(1)}, f32[256,128]{1,0:T(8,128)S(1)}, u32[]{:S(2)}, u32[]{:S(2)}) collective-permute-start(f32[256,128]{1,0:T(8,128)S(1)} %collective-permute-done.6.own_ref.refs_1_.refs_3_), channel_id=1, source_target_pairs={{0,4},{4,0},{8,12},{12,8},{16,20},{20,16},{24,28},{28,24},{1,5},{5... | collective-permute-start | bytes 393224 | tf_op jit(solution)/shard_map/ppermute | solution.py:24
  42.0 7.6 %collective-permute-start.9 = (f32[256,128]{1,0:T(8,128)S(1)}, f32[256,128]{1,0:T(8,128)S(1)}, u32[]{:S(2)}, u32[]{:S(2)}) collective-permute-start(f32[256,128]{1,0:T(8,128)S(1)} %get-tuple-element.48), channel_id=1, source_target_pairs={{0,1},{1,2},{2,3},{3,0},{4,5},{5,6},{6,7},{7,4},{8,9},{9,10},{10,1... | collective-permute-start | bytes 393224 | tf_op jit(solution)/shard_map/ppermute | solution.py:18
  61.1 1.6 %collective-permute-start.10 = (f32[264,128]{1,0:T(8,128)S(1)}, f32[264,128]{1,0:T(8,128)S(1)}, u32[]{:S(2)}, u32[]{:S(2)}) collective-permute-start(f32[264,128]{1,0:T(8,128)S(1)} %reduce_sum.19.own_sum), channel_id=1, source_target_pairs={{0,4},{4,0},{8,12},{12,8},{16,20},{20,16},{24,28},{28,24},{1,5},{5... | collective-permute-start | bytes 405512 | tf_op jit(solution)/shard_map/ppermute | solution.py:24
  61.2 1.5 %collective-permute-start.11 = (f32[256,128]{1,0:T(8,128)S(1)}, f32[256,128]{1,0:T(8,128)S(1)}, u32[]{:S(2)}, u32[]{:S(2)}) collective-permute-start(f32[256,128]{1,0:T(8,128)S(1)} %collective-permute-done.9.own_ref.refs_1_.refs_3_), channel_id=1, source_target_pairs={{0,4},{4,0},{8,12},{12,8},{16,20},{20,16},{24,28},{28,24},{1,5},{5... | collective-permute-start | bytes 393224 | tf_op jit(solution)/shard_map/ppermute | solution.py:24
  64.7 7.7 %collective-permute-start.12 = (f32[128,256]{1,0:T(8,128)S(1)}, f32[128,256]{1,0:T(8,128)S(1)}, u32[]{:S(2)}, u32[]{:S(2)}) collective-permute-start(f32[128,256]{1,0:T(8,128)S(1)} %get-tuple-element.50), channel_id=1, source_target_pairs={{0,2},{1,3},{2,0},{3,1},{4,6},{5,7},{6,4},{7,5},{8,10},{9,11},{10,... | collective-permute-start | bytes 393224 | tf_op jit(solution)/shard_map/ppermute | solution.py:18

commit v9 on v6

--- a/solution.py
+++ b/solution.py
@@ -239,8 +239,8 @@
             pltpu.SemaphoreType.DMA(()),
             pltpu.SemaphoreType.DMA(()),
         ],
-        compiler_params=pltpu.CompilerParams(vmem_limit_bytes=(64 << 20) - (10752 << 10)),
-    )(snapshot, weights[None])
+        compiler_params=GRANT,
+    )(*(pltpu.with_memory_space_constraint(value, pltpu.HBM) for value in (snapshot, weights[None])))
     own_part, other_part, damping = lax.optimization_barrier((own_part, other_part, damping))
     payload = own_part + swapped(other_part, 1, 1)
     weight = jnp.concatenate([weights, swapped(weights, 1, 1)])[:, None]

time: 69.1 us -> 68.5 us (level)
    unnamed x6, local copies, waits for them, and re-layouts: 0.71 us -> 0.02 us
where the time goes in v9:
time: 68.5 us; the launch traced here: 68.4 us
  waiting for transfers between devices  39 us (57%)
  Pallas kernels  14.5 us (21%)
  starting transfers between devices  14.4 us (21%)
    ppermute x14, waiting for transfers between devices, swapped(): return lax.ppermute(value, 'pts', pairs)  26 us
    ppermute x3, waiting for transfers between devices, shifted(): return lax.ppermute(value, axis, pairs)  13 us
    ppermute x14, starting transfers between devices, swapped(): return lax.ppermute(value, 'pts', pairs)  12.1 us
    pallas_call x7, Pallas kernels, in_vmem(): pl.pallas_call(kernel, out_shape=[jax.ShapeDtypeStruct(shape, dtype) for...  10.1 us
    pallas_call x1, Pallas kernels, body(): pl.pallas_call(functools.partial(last_upper_kernel, blocks), out_shape=ou...  2.32 us
    ppermute x3, starting transfers between devices, shifted(): return lax.ppermute(value, axis, pairs)  2.26 us
    pallas_call x1, Pallas kernels, body(): pl.pallas_call(start_kernel, out_shape=[jax.ShapeDtypeStruct((width + 8,...  1.45 us
  transfers between devices with their start and end apart: 17, of which 14 were waited for; matrix products, arithmetic and copies ran while one was open for 0% of the time, Pallas kernels for 9%

profile of v9, /device:TPU:0, one launch (start us, length us, event | category | flops | bytes accessed | tf_op | source)
XLA Modules:
  0.0 68.4 jit_solution(14026128105180318819)
XLA Ops:
  0.0 1.5 %shard_map.37 = (f32[264,128]{1,0:T(8,128)S(1)}, f32[264,128]{1,0:T(8,128)S(1)}) custom-call(f32[128,512]{1,0:T(8,128)} %refs_2_.1, f32[1,128]{1,0:T(1,128)} %bitcast.5), custom_call_target="tpu_custom_call" | custom-call | tf_op jit(solution)/shard_map/pallas_call | solution.py:231
  3.0 2.9 %collective-permute-start.2 = (f32[264,128]{1,0:T(8,128)S(1)}, f32[264,128]{1,0:T(8,128)S(1)}, u32[]{:S(2)}, u32[]{:S(2)}) collective-permute-start(f32[264,128]{1,0:T(8,128)S(1)} %add.26), channel_id=1, source_target_pairs={{0,8},{4,20},{8,0},{12,28},{16,24},{20,4},{24,16},{28,12},{1,9},{5... | collective-permute-start | bytes 405512 | tf_op jit(solution)/shard_map/ppermute | solution.py:24
  5.9 3.0 %collective-permute-done.2 = f32[264,128]{1,0:T(8,128)S(1)} collective-permute-done((f32[264,128]{1,0:T(8,128)S(1)}, f32[264,128]{1,0:T(8,128)S(1)}, u32[]{:S(2)}, u32[]{:S(2)}) %collective-permute-start.2) | collective-permute-done | bytes 135200 | tf_op jit(solution)/shard_map/ppermute | solution.py:24
  8.9 2.1 %collective-permute-start.4 = (f32[264,128]{1,0:T(8,128)S(1)}, f32[264,128]{1,0:T(8,128)S(1)}, u32[]{:S(2)}, u32[]{:S(2)}) collective-permute-start(f32[264,128]{1,0:T(8,128)S(1)} %add.27), channel_id=1, source_target_pairs={{0,16},{4,12},{8,24},{12,4},{16,0},{20,28},{24,8},{28,20},{1,17},{... | collective-permute-start | bytes 405512 | tf_op jit(solution)/shard_map/ppermute | solution.py:24
  11.1 3.0 %collective-permute-done.4 = f32[264,128]{1,0:T(8,128)S(1)} collective-permute-done((f32[264,128]{1,0:T(8,128)S(1)}, f32[264,128]{1,0:T(8,128)S(1)}, u32[]{:S(2)}, u32[]{:S(2)}) %collective-permute-start.4) | collective-permute-done | bytes 135200 | tf_op jit(solution)/shard_map/ppermute | solution.py:24
  15.5 2.0 %shard_map.38 = (f32[256,128]{1,0:T(8,128)S(1)}, f32[256,256]{1,0:T(8,128)S(1)}, f32[8,128]{1,0:T(8,128)S(1)}) custom-call(f32[3,128]{1,0:T(4,128)S(1)} %broadcast_in_dim.16.damps, f32[264,128]{1,0:T(8,128)S(1)} %add.28.own_sum, f32[264,128]{1,0:T(8,128)S(1)} %collective-permute-done.5.other_sum, f32[128,512]{1,0:T(8,128)S(1)} %copy-done, ...), custom_call_target="tpu_custom_call" | custom-call | tf_op jit(solution)/shard_map/pallas_call | solution.py:217
  17.5 2.1 %collective-permute-start.6 = (f32[256,128]{1,0:T(8,128)S(1)}, f32[256,128]{1,0:T(8,128)S(1)}, u32[]{:S(2)}, u32[]{:S(2)}) collective-permute-start(f32[256,128]{1,0:T(8,128)S(1)} %get-tuple-element.50), channel_id=1, source_target_pairs={{0,1},{1,2},{2,3},{3,0},{4,5},{5,6},{6,7},{7,4},{8,9},{9,10},{10,1... | collective-permute-start | bytes 393224 | tf_op jit(solution)/shard_map/ppermute | solution.py:18
  20.9 1.9 %shard_map.39 = (bf16[256,768]{1,0:T(8,128)(2,1)S(1)}, f32[1,128]{1,0:T(1,128)S(1)}, f32[256,256]{1,0:T(8,128)S(1)}) custom-call(f32[256,1]{1,0:T(8,128)S(1)} %copy.7.weight, f32[256,256]{1,0:T(8,128)S(1)} %get-tuple-element.46.refs_0_, f32[8,128]{1,0:T(8,128)S(1)} %get-tuple-element.47.refs_1_, f32[128,512]{1,0:T(8,128)S(1)} %copy-done, ...), custom_call_target="tpu_custom_call" | custom-call | tf_op jit(solution)/shard_map/pallas_call | solution.py:217
  22.7 2.7 %collective-permute-done.6.own_ref.refs_1_.refs_3_ = f32[256,128]{1,0:T(8,128)S(1)} collective-permute-done((f32[256,128]{1,0:T(8,128)S(1)}, f32[256,128]{1,0:T(8,128)S(1)}, u32[]{:S(2)}, u32[]{:S(2)}) %collective-permute-start.6) | collective-permute-done | bytes 131104 | tf_op jit(solution)/shard_map/ppermute | solution.py:18
  25.7 1.6 %collective-permute-start.7 = (f32[264,128]{1,0:T(8,128)S(1)}, f32[264,128]{1,0:T(8,128)S(1)}, u32[]{:S(2)}, u32[]{:S(2)}) collective-permute-start(f32[264,128]{1,0:T(8,128)S(1)} %shard_map.40), channel_id=1, source_target_pairs={{0,8},{4,20},{8,0},{12,28},{16,24},{20,4},{24,16},{28,12},{1,9},{5... | collective-permute-start | bytes 405512 | tf_op jit(solution)/shard_map/ppermute | solution.py:24
  27.3 3.5 %collective-permute-done.7 = f32[264,128]{1,0:T(8,128)S(1)} collective-permute-done((f32[264,128]{1,0:T(8,128)S(1)}, f32[264,128]{1,0:T(8,128)S(1)}, u32[]{:S(2)}, u32[]{:S(2)}) %collective-permute-start.7) | collective-permute-done | bytes 135200 | tf_op jit(solution)/shard_map/ppermute | solution.py:24
  30.8 1.6 %collective-permute-start.9 = (f32[264,128]{1,0:T(8,128)S(1)}, f32[264,128]{1,0:T(8,128)S(1)}, u32[]{:S(2)}, u32[]{:S(2)}) collective-permute-start(f32[264,128]{1,0:T(8,128)S(1)} %add.29), channel_id=1, source_target_pairs={{0,16},{4,12},{8,24},{12,4},{16,0},{20,28},{24,8},{28,20},{1,17},{... | collective-permute-start | bytes 405512 | tf_op jit(solution)/shard_map/ppermute | solution.py:24
  32.4 3.5 %collective-permute-done.9 = f32[264,128]{1,0:T(8,128)S(1)} collective-permute-done((f32[264,128]{1,0:T(8,128)S(1)}, f32[264,128]{1,0:T(8,128)S(1)}, u32[]{:S(2)}, u32[]{:S(2)}) %collective-permute-start.9) | collective-permute-done | bytes 135200 | tf_op jit(solution)/shard_map/ppermute | solution.py:24
  36.0 1.3 %collective-permute-done.10.other_sum = f32[264,128]{1,0:T(8,128)S(1)} collective-permute-done((f32[264,128]{1,0:T(8,128)S(1)}, f32[264,128]{1,0:T(8,128)S(1)}, u32[]{:S(2)}, u32[]{:S(2)}) %collective-permute-start.10) | collective-permute-done | bytes 135200 | tf_op jit(solution)/shard_map/ppermute | solution.py:24
  37.3 2.0 %shard_map.41 = (f32[256,128]{1,0:T(8,128)S(1)}, f32[256,256]{1,0:T(8,128)S(1)}, f32[8,128]{1,0:T(8,128)S(1)}) custom-call(f32[3,128]{1,0:T(4,128)S(1)} %broadcast_in_dim.16.damps, f32[264,128]{1,0:T(8,128)S(1)} %add.30.own_sum, f32[264,128]{1,0:T(8,128)S(1)} %collective-permute-done.10.other_sum, f32[256,256]{1,0:T(8,128)S(1)} %get-tuple-element.54.refs_0_.refs_2_, ...), custom_call_target="tpu_custom_call" | custom-call | tf_op jit(solution)/shard_map/pallas_call | solution.py:217
  39.4 1.9 %shard_map.42 = (bf16[256,768]{1,0:T(8,128)(2,1)S(1)}, f32[1,128]{1,0:T(1,128)S(1)}, f32[256,256]{1,0:T(8,128)S(1)}) custom-call(f32[256,1]{1,0:T(8,128)S(1)} %copy.7.weight, f32[256,256]{1,0:T(8,128)S(1)} %get-tuple-element.56.refs_0_, f32[8,128]{1,0:T(8,128)S(1)} %get-tuple-element.57.refs_1_, f32[256,256]{1,0:T(8,128)S(1)} %get-tuple-element.54.refs_0_.refs_2_, ...), custom_call_target="tpu_custom_call" | custom-call | tf_op jit(solution)/shard_map/pallas_call | solution.py:217
  41.2 5.5 %collective-permute-done.11.own_ref.refs_1_.refs_3_ = f32[256,128]{1,0:T(8,128)S(1)} collective-permute-done((f32[256,128]{1,0:T(8,128)S(1)}, f32[256,128]{1,0:T(8,128)S(1)}, u32[]{:S(2)}, u32[]{:S(2)}) %collective-permute-start.11) | collective-permute-done | bytes 131104 | tf_op jit(solution)/shard_map/ppermute | solution.py:18
  47.0 1.6 %collective-permute-start.12 = (f32[264,128]{1,0:T(8,128)S(1)}, f32[264,128]{1,0:T(8,128)S(1)}, u32[]{:S(2)}, u32[]{:S(2)}) collective-permute-start(f32[264,128]{1,0:T(8,128)S(1)} %shard_map.43), channel_id=1, source_target_pairs={{0,8},{4,20},{8,0},{12,28},{16,24},{20,4},{24,16},{28,12},{1,9},{5... | collective-permute-start | bytes 405512 | tf_op jit(solution)/shard_map/ppermute | solution.py:24
  48.5 3.5 %collective-permute-done.12 = f32[264,128]{1,0:T(8,128)S(1)} collective-permute-done((f32[264,128]{1,0:T(8,128)S(1)}, f32[264,128]{1,0:T(8,128)S(1)}, u32[]{:S(2)}, u32[]{:S(2)}) %collective-permute-start.12) | collective-permute-done | bytes 135200 | tf_op jit(solution)/shard_map/ppermute | solution.py:24
  52.1 1.6 %collective-permute-start.14 = (f32[264,128]{1,0:T(8,128)S(1)}, f32[264,128]{1,0:T(8,128)S(1)}, u32[]{:S(2)}, u32[]{:S(2)}) collective-permute-start(f32[264,128]{1,0:T(8,128)S(1)} %add.31), channel_id=1, source_target_pairs={{0,16},{4,12},{8,24},{12,4},{16,0},{20,28},{24,8},{28,20},{1,17},{... | collective-permute-start | bytes 405512 | tf_op jit(solution)/shard_map/ppermute | solution.py:24
  53.6 3.5 %collective-permute-done.14 = f32[264,128]{1,0:T(8,128)S(1)} collective-permute-done((f32[264,128]{1,0:T(8,128)S(1)}, f32[264,128]{1,0:T(8,128)S(1)}, u32[]{:S(2)}, u32[]{:S(2)}) %collective-permute-start.14) | collective-permute-done | bytes 135200 | tf_op jit(solution)/shard_map/ppermute | solution.py:24
  58.6 1.9 %shard_map.44 = (f32[128,256]{1,0:T(8,128)S(1)}, f32[256,256]{1,0:T(8,128)S(1)}, f32[8,128]{1,0:T(8,128)S(1)}) custom-call(f32[3,128]{1,0:T(4,128)S(1)} %broadcast_in_dim.16.damps, f32[264,128]{1,0:T(8,128)S(1)} %add.32.own_sum, f32[264,128]{1,0:T(8,128)S(1)} %collective-permute-done.15.other_sum, f32[256,256]{1,0:T(8,128)S(1)} %get-tuple-element.64.refs_0_.refs_2_, ...), custom_call_target="tpu_custom_call" | custom-call | tf_op jit(solution)/shard_map/pallas_call | solution.py:217
  60.6 2.3 %shard_map.45.filled = f32[128,512]{1,0:T(8,128)} custom-call(f32[256,256]{1,0:T(8,128)S(1)} %get-tuple-element.67.refs_0_, f32[8,128]{1,0:T(8,128)S(1)} %get-tuple-element.68.refs_1_, f32[256,256]{1,0:T(8,128)S(1)} %get-tuple-element.64.refs_0_.refs_2_, f32[256,128]{1,0:T(8,128)S(1)} %collective-permute-done.11.own_ref.refs_1_.refs_3_, ...), custom_call_target="tpu_custom_call" | custom-call | tf_op jit(solution)/shard_map/pallas_call | solution.py:277
  62.9 4.8 %collective-permute-done.16.lower = f32[128,256]{1,0:T(8,128)S(1)} collective-permute-done((f32[128,256]{1,0:T(8,128)S(1)}, f32[128,256]{1,0:T(8,128)S(1)}, u32[]{:S(2)}, u32[]{:S(2)}) %collective-permute-start.16) | collective-permute-done | bytes 131104 | tf_op jit(solution)/shard_map/ppermute | solution.py:18
  (37 shorter events, 7.1 us)
Async XLA Ops:
  0.0 2.0 %copy-start = (f32[128,512]{1,0:T(8,128)S(1)}, f32[128,512]{1,0:T(8,128)}, u32[]{:S(2)}) copy-start(f32[128,512]{1,0:T(8,128)} %refs_2_.1) | copy-start | bytes 786436
  1.5 1.5 %collective-permute-start.1 = (f32[264,128]{1,0:T(8,128)S(1)}, f32[264,128]{1,0:T(8,128)S(1)}, u32[]{:S(2)}, u32[]{:S(2)}) collective-permute-start(f32[264,128]{1,0:T(8,128)S(1)} %get-tuple-element.41), channel_id=1, source_target_pairs={{0,4},{4,0},{8,12},{12,8},{16,20},{20,16},{24,28},{28,24},{1,5},{5... | collective-permute-start | bytes 405512 | tf_op jit(solution)/shard_map/ppermute | solution.py:24
  2.0 7.0 %collective-permute-start.3 = (f32[128,512]{1,0:T(8,128)S(1)}, f32[128,512]{1,0:T(8,128)S(1)}, u32[]{:S(2)}, u32[]{:S(2)}) collective-permute-start(f32[128,512]{1,0:T(8,128)S(1)} %copy-done), channel_id=1, source_target_pairs={{0,4},{4,0},{8,12},{12,8},{16,20},{20,16},{24,28},{28,24},{1,5},{5... | collective-permute-start | bytes 786440 | tf_op jit(solution)/shard_map/ppermute | solution.py:24
  3.0 5.9 %collective-permute-start.2 = (f32[264,128]{1,0:T(8,128)S(1)}, f32[264,128]{1,0:T(8,128)S(1)}, u32[]{:S(2)}, u32[]{:S(2)}) collective-permute-start(f32[264,128]{1,0:T(8,128)S(1)} %add.26), channel_id=1, source_target_pairs={{0,8},{4,20},{8,0},{12,28},{16,24},{20,4},{24,16},{28,12},{1,9},{5... | collective-permute-start | bytes 405512 | tf_op jit(solution)/shard_map/ppermute | solution.py:24
  8.9 5.2 %copy-start.2 = (s32[3,2]{0,1:T(2,128)S(1)}, s32[3,2]{0,1:T(2,128)}, u32[]{:S(2)}) copy-start(s32[3,2]{0,1:T(2,128)} %param.5) | copy-start | bytes 76
  8.9 5.1 %collective-permute-start.4 = (f32[264,128]{1,0:T(8,128)S(1)}, f32[264,128]{1,0:T(8,128)S(1)}, u32[]{:S(2)}, u32[]{:S(2)}) collective-permute-start(f32[264,128]{1,0:T(8,128)S(1)} %add.27), channel_id=1, source_target_pairs={{0,16},{4,12},{8,24},{12,4},{16,0},{20,28},{24,8},{28,20},{1,17},{... | collective-permute-start | bytes 405512 | tf_op jit(solution)/shard_map/ppermute | solution.py:24
  14.1 1.4 %collective-permute-start.5 = (f32[264,128]{1,0:T(8,128)S(1)}, f32[264,128]{1,0:T(8,128)S(1)}, u32[]{:S(2)}, u32[]{:S(2)}) collective-permute-start(f32[264,128]{1,0:T(8,128)S(1)} %add.28.own_sum), channel_id=1, source_target_pairs={{0,4},{4,0},{8,12},{12,8},{16,20},{20,16},{24,28},{28,24},{1,5},{5... | collective-permute-start | bytes 405512 | tf_op jit(solution)/shard_map/ppermute | solution.py:24
  17.5 2.1 %copy-start.1 = (f32[128]{0:T(128)S(1)}, f32[128]{0:T(128)}, u32[]{:S(2)}) copy-start(f32[128]{0:T(128)} %param.4) | copy-start | bytes 1540
  17.5 8.0 %collective-permute-start.6 = (f32[256,128]{1,0:T(8,128)S(1)}, f32[256,128]{1,0:T(8,128)S(1)}, u32[]{:S(2)}, u32[]{:S(2)}) collective-permute-start(f32[256,128]{1,0:T(8,128)S(1)} %get-tuple-element.50), channel_id=1, source_target_pairs={{0,1},{1,2},{2,3},{3,0},{4,5},{5,6},{6,7},{7,4},{8,9},{9,10},{10,1... | collective-permute-start | bytes 393224 | tf_op jit(solution)/shard_map/ppermute | solution.py:18
  19.6 1.1 %collective-permute-start = (f32[128]{0:T(128)S(1)}, f32[128]{0:T(128)S(1)}, u32[]{:S(2)}, u32[]{:S(2)}) collective-permute-start(f32[128]{0:T(128)S(1)} %copy-done.1), channel_id=1, source_target_pairs={{0,4},{4,0},{8,12},{12,8},{16,20},{20,16},{24,28},{28,24},{1,5},{5... | collective-permute-start | bytes 1544 | tf_op jit(solution)/shard_map/ppermute | solution.py:24
  25.7 5.1 %collective-permute-start.7 = (f32[264,128]{1,0:T(8,128)S(1)}, f32[264,128]{1,0:T(8,128)S(1)}, u32[]{:S(2)}, u32[]{:S(2)}) collective-permute-start(f32[264,128]{1,0:T(8,128)S(1)} %shard_map.40), channel_id=1, source_target_pairs={{0,8},{4,20},{8,0},{12,28},{16,24},{20,4},{24,16},{28,12},{1,9},{5... | collective-permute-start | bytes 405512 | tf_op jit(solution)/shard_map/ppermute | solution.py:24
  27.2 3.5 %collective-permute-start.8 = (f32[256,128]{1,0:T(8,128)S(1)}, f32[256,128]{1,0:T(8,128)S(1)}, u32[]{:S(2)}, u32[]{:S(2)}) collective-permute-start(f32[256,128]{1,0:T(8,128)S(1)} %collective-permute-done.6.own_ref.refs_1_.refs_3_), channel_id=1, source_target_pairs={{0,4},{4,0},{8,12},{12,8},{16,20},{20,16},{24,28},{28,24},{1,5},{5... | collective-permute-start | bytes 393224 | tf_op jit(solution)/shard_map/ppermute | solution.py:24
  30.8 5.1 %collective-permute-start.9 = (f32[264,128]{1,0:T(8,128)S(1)}, f32[264,128]{1,0:T(8,128)S(1)}, u32[]{:S(2)}, u32[]{:S(2)}) collective-permute-start(f32[264,128]{1,0:T(8,128)S(1)} %add.29), channel_id=1, source_target_pairs={{0,16},{4,12},{8,24},{12,4},{16,0},{20,28},{24,8},{28,20},{1,17},{... | collective-permute-start | bytes 405512 | tf_op jit(solution)/shard_map/ppermute | solution.py:24
  35.9 1.4 %collective-permute-start.10 = (f32[264,128]{1,0:T(8,128)S(1)}, f32[264,128]{1,0:T(8,128)S(1)}, u32[]{:S(2)}, u32[]{:S(2)}) collective-permute-start(f32[264,128]{1,0:T(8,128)S(1)} %add.30.own_sum), channel_id=1, source_target_pairs={{0,4},{4,0},{8,12},{12,8},{16,20},{20,16},{24,28},{28,24},{1,5},{5... | collective-permute-start | bytes 405512 | tf_op jit(solution)/shard_map/ppermute | solution.py:24
  39.3 7.4 %collective-permute-start.11 = (f32[256,128]{1,0:T(8,128)S(1)}, f32[256,128]{1,0:T(8,128)S(1)}, u32[]{:S(2)}, u32[]{:S(2)}) collective-permute-start(f32[256,128]{1,0:T(8,128)S(1)} %get-tuple-element.60), channel_id=1, source_target_pairs={{0,1},{1,2},{2,3},{3,0},{4,5},{5,6},{6,7},{7,4},{8,9},{9,10},{10,1... | collective-permute-start | bytes 393224 | tf_op jit(solution)/shard_map/ppermute | solution.py:18
  47.0 5.1 %collective-permute-start.12 = (f32[264,128]{1,0:T(8,128)S(1)}, f32[264,128]{1,0:T(8,128)S(1)}, u32[]{:S(2)}, u32[]{:S(2)}) collective-permute-start(f32[264,128]{1,0:T(8,128)S(1)} %shard_map.43), channel_id=1, source_target_pairs={{0,8},{4,20},{8,0},{12,28},{16,24},{20,4},{24,16},{28,12},{1,9},{5... | collective-permute-start | bytes 405512 | tf_op jit(solution)/shard_map/ppermute | solution.py:24
  48.5 3.5 %collective-permute-start.13 = (f32[256,128]{1,0:T(8,128)S(1)}, f32[256,128]{1,0:T(8,128)S(1)}, u32[]{:S(2)}, u32[]{:S(2)}) collective-permute-start(f32[256,128]{1,0:T(8,128)S(1)} %collective-permute-done.11.own_ref.refs_1_.refs_3_), channel_id=1, source_target_pairs={{0,4},{4,0},{8,12},{12,8},{16,20},{20,16},{24,28},{28,24},{1,5},{5... | collective-permute-start | bytes 393224 | tf_op jit(solution)/shard_map/ppermute | solution.py:24
  52.1 5.1 %collective-permute-start.14 = (f32[264,128]{1,0:T(8,128)S(1)}, f32[264,128]{1,0:T(8,128)S(1)}, u32[]{:S(2)}, u32[]{:S(2)}) collective-permute-start(f32[264,128]{1,0:T(8,128)S(1)} %add.31), channel_id=1, source_target_pairs={{0,16},{4,12},{8,24},{12,4},{16,0},{20,28},{24,8},{28,20},{1,17},{... | collective-permute-start | bytes 405512 | tf_op jit(solution)/shard_map/ppermute | solution.py:24
  57.2 1.4 %collective-permute-start.15 = (f32[264,128]{1,0:T(8,128)S(1)}, f32[264,128]{1,0:T(8,128)S(1)}, u32[]{:S(2)}, u32[]{:S(2)}) collective-permute-start(f32[264,128]{1,0:T(8,128)S(1)} %add.32.own_sum), channel_id=1, source_target_pairs={{0,4},{4,0},{8,12},{12,8},{16,20},{20,16},{24,28},{28,24},{1,5},{5... | collective-permute-start | bytes 405512 | tf_op jit(solution)/shard_map/ppermute | solution.py:24
  60.5 7.2 %collective-permute-start.16 = (f32[128,256]{1,0:T(8,128)S(1)}, f32[128,256]{1,0:T(8,128)S(1)}, u32[]{:S(2)}, u32[]{:S(2)}) collective-permute-start(f32[128,256]{1,0:T(8,128)S(1)} %get-tuple-element.66), channel_id=1, source_target_pairs={{0,2},{1,3},{2,0},{3,1},{4,6},{5,7},{6,4},{7,5},{8,10},{9,11},{10,... | collective-permute-start | bytes 393224 | tf_op jit(solution)/shard_map/ppermute | solution.py:18

commit v10 on v9

v10 whole, which is shorter than its diff:
```python
import functools

import jax
import jax.numpy as jnp
from jax import lax
from jax.experimental import pallas as pl
from jax.experimental.pallas import tpu as pltpu
from jax.sharding import PartitionSpec as P

STEPS = 3
EPSILON = 1e-06
F32 = jnp.float32


def permuted(value, target):
    points, columns = lax.axis_size("pts"), lax.axis_size("cols")
    pairs = []
    for source in range(points * columns):
        point, column = target(source // columns, source % columns)
        pairs.append((source, point * columns + column % columns))
    return lax.ppermute(value, ("pts", "cols"), pairs)


def core_exchange(value):
    return permuted(value, lambda point, column: (point ^ 1, column))


def chip_exchange(value, bit):
    return permuted(value, lambda p, c: (p ^ bit, c) if p % 2 else (p, c ^ 1))


def column_shift(value, steps):
    return permuted(value, lambda p, c: (p, c + steps) if p % 2 else (p ^ 2, c))


def chip_sums(values, beside):
    count = lax.axis_size("pts")
    bit = 2
    while bit < count:
        rounds = [(bit, 2 * bit), (2 * bit, bit)] if 2 * bit < count else [(bit, bit)]
        for bits in rounds:
            values = tuple(value + chip_exchange(value, b) for value, b in zip(values, bits))
            values, beside = lax.optimization_barrier((values, beside))
        bit *= 2 ** len(rounds)
    return values, beside


def two_parts(value):
    high = value.astype(jnp.bfloat16)
    return high, (value - high.astype(F32)).astype(jnp.bfloat16)


def first_columns(parts, columns):
    return parts[0][:, :columns], parts[1][:, :columns]


def product(left, right, left_axis=1, right_axis=0):
    return lax.dot_general(
        jnp.concatenate([left[0], left[0], left[1]], axis=left_axis),
        jnp.concatenate([right[0], right[1], right[0]], axis=right_axis),
        (((left_axis,), (right_axis,)), ((), ())),
        preferred_element_type=F32,
    )


def times_inverse_root(left, square, scale, columns):
    rows = lax.broadcasted_iota(jnp.int32, square.shape, 0)
    identity = jnp.where(rows == lax.broadcasted_iota(jnp.int32, square.shape, 1), 1.0, 0.0)
    base = (identity + square) * (1.0 / scale)
    base_parts = two_parts(base)
    left_parts = two_parts(left)
    second = product(base_parts, base_parts)
    left_base = product(left_parts, base_parts)
    first_square = two_parts(2.25 * identity - 1.5 * base + 0.25 * second)
    cubic = product(two_parts(1.5 * base - 0.5 * second), first_square)
    both = two_parts(2.25 * identity - 0.75 * base - 0.5 * cubic)
    both_first = first_columns(both, columns)
    both_square = product(both, both_first)
    left_cubic = product(two_parts(left_base), both)
    left_both = product(left_parts, both_first)
    left_last = product(two_parts(left_cubic), two_parts(both_square))
    return (1.5 * left_both - 0.5 * left_last) * lax.rsqrt(scale)


def start_blocks(far, near):
    width = near.shape[1] // 2
    whole = jnp.concatenate([far[...], near[...]], axis=0)
    return whole[:, :width], whole[:, width:]


def later_blocks(upper, lower):
    return upper[...], lower[...]


def put_sums(outs, gram, norm_lower, norm_upper):
    width = gram.shape[0]
    rows = lax.broadcasted_iota(jnp.int32, (8, width), 0)
    norms = jnp.where(rows == 0, norm_lower, jnp.where(rows == 1, norm_upper, 0.0))
    for index, out in enumerate(outs):
        columns = slice(index * (width // 2), (index + 1) * (width // 2))
        out[:width] = gram[:, columns]
        out[width:] = norms[:, columns]


def start_kernel(near_ref, weight_ref, first, second, near, weight, near_sent, weight_sent):
    copies = [
        pltpu.make_async_copy(near_ref, near, near_sent),
        pltpu.make_async_copy(weight_ref, weight, weight_sent),
    ]
    for copy in copies:
        copy.start()
    for copy in copies:
        copy.wait()
    width = near.shape[1] // 2
    point_weight = jnp.broadcast_to(weight[...], (8, weight.shape[1])).T[:, 0:1]
    upper, lower = near[:, :width], near[:, width:]
    weighted = point_weight * lower
    gram = product(two_parts(upper), two_parts(weighted), 0, 0)
    norm_lower = jnp.sum(weighted * lower, axis=0, keepdims=True)
    norm_upper = jnp.sum(point_weight * upper * upper, axis=0, keepdims=True)
    put_sums((first, second), gram, norm_lower, norm_upper)


def lower_kernel(blocks, step, damps, first_sum, second_sum, *refs):
    *block_refs, coupling_out, scale_out = refs[: len(refs) - (2 if step + 1 == STEPS else 1)]
    moved = refs[len(block_refs) + 2 :]
    width = coupling_out.shape[0]
    upper, lower = blocks(*block_refs)
    gram = jnp.concatenate([first_sum[:width], second_sum[:width]], axis=1)
    norms = jnp.concatenate([first_sum[width:], second_sum[width:]], axis=1)
    inverse = lax.rsqrt(norms + EPSILON)
    coupling = gram * (damps[step : step + 1, 0:1] * inverse.T[:, 1:2]) * inverse[0:1]
    scale = 1.0 + jnp.sum(coupling * coupling, keepdims=True)
    coupling_out[...] = coupling
    scale_out[...] = jnp.broadcast_to(scale, scale_out.shape)
    parts = two_parts(coupling)
    square = product(parts, parts, 0, 0)
    mixed = lower + product(two_parts(upper), parts)
    put_rows(moved, times_inverse_root(mixed, square, scale, width))


def put_rows(outs, value):
    rows = outs[0].shape[0]
    for index, out in enumerate(outs):
        out[...] = value[index * rows : (index + 1) * rows]


def rotated_upper(blocks, coupling_ref, scale_ref, *block_refs):
    coupling = coupling_ref[...]
    upper, lower = blocks(*block_refs)
    parts = two_parts(coupling)
    mixed = upper - product(two_parts(lower), parts, 1, 1)
    square = product(parts, parts, 1, 1)
    return times_inverse_root(mixed, square, scale_ref[0:1, 0:1], coupling.shape[1])


def upper_kernel(blocks, weight, *refs):
    *ins, gram_left, norm_out, upper_out = refs
    upper = rotated_upper(blocks, *ins)
    upper_out[...] = upper
    weighted = weight[...] * upper
    norm_out[...] = jnp.sum(weighted * upper, axis=0, keepdims=True)
    high, low = two_parts(weighted.T)
    gram_left[...] = jnp.concatenate([high, high, low], axis=1)


def last_upper_kernel(blocks, *refs):
    *ins, first, second = refs
    put_rows((first, second), rotated_upper(blocks, *ins))


def gram_kernel(gram_left, norm_upper, weight, lower_ref, first, second):
    lower = lower_ref[...]
    high, low = two_parts(lower)
    right = jnp.concatenate([high, low, high], axis=0)
    gram = jnp.dot(gram_left[...], right, preferred_element_type=F32)
    norm_lower = jnp.sum(weight[...] * lower * lower, axis=0, keepdims=True)
    put_sums((first, second), gram, norm_lower, norm_upper[...])


def put_columns(start, own, given, out, sent):
    core = lax.axis_index("pts") % 2
    for index, ref in enumerate((given, own)):

        @pl.when(core == index)
        def _(ref=ref):
            copy = pltpu.make_async_copy(ref, out.at[:, pl.ds(start, ref.shape[1])], sent)
            copy.start()
            copy.wait()


def first_columns_kernel(own, given, out, sent):
    put_columns(0, own, given, out, sent)


def last_columns_kernel(own, given, filled, out, sent):
    del filled
    put_columns(own.shape[1], own, given, out, sent)


ON_CHIP = pl.BlockSpec(memory_space=pltpu.VMEM)
ANYWHERE = pl.BlockSpec(memory_space=pl.ANY)
GRANT = pltpu.CompilerParams(vmem_limit_bytes=24 << 20)


def in_vmem(kernel, outs, *args, flops=None):
    cost = None if flops is None else pl.CostEstimate(flops=flops, bytes_accessed=0, transcendentals=0)
    return pl.pallas_call(
        kernel,
        out_shape=[jax.ShapeDtypeStruct(shape, dtype) for shape, dtype in outs],
        in_specs=[ON_CHIP] * len(args),
        out_specs=[ON_CHIP] * len(outs),
        compiler_params=GRANT,
        cost_estimate=cost,
    )(*args)


def body(snapshot, weights, damping):
    rows, columns = snapshot.shape
    width = columns // 2
    sums = [((width + 8, width // 2), F32)] * 2
    whole = ((2 * rows, width), F32)
    parts = pl.pallas_call(
        start_kernel,
        out_shape=[jax.ShapeDtypeStruct(*one) for one in sums],
        in_specs=[pl.BlockSpec(memory_space=pltpu.HBM)] * 2,
        out_specs=[ON_CHIP] * 2,
        scratch_shapes=[
            pltpu.VMEM((rows, columns), F32),
            pltpu.VMEM((1, rows), F32),
            pltpu.SemaphoreType.DMA(()),
            pltpu.SemaphoreType.DMA(()),
        ],
        compiler_params=GRANT,
    )(*(pltpu.with_memory_space_constraint(value, pltpu.HBM) for value in (snapshot, weights[None])))
    *parts, damping = lax.optimization_barrier((*parts, damping))
    parts = tuple(part + core_exchange(part) for part in parts)
    weight = jnp.concatenate([core_exchange(weights), weights])[:, None]
    far = core_exchange(snapshot)
    damps = damping[:, 0].astype(F32) / (damping[:, 0] + damping[:, 1]).astype(F32)
    damps = lax.optimization_barrier(jnp.broadcast_to(damps[:, None], (STEPS, 128)))
    blocks, held = start_blocks, (far, snapshot)
    for step in range(STEPS):
        last = step + 1 == STEPS
        if step == 0:
            parts, far = chip_sums(parts, far)
            held = (far, snapshot)
        else:
            parts, _ = chip_sums(parts, ())
        halves = [((rows, width), F32)] * 2
        coupling, scale, *moved = in_vmem(
            functools.partial(lower_kernel, blocks, step),
            [((width, width), F32), ((8, 128), F32)] + (halves if last else [whole]),
            damps,
            *parts,
            *held,
        )
        if last:
            break
        moved = column_shift(moved[0], 1)
        gram_left, norm_upper, upper = in_vmem(
            functools.partial(upper_kernel, blocks),
            [((width, 6 * rows), jnp.bfloat16), ((1, width), F32), whole],
            weight,
            coupling,
            scale,
            *held,
        )
        gram_left, norm_upper, upper, moved = lax.optimization_barrier((gram_left, norm_upper, upper, moved))
        blocks, held = later_blocks, (upper, moved)
        parts = in_vmem(gram_kernel, sums, gram_left, norm_upper, weight, moved)
        parts = tuple(parts)
    back = 1 - STEPS
    given = permuted(moved[0], lambda p, c: (p ^ 1, c + back) if p % 2 else (p ^ 1, c))
    own = column_shift(moved[1], back)
    upper_given, upper_own = in_vmem(
        functools.partial(last_upper_kernel, blocks), halves, coupling, scale, *held, flops=48 * width**3
    )
    upper_given = core_exchange(upper_given)
    result = dict(
        out_shape=jax.ShapeDtypeStruct((rows, columns), F32),
        out_specs=ANYWHERE,
        scratch_shapes=[pltpu.SemaphoreType.DMA(())],
        compiler_params=GRANT,
    )
    rotated = pl.pallas_call(first_columns_kernel, in_specs=[ON_CHIP] * 2, **result)(upper_own, upper_given)
    return pl.pallas_call(
        last_columns_kernel,
        in_specs=[ON_CHIP, ON_CHIP, ANYWHERE],
        input_output_aliases={2: 0},
        **result,
    )(own, given, rotated)


def solution(mesh):
    placed = (P("pts", "cols"), P("pts"), P())
    return jax.shard_map(
        body, mesh=mesh, in_specs=placed, out_specs=P("pts", "cols"), check_vma=False
    )
```

time: 68.5 us -> 76.7 us (1.12)
  starting transfers between devices: 14.4 us -> 20.7 us
  waiting for transfers between devices: 39 us -> 40.6 us
    ppermute x17 -> x21, starting transfers between devices: 14.4 us -> 20.7 us  [permuted(): return lax.ppermute(value, ('pts', 'cols'), pairs)]
    pallas_call x7 -> x8, Pallas kernels: 10.1 us -> 11.8 us  [in_vmem(): pl.pallas_call(kernel, out_shape=[jax.ShapeDtypeStruct(shape, dtype) for...]
    pallas_call x3, Pallas kernels: 4.43 us -> 2.74 us  [the longest x1 1.41 us: body(): pl.pallas_call(start_kernel, out_shape=[jax.ShapeDtypeStruct(*one) for on...]
    ppermute x17 -> x21, waiting for transfers between devices: 39 us -> 40.6 us  [permuted(): return lax.ppermute(value, ('pts', 'cols'), pairs)]
  transfers between devices with their start and end apart: 17 -> 21, of which waited for: 14 -> 18; matrix products, arithmetic and copies ran while one was open for 0% -> 0% of each run, Pallas kernels for 9% -> 6%
where the time goes in v10:
time: 76.7 us; the launch traced here: 76.6 us
  waiting for transfers between devices  40.6 us (53%)
  starting transfers between devices  20.7 us (27%)
  Pallas kernels  14.6 us (19%)
    ppermute x21, waiting for transfers between devices, permuted(): return lax.ppermute(value, ('pts', 'cols'), pairs)  40.6 us
    ppermute x21, starting transfers between devices, permuted(): return lax.ppermute(value, ('pts', 'cols'), pairs)  20.7 us
    pallas_call x8, Pallas kernels, in_vmem(): pl.pallas_call(kernel, out_shape=[jax.ShapeDtypeStruct(shape, dtype) for...  11.8 us
  transfers between devices with their start and end apart: 21, of which 18 were waited for; matrix products, arithmetic and copies ran while one was open for 0% of the time, Pallas kernels for 6%

profile of v10, /device:TPU:0, one launch (start us, length us, event | category | flops | bytes accessed | tf_op | source)
XLA Modules:
  0.0 76.6 jit_solution(3512056473591219320)
XLA Ops:
  3.0 3.0 %collective-permute-start.2 = (f32[264,128]{1,0:T(8,128)S(1)}, f32[264,128]{1,0:T(8,128)S(1)}, u32[]{:S(2)}, u32[]{:S(2)}) collective-permute-start(f32[264,128]{1,0:T(8,128)S(1)} %add.47), channel_id=1, source_target_pairs={{0,1},{1,0},{2,3},{3,2},{4,12},{5,13},{6,14},{7,15},{8,9},{9,8},{1... | collective-permute-start | bytes 405512 | tf_op jit(solution)/shard_map/ppermute | solution.py:21
  6.1 2.8 %collective-permute-done.2 = f32[264,128]{1,0:T(8,128)S(1)} collective-permute-done((f32[264,128]{1,0:T(8,128)S(1)}, f32[264,128]{1,0:T(8,128)S(1)}, u32[]{:S(2)}, u32[]{:S(2)}) %collective-permute-start.2) | collective-permute-done | bytes 135200 | tf_op jit(solution)/shard_map/ppermute | solution.py:21
  9.0 2.1 %collective-permute-done.4 = f32[264,128]{1,0:T(8,128)S(1)} collective-permute-done((f32[264,128]{1,0:T(8,128)S(1)}, f32[264,128]{1,0:T(8,128)S(1)}, u32[]{:S(2)}, u32[]{:S(2)}) %collective-permute-start.4) | collective-permute-done | bytes 135200 | tf_op jit(solution)/shard_map/ppermute | solution.py:21
  13.3 2.9 %collective-permute-done.6 = f32[264,128]{1,0:T(8,128)S(1)} collective-permute-done((f32[264,128]{1,0:T(8,128)S(1)}, f32[264,128]{1,0:T(8,128)S(1)}, u32[]{:S(2)}, u32[]{:S(2)}) %collective-permute-start.6) | collective-permute-done | bytes 135200 | tf_op jit(solution)/shard_map/ppermute | solution.py:21
  17.6 1.9 %shard_map.38 = (f32[256,256]{1,0:T(8,128)S(1)}, f32[8,128]{1,0:T(8,128)S(1)}, f32[256,256]{1,0:T(8,128)S(1)}) custom-call(f32[3,128]{1,0:T(4,128)S(1)} %broadcast_in_dim.16.damps, f32[264,128]{1,0:T(8,128)S(1)} %add.51.first_sum, f32[264,128]{1,0:T(8,128)S(1)} %add.52.second_sum, f32[128,512]{1,0:T(8,128)S(1)} %collective-permute-done.5.refs_0_.refs_2_, ...), custom_call_target="tpu_custom_call" | custom-call | tf_op jit(solution)/shard_map/pallas_call | solution.py:208
  19.6 1.5 %collective-permute-start.8 = (f32[256,256]{1,0:T(8,128)S(1)}, f32[256,256]{1,0:T(8,128)S(1)}, u32[]{:S(2)}, u32[]{:S(2)}) collective-permute-start(f32[256,256]{1,0:T(8,128)S(1)} %get-tuple-element.70), channel_id=1, source_target_pairs={{0,8},{1,9},{2,10},{3,11},{4,5},{5,6},{6,7},{7,4},{8,0},{9,1},{10,... | collective-permute-start | bytes 786440 | tf_op jit(solution)/shard_map/ppermute | solution.py:21
  22.4 1.9 %shard_map.39 = (bf16[256,768]{1,0:T(8,128)(2,1)S(1)}, f32[1,256]{1,0:T(1,128)S(1)}, f32[256,256]{1,0:T(8,128)S(1)}) custom-call(f32[256,1]{1,0:T(8,128)S(1)} %copy.7.weight, f32[256,256]{1,0:T(8,128)S(1)} %get-tuple-element.65.refs_0_, f32[8,128]{1,0:T(8,128)S(1)} %get-tuple-element.66.refs_1_, f32[128,512]{1,0:T(8,128)S(1)} %collective-permute-done.5.refs_0_.refs_2_, ...), custom_call_target="tpu_custom_call" | custom-call | tf_op jit(solution)/shard_map/pallas_call | solution.py:208
  24.3 1.7 %collective-permute-done.8.lower_ref.refs_1_.refs_3_ = f32[256,256]{1,0:T(8,128)S(1)} collective-permute-done((f32[256,256]{1,0:T(8,128)S(1)}, f32[256,256]{1,0:T(8,128)S(1)}, u32[]{:S(2)}, u32[]{:S(2)}) %collective-permute-start.8) | collective-permute-done | bytes 262176 | tf_op jit(solution)/shard_map/ppermute | solution.py:21
  28.4 3.0 %collective-permute-done.9 = f32[264,128]{1,0:T(8,128)S(1)} collective-permute-done((f32[264,128]{1,0:T(8,128)S(1)}, f32[264,128]{1,0:T(8,128)S(1)}, u32[]{:S(2)}, u32[]{:S(2)}) %collective-permute-start.9) | collective-permute-done | bytes 135200 | tf_op jit(solution)/shard_map/ppermute | solution.py:21
  34.9 3.0 %collective-permute-done.11 = f32[264,128]{1,0:T(8,128)S(1)} collective-permute-done((f32[264,128]{1,0:T(8,128)S(1)}, f32[264,128]{1,0:T(8,128)S(1)}, u32[]{:S(2)}, u32[]{:S(2)}) %collective-permute-start.11) | collective-permute-done | bytes 135200 | tf_op jit(solution)/shard_map/ppermute | solution.py:21
  39.4 1.9 %shard_map.41 = (f32[256,256]{1,0:T(8,128)S(1)}, f32[8,128]{1,0:T(8,128)S(1)}, f32[256,256]{1,0:T(8,128)S(1)}) custom-call(f32[3,128]{1,0:T(4,128)S(1)} %broadcast_in_dim.16.damps, f32[264,128]{1,0:T(8,128)S(1)} %add.55.first_sum, f32[264,128]{1,0:T(8,128)S(1)} %add.56.second_sum, f32[256,256]{1,0:T(8,128)S(1)} %get-tuple-element.80.refs_0_.refs_2_, ...), custom_call_target="tpu_custom_call" | custom-call | tf_op jit(solution)/shard_map/pallas_call | solution.py:208
  41.3 1.5 %collective-permute-start.13 = (f32[256,256]{1,0:T(8,128)S(1)}, f32[256,256]{1,0:T(8,128)S(1)}, u32[]{:S(2)}, u32[]{:S(2)}) collective-permute-start(f32[256,256]{1,0:T(8,128)S(1)} %get-tuple-element.86), channel_id=1, source_target_pairs={{0,8},{1,9},{2,10},{3,11},{4,5},{5,6},{6,7},{7,4},{8,0},{9,1},{10,... | collective-permute-start | bytes 786440 | tf_op jit(solution)/shard_map/ppermute | solution.py:21
  42.9 1.8 %shard_map.42 = (bf16[256,768]{1,0:T(8,128)(2,1)S(1)}, f32[1,256]{1,0:T(1,128)S(1)}, f32[256,256]{1,0:T(8,128)S(1)}) custom-call(f32[256,1]{1,0:T(8,128)S(1)} %copy.7.weight, f32[256,256]{1,0:T(8,128)S(1)} %get-tuple-element.81.refs_0_, f32[8,128]{1,0:T(8,128)S(1)} %get-tuple-element.82.refs_1_, f32[256,256]{1,0:T(8,128)S(1)} %get-tuple-element.80.refs_0_.refs_2_, ...), custom_call_target="tpu_custom_call" | custom-call | tf_op jit(solution)/shard_map/pallas_call | solution.py:208
  44.7 3.8 %collective-permute-done.13.lower_ref.refs_1_.refs_3_ = f32[256,256]{1,0:T(8,128)S(1)} collective-permute-done((f32[256,256]{1,0:T(8,128)S(1)}, f32[256,256]{1,0:T(8,128)S(1)}, u32[]{:S(2)}, u32[]{:S(2)}) %collective-permute-start.13) | collective-permute-done | bytes 262176 | tf_op jit(solution)/shard_map/ppermute | solution.py:21
  48.8 2.1 %collective-permute-start.14 = (f32[264,128]{1,0:T(8,128)S(1)}, f32[264,128]{1,0:T(8,128)S(1)}, u32[]{:S(2)}, u32[]{:S(2)}) collective-permute-start(f32[264,128]{1,0:T(8,128)S(1)} %get-tuple-element.90), channel_id=1, source_target_pairs={{0,1},{1,0},{2,3},{3,2},{4,12},{5,13},{6,14},{7,15},{8,9},{9,8},{1... | collective-permute-start | bytes 405512 | tf_op jit(solution)/shard_map/ppermute | solution.py:21
  51.0 2.9 %collective-permute-done.14 = f32[264,128]{1,0:T(8,128)S(1)} collective-permute-done((f32[264,128]{1,0:T(8,128)S(1)}, f32[264,128]{1,0:T(8,128)S(1)}, u32[]{:S(2)}, u32[]{:S(2)}) %collective-permute-start.14) | collective-permute-done | bytes 135200 | tf_op jit(solution)/shard_map/ppermute | solution.py:21
  53.9 2.0 %collective-permute-done.15 = f32[264,128]{1,0:T(8,128)S(1)} collective-permute-done((f32[264,128]{1,0:T(8,128)S(1)}, f32[264,128]{1,0:T(8,128)S(1)}, u32[]{:S(2)}, u32[]{:S(2)}) %collective-permute-start.15) | collective-permute-done | bytes 135200 | tf_op jit(solution)/shard_map/ppermute | solution.py:21
  55.9 1.5 %collective-permute-start.16 = (f32[264,128]{1,0:T(8,128)S(1)}, f32[264,128]{1,0:T(8,128)S(1)}, u32[]{:S(2)}, u32[]{:S(2)}) collective-permute-start(f32[264,128]{1,0:T(8,128)S(1)} %add.57), channel_id=1, source_target_pairs={{0,1},{1,0},{2,3},{3,2},{4,20},{5,21},{6,22},{7,23},{8,9},{9,8},{1... | collective-permute-start | bytes 405512 | tf_op jit(solution)/shard_map/ppermute | solution.py:21
  58.0 3.0 %collective-permute-done.16 = f32[264,128]{1,0:T(8,128)S(1)} collective-permute-done((f32[264,128]{1,0:T(8,128)S(1)}, f32[264,128]{1,0:T(8,128)S(1)}, u32[]{:S(2)}, u32[]{:S(2)}) %collective-permute-start.16) | collective-permute-done | bytes 135200 | tf_op jit(solution)/shard_map/ppermute | solution.py:21
  62.5 1.9 %shard_map.44 = (f32[256,256]{1,0:T(8,128)S(1)}, f32[8,128]{1,0:T(8,128)S(1)}, f32[128,256]{1,0:T(8,128)S(1)}, f32[128,256]{1,0:T(8,128)S(1)}) custom-call(f32[3,128]{1,0:T(4,128)S(1)} %broadcast_in_dim.16.damps, f32[264,128]{1,0:T(8,128)S(1)} %add.59.first_sum, f32[264,128]{1,0:T(8,128)S(1)} %add.60.second_sum, ...), custom_call_target="tpu_custom_call" | custom-call | tf_op jit(solution)/shard_map/pallas_call | solution.py:208
  64.4 1.8 %shard_map.45 = (f32[128,256]{1,0:T(8,128)S(1)}, f32[128,256]{1,0:T(8,128)S(1)}) custom-call(f32[256,256]{1,0:T(8,128)S(1)} %get-tuple-element.99.refs_0_, f32[8,128]{1,0:T(8,128)S(1)} %get-tuple-element.100.refs_1_, f32[256,256]{1,0:T(8,128)S(1)} %get-tuple-element.96.refs_0_.refs_2_, f32[256,256]{1,0:T(8,128)S(1)} %collective-permute-done.13.lower_ref.refs_1_.refs_3_), custom_call_target="tpu_custom_call" | custom-call | flops 805306368 | tf_op jit(solution)/shard_map/pallas_call | solution.py:208
  66.3 1.6 %collective-permute-start.18 = (f32[128,256]{1,0:T(8,128)S(1)}, f32[128,256]{1,0:T(8,128)S(1)}, u32[]{:S(2)}, u32[]{:S(2)}) collective-permute-start(f32[128,256]{1,0:T(8,128)S(1)} %get-tuple-element.97), channel_id=1, source_target_pairs={{0,8},{1,9},{2,10},{3,11},{4,6},{5,7},{6,4},{7,5},{8,0},{9,1},{10,... | collective-permute-start | bytes 393224 | tf_op jit(solution)/shard_map/ppermute | solution.py:21
  69.8 1.6 %collective-permute-done.18.own = f32[128,256]{1,0:T(8,128)S(1)} collective-permute-done((f32[128,256]{1,0:T(8,128)S(1)}, f32[128,256]{1,0:T(8,128)S(1)}, u32[]{:S(2)}, u32[]{:S(2)}) %collective-permute-start.18) | collective-permute-done | bytes 131104 | tf_op jit(solution)/shard_map/ppermute | solution.py:21
  71.3 4.6 %collective-permute-done.19.given = f32[128,256]{1,0:T(8,128)S(1)} collective-permute-done((f32[128,256]{1,0:T(8,128)S(1)}, f32[128,256]{1,0:T(8,128)S(1)}, u32[]{:S(2)}, u32[]{:S(2)}) %collective-permute-start.19) | collective-permute-done | bytes 131104 | tf_op jit(solution)/shard_map/ppermute | solution.py:21
  (53 shorter events, 20.5 us)
Async XLA Ops:
  0.0 2.0 %copy-start = (f32[128,512]{1,0:T(8,128)S(1)}, f32[128,512]{1,0:T(8,128)}, u32[]{:S(2)}) copy-start(f32[128,512]{1,0:T(8,128)} %refs_3_.1) | copy-start | bytes 786436
  1.4 1.5 %collective-permute-start.1 = (f32[264,128]{1,0:T(8,128)S(1)}, f32[264,128]{1,0:T(8,128)S(1)}, u32[]{:S(2)}, u32[]{:S(2)}) collective-permute-start(f32[264,128]{1,0:T(8,128)S(1)} %get-tuple-element.57), channel_id=1, source_target_pairs={{0,4},{1,5},{2,6},{3,7},{4,0},{5,1},{6,2},{7,3},{8,12},{9,13},{10,... | collective-permute-start | bytes 405512 | tf_op jit(solution)/shard_map/ppermute | solution.py:21
  1.9 4.0 %collective-permute-start.3 = (f32[264,128]{1,0:T(8,128)S(1)}, f32[264,128]{1,0:T(8,128)S(1)}, u32[]{:S(2)}, u32[]{:S(2)}) collective-permute-start(f32[264,128]{1,0:T(8,128)S(1)} %get-tuple-element.58), channel_id=1, source_target_pairs={{0,4},{1,5},{2,6},{3,7},{4,0},{5,1},{6,2},{7,3},{8,12},{9,13},{10,... | collective-permute-start | bytes 405512 | tf_op jit(solution)/shard_map/ppermute | solution.py:21
  2.0 9.1 %collective-permute-start.5 = (f32[128,512]{1,0:T(8,128)S(1)}, f32[128,512]{1,0:T(8,128)S(1)}, u32[]{:S(2)}, u32[]{:S(2)}) collective-permute-start(f32[128,512]{1,0:T(8,128)S(1)} %copy-done), channel_id=1, source_target_pairs={{0,4},{1,5},{2,6},{3,7},{4,0},{5,1},{6,2},{7,3},{8,12},{9,13},{10,... | collective-permute-start | bytes 786440 | tf_op jit(solution)/shard_map/ppermute | solution.py:21
  3.0 6.0 %collective-permute-start.2 = (f32[264,128]{1,0:T(8,128)S(1)}, f32[264,128]{1,0:T(8,128)S(1)}, u32[]{:S(2)}, u32[]{:S(2)}) collective-permute-start(f32[264,128]{1,0:T(8,128)S(1)} %add.47), channel_id=1, source_target_pairs={{0,1},{1,0},{2,3},{3,2},{4,12},{5,13},{6,14},{7,15},{8,9},{9,8},{1... | collective-permute-start | bytes 405512 | tf_op jit(solution)/shard_map/ppermute | solution.py:21
  6.0 5.1 %collective-permute-start.4 = (f32[264,128]{1,0:T(8,128)S(1)}, f32[264,128]{1,0:T(8,128)S(1)}, u32[]{:S(2)}, u32[]{:S(2)}) collective-permute-start(f32[264,128]{1,0:T(8,128)S(1)} %add.49), channel_id=1, source_target_pairs={{0,1},{1,0},{2,3},{3,2},{4,20},{5,21},{6,22},{7,23},{8,9},{9,8},{1... | collective-permute-start | bytes 405512 | tf_op jit(solution)/shard_map/ppermute | solution.py:21
  9.0 4.2 %copy-start.2 = (s32[3,2]{0,1:T(2,128)S(1)}, s32[3,2]{0,1:T(2,128)}, u32[]{:S(2)}) copy-start(s32[3,2]{0,1:T(2,128)} %param.5) | copy-start | bytes 76
  11.1 5.1 %collective-permute-start.6 = (f32[264,128]{1,0:T(8,128)S(1)}, f32[264,128]{1,0:T(8,128)S(1)}, u32[]{:S(2)}, u32[]{:S(2)}) collective-permute-start(f32[264,128]{1,0:T(8,128)S(1)} %add.48), channel_id=1, source_target_pairs={{0,1},{1,0},{2,3},{3,2},{4,20},{5,21},{6,22},{7,23},{8,9},{9,8},{1... | collective-permute-start | bytes 405512 | tf_op jit(solution)/shard_map/ppermute | solution.py:21
  12.5 5.1 %collective-permute-start.7 = (f32[264,128]{1,0:T(8,128)S(1)}, f32[264,128]{1,0:T(8,128)S(1)}, u32[]{:S(2)}, u32[]{:S(2)}) collective-permute-start(f32[264,128]{1,0:T(8,128)S(1)} %add.50), channel_id=1, source_target_pairs={{0,1},{1,0},{2,3},{3,2},{4,12},{5,13},{6,14},{7,15},{8,9},{9,8},{1... | collective-permute-start | bytes 405512 | tf_op jit(solution)/shard_map/ppermute | solution.py:21
  19.6 1.6 %copy-start.1 = (f32[128]{0:T(128)S(1)}, f32[128]{0:T(128)}, u32[]{:S(2)}) copy-start(f32[128]{0:T(128)} %param.4) | copy-start | bytes 1540
  19.6 6.4 %collective-permute-start.8 = (f32[256,256]{1,0:T(8,128)S(1)}, f32[256,256]{1,0:T(8,128)S(1)}, u32[]{:S(2)}, u32[]{:S(2)}) collective-permute-start(f32[256,256]{1,0:T(8,128)S(1)} %get-tuple-element.70), channel_id=1, source_target_pairs={{0,8},{1,9},{2,10},{3,11},{4,5},{5,6},{6,7},{7,4},{8,0},{9,1},{10,... | collective-permute-start | bytes 786440 | tf_op jit(solution)/shard_map/ppermute | solution.py:21
  21.1 1.1 %collective-permute-start = (f32[128]{0:T(128)S(1)}, f32[128]{0:T(128)S(1)}, u32[]{:S(2)}, u32[]{:S(2)}) collective-permute-start(f32[128]{0:T(128)S(1)} %copy-done.1), channel_id=1, source_target_pairs={{0,4},{1,5},{2,6},{3,7},{4,0},{5,1},{6,2},{7,3},{8,12},{9,13},{10,... | collective-permute-start | bytes 1544 | tf_op jit(solution)/shard_map/ppermute | solution.py:21
  26.3 5.1 %collective-permute-start.9 = (f32[264,128]{1,0:T(8,128)S(1)}, f32[264,128]{1,0:T(8,128)S(1)}, u32[]{:S(2)}, u32[]{:S(2)}) collective-permute-start(f32[264,128]{1,0:T(8,128)S(1)} %get-tuple-element.74), channel_id=1, source_target_pairs={{0,1},{1,0},{2,3},{3,2},{4,12},{5,13},{6,14},{7,15},{8,9},{9,8},{1... | collective-permute-start | bytes 405512 | tf_op jit(solution)/shard_map/ppermute | solution.py:21
  27.7 5.1 %collective-permute-start.10 = (f32[264,128]{1,0:T(8,128)S(1)}, f32[264,128]{1,0:T(8,128)S(1)}, u32[]{:S(2)}, u32[]{:S(2)}) collective-permute-start(f32[264,128]{1,0:T(8,128)S(1)} %get-tuple-element.75), channel_id=1, source_target_pairs={{0,1},{1,0},{2,3},{3,2},{4,20},{5,21},{6,22},{7,23},{8,9},{9,8},{1... | collective-permute-start | bytes 405512 | tf_op jit(solution)/shard_map/ppermute | solution.py:21
  32.8 5.1 %collective-permute-start.11 = (f32[264,128]{1,0:T(8,128)S(1)}, f32[264,128]{1,0:T(8,128)S(1)}, u32[]{:S(2)}, u32[]{:S(2)}) collective-permute-start(f32[264,128]{1,0:T(8,128)S(1)} %add.53), channel_id=1, source_target_pairs={{0,1},{1,0},{2,3},{3,2},{4,20},{5,21},{6,22},{7,23},{8,9},{9,8},{1... | collective-permute-start | bytes 405512 | tf_op jit(solution)/shard_map/ppermute | solution.py:21
  34.3 5.1 %collective-permute-start.12 = (f32[264,128]{1,0:T(8,128)S(1)}, f32[264,128]{1,0:T(8,128)S(1)}, u32[]{:S(2)}, u32[]{:S(2)}) collective-permute-start(f32[264,128]{1,0:T(8,128)S(1)} %add.54), channel_id=1, source_target_pairs={{0,1},{1,0},{2,3},{3,2},{4,12},{5,13},{6,14},{7,15},{8,9},{9,8},{1... | collective-permute-start | bytes 405512 | tf_op jit(solution)/shard_map/ppermute | solution.py:21
  41.3 7.2 %collective-permute-start.13 = (f32[256,256]{1,0:T(8,128)S(1)}, f32[256,256]{1,0:T(8,128)S(1)}, u32[]{:S(2)}, u32[]{:S(2)}) collective-permute-start(f32[256,256]{1,0:T(8,128)S(1)} %get-tuple-element.86), channel_id=1, source_target_pairs={{0,8},{1,9},{2,10},{3,11},{4,5},{5,6},{6,7},{7,4},{8,0},{9,1},{10,... | collective-permute-start | bytes 786440 | tf_op jit(solution)/shard_map/ppermute | solution.py:21
  48.8 5.1 %collective-permute-start.14 = (f32[264,128]{1,0:T(8,128)S(1)}, f32[264,128]{1,0:T(8,128)S(1)}, u32[]{:S(2)}, u32[]{:S(2)}) collective-permute-start(f32[264,128]{1,0:T(8,128)S(1)} %get-tuple-element.90), channel_id=1, source_target_pairs={{0,1},{1,0},{2,3},{3,2},{4,12},{5,13},{6,14},{7,15},{8,9},{9,8},{1... | collective-permute-start | bytes 405512 | tf_op jit(solution)/shard_map/ppermute | solution.py:21
  50.9 5.0 %collective-permute-start.15 = (f32[264,128]{1,0:T(8,128)S(1)}, f32[264,128]{1,0:T(8,128)S(1)}, u32[]{:S(2)}, u32[]{:S(2)}) collective-permute-start(f32[264,128]{1,0:T(8,128)S(1)} %get-tuple-element.91), channel_id=1, source_target_pairs={{0,1},{1,0},{2,3},{3,2},{4,20},{5,21},{6,22},{7,23},{8,9},{9,8},{1... | collective-permute-start | bytes 405512 | tf_op jit(solution)/shard_map/ppermute | solution.py:21
  55.9 5.1 %collective-permute-start.16 = (f32[264,128]{1,0:T(8,128)S(1)}, f32[264,128]{1,0:T(8,128)S(1)}, u32[]{:S(2)}, u32[]{:S(2)}) collective-permute-start(f32[264,128]{1,0:T(8,128)S(1)} %add.57), channel_id=1, source_target_pairs={{0,1},{1,0},{2,3},{3,2},{4,20},{5,21},{6,22},{7,23},{8,9},{9,8},{1... | collective-permute-start | bytes 405512 | tf_op jit(solution)/shard_map/ppermute | solution.py:21
  57.4 5.0 %collective-permute-start.17 = (f32[264,128]{1,0:T(8,128)S(1)}, f32[264,128]{1,0:T(8,128)S(1)}, u32[]{:S(2)}, u32[]{:S(2)}) collective-permute-start(f32[264,128]{1,0:T(8,128)S(1)} %add.58), channel_id=1, source_target_pairs={{0,1},{1,0},{2,3},{3,2},{4,12},{5,13},{6,14},{7,15},{8,9},{9,8},{1... | collective-permute-start | bytes 405512 | tf_op jit(solution)/shard_map/ppermute | solution.py:21
  66.2 2.9 %collective-permute-start.20 = (f32[128,256]{1,0:T(8,128)S(1)}, f32[128,256]{1,0:T(8,128)S(1)}, u32[]{:S(2)}, u32[]{:S(2)}) collective-permute-start(f32[128,256]{1,0:T(8,128)S(1)} %get-tuple-element.102), channel_id=1, source_target_pairs={{0,4},{1,5},{2,6},{3,7},{4,0},{5,1},{6,2},{7,3},{8,12},{9,13},{10,... | collective-permute-start | bytes 393224 | tf_op jit(solution)/shard_map/ppermute | solution.py:21
  66.3 5.0 %collective-permute-start.18 = (f32[128,256]{1,0:T(8,128)S(1)}, f32[128,256]{1,0:T(8,128)S(1)}, u32[]{:S(2)}, u32[]{:S(2)}) collective-permute-start(f32[128,256]{1,0:T(8,128)S(1)} %get-tuple-element.97), channel_id=1, source_target_pairs={{0,8},{1,9},{2,10},{3,11},{4,6},{5,7},{6,4},{7,5},{8,0},{9,1},{10,... | collective-permute-start | bytes 393224 | tf_op jit(solution)/shard_map/ppermute | solution.py:21
  67.9 8.0 %collective-permute-start.19 = (f32[128,256]{1,0:T(8,128)S(1)}, f32[128,256]{1,0:T(8,128)S(1)}, u32[]{:S(2)}, u32[]{:S(2)}) collective-permute-start(f32[128,256]{1,0:T(8,128)S(1)} %get-tuple-element.98), channel_id=1, source_target_pairs={{0,4},{1,5},{2,6},{3,7},{4,2},{5,3},{6,0},{7,1},{8,12},{9,13},{10,... | collective-permute-start | bytes 393224 | tf_op jit(solution)/shard_map/ppermute | solution.py:21

commit v11 on v9

--- a/solution.py
+++ b/solution.py
@@ -12,10 +12,14 @@
 F32 = jnp.float32
 
 
-def shifted(value, axis, steps):
-    count = lax.axis_size(axis)
-    pairs = [(source, (source + steps) % count) for source in range(count)]
-    return lax.ppermute(value, axis, pairs)
+def column_shift(value, steps):
+    points, columns = lax.axis_size("pts"), lax.axis_size("cols")
+    pairs = [
+        (point * columns + column, (point ^ 1) * columns + (column + steps) % columns)
+        for point in range(points)
+        for column in range(columns)
+    ]
+    return lax.ppermute(value, ("pts", "cols"), pairs)
 
 
 def swapped(value, even_bits, odd_bits):
@@ -24,19 +28,17 @@
     return lax.ppermute(value, "pts", pairs)
 
 
-def chip_sum(value, beside=None):
+def chip_sum(value, beside):
     count = lax.axis_size("pts")
     bit = 2
     while bit < count:
         if 2 * bit < count:
-            rounds = [(bit, 2 * bit), (2 * bit, bit)]
+            for _ in range(2):
+                value = swapped(value, bit ^ 1, 2 * bit ^ 1) + swapped(value, 1, 1)
+                value, beside = lax.optimization_barrier((value, beside))
         else:
-            rounds = [(bit, bit)]
-        for even_bits, odd_bits in rounds:
-            value = value + swapped(value, even_bits, odd_bits)
-            if beside is not None:
-                value, beside = lax.optimization_barrier((value, beside))
-        bit *= 2 ** len(rounds)
+            value = value + swapped(value, bit, bit)
+        bit *= 4
     return value, beside
 
 
@@ -104,7 +106,7 @@
 
 
 def later_blocks(upper, own, other):
-    return upper[...], joined(own[...], other[...])
+    return upper[...], jnp.concatenate([halves_swapped(own[...]), other[...]], axis=1)
 
 
 def stored(ref, value):
@@ -154,7 +156,8 @@
     parts = two_parts(coupling)
     square = product(parts, parts, 0, 0)
     rows, columns = moved.shape
-    mixed = lower[:rows] + product(two_parts(upper[:rows]), parts)
+    taken = slice(rows, 2 * rows) if last else slice(0, rows)
+    mixed = lower[taken] + product(two_parts(upper[taken]), parts)
     result = times_inverse_root(mixed, square, scale, columns)
     if last:
         stored(moved, result)
@@ -199,7 +202,7 @@
 
 def gram_kernel(gram_left, norm_upper, weight, own_ref, payload):
     width = gram_left.shape[0]
-    own = own_ref[...]
+    own = halves_swapped(own_ref[...])
     high, low = two_parts(own)
     right = jnp.concatenate([high, low, high], axis=0)
     payload[:width] = jnp.dot(gram_left[...], right, preferred_element_type=F32)
@@ -261,7 +264,7 @@
         )
         if last:
             break
-        moved = shifted(moved, "cols", 1)
+        moved = column_shift(moved, 1)
         gram_left, norm_upper, upper = in_vmem(
             functools.partial(upper_kernel, blocks),
             [((width, 6 * rows), jnp.bfloat16), ((1, half), F32), (whole, F32)],
@@ -272,7 +275,7 @@
         )
         blocks, held, arriving = later_blocks, (upper, moved), swapped(moved, 1, 1)
         (payload,) = in_vmem(gram_kernel, [((width + 8, half), F32)], gram_left, norm_upper, weight, moved)
-    moved = shifted(moved, "cols", 1 - STEPS)
+    moved = column_shift(moved, 1 - STEPS)
     out_shape = jax.ShapeDtypeStruct((rows, columns), F32)
     rotated = pl.pallas_call(
         functools.partial(last_upper_kernel, blocks),

time: 68.5 us -> 66.2 us (0.966)
  waiting for transfers between devices: 39 us -> 33.5 us
  starting transfers between devices: 14.4 us -> 17.5 us
    ppermute x14 -> x20, waiting for transfers between devices: 26 us -> 20.8 us  [swapped(): return lax.ppermute(value, 'pts', pairs)]
    ppermute x14 -> x20, starting transfers between devices: 12.1 us -> 15.6 us  [swapped(): return lax.ppermute(value, 'pts', pairs)]
  transfers between devices with their start and end apart: 17 -> 23, of which waited for: 14 -> 14; matrix products, arithmetic and copies ran while one was open for 0% -> 0% of each run, Pallas kernels for 9% -> 9%
where the time goes in v11:
time: 66.2 us; the launch traced here: 66 us
  waiting for transfers between devices  33.5 us (51%)
  starting transfers between devices  17.5 us (26%)
  Pallas kernels  14.5 us (22%)
    ppermute x20, waiting for transfers between devices, swapped(): return lax.ppermute(value, 'pts', pairs)  20.8 us
    ppermute x20, starting transfers between devices, swapped(): return lax.ppermute(value, 'pts', pairs)  15.6 us
    ppermute x3, waiting for transfers between devices, column_shift(): return lax.ppermute(value, ('pts', 'cols'), pairs)  12.7 us
    pallas_call x7, Pallas kernels, in_vmem(): pl.pallas_call(kernel, out_shape=[jax.ShapeDtypeStruct(shape, dtype) for...  10 us
    pallas_call x1, Pallas kernels, body(): pl.pallas_call(functools.partial(last_upper_kernel, blocks), out_shape=ou...  2.32 us
    ppermute x3, starting transfers between devices, column_shift(): return lax.ppermute(value, ('pts', 'cols'), pairs)  1.97 us
    pallas_call x1, Pallas kernels, body(): pl.pallas_call(start_kernel, out_shape=[jax.ShapeDtypeStruct((width + 8,...  1.45 us
  transfers between devices with their start and end apart: 23, of which 14 were waited for; matrix products, arithmetic and copies ran while one was open for 0% of the time, Pallas kernels for 9%

profile of v11, /device:TPU:0, one launch (start us, length us, event | category | flops | bytes accessed | tf_op | source)
XLA Modules:
  0.0 66.0 jit_solution(5406934795396737261)
XLA Ops:
  0.0 1.5 %shard_map.37 = (f32[264,128]{1,0:T(8,128)S(1)}, f32[264,128]{1,0:T(8,128)S(1)}) custom-call(f32[128,512]{1,0:T(8,128)} %refs_2_.1, f32[1,128]{1,0:T(1,128)} %bitcast.5), custom_call_target="tpu_custom_call" | custom-call | tf_op jit(solution)/shard_map/pallas_call | solution.py:234
  3.4 2.6 %collective-permute-start.2 = (f32[264,128]{1,0:T(8,128)S(1)}, f32[264,128]{1,0:T(8,128)S(1)}, u32[]{:S(2)}, u32[]{:S(2)}) collective-permute-start(f32[264,128]{1,0:T(8,128)S(1)} %add.26), channel_id=1, source_target_pairs={{0,12},{4,16},{8,4},{12,24},{16,28},{20,0},{24,20},{28,8},{1,13},{... | collective-permute-start | bytes 405512 | tf_op jit(solution)/shard_map/ppermute | solution.py:28
  6.0 2.7 %collective-permute-done.2 = f32[264,128]{1,0:T(8,128)S(1)} collective-permute-done((f32[264,128]{1,0:T(8,128)S(1)}, f32[264,128]{1,0:T(8,128)S(1)}, u32[]{:S(2)}, u32[]{:S(2)}) %collective-permute-start.2) | collective-permute-done | bytes 135200 | tf_op jit(solution)/shard_map/ppermute | solution.py:28
  9.0 1.7 %collective-permute-start.5 = (f32[264,128]{1,0:T(8,128)S(1)}, f32[264,128]{1,0:T(8,128)S(1)}, u32[]{:S(2)}, u32[]{:S(2)}) collective-permute-start(f32[264,128]{1,0:T(8,128)S(1)} %add.27), channel_id=1, source_target_pairs={{0,12},{4,16},{8,4},{12,24},{16,28},{20,0},{24,20},{28,8},{1,13},{... | collective-permute-start | bytes 405512 | tf_op jit(solution)/shard_map/ppermute | solution.py:28
  10.7 2.7 %collective-permute-done.5 = f32[264,128]{1,0:T(8,128)S(1)} collective-permute-done((f32[264,128]{1,0:T(8,128)S(1)}, f32[264,128]{1,0:T(8,128)S(1)}, u32[]{:S(2)}, u32[]{:S(2)}) %collective-permute-start.5) | collective-permute-done | bytes 135200 | tf_op jit(solution)/shard_map/ppermute | solution.py:28
  14.9 2.0 %shard_map.38 = (f32[256,128]{1,0:T(8,128)S(1)}, f32[256,256]{1,0:T(8,128)S(1)}, f32[8,128]{1,0:T(8,128)S(1)}) custom-call(f32[3,128]{1,0:T(4,128)S(1)} %broadcast_in_dim.16.damps, f32[264,128]{1,0:T(8,128)S(1)} %add.28.own_sum, f32[264,128]{1,0:T(8,128)S(1)} %collective-permute-done.7.other_sum, f32[128,512]{1,0:T(8,128)S(1)} %copy-done, ...), custom_call_target="tpu_custom_call" | custom-call | tf_op jit(solution)/shard_map/pallas_call | solution.py:220
  16.9 1.8 %collective-permute-start.8 = (f32[256,128]{1,0:T(8,128)S(1)}, f32[256,128]{1,0:T(8,128)S(1)}, u32[]{:S(2)}, u32[]{:S(2)}) collective-permute-start(f32[256,128]{1,0:T(8,128)S(1)} %get-tuple-element.50), channel_id=1, source_target_pairs={{0,5},{1,6},{2,7},{3,4},{4,1},{5,2},{6,3},{7,0},{8,13},{9,14},{10,... | collective-permute-start | bytes 393224 | tf_op jit(solution)/shard_map/ppermute | solution.py:22
  20.1 1.9 %shard_map.39 = (bf16[256,768]{1,0:T(8,128)(2,1)S(1)}, f32[1,128]{1,0:T(1,128)S(1)}, f32[256,256]{1,0:T(8,128)S(1)}) custom-call(f32[256,1]{1,0:T(8,128)S(1)} %copy.7.weight, f32[256,256]{1,0:T(8,128)S(1)} %get-tuple-element.46.refs_0_, f32[8,128]{1,0:T(8,128)S(1)} %get-tuple-element.47.refs_1_, f32[128,512]{1,0:T(8,128)S(1)} %copy-done, ...), custom_call_target="tpu_custom_call" | custom-call | tf_op jit(solution)/shard_map/pallas_call | solution.py:220
  21.9 2.4 %collective-permute-done.8.own_ref.refs_1_.refs_3_ = f32[256,128]{1,0:T(8,128)S(1)} collective-permute-done((f32[256,128]{1,0:T(8,128)S(1)}, f32[256,128]{1,0:T(8,128)S(1)}, u32[]{:S(2)}, u32[]{:S(2)}) %collective-permute-start.8) | collective-permute-done | bytes 131104 | tf_op jit(solution)/shard_map/ppermute | solution.py:22
  24.9 1.7 %collective-permute-start.9 = (f32[264,128]{1,0:T(8,128)S(1)}, f32[264,128]{1,0:T(8,128)S(1)}, u32[]{:S(2)}, u32[]{:S(2)}) collective-permute-start(f32[264,128]{1,0:T(8,128)S(1)} %shard_map.40), channel_id=1, source_target_pairs={{0,12},{4,16},{8,4},{12,24},{16,28},{20,0},{24,20},{28,8},{1,13},{... | collective-permute-start | bytes 405512 | tf_op jit(solution)/shard_map/ppermute | solution.py:28
  26.8 2.6 %collective-permute-done.9 = f32[264,128]{1,0:T(8,128)S(1)} collective-permute-done((f32[264,128]{1,0:T(8,128)S(1)}, f32[264,128]{1,0:T(8,128)S(1)}, u32[]{:S(2)}, u32[]{:S(2)}) %collective-permute-start.9) | collective-permute-done | bytes 135200 | tf_op jit(solution)/shard_map/ppermute | solution.py:28
  29.7 1.6 %collective-permute-start.12 = (f32[264,128]{1,0:T(8,128)S(1)}, f32[264,128]{1,0:T(8,128)S(1)}, u32[]{:S(2)}, u32[]{:S(2)}) collective-permute-start(f32[264,128]{1,0:T(8,128)S(1)} %add.29), channel_id=1, source_target_pairs={{0,12},{4,16},{8,4},{12,24},{16,28},{20,0},{24,20},{28,8},{1,13},{... | collective-permute-start | bytes 405512 | tf_op jit(solution)/shard_map/ppermute | solution.py:28
  31.3 2.8 %collective-permute-done.12 = f32[264,128]{1,0:T(8,128)S(1)} collective-permute-done((f32[264,128]{1,0:T(8,128)S(1)}, f32[264,128]{1,0:T(8,128)S(1)}, u32[]{:S(2)}, u32[]{:S(2)}) %collective-permute-start.12) | collective-permute-done | bytes 135200 | tf_op jit(solution)/shard_map/ppermute | solution.py:28
  34.5 1.0 %collective-permute-done.14.other_sum = f32[264,128]{1,0:T(8,128)S(1)} collective-permute-done((f32[264,128]{1,0:T(8,128)S(1)}, f32[264,128]{1,0:T(8,128)S(1)}, u32[]{:S(2)}, u32[]{:S(2)}) %collective-permute-start.14) | collective-permute-done | bytes 135200 | tf_op jit(solution)/shard_map/ppermute | solution.py:28
  35.5 2.0 %shard_map.41 = (f32[256,128]{1,0:T(8,128)S(1)}, f32[256,256]{1,0:T(8,128)S(1)}, f32[8,128]{1,0:T(8,128)S(1)}) custom-call(f32[3,128]{1,0:T(4,128)S(1)} %broadcast_in_dim.16.damps, f32[264,128]{1,0:T(8,128)S(1)} %add.30.own_sum, f32[264,128]{1,0:T(8,128)S(1)} %collective-permute-done.14.other_sum, f32[256,256]{1,0:T(8,128)S(1)} %get-tuple-element.54.refs_0_.refs_2_, ...), custom_call_target="tpu_custom_call" | custom-call | tf_op jit(solution)/shard_map/pallas_call | solution.py:220
  37.6 1.9 %shard_map.42 = (bf16[256,768]{1,0:T(8,128)(2,1)S(1)}, f32[1,128]{1,0:T(1,128)S(1)}, f32[256,256]{1,0:T(8,128)S(1)}) custom-call(f32[256,1]{1,0:T(8,128)S(1)} %copy.7.weight, f32[256,256]{1,0:T(8,128)S(1)} %get-tuple-element.56.refs_0_, f32[8,128]{1,0:T(8,128)S(1)} %get-tuple-element.57.refs_1_, f32[256,256]{1,0:T(8,128)S(1)} %get-tuple-element.54.refs_0_.refs_2_, ...), custom_call_target="tpu_custom_call" | custom-call | tf_op jit(solution)/shard_map/pallas_call | solution.py:220
  39.4 5.3 %collective-permute-done.15.own_ref.refs_1_.refs_3_ = f32[256,128]{1,0:T(8,128)S(1)} collective-permute-done((f32[256,128]{1,0:T(8,128)S(1)}, f32[256,128]{1,0:T(8,128)S(1)}, u32[]{:S(2)}, u32[]{:S(2)}) %collective-permute-start.15) | collective-permute-done | bytes 131104 | tf_op jit(solution)/shard_map/ppermute | solution.py:22
  45.3 1.9 %collective-permute-start.16 = (f32[264,128]{1,0:T(8,128)S(1)}, f32[264,128]{1,0:T(8,128)S(1)}, u32[]{:S(2)}, u32[]{:S(2)}) collective-permute-start(f32[264,128]{1,0:T(8,128)S(1)} %shard_map.43), channel_id=1, source_target_pairs={{0,12},{4,16},{8,4},{12,24},{16,28},{20,0},{24,20},{28,8},{1,13},{... | collective-permute-start | bytes 405512 | tf_op jit(solution)/shard_map/ppermute | solution.py:28
  47.4 2.5 %collective-permute-done.16 = f32[264,128]{1,0:T(8,128)S(1)} collective-permute-done((f32[264,128]{1,0:T(8,128)S(1)}, f32[264,128]{1,0:T(8,128)S(1)}, u32[]{:S(2)}, u32[]{:S(2)}) %collective-permute-start.16) | collective-permute-done | bytes 135200 | tf_op jit(solution)/shard_map/ppermute | solution.py:28
  50.1 1.7 %collective-permute-start.19 = (f32[264,128]{1,0:T(8,128)S(1)}, f32[264,128]{1,0:T(8,128)S(1)}, u32[]{:S(2)}, u32[]{:S(2)}) collective-permute-start(f32[264,128]{1,0:T(8,128)S(1)} %add.31), channel_id=1, source_target_pairs={{0,12},{4,16},{8,4},{12,24},{16,28},{20,0},{24,20},{28,8},{1,13},{... | collective-permute-start | bytes 405512 | tf_op jit(solution)/shard_map/ppermute | solution.py:28
  51.9 2.7 %collective-permute-done.19 = f32[264,128]{1,0:T(8,128)S(1)} collective-permute-done((f32[264,128]{1,0:T(8,128)S(1)}, f32[264,128]{1,0:T(8,128)S(1)}, u32[]{:S(2)}, u32[]{:S(2)}) %collective-permute-start.19) | collective-permute-done | bytes 135200 | tf_op jit(solution)/shard_map/ppermute | solution.py:28
  56.0 1.9 %shard_map.44 = (f32[128,256]{1,0:T(8,128)S(1)}, f32[256,256]{1,0:T(8,128)S(1)}, f32[8,128]{1,0:T(8,128)S(1)}) custom-call(f32[3,128]{1,0:T(4,128)S(1)} %broadcast_in_dim.16.damps, f32[264,128]{1,0:T(8,128)S(1)} %add.32.own_sum, f32[264,128]{1,0:T(8,128)S(1)} %collective-permute-done.21.other_sum, f32[256,256]{1,0:T(8,128)S(1)} %get-tuple-element.64.refs_0_.refs_2_, ...), custom_call_target="tpu_custom_call" | custom-call | tf_op jit(solution)/shard_map/pallas_call | solution.py:220
  58.0 2.3 %shard_map.45.filled = f32[128,512]{1,0:T(8,128)} custom-call(f32[256,256]{1,0:T(8,128)S(1)} %get-tuple-element.67.refs_0_, f32[8,128]{1,0:T(8,128)S(1)} %get-tuple-element.68.refs_1_, f32[256,256]{1,0:T(8,128)S(1)} %get-tuple-element.64.refs_0_.refs_2_, f32[256,128]{1,0:T(8,128)S(1)} %collective-permute-done.15.own_ref.refs_1_.refs_3_, ...), custom_call_target="tpu_custom_call" | custom-call | tf_op jit(solution)/shard_map/pallas_call | solution.py:280
  60.3 5.0 %collective-permute-done.22.lower = f32[128,256]{1,0:T(8,128)S(1)} collective-permute-done((f32[128,256]{1,0:T(8,128)S(1)}, f32[128,256]{1,0:T(8,128)S(1)}, u32[]{:S(2)}, u32[]{:S(2)}) %collective-permute-start.22) | collective-permute-done | bytes 131104 | tf_op jit(solution)/shard_map/ppermute | solution.py:22
  (49 shorter events, 9.6 us)
Async XLA Ops:
  1.5 1.5 %collective-permute-start.1 = (f32[264,128]{1,0:T(8,128)S(1)}, f32[264,128]{1,0:T(8,128)S(1)}, u32[]{:S(2)}, u32[]{:S(2)}) collective-permute-start(f32[264,128]{1,0:T(8,128)S(1)} %get-tuple-element.41), channel_id=1, source_target_pairs={{0,4},{4,0},{8,12},{12,8},{16,20},{20,16},{24,28},{28,24},{1,5},{5... | collective-permute-start | bytes 405512 | tf_op jit(solution)/shard_map/ppermute | solution.py:28
  2.0 6.8 %collective-permute-start.4 = (f32[128,512]{1,0:T(8,128)S(1)}, f32[128,512]{1,0:T(8,128)S(1)}, u32[]{:S(2)}, u32[]{:S(2)}) collective-permute-start(f32[128,512]{1,0:T(8,128)S(1)} %copy-done), channel_id=1, source_target_pairs={{0,4},{4,0},{8,12},{12,8},{16,20},{20,16},{24,28},{28,24},{1,5},{5... | collective-permute-start | bytes 786440 | tf_op jit(solution)/shard_map/ppermute | solution.py:28
  3.0 3.0 %collective-permute-start.3 = (f32[264,128]{1,0:T(8,128)S(1)}, f32[264,128]{1,0:T(8,128)S(1)}, u32[]{:S(2)}, u32[]{:S(2)}) collective-permute-start(f32[264,128]{1,0:T(8,128)S(1)} %add.26), channel_id=1, source_target_pairs={{0,4},{4,0},{8,12},{12,8},{16,20},{20,16},{24,28},{28,24},{1,5},{5... | collective-permute-start | bytes 405512 | tf_op jit(solution)/shard_map/ppermute | solution.py:28
  3.4 5.3 %collective-permute-start.2 = (f32[264,128]{1,0:T(8,128)S(1)}, f32[264,128]{1,0:T(8,128)S(1)}, u32[]{:S(2)}, u32[]{:S(2)}) collective-permute-start(f32[264,128]{1,0:T(8,128)S(1)} %add.26), channel_id=1, source_target_pairs={{0,12},{4,16},{8,4},{12,24},{16,28},{20,0},{24,20},{28,8},{1,13},{... | collective-permute-start | bytes 405512 | tf_op jit(solution)/shard_map/ppermute | solution.py:28
  8.8 5.1 %copy-start.2 = (s32[3,2]{0,1:T(2,128)S(1)}, s32[3,2]{0,1:T(2,128)}, u32[]{:S(2)}) copy-start(s32[3,2]{0,1:T(2,128)} %param.5) | copy-start | bytes 76
  8.8 1.9 %collective-permute-start.6 = (f32[264,128]{1,0:T(8,128)S(1)}, f32[264,128]{1,0:T(8,128)S(1)}, u32[]{:S(2)}, u32[]{:S(2)}) collective-permute-start(f32[264,128]{1,0:T(8,128)S(1)} %add.27), channel_id=1, source_target_pairs={{0,4},{4,0},{8,12},{12,8},{16,20},{20,16},{24,28},{28,24},{1,5},{5... | collective-permute-start | bytes 405512 | tf_op jit(solution)/shard_map/ppermute | solution.py:28
  9.0 4.5 %collective-permute-start.5 = (f32[264,128]{1,0:T(8,128)S(1)}, f32[264,128]{1,0:T(8,128)S(1)}, u32[]{:S(2)}, u32[]{:S(2)}) collective-permute-start(f32[264,128]{1,0:T(8,128)S(1)} %add.27), channel_id=1, source_target_pairs={{0,12},{4,16},{8,4},{12,24},{16,28},{20,0},{24,20},{28,8},{1,13},{... | collective-permute-start | bytes 405512 | tf_op jit(solution)/shard_map/ppermute | solution.py:28
  13.5 1.4 %collective-permute-start.7 = (f32[264,128]{1,0:T(8,128)S(1)}, f32[264,128]{1,0:T(8,128)S(1)}, u32[]{:S(2)}, u32[]{:S(2)}) collective-permute-start(f32[264,128]{1,0:T(8,128)S(1)} %add.28.own_sum), channel_id=1, source_target_pairs={{0,4},{4,0},{8,12},{12,8},{16,20},{20,16},{24,28},{28,24},{1,5},{5... | collective-permute-start | bytes 405512 | tf_op jit(solution)/shard_map/ppermute | solution.py:28
  16.9 7.4 %collective-permute-start.8 = (f32[256,128]{1,0:T(8,128)S(1)}, f32[256,128]{1,0:T(8,128)S(1)}, u32[]{:S(2)}, u32[]{:S(2)}) collective-permute-start(f32[256,128]{1,0:T(8,128)S(1)} %get-tuple-element.50), channel_id=1, source_target_pairs={{0,5},{1,6},{2,7},{3,4},{4,1},{5,2},{6,3},{7,0},{8,13},{9,14},{10,... | collective-permute-start | bytes 393224 | tf_op jit(solution)/shard_map/ppermute | solution.py:22
  18.7 1.2 %collective-permute-start = (f32[128]{0:T(128)S(1)}, f32[128]{0:T(128)S(1)}, u32[]{:S(2)}, u32[]{:S(2)}) collective-permute-start(f32[128]{0:T(128)S(1)} %copy-done.1), channel_id=1, source_target_pairs={{0,4},{4,0},{8,12},{12,8},{16,20},{20,16},{24,28},{28,24},{1,5},{5... | collective-permute-start | bytes 1544 | tf_op jit(solution)/shard_map/ppermute | solution.py:28
  24.6 2.2 %collective-permute-start.10 = (f32[264,128]{1,0:T(8,128)S(1)}, f32[264,128]{1,0:T(8,128)S(1)}, u32[]{:S(2)}, u32[]{:S(2)}) collective-permute-start(f32[264,128]{1,0:T(8,128)S(1)} %shard_map.40), channel_id=1, source_target_pairs={{0,4},{4,0},{8,12},{12,8},{16,20},{20,16},{24,28},{28,24},{1,5},{5... | collective-permute-start | bytes 405512 | tf_op jit(solution)/shard_map/ppermute | solution.py:28
  24.9 4.4 %collective-permute-start.9 = (f32[264,128]{1,0:T(8,128)S(1)}, f32[264,128]{1,0:T(8,128)S(1)}, u32[]{:S(2)}, u32[]{:S(2)}) collective-permute-start(f32[264,128]{1,0:T(8,128)S(1)} %shard_map.40), channel_id=1, source_target_pairs={{0,12},{4,16},{8,4},{12,24},{16,28},{20,0},{24,20},{28,8},{1,13},{... | collective-permute-start | bytes 405512 | tf_op jit(solution)/shard_map/ppermute | solution.py:28
  26.6 2.8 %collective-permute-start.11 = (f32[256,128]{1,0:T(8,128)S(1)}, f32[256,128]{1,0:T(8,128)S(1)}, u32[]{:S(2)}, u32[]{:S(2)}) collective-permute-start(f32[256,128]{1,0:T(8,128)S(1)} %collective-permute-done.8.own_ref.refs_1_.refs_3_), channel_id=1, source_target_pairs={{0,4},{4,0},{8,12},{12,8},{16,20},{20,16},{24,28},{28,24},{1,5},{5... | collective-permute-start | bytes 393224 | tf_op jit(solution)/shard_map/ppermute | solution.py:28
  29.4 1.9 %collective-permute-start.13 = (f32[264,128]{1,0:T(8,128)S(1)}, f32[264,128]{1,0:T(8,128)S(1)}, u32[]{:S(2)}, u32[]{:S(2)}) collective-permute-start(f32[264,128]{1,0:T(8,128)S(1)} %add.29), channel_id=1, source_target_pairs={{0,4},{4,0},{8,12},{12,8},{16,20},{20,16},{24,28},{28,24},{1,5},{5... | collective-permute-start | bytes 405512 | tf_op jit(solution)/shard_map/ppermute | solution.py:28
  29.7 4.4 %collective-permute-start.12 = (f32[264,128]{1,0:T(8,128)S(1)}, f32[264,128]{1,0:T(8,128)S(1)}, u32[]{:S(2)}, u32[]{:S(2)}) collective-permute-start(f32[264,128]{1,0:T(8,128)S(1)} %add.29), channel_id=1, source_target_pairs={{0,12},{4,16},{8,4},{12,24},{16,28},{20,0},{24,20},{28,8},{1,13},{... | collective-permute-start | bytes 405512 | tf_op jit(solution)/shard_map/ppermute | solution.py:28
  34.1 1.4 %collective-permute-start.14 = (f32[264,128]{1,0:T(8,128)S(1)}, f32[264,128]{1,0:T(8,128)S(1)}, u32[]{:S(2)}, u32[]{:S(2)}) collective-permute-start(f32[264,128]{1,0:T(8,128)S(1)} %add.30.own_sum), channel_id=1, source_target_pairs={{0,4},{4,0},{8,12},{12,8},{16,20},{20,16},{24,28},{28,24},{1,5},{5... | collective-permute-start | bytes 405512 | tf_op jit(solution)/shard_map/ppermute | solution.py:28
  37.5 7.2 %collective-permute-start.15 = (f32[256,128]{1,0:T(8,128)S(1)}, f32[256,128]{1,0:T(8,128)S(1)}, u32[]{:S(2)}, u32[]{:S(2)}) collective-permute-start(f32[256,128]{1,0:T(8,128)S(1)} %get-tuple-element.60), channel_id=1, source_target_pairs={{0,5},{1,6},{2,7},{3,4},{4,1},{5,2},{6,3},{7,0},{8,13},{9,14},{10,... | collective-permute-start | bytes 393224 | tf_op jit(solution)/shard_map/ppermute | solution.py:22
  45.0 2.4 %collective-permute-start.17 = (f32[264,128]{1,0:T(8,128)S(1)}, f32[264,128]{1,0:T(8,128)S(1)}, u32[]{:S(2)}, u32[]{:S(2)}) collective-permute-start(f32[264,128]{1,0:T(8,128)S(1)} %shard_map.43), channel_id=1, source_target_pairs={{0,4},{4,0},{8,12},{12,8},{16,20},{20,16},{24,28},{28,24},{1,5},{5... | collective-permute-start | bytes 405512 | tf_op jit(solution)/shard_map/ppermute | solution.py:28
  45.3 4.6 %collective-permute-start.16 = (f32[264,128]{1,0:T(8,128)S(1)}, f32[264,128]{1,0:T(8,128)S(1)}, u32[]{:S(2)}, u32[]{:S(2)}) collective-permute-start(f32[264,128]{1,0:T(8,128)S(1)} %shard_map.43), channel_id=1, source_target_pairs={{0,12},{4,16},{8,4},{12,24},{16,28},{20,0},{24,20},{28,8},{1,13},{... | collective-permute-start | bytes 405512 | tf_op jit(solution)/shard_map/ppermute | solution.py:28
  47.2 2.7 %collective-permute-start.18 = (f32[256,128]{1,0:T(8,128)S(1)}, f32[256,128]{1,0:T(8,128)S(1)}, u32[]{:S(2)}, u32[]{:S(2)}) collective-permute-start(f32[256,128]{1,0:T(8,128)S(1)} %collective-permute-done.15.own_ref.refs_1_.refs_3_), channel_id=1, source_target_pairs={{0,4},{4,0},{8,12},{12,8},{16,20},{20,16},{24,28},{28,24},{1,5},{5... | collective-permute-start | bytes 393224 | tf_op jit(solution)/shard_map/ppermute | solution.py:28
  49.9 1.9 %collective-permute-start.20 = (f32[264,128]{1,0:T(8,128)S(1)}, f32[264,128]{1,0:T(8,128)S(1)}, u32[]{:S(2)}, u32[]{:S(2)}) collective-permute-start(f32[264,128]{1,0:T(8,128)S(1)} %add.31), channel_id=1, source_target_pairs={{0,4},{4,0},{8,12},{12,8},{16,20},{20,16},{24,28},{28,24},{1,5},{5... | collective-permute-start | bytes 405512 | tf_op jit(solution)/shard_map/ppermute | solution.py:28
  50.1 4.5 %collective-permute-start.19 = (f32[264,128]{1,0:T(8,128)S(1)}, f32[264,128]{1,0:T(8,128)S(1)}, u32[]{:S(2)}, u32[]{:S(2)}) collective-permute-start(f32[264,128]{1,0:T(8,128)S(1)} %add.31), channel_id=1, source_target_pairs={{0,12},{4,16},{8,4},{12,24},{16,28},{20,0},{24,20},{28,8},{1,13},{... | collective-permute-start | bytes 405512 | tf_op jit(solution)/shard_map/ppermute | solution.py:28
  54.6 1.4 %collective-permute-start.21 = (f32[264,128]{1,0:T(8,128)S(1)}, f32[264,128]{1,0:T(8,128)S(1)}, u32[]{:S(2)}, u32[]{:S(2)}) collective-permute-start(f32[264,128]{1,0:T(8,128)S(1)} %add.32.own_sum), channel_id=1, source_target_pairs={{0,4},{4,0},{8,12},{12,8},{16,20},{20,16},{24,28},{28,24},{1,5},{5... | collective-permute-start | bytes 405512 | tf_op jit(solution)/shard_map/ppermute | solution.py:28
  57.9 7.4 %collective-permute-start.22 = (f32[128,256]{1,0:T(8,128)S(1)}, f32[128,256]{1,0:T(8,128)S(1)}, u32[]{:S(2)}, u32[]{:S(2)}) collective-permute-start(f32[128,256]{1,0:T(8,128)S(1)} %get-tuple-element.66), channel_id=1, source_target_pairs={{0,6},{1,7},{2,4},{3,5},{4,2},{5,3},{6,0},{7,1},{8,14},{9,15},{10,... | collective-permute-start | bytes 393224 | tf_op jit(solution)/shard_map/ppermute | solution.py:22
  (2 other events, 3.8 us)

commit v12 on v11

--- a/solution.py
+++ b/solution.py
@@ -34,7 +34,8 @@
     while bit < count:
         if 2 * bit < count:
             for _ in range(2):
-                value = swapped(value, bit ^ 1, 2 * bit ^ 1) + swapped(value, 1, 1)
+                near = swapped(value, 1, 1)
+                value = near + swapped(value, bit ^ 1, 2 * bit ^ 1)
                 value, beside = lax.optimization_barrier((value, beside))
         else:
             value = value + swapped(value, bit, bit)

time: 66.2 us -> 64.6 us (0.976)
  waiting for transfers between devices: 33.5 us -> 31.6 us
    ppermute x20, waiting for transfers between devices: 20.8 us -> 18.9 us  [swapped(): return lax.ppermute(value, 'pts', pairs)]
where the time goes in v12:
time: 64.6 us; the launch traced here: 64.4 us
  waiting for transfers between devices  31.6 us (49%)
  starting transfers between devices  17.8 us (28%)
  Pallas kernels  14.5 us (22%)
    ppermute x20, waiting for transfers between devices, swapped(): return lax.ppermute(value, 'pts', pairs)  18.9 us
    ppermute x20, starting transfers between devices, swapped(): return lax.ppermute(value, 'pts', pairs)  15.8 us
    ppermute x3, waiting for transfers between devices, column_shift(): return lax.ppermute(value, ('pts', 'cols'), pairs)  12.8 us
    pallas_call x7, Pallas kernels, in_vmem(): pl.pallas_call(kernel, out_shape=[jax.ShapeDtypeStruct(shape, dtype) for...  10.1 us
    pallas_call x1, Pallas kernels, body(): pl.pallas_call(functools.partial(last_upper_kernel, blocks), out_shape=ou...  2.32 us
    ppermute x3, starting transfers between devices, column_shift(): return lax.ppermute(value, ('pts', 'cols'), pairs)  1.97 us
    pallas_call x1, Pallas kernels, body(): pl.pallas_call(start_kernel, out_shape=[jax.ShapeDtypeStruct((width + 8,...  1.45 us
  transfers between devices with their start and end apart: 23, of which 14 were waited for; matrix products, arithmetic and copies ran while one was open for 0% of the time, Pallas kernels for 9%

profile of v12, /device:TPU:0, one launch (start us, length us, event | category | flops | bytes accessed | tf_op | source)
XLA Modules:
  0.0 64.4 jit_solution(6528348542976508840)
XLA Ops:
  0.0 1.5 %shard_map.37 = (f32[264,128]{1,0:T(8,128)S(1)}, f32[264,128]{1,0:T(8,128)S(1)}) custom-call(f32[128,512]{1,0:T(8,128)} %refs_2_.1, f32[1,128]{1,0:T(1,128)} %bitcast.5), custom_call_target="tpu_custom_call" | custom-call | tf_op jit(solution)/shard_map/pallas_call | solution.py:235
  3.0 2.7 %collective-permute-start.3 = (f32[264,128]{1,0:T(8,128)S(1)}, f32[264,128]{1,0:T(8,128)S(1)}, u32[]{:S(2)}, u32[]{:S(2)}) collective-permute-start(f32[264,128]{1,0:T(8,128)S(1)} %add.26), channel_id=1, source_target_pairs={{0,12},{4,16},{8,4},{12,24},{16,28},{20,0},{24,20},{28,8},{1,13},{... | collective-permute-start | bytes 405512 | tf_op jit(solution)/shard_map/ppermute | solution.py:28
  6.0 2.3 %collective-permute-done.3 = f32[264,128]{1,0:T(8,128)S(1)} collective-permute-done((f32[264,128]{1,0:T(8,128)S(1)}, f32[264,128]{1,0:T(8,128)S(1)}, u32[]{:S(2)}, u32[]{:S(2)}) %collective-permute-start.3) | collective-permute-done | bytes 135200 | tf_op jit(solution)/shard_map/ppermute | solution.py:28
  8.4 1.8 %collective-permute-start.6 = (f32[264,128]{1,0:T(8,128)S(1)}, f32[264,128]{1,0:T(8,128)S(1)}, u32[]{:S(2)}, u32[]{:S(2)}) collective-permute-start(f32[264,128]{1,0:T(8,128)S(1)} %add.27), channel_id=1, source_target_pairs={{0,12},{4,16},{8,4},{12,24},{16,28},{20,0},{24,20},{28,8},{1,13},{... | collective-permute-start | bytes 405512 | tf_op jit(solution)/shard_map/ppermute | solution.py:28
  10.6 2.3 %collective-permute-done.6 = f32[264,128]{1,0:T(8,128)S(1)} collective-permute-done((f32[264,128]{1,0:T(8,128)S(1)}, f32[264,128]{1,0:T(8,128)S(1)}, u32[]{:S(2)}, u32[]{:S(2)}) %collective-permute-start.6) | collective-permute-done | bytes 135200 | tf_op jit(solution)/shard_map/ppermute | solution.py:28
  14.3 2.0 %shard_map.38 = (f32[256,128]{1,0:T(8,128)S(1)}, f32[256,256]{1,0:T(8,128)S(1)}, f32[8,128]{1,0:T(8,128)S(1)}) custom-call(f32[3,128]{1,0:T(4,128)S(1)} %broadcast_in_dim.16.damps, f32[264,128]{1,0:T(8,128)S(1)} %add.28.own_sum, f32[264,128]{1,0:T(8,128)S(1)} %collective-permute-done.7.other_sum, f32[128,512]{1,0:T(8,128)S(1)} %copy-done, ...), custom_call_target="tpu_custom_call" | custom-call | tf_op jit(solution)/shard_map/pallas_call | solution.py:221
  16.3 1.8 %collective-permute-start.8 = (f32[256,128]{1,0:T(8,128)S(1)}, f32[256,128]{1,0:T(8,128)S(1)}, u32[]{:S(2)}, u32[]{:S(2)}) collective-permute-start(f32[256,128]{1,0:T(8,128)S(1)} %get-tuple-element.50), channel_id=1, source_target_pairs={{0,5},{1,6},{2,7},{3,4},{4,1},{5,2},{6,3},{7,0},{8,13},{9,14},{10,... | collective-permute-start | bytes 393224 | tf_op jit(solution)/shard_map/ppermute | solution.py:22
  19.5 1.9 %shard_map.39 = (bf16[256,768]{1,0:T(8,128)(2,1)S(1)}, f32[1,128]{1,0:T(1,128)S(1)}, f32[256,256]{1,0:T(8,128)S(1)}) custom-call(f32[256,1]{1,0:T(8,128)S(1)} %copy.7.weight, f32[256,256]{1,0:T(8,128)S(1)} %get-tuple-element.46.refs_0_, f32[8,128]{1,0:T(8,128)S(1)} %get-tuple-element.47.refs_1_, f32[128,512]{1,0:T(8,128)S(1)} %copy-done, ...), custom_call_target="tpu_custom_call" | custom-call | tf_op jit(solution)/shard_map/pallas_call | solution.py:221
  21.4 2.4 %collective-permute-done.8.own_ref.refs_1_.refs_3_ = f32[256,128]{1,0:T(8,128)S(1)} collective-permute-done((f32[256,128]{1,0:T(8,128)S(1)}, f32[256,128]{1,0:T(8,128)S(1)}, u32[]{:S(2)}, u32[]{:S(2)}) %collective-permute-start.8) | collective-permute-done | bytes 131104 | tf_op jit(solution)/shard_map/ppermute | solution.py:22
  24.1 1.6 %collective-permute-start.10 = (f32[264,128]{1,0:T(8,128)S(1)}, f32[264,128]{1,0:T(8,128)S(1)}, u32[]{:S(2)}, u32[]{:S(2)}) collective-permute-start(f32[264,128]{1,0:T(8,128)S(1)} %shard_map.40), channel_id=1, source_target_pairs={{0,12},{4,16},{8,4},{12,24},{16,28},{20,0},{24,20},{28,8},{1,13},{... | collective-permute-start | bytes 405512 | tf_op jit(solution)/shard_map/ppermute | solution.py:28
  26.2 2.3 %collective-permute-done.10 = f32[264,128]{1,0:T(8,128)S(1)} collective-permute-done((f32[264,128]{1,0:T(8,128)S(1)}, f32[264,128]{1,0:T(8,128)S(1)}, u32[]{:S(2)}, u32[]{:S(2)}) %collective-permute-start.10) | collective-permute-done | bytes 135200 | tf_op jit(solution)/shard_map/ppermute | solution.py:28
  28.6 1.6 %collective-permute-start.13 = (f32[264,128]{1,0:T(8,128)S(1)}, f32[264,128]{1,0:T(8,128)S(1)}, u32[]{:S(2)}, u32[]{:S(2)}) collective-permute-start(f32[264,128]{1,0:T(8,128)S(1)} %add.29), channel_id=1, source_target_pairs={{0,12},{4,16},{8,4},{12,24},{16,28},{20,0},{24,20},{28,8},{1,13},{... | collective-permute-start | bytes 405512 | tf_op jit(solution)/shard_map/ppermute | solution.py:28
  30.6 2.4 %collective-permute-done.13 = f32[264,128]{1,0:T(8,128)S(1)} collective-permute-done((f32[264,128]{1,0:T(8,128)S(1)}, f32[264,128]{1,0:T(8,128)S(1)}, u32[]{:S(2)}, u32[]{:S(2)}) %collective-permute-start.13) | collective-permute-done | bytes 135200 | tf_op jit(solution)/shard_map/ppermute | solution.py:28
  33.5 1.1 %collective-permute-done.14.other_sum = f32[264,128]{1,0:T(8,128)S(1)} collective-permute-done((f32[264,128]{1,0:T(8,128)S(1)}, f32[264,128]{1,0:T(8,128)S(1)}, u32[]{:S(2)}, u32[]{:S(2)}) %collective-permute-start.14) | collective-permute-done | bytes 135200 | tf_op jit(solution)/shard_map/ppermute | solution.py:28
  34.5 2.0 %shard_map.41 = (f32[256,128]{1,0:T(8,128)S(1)}, f32[256,256]{1,0:T(8,128)S(1)}, f32[8,128]{1,0:T(8,128)S(1)}) custom-call(f32[3,128]{1,0:T(4,128)S(1)} %broadcast_in_dim.16.damps, f32[264,128]{1,0:T(8,128)S(1)} %add.30.own_sum, f32[264,128]{1,0:T(8,128)S(1)} %collective-permute-done.14.other_sum, f32[256,256]{1,0:T(8,128)S(1)} %get-tuple-element.54.refs_0_.refs_2_, ...), custom_call_target="tpu_custom_call" | custom-call | tf_op jit(solution)/shard_map/pallas_call | solution.py:221
  36.6 1.9 %shard_map.42 = (bf16[256,768]{1,0:T(8,128)(2,1)S(1)}, f32[1,128]{1,0:T(1,128)S(1)}, f32[256,256]{1,0:T(8,128)S(1)}) custom-call(f32[256,1]{1,0:T(8,128)S(1)} %copy.7.weight, f32[256,256]{1,0:T(8,128)S(1)} %get-tuple-element.56.refs_0_, f32[8,128]{1,0:T(8,128)S(1)} %get-tuple-element.57.refs_1_, f32[256,256]{1,0:T(8,128)S(1)} %get-tuple-element.54.refs_0_.refs_2_, ...), custom_call_target="tpu_custom_call" | custom-call | tf_op jit(solution)/shard_map/pallas_call | solution.py:221
  38.4 5.3 %collective-permute-done.15.own_ref.refs_1_.refs_3_ = f32[256,128]{1,0:T(8,128)S(1)} collective-permute-done((f32[256,128]{1,0:T(8,128)S(1)}, f32[256,128]{1,0:T(8,128)S(1)}, u32[]{:S(2)}, u32[]{:S(2)}) %collective-permute-start.15) | collective-permute-done | bytes 131104 | tf_op jit(solution)/shard_map/ppermute | solution.py:22
  44.0 1.7 %collective-permute-start.17 = (f32[264,128]{1,0:T(8,128)S(1)}, f32[264,128]{1,0:T(8,128)S(1)}, u32[]{:S(2)}, u32[]{:S(2)}) collective-permute-start(f32[264,128]{1,0:T(8,128)S(1)} %shard_map.43), channel_id=1, source_target_pairs={{0,12},{4,16},{8,4},{12,24},{16,28},{20,0},{24,20},{28,8},{1,13},{... | collective-permute-start | bytes 405512 | tf_op jit(solution)/shard_map/ppermute | solution.py:28
  46.3 2.3 %collective-permute-done.17 = f32[264,128]{1,0:T(8,128)S(1)} collective-permute-done((f32[264,128]{1,0:T(8,128)S(1)}, f32[264,128]{1,0:T(8,128)S(1)}, u32[]{:S(2)}, u32[]{:S(2)}) %collective-permute-start.17) | collective-permute-done | bytes 135200 | tf_op jit(solution)/shard_map/ppermute | solution.py:28
  48.5 1.7 %collective-permute-start.20 = (f32[264,128]{1,0:T(8,128)S(1)}, f32[264,128]{1,0:T(8,128)S(1)}, u32[]{:S(2)}, u32[]{:S(2)}) collective-permute-start(f32[264,128]{1,0:T(8,128)S(1)} %add.31), channel_id=1, source_target_pairs={{0,12},{4,16},{8,4},{12,24},{16,28},{20,0},{24,20},{28,8},{1,13},{... | collective-permute-start | bytes 405512 | tf_op jit(solution)/shard_map/ppermute | solution.py:28
  50.7 2.4 %collective-permute-done.20 = f32[264,128]{1,0:T(8,128)S(1)} collective-permute-done((f32[264,128]{1,0:T(8,128)S(1)}, f32[264,128]{1,0:T(8,128)S(1)}, u32[]{:S(2)}, u32[]{:S(2)}) %collective-permute-start.20) | collective-permute-done | bytes 135200 | tf_op jit(solution)/shard_map/ppermute | solution.py:28
  54.5 1.9 %shard_map.44 = (f32[128,256]{1,0:T(8,128)S(1)}, f32[256,256]{1,0:T(8,128)S(1)}, f32[8,128]{1,0:T(8,128)S(1)}) custom-call(f32[3,128]{1,0:T(4,128)S(1)} %broadcast_in_dim.16.damps, f32[264,128]{1,0:T(8,128)S(1)} %add.32.own_sum, f32[264,128]{1,0:T(8,128)S(1)} %collective-permute-done.21.other_sum, f32[256,256]{1,0:T(8,128)S(1)} %get-tuple-element.64.refs_0_.refs_2_, ...), custom_call_target="tpu_custom_call" | custom-call | tf_op jit(solution)/shard_map/pallas_call | solution.py:221
  56.5 2.3 %shard_map.45.filled = f32[128,512]{1,0:T(8,128)} custom-call(f32[256,256]{1,0:T(8,128)S(1)} %get-tuple-element.67.refs_0_, f32[8,128]{1,0:T(8,128)S(1)} %get-tuple-element.68.refs_1_, f32[256,256]{1,0:T(8,128)S(1)} %get-tuple-element.64.refs_0_.refs_2_, f32[256,128]{1,0:T(8,128)S(1)} %collective-permute-done.15.own_ref.refs_1_.refs_3_, ...), custom_call_target="tpu_custom_call" | custom-call | tf_op jit(solution)/shard_map/pallas_call | solution.py:281
  58.8 5.0 %collective-permute-done.22.lower = f32[128,256]{1,0:T(8,128)S(1)} collective-permute-done((f32[128,256]{1,0:T(8,128)S(1)}, f32[128,256]{1,0:T(8,128)S(1)}, u32[]{:S(2)}, u32[]{:S(2)}) %collective-permute-start.22) | collective-permute-done | bytes 131104 | tf_op jit(solution)/shard_map/ppermute | solution.py:22
  (49 shorter events, 10.1 us)
Async XLA Ops:
  1.5 1.5 %collective-permute-start.1 = (f32[264,128]{1,0:T(8,128)S(1)}, f32[264,128]{1,0:T(8,128)S(1)}, u32[]{:S(2)}, u32[]{:S(2)}) collective-permute-start(f32[264,128]{1,0:T(8,128)S(1)} %get-tuple-element.41), channel_id=1, source_target_pairs={{0,4},{4,0},{8,12},{12,8},{16,20},{20,16},{24,28},{28,24},{1,5},{5... | collective-permute-start | bytes 405512 | tf_op jit(solution)/shard_map/ppermute | solution.py:28
  2.0 6.4 %collective-permute-start.4 = (f32[128,512]{1,0:T(8,128)S(1)}, f32[128,512]{1,0:T(8,128)S(1)}, u32[]{:S(2)}, u32[]{:S(2)}) collective-permute-start(f32[128,512]{1,0:T(8,128)S(1)} %copy-done), channel_id=1, source_target_pairs={{0,4},{4,0},{8,12},{12,8},{16,20},{20,16},{24,28},{28,24},{1,5},{5... | collective-permute-start | bytes 786440 | tf_op jit(solution)/shard_map/ppermute | solution.py:28
  3.0 5.4 %collective-permute-start.3 = (f32[264,128]{1,0:T(8,128)S(1)}, f32[264,128]{1,0:T(8,128)S(1)}, u32[]{:S(2)}, u32[]{:S(2)}) collective-permute-start(f32[264,128]{1,0:T(8,128)S(1)} %add.26), channel_id=1, source_target_pairs={{0,12},{4,16},{8,4},{12,24},{16,28},{20,0},{24,20},{28,8},{1,13},{... | collective-permute-start | bytes 405512 | tf_op jit(solution)/shard_map/ppermute | solution.py:28
  5.6 2.7 %collective-permute-start.2 = (f32[264,128]{1,0:T(8,128)S(1)}, f32[264,128]{1,0:T(8,128)S(1)}, u32[]{:S(2)}, u32[]{:S(2)}) collective-permute-start(f32[264,128]{1,0:T(8,128)S(1)} %add.26), channel_id=1, source_target_pairs={{0,4},{4,0},{8,12},{12,8},{16,20},{20,16},{24,28},{28,24},{1,5},{5... | collective-permute-start | bytes 405512 | tf_op jit(solution)/shard_map/ppermute | solution.py:28
  8.4 4.9 %copy-start.2 = (s32[3,2]{0,1:T(2,128)S(1)}, s32[3,2]{0,1:T(2,128)}, u32[]{:S(2)}) copy-start(s32[3,2]{0,1:T(2,128)} %param.5) | copy-start | bytes 76
  8.4 4.5 %collective-permute-start.6 = (f32[264,128]{1,0:T(8,128)S(1)}, f32[264,128]{1,0:T(8,128)S(1)}, u32[]{:S(2)}, u32[]{:S(2)}) collective-permute-start(f32[264,128]{1,0:T(8,128)S(1)} %add.27), channel_id=1, source_target_pairs={{0,12},{4,16},{8,4},{12,24},{16,28},{20,0},{24,20},{28,8},{1,13},{... | collective-permute-start | bytes 405512 | tf_op jit(solution)/shard_map/ppermute | solution.py:28
  10.2 2.7 %collective-permute-start.5 = (f32[264,128]{1,0:T(8,128)S(1)}, f32[264,128]{1,0:T(8,128)S(1)}, u32[]{:S(2)}, u32[]{:S(2)}) collective-permute-start(f32[264,128]{1,0:T(8,128)S(1)} %add.27), channel_id=1, source_target_pairs={{0,4},{4,0},{8,12},{12,8},{16,20},{20,16},{24,28},{28,24},{1,5},{5... | collective-permute-start | bytes 405512 | tf_op jit(solution)/shard_map/ppermute | solution.py:28
  12.9 1.4 %collective-permute-start.7 = (f32[264,128]{1,0:T(8,128)S(1)}, f32[264,128]{1,0:T(8,128)S(1)}, u32[]{:S(2)}, u32[]{:S(2)}) collective-permute-start(f32[264,128]{1,0:T(8,128)S(1)} %add.28.own_sum), channel_id=1, source_target_pairs={{0,4},{4,0},{8,12},{12,8},{16,20},{20,16},{24,28},{28,24},{1,5},{5... | collective-permute-start | bytes 405512 | tf_op jit(solution)/shard_map/ppermute | solution.py:28
  16.3 7.5 %collective-permute-start.8 = (f32[256,128]{1,0:T(8,128)S(1)}, f32[256,128]{1,0:T(8,128)S(1)}, u32[]{:S(2)}, u32[]{:S(2)}) collective-permute-start(f32[256,128]{1,0:T(8,128)S(1)} %get-tuple-element.50), channel_id=1, source_target_pairs={{0,5},{1,6},{2,7},{3,4},{4,1},{5,2},{6,3},{7,0},{8,13},{9,14},{10,... | collective-permute-start | bytes 393224 | tf_op jit(solution)/shard_map/ppermute | solution.py:22
  18.2 1.2 %collective-permute-start = (f32[128]{0:T(128)S(1)}, f32[128]{0:T(128)S(1)}, u32[]{:S(2)}, u32[]{:S(2)}) collective-permute-start(f32[128]{0:T(128)S(1)} %copy-done.1), channel_id=1, source_target_pairs={{0,4},{4,0},{8,12},{12,8},{16,20},{20,16},{24,28},{28,24},{1,5},{5... | collective-permute-start | bytes 1544 | tf_op jit(solution)/shard_map/ppermute | solution.py:28
  24.1 4.5 %collective-permute-start.10 = (f32[264,128]{1,0:T(8,128)S(1)}, f32[264,128]{1,0:T(8,128)S(1)}, u32[]{:S(2)}, u32[]{:S(2)}) collective-permute-start(f32[264,128]{1,0:T(8,128)S(1)} %shard_map.40), channel_id=1, source_target_pairs={{0,12},{4,16},{8,4},{12,24},{16,28},{20,0},{24,20},{28,8},{1,13},{... | collective-permute-start | bytes 405512 | tf_op jit(solution)/shard_map/ppermute | solution.py:28
  25.7 2.8 %collective-permute-start.9 = (f32[264,128]{1,0:T(8,128)S(1)}, f32[264,128]{1,0:T(8,128)S(1)}, u32[]{:S(2)}, u32[]{:S(2)}) collective-permute-start(f32[264,128]{1,0:T(8,128)S(1)} %shard_map.40), channel_id=1, source_target_pairs={{0,4},{4,0},{8,12},{12,8},{16,20},{20,16},{24,28},{28,24},{1,5},{5... | collective-permute-start | bytes 405512 | tf_op jit(solution)/shard_map/ppermute | solution.py:28
  26.1 2.5 %collective-permute-start.11 = (f32[256,128]{1,0:T(8,128)S(1)}, f32[256,128]{1,0:T(8,128)S(1)}, u32[]{:S(2)}, u32[]{:S(2)}) collective-permute-start(f32[256,128]{1,0:T(8,128)S(1)} %collective-permute-done.8.own_ref.refs_1_.refs_3_), channel_id=1, source_target_pairs={{0,4},{4,0},{8,12},{12,8},{16,20},{20,16},{24,28},{28,24},{1,5},{5... | collective-permute-start | bytes 393224 | tf_op jit(solution)/shard_map/ppermute | solution.py:28
  28.6 4.5 %collective-permute-start.13 = (f32[264,128]{1,0:T(8,128)S(1)}, f32[264,128]{1,0:T(8,128)S(1)}, u32[]{:S(2)}, u32[]{:S(2)}) collective-permute-start(f32[264,128]{1,0:T(8,128)S(1)} %add.29), channel_id=1, source_target_pairs={{0,12},{4,16},{8,4},{12,24},{16,28},{20,0},{24,20},{28,8},{1,13},{... | collective-permute-start | bytes 405512 | tf_op jit(solution)/shard_map/ppermute | solution.py:28
  30.2 2.8 %collective-permute-start.12 = (f32[264,128]{1,0:T(8,128)S(1)}, f32[264,128]{1,0:T(8,128)S(1)}, u32[]{:S(2)}, u32[]{:S(2)}) collective-permute-start(f32[264,128]{1,0:T(8,128)S(1)} %add.29), channel_id=1, source_target_pairs={{0,4},{4,0},{8,12},{12,8},{16,20},{20,16},{24,28},{28,24},{1,5},{5... | collective-permute-start | bytes 405512 | tf_op jit(solution)/shard_map/ppermute | solution.py:28
  33.1 1.4 %collective-permute-start.14 = (f32[264,128]{1,0:T(8,128)S(1)}, f32[264,128]{1,0:T(8,128)S(1)}, u32[]{:S(2)}, u32[]{:S(2)}) collective-permute-start(f32[264,128]{1,0:T(8,128)S(1)} %add.30.own_sum), channel_id=1, source_target_pairs={{0,4},{4,0},{8,12},{12,8},{16,20},{20,16},{24,28},{28,24},{1,5},{5... | collective-permute-start | bytes 405512 | tf_op jit(solution)/shard_map/ppermute | solution.py:28
  36.5 7.3 %collective-permute-start.15 = (f32[256,128]{1,0:T(8,128)S(1)}, f32[256,128]{1,0:T(8,128)S(1)}, u32[]{:S(2)}, u32[]{:S(2)}) collective-permute-start(f32[256,128]{1,0:T(8,128)S(1)} %get-tuple-element.60), channel_id=1, source_target_pairs={{0,5},{1,6},{2,7},{3,4},{4,1},{5,2},{6,3},{7,0},{8,13},{9,14},{10,... | collective-permute-start | bytes 393224 | tf_op jit(solution)/shard_map/ppermute | solution.py:22
  44.0 4.5 %collective-permute-start.17 = (f32[264,128]{1,0:T(8,128)S(1)}, f32[264,128]{1,0:T(8,128)S(1)}, u32[]{:S(2)}, u32[]{:S(2)}) collective-permute-start(f32[264,128]{1,0:T(8,128)S(1)} %shard_map.43), channel_id=1, source_target_pairs={{0,12},{4,16},{8,4},{12,24},{16,28},{20,0},{24,20},{28,8},{1,13},{... | collective-permute-start | bytes 405512 | tf_op jit(solution)/shard_map/ppermute | solution.py:28
  45.7 2.8 %collective-permute-start.16 = (f32[264,128]{1,0:T(8,128)S(1)}, f32[264,128]{1,0:T(8,128)S(1)}, u32[]{:S(2)}, u32[]{:S(2)}) collective-permute-start(f32[264,128]{1,0:T(8,128)S(1)} %shard_map.43), channel_id=1, source_target_pairs={{0,4},{4,0},{8,12},{12,8},{16,20},{20,16},{24,28},{28,24},{1,5},{5... | collective-permute-start | bytes 405512 | tf_op jit(solution)/shard_map/ppermute | solution.py:28
  46.1 2.4 %collective-permute-start.18 = (f32[256,128]{1,0:T(8,128)S(1)}, f32[256,128]{1,0:T(8,128)S(1)}, u32[]{:S(2)}, u32[]{:S(2)}) collective-permute-start(f32[256,128]{1,0:T(8,128)S(1)} %collective-permute-done.15.own_ref.refs_1_.refs_3_), channel_id=1, source_target_pairs={{0,4},{4,0},{8,12},{12,8},{16,20},{20,16},{24,28},{28,24},{1,5},{5... | collective-permute-start | bytes 393224 | tf_op jit(solution)/shard_map/ppermute | solution.py:28
  48.5 4.5 %collective-permute-start.20 = (f32[264,128]{1,0:T(8,128)S(1)}, f32[264,128]{1,0:T(8,128)S(1)}, u32[]{:S(2)}, u32[]{:S(2)}) collective-permute-start(f32[264,128]{1,0:T(8,128)S(1)} %add.31), channel_id=1, source_target_pairs={{0,12},{4,16},{8,4},{12,24},{16,28},{20,0},{24,20},{28,8},{1,13},{... | collective-permute-start | bytes 405512 | tf_op jit(solution)/shard_map/ppermute | solution.py:28
  50.3 2.8 %collective-permute-start.19 = (f32[264,128]{1,0:T(8,128)S(1)}, f32[264,128]{1,0:T(8,128)S(1)}, u32[]{:S(2)}, u32[]{:S(2)}) collective-permute-start(f32[264,128]{1,0:T(8,128)S(1)} %add.31), channel_id=1, source_target_pairs={{0,4},{4,0},{8,12},{12,8},{16,20},{20,16},{24,28},{28,24},{1,5},{5... | collective-permute-start | bytes 405512 | tf_op jit(solution)/shard_map/ppermute | solution.py:28
  53.1 1.4 %collective-permute-start.21 = (f32[264,128]{1,0:T(8,128)S(1)}, f32[264,128]{1,0:T(8,128)S(1)}, u32[]{:S(2)}, u32[]{:S(2)}) collective-permute-start(f32[264,128]{1,0:T(8,128)S(1)} %add.32.own_sum), channel_id=1, source_target_pairs={{0,4},{4,0},{8,12},{12,8},{16,20},{20,16},{24,28},{28,24},{1,5},{5... | collective-permute-start | bytes 405512 | tf_op jit(solution)/shard_map/ppermute | solution.py:28
  56.4 7.4 %collective-permute-start.22 = (f32[128,256]{1,0:T(8,128)S(1)}, f32[128,256]{1,0:T(8,128)S(1)}, u32[]{:S(2)}, u32[]{:S(2)}) collective-permute-start(f32[128,256]{1,0:T(8,128)S(1)} %get-tuple-element.66), channel_id=1, source_target_pairs={{0,6},{1,7},{2,4},{3,5},{4,2},{5,3},{6,0},{7,1},{8,14},{9,15},{10,... | collective-permute-start | bytes 393224 | tf_op jit(solution)/shard_map/ppermute | solution.py:22
  (2 other events, 3.8 us)

commit v13 on v12

--- a/solution.py
+++ b/solution.py
@@ -117,6 +117,12 @@
     ref[:, pl.ds(other, half)] = value[:, half:]
 
 
+def norm_rows(norm_lower, norm_upper, norm_upper_other):
+    rows = lax.broadcasted_iota(jnp.int32, (8, norm_lower.shape[1]), 0)
+    uppers = jnp.where(rows == 1, norm_upper, jnp.where(rows == 2, norm_upper_other, 0.0))
+    return jnp.where(rows == 0, norm_lower, uppers)
+
+
 def start_kernel(near_ref, weight_ref, own_part, other_part, near, weight, near_sent, weight_sent):
     copies = [
         pltpu.make_async_copy(near_ref, near, near_sent),
@@ -132,33 +138,52 @@
     point_weight = jnp.broadcast_to(weight[...], (8, weight.shape[1])).T[:, 0:1]
     upper_own, upper_other = near[:, pl.ds(own, half)], near[:, pl.ds(other, half)]
     upper_parts = two_parts(jnp.concatenate([upper_own, upper_other], axis=1))
-    rows = lax.broadcasted_iota(jnp.int32, (8, half), 0)
-    for start, norm_of, out in ((own, upper_own, own_part), (other, upper_other, other_part)):
+    orders = ((upper_own, upper_other), (upper_other, upper_own))
+    for start, order, out in zip((own, other), orders, (own_part, other_part)):
         lower = near[:, pl.ds(width + start, half)]
         weighted = point_weight * lower
         gram = product(upper_parts, two_parts(weighted), 0, 0)
         out[:width] = gram if out is own_part else halves_swapped(gram)
         norm_lower = jnp.sum(weighted * lower, axis=0, keepdims=True)
-        norm_upper = jnp.sum(point_weight * norm_of * norm_of, axis=0, keepdims=True)
-        out[width:] = jnp.where(rows == 0, norm_lower, jnp.where(rows == 1, norm_upper, 0.0))
-
-
-def lower_kernel(blocks, step, last, damps, own_sum, other_sum, *refs):
-    *block_refs, moved, coupling_out, scale_out = refs
-    width = coupling_out.shape[0]
+        uppers = [jnp.sum(point_weight * value * value, axis=0, keepdims=True) for value in order]
+        out[width:] = norm_rows(norm_lower, *uppers)
+
+
+def taken_rows(last, rows):
+    return slice(rows, 2 * rows) if last else slice(0, rows)
+
+
+def half_kernel(blocks, step, last, damps, own_sum, *refs):
+    *block_refs, own_coupling, left_scale, own_mixed = refs
+    width, half = own_coupling.shape
     upper, lower = blocks(*block_refs)
-    gram = joined(own_sum[:width], other_sum[:width])
-    norms = jnp.concatenate([own_sum[width:], other_sum[width:]], axis=1)
-    inverse = lax.rsqrt(norms + EPSILON)
-    coupling = gram * (damps[step : step + 1, 0:1] * inverse.T[:, 1:2]) * inverse[0:1]
-    scale = 1.0 + jnp.sum(coupling * coupling, keepdims=True)
-    coupling_out[...] = coupling
+    inverse = lax.rsqrt(own_sum[width:] + EPSILON)
+    uppers = jnp.broadcast_to(jnp.concatenate([inverse[1:2], inverse[2:3]], axis=1), (8, width))
+    scaled = damps[step : step + 1, 0:1] * uppers.T[:, 0:1]
+    left_scale[...] = jnp.broadcast_to(scaled, left_scale.shape)
+    coupling = own_sum[:width] * scaled * inverse[0:1]
+    own_coupling[...] = coupling
+    taken = taken_rows(last, own_mixed.shape[0])
+    own_mixed[...] = lower[taken, :half] + product(two_parts(upper[taken]), two_parts(coupling))
+
+
+def lower_kernel(blocks, last, own_coupling, left_scale, own_mixed, other_sum, *refs):
+    *block_refs, moved, other_coupling, scale_out = refs
+    width, half = own_coupling.shape
+    upper, lower = blocks(*block_refs)
+    inverse = lax.rsqrt(other_sum[width : width + 1] + EPSILON)
+    coupling = halves_swapped(other_sum[:width]) * left_scale[...] * inverse
+    other_coupling[...] = coupling
+    other_parts = two_parts(coupling)
+    parts = [jnp.concatenate(pair, axis=1) for pair in zip(two_parts(own_coupling[...]), other_parts)]
+    square = product(parts, parts, 0, 0)
+    both = own_coupling[...] ** 2 + coupling**2
+    scale = 1.0 + jnp.sum(both, keepdims=True)
     scale_out[...] = jnp.broadcast_to(scale, scale_out.shape)
-    parts = two_parts(coupling)
-    square = product(parts, parts, 0, 0)
     rows, columns = moved.shape
-    taken = slice(rows, 2 * rows) if last else slice(0, rows)
-    mixed = lower[taken] + product(two_parts(upper[taken]), parts)
+    taken = taken_rows(last, rows)
+    other_mixed = lower[taken, half:] + product(two_parts(upper[taken]), other_parts)
+    mixed = jnp.concatenate([own_mixed[...], other_mixed], axis=1)
     result = times_inverse_root(mixed, square, scale, columns)
     if last:
         stored(moved, result)
@@ -166,8 +191,8 @@
         moved[...] = result
 
 
-def rotated_upper(blocks, rows, coupling_ref, scale_ref, *block_refs):
-    coupling = coupling_ref[...]
+def rotated_upper(blocks, rows, own_coupling, other_coupling, scale_ref, *block_refs):
+    coupling = jnp.concatenate([own_coupling[...], other_coupling[...]], axis=1)
     upper, lower = blocks(*block_refs)
     parts = two_parts(coupling)
     mixed = upper[:rows] - product(two_parts(lower[:rows]), parts, 1, 1)
@@ -180,7 +205,7 @@
     upper = rotated_upper(blocks, upper_out.shape[0], *ins)
     upper_out[...] = upper
     weighted = weight[...] * upper
-    norm_out[...] = jnp.sum(weighted * upper, axis=0, keepdims=True)[:, : norm_out.shape[1]]
+    norm_out[...] = jnp.sum(weighted * upper, axis=0, keepdims=True)
     high, low = two_parts(weighted.T)
     gram_left[...] = jnp.concatenate([high, high, low], axis=1)
 
@@ -208,8 +233,8 @@
     right = jnp.concatenate([high, low, high], axis=0)
     payload[:width] = jnp.dot(gram_left[...], right, preferred_element_type=F32)
     norm_lower = jnp.sum(weight[...] * own * own, axis=0, keepdims=True)
-    rows = lax.broadcasted_iota(jnp.int32, (8, own.shape[1]), 0)
-    payload[width:] = jnp.where(rows == 0, norm_lower, jnp.where(rows == 1, norm_upper[...], 0.0))
+    half = own.shape[1]
+    payload[width:] = norm_rows(norm_lower, norm_upper[:, :half], norm_upper[:, half:])
 
 
 ON_CHIP = pl.BlockSpec(memory_space=pltpu.VMEM)
@@ -255,22 +280,31 @@
         last = step + 1 == STEPS
         payload, arriving = chip_sum(payload, arriving)
         held = held + (arriving,)
-        moved, coupling, scale = in_vmem(
-            functools.partial(lower_kernel, blocks, step, last),
-            [((rows, width) if last else (2 * rows, half), F32), ((width, width), F32), ((8, 128), F32)],
+        remote = swapped(payload, 1, 1)
+        shape = (rows, width) if last else (2 * rows, half)
+        pieces = in_vmem(
+            functools.partial(half_kernel, blocks, step, last),
+            [((width, half), F32), ((width, half), F32), ((shape[0], half), F32)],
             damps,
             payload,
-            swapped(payload, 1, 1),
             *held,
         )
+        moved, other_coupling, scale = in_vmem(
+            functools.partial(lower_kernel, blocks, last),
+            [(shape, F32), ((width, half), F32), ((8, 128), F32)],
+            *pieces,
+            remote,
+            *held,
+        )
+        coupling = (pieces[0], other_coupling)
         if last:
             break
         moved = column_shift(moved, 1)
         gram_left, norm_upper, upper = in_vmem(
             functools.partial(upper_kernel, blocks),
-            [((width, 6 * rows), jnp.bfloat16), ((1, half), F32), (whole, F32)],
+            [((width, 6 * rows), jnp.bfloat16), ((1, width), F32), (whole, F32)],
             weight,
-            coupling,
+            *coupling,
             scale,
             *held,
         )
@@ -281,11 +315,11 @@
     rotated = pl.pallas_call(
         functools.partial(last_upper_kernel, blocks),
         out_shape=out_shape,
-        in_specs=[ON_CHIP] * (2 + len(held)),
+        in_specs=[ON_CHIP] * (3 + len(held)),
         out_specs=ANYWHERE,
         scratch_shapes=[pltpu.VMEM((rows, width), F32), pltpu.SemaphoreType.DMA(())],
         compiler_params=GRANT,
-    )(coupling, scale, *held)
+    )(*coupling, scale, *held)
     return pl.pallas_call(
         last_lower_kernel,
         out_shape=out_shape,

time: 64.6 us -> 63.8 us (0.988)
  waiting for transfers between devices: 31.6 us -> 29.9 us
    ppermute x20, waiting for transfers between devices: 18.9 us -> 17.2 us  [swapped(): return lax.ppermute(value, 'pts', pairs)]
    pallas_call x7 -> x10, Pallas kernels: 10.1 us -> 10.7 us  [in_vmem(): pl.pallas_call(kernel, out_shape=[jax.ShapeDtypeStruct(shape, dtype) for...]
  transfers between devices with their start and end apart: 23 -> 23, of which waited for: 14 -> 14; matrix products, arithmetic and copies ran while one was open for 0% -> 0% of each run, Pallas kernels for 9% -> 12%
where the time goes in v13:
time: 63.8 us; the launch traced here: 63.6 us
  waiting for transfers between devices  29.9 us (47%)
  starting transfers between devices  18.1 us (28%)
  Pallas kernels  15.1 us (24%)
    ppermute x20, waiting for transfers between devices, swapped(): return lax.ppermute(value, 'pts', pairs)  17.2 us
    ppermute x20, starting transfers between devices, swapped(): return lax.ppermute(value, 'pts', pairs)  16.1 us
    ppermute x3, waiting for transfers between devices, column_shift(): return lax.ppermute(value, ('pts', 'cols'), pairs)  12.7 us
    pallas_call x10, Pallas kernels, in_vmem(): pl.pallas_call(kernel, out_shape=[jax.ShapeDtypeStruct(shape, dtype) for...  10.7 us
    pallas_call x1, Pallas kernels, body(): pl.pallas_call(functools.partial(last_upper_kernel, blocks), out_shape=ou...  2.33 us
    ppermute x3, starting transfers between devices, column_shift(): return lax.ppermute(value, ('pts', 'cols'), pairs)  1.98 us
    pallas_call x1, Pallas kernels, body(): pl.pallas_call(start_kernel, out_shape=[jax.ShapeDtypeStruct((width + 8,...  1.45 us
  transfers between devices with their start and end apart: 23, of which 14 were waited for; matrix products, arithmetic and copies ran while one was open for 0% of the time, Pallas kernels for 12%

profile of v13, /device:TPU:0, one launch (start us, length us, event | category | flops | bytes accessed | tf_op | source)
XLA Modules:
  0.0 63.6 jit_solution(17256919235905143235)
XLA Ops:
  0.0 1.5 %shard_map.37 = (f32[264,128]{1,0:T(8,128)S(1)}, f32[264,128]{1,0:T(8,128)S(1)}) custom-call(f32[128,512]{1,0:T(8,128)} %refs_3_.1, f32[1,128]{1,0:T(1,128)} %bitcast.5), custom_call_target="tpu_custom_call" | custom-call | tf_op jit(solution)/shard_map/pallas_call | solution.py:260
  2.1 0.9 %collective-permute-done.1 = f32[264,128]{1,0:T(8,128)S(1)} collective-permute-done((f32[264,128]{1,0:T(8,128)S(1)}, f32[264,128]{1,0:T(8,128)S(1)}, u32[]{:S(2)}, u32[]{:S(2)}) %collective-permute-start.1) | collective-permute-done | bytes 135200 | tf_op jit(solution)/shard_map/ppermute | solution.py:28
  3.0 2.7 %collective-permute-start.3 = (f32[264,128]{1,0:T(8,128)S(1)}, f32[264,128]{1,0:T(8,128)S(1)}, u32[]{:S(2)}, u32[]{:S(2)}) collective-permute-start(f32[264,128]{1,0:T(8,128)S(1)} %add.26), channel_id=1, source_target_pairs={{0,12},{4,16},{8,4},{12,24},{16,28},{20,0},{24,20},{28,8},{1,13},{... | collective-permute-start | bytes 405512 | tf_op jit(solution)/shard_map/ppermute | solution.py:28
  6.0 2.3 %collective-permute-done.3 = f32[264,128]{1,0:T(8,128)S(1)} collective-permute-done((f32[264,128]{1,0:T(8,128)S(1)}, f32[264,128]{1,0:T(8,128)S(1)}, u32[]{:S(2)}, u32[]{:S(2)}) %collective-permute-start.3) | collective-permute-done | bytes 135200 | tf_op jit(solution)/shard_map/ppermute | solution.py:28
  8.4 1.8 %collective-permute-start.6 = (f32[264,128]{1,0:T(8,128)S(1)}, f32[264,128]{1,0:T(8,128)S(1)}, u32[]{:S(2)}, u32[]{:S(2)}) collective-permute-start(f32[264,128]{1,0:T(8,128)S(1)} %add.27), channel_id=1, source_target_pairs={{0,12},{4,16},{8,4},{12,24},{16,28},{20,0},{24,20},{28,8},{1,13},{... | collective-permute-start | bytes 405512 | tf_op jit(solution)/shard_map/ppermute | solution.py:28
  10.6 2.3 %collective-permute-done.6 = f32[264,128]{1,0:T(8,128)S(1)} collective-permute-done((f32[264,128]{1,0:T(8,128)S(1)}, f32[264,128]{1,0:T(8,128)S(1)}, u32[]{:S(2)}, u32[]{:S(2)}) %collective-permute-start.6) | collective-permute-done | bytes 135200 | tf_op jit(solution)/shard_map/ppermute | solution.py:28
  14.3 1.7 %shard_map.39 = (f32[256,128]{1,0:T(8,128)S(1)}, f32[256,128]{1,0:T(8,128)S(1)}, f32[8,128]{1,0:T(8,128)S(1)}) custom-call(f32[256,128]{1,0:T(8,128)S(1)} %get-tuple-element.55.own_coupling.refs_0_, f32[256,128]{1,0:T(8,128)S(1)} %get-tuple-element.56.left_scale, f32[256,128]{1,0:T(8,128)S(1)} %get-tuple-element.57.own_mixed, ...), custom_call_target="tpu_custom_call" | custom-call | tf_op jit(solution)/shard_map/pallas_call | solution.py:246
  16.1 1.8 %collective-permute-start.8 = (f32[256,128]{1,0:T(8,128)S(1)}, f32[256,128]{1,0:T(8,128)S(1)}, u32[]{:S(2)}, u32[]{:S(2)}) collective-permute-start(f32[256,128]{1,0:T(8,128)S(1)} %get-tuple-element.62), channel_id=1, source_target_pairs={{0,5},{1,6},{2,7},{3,4},{4,1},{5,2},{6,3},{7,0},{8,13},{9,14},{10,... | collective-permute-start | bytes 393224 | tf_op jit(solution)/shard_map/ppermute | solution.py:22
  19.2 1.9 %shard_map.40 = (bf16[256,768]{1,0:T(8,128)(2,1)S(1)}, f32[1,256]{1,0:T(1,128)S(1)}, f32[256,256]{1,0:T(8,128)S(1)}) custom-call(f32[256,1]{1,0:T(8,128)S(1)} %copy.7.weight, f32[256,128]{1,0:T(8,128)S(1)} %get-tuple-element.55.own_coupling.refs_0_, f32[256,128]{1,0:T(8,128)S(1)} %get-tuple-element.58.refs_1_, f32[8,128]{1,0:T(8,128)S(1)} %get-tuple-element.59.refs_2_, ...), custom_call_target="tpu_custom_call" | custom-call | tf_op jit(solution)/shard_map/pallas_call | solution.py:246
  21.1 2.4 %collective-permute-done.8.own_ref.refs_1_.refs_4_ = f32[256,128]{1,0:T(8,128)S(1)} collective-permute-done((f32[256,128]{1,0:T(8,128)S(1)}, f32[256,128]{1,0:T(8,128)S(1)}, u32[]{:S(2)}, u32[]{:S(2)}) %collective-permute-start.8) | collective-permute-done | bytes 131104 | tf_op jit(solution)/shard_map/ppermute | solution.py:22
  23.8 1.7 %collective-permute-start.10 = (f32[264,128]{1,0:T(8,128)S(1)}, f32[264,128]{1,0:T(8,128)S(1)}, u32[]{:S(2)}, u32[]{:S(2)}) collective-permute-start(f32[264,128]{1,0:T(8,128)S(1)} %shard_map.41), channel_id=1, source_target_pairs={{0,12},{4,16},{8,4},{12,24},{16,28},{20,0},{24,20},{28,8},{1,13},{... | collective-permute-start | bytes 405512 | tf_op jit(solution)/shard_map/ppermute | solution.py:28
  25.9 2.3 %collective-permute-done.10 = f32[264,128]{1,0:T(8,128)S(1)} collective-permute-done((f32[264,128]{1,0:T(8,128)S(1)}, f32[264,128]{1,0:T(8,128)S(1)}, u32[]{:S(2)}, u32[]{:S(2)}) %collective-permute-start.10) | collective-permute-done | bytes 135200 | tf_op jit(solution)/shard_map/ppermute | solution.py:28
  28.3 1.7 %collective-permute-start.13 = (f32[264,128]{1,0:T(8,128)S(1)}, f32[264,128]{1,0:T(8,128)S(1)}, u32[]{:S(2)}, u32[]{:S(2)}) collective-permute-start(f32[264,128]{1,0:T(8,128)S(1)} %add.29), channel_id=1, source_target_pairs={{0,12},{4,16},{8,4},{12,24},{16,28},{20,0},{24,20},{28,8},{1,13},{... | collective-permute-start | bytes 405512 | tf_op jit(solution)/shard_map/ppermute | solution.py:28
  30.4 2.4 %collective-permute-done.13 = f32[264,128]{1,0:T(8,128)S(1)} collective-permute-done((f32[264,128]{1,0:T(8,128)S(1)}, f32[264,128]{1,0:T(8,128)S(1)}, u32[]{:S(2)}, u32[]{:S(2)}) %collective-permute-start.13) | collective-permute-done | bytes 135200 | tf_op jit(solution)/shard_map/ppermute | solution.py:28
  34.2 1.7 %shard_map.43 = (f32[256,128]{1,0:T(8,128)S(1)}, f32[256,128]{1,0:T(8,128)S(1)}, f32[8,128]{1,0:T(8,128)S(1)}) custom-call(f32[256,128]{1,0:T(8,128)S(1)} %get-tuple-element.68.own_coupling.refs_0_, f32[256,128]{1,0:T(8,128)S(1)} %get-tuple-element.69.left_scale, f32[256,128]{1,0:T(8,128)S(1)} %get-tuple-element.70.own_mixed, ...), custom_call_target="tpu_custom_call" | custom-call | tf_op jit(solution)/shard_map/pallas_call | solution.py:246
  36.0 1.9 %shard_map.44 = (bf16[256,768]{1,0:T(8,128)(2,1)S(1)}, f32[1,256]{1,0:T(1,128)S(1)}, f32[256,256]{1,0:T(8,128)S(1)}) custom-call(f32[256,1]{1,0:T(8,128)S(1)} %copy.7.weight, f32[256,128]{1,0:T(8,128)S(1)} %get-tuple-element.68.own_coupling.refs_0_, f32[256,128]{1,0:T(8,128)S(1)} %get-tuple-element.71.refs_1_, f32[8,128]{1,0:T(8,128)S(1)} %get-tuple-element.72.refs_2_, ...), custom_call_target="tpu_custom_call" | custom-call | tf_op jit(solution)/shard_map/pallas_call | solution.py:246
  37.8 5.3 %collective-permute-done.15.own_ref.refs_1_.refs_4_ = f32[256,128]{1,0:T(8,128)S(1)} collective-permute-done((f32[256,128]{1,0:T(8,128)S(1)}, f32[256,128]{1,0:T(8,128)S(1)}, u32[]{:S(2)}, u32[]{:S(2)}) %collective-permute-start.15) | collective-permute-done | bytes 131104 | tf_op jit(solution)/shard_map/ppermute | solution.py:22
  43.4 1.8 %collective-permute-start.17 = (f32[264,128]{1,0:T(8,128)S(1)}, f32[264,128]{1,0:T(8,128)S(1)}, u32[]{:S(2)}, u32[]{:S(2)}) collective-permute-start(f32[264,128]{1,0:T(8,128)S(1)} %shard_map.45), channel_id=1, source_target_pairs={{0,12},{4,16},{8,4},{12,24},{16,28},{20,0},{24,20},{28,8},{1,13},{... | collective-permute-start | bytes 405512 | tf_op jit(solution)/shard_map/ppermute | solution.py:28
  45.7 2.2 %collective-permute-done.17 = f32[264,128]{1,0:T(8,128)S(1)} collective-permute-done((f32[264,128]{1,0:T(8,128)S(1)}, f32[264,128]{1,0:T(8,128)S(1)}, u32[]{:S(2)}, u32[]{:S(2)}) %collective-permute-start.17) | collective-permute-done | bytes 135200 | tf_op jit(solution)/shard_map/ppermute | solution.py:28
  48.0 1.8 %collective-permute-start.20 = (f32[264,128]{1,0:T(8,128)S(1)}, f32[264,128]{1,0:T(8,128)S(1)}, u32[]{:S(2)}, u32[]{:S(2)}) collective-permute-start(f32[264,128]{1,0:T(8,128)S(1)} %add.31), channel_id=1, source_target_pairs={{0,12},{4,16},{8,4},{12,24},{16,28},{20,0},{24,20},{28,8},{1,13},{... | collective-permute-start | bytes 405512 | tf_op jit(solution)/shard_map/ppermute | solution.py:28
  50.1 2.3 %collective-permute-done.20 = f32[264,128]{1,0:T(8,128)S(1)} collective-permute-done((f32[264,128]{1,0:T(8,128)S(1)}, f32[264,128]{1,0:T(8,128)S(1)}, u32[]{:S(2)}, u32[]{:S(2)}) %collective-permute-start.20) | collective-permute-done | bytes 135200 | tf_op jit(solution)/shard_map/ppermute | solution.py:28
  53.9 1.6 %shard_map.47 = (f32[128,256]{1,0:T(8,128)S(1)}, f32[256,128]{1,0:T(8,128)S(1)}, f32[8,128]{1,0:T(8,128)S(1)}) custom-call(f32[256,128]{1,0:T(8,128)S(1)} %get-tuple-element.81.own_coupling.refs_0_, f32[256,128]{1,0:T(8,128)S(1)} %get-tuple-element.82.left_scale, f32[128,128]{1,0:T(8,128)S(1)} %get-tuple-element.83.own_mixed, ...), custom_call_target="tpu_custom_call" | custom-call | tf_op jit(solution)/shard_map/pallas_call | solution.py:246
  55.6 2.3 %shard_map.48.filled = f32[128,512]{1,0:T(8,128)} custom-call(f32[256,128]{1,0:T(8,128)S(1)} %get-tuple-element.81.own_coupling.refs_0_, f32[256,128]{1,0:T(8,128)S(1)} %get-tuple-element.85.refs_1_, f32[8,128]{1,0:T(8,128)S(1)} %get-tuple-element.86.refs_2_, f32[256,256]{1,0:T(8,128)S(1)} %get-tuple-element.79.refs_0_.refs_3_, ...), custom_call_target="tpu_custom_call" | custom-call | tf_op jit(solution)/shard_map/pallas_call | solution.py:315
  58.0 5.0 %collective-permute-done.22.lower = f32[128,256]{1,0:T(8,128)S(1)} collective-permute-done((f32[128,256]{1,0:T(8,128)S(1)}, f32[128,256]{1,0:T(8,128)S(1)}, u32[]{:S(2)}, u32[]{:S(2)}) %collective-permute-start.22) | collective-permute-done | bytes 131104 | tf_op jit(solution)/shard_map/ppermute | solution.py:22
  (52 shorter events, 10.2 us)
Async XLA Ops:
  1.5 1.5 %collective-permute-start.1 = (f32[264,128]{1,0:T(8,128)S(1)}, f32[264,128]{1,0:T(8,128)S(1)}, u32[]{:S(2)}, u32[]{:S(2)}) collective-permute-start(f32[264,128]{1,0:T(8,128)S(1)} %get-tuple-element.50), channel_id=1, source_target_pairs={{0,4},{4,0},{8,12},{12,8},{16,20},{20,16},{24,28},{28,24},{1,5},{5... | collective-permute-start | bytes 405512 | tf_op jit(solution)/shard_map/ppermute | solution.py:28
  2.0 6.4 %collective-permute-start.4 = (f32[128,512]{1,0:T(8,128)S(1)}, f32[128,512]{1,0:T(8,128)S(1)}, u32[]{:S(2)}, u32[]{:S(2)}) collective-permute-start(f32[128,512]{1,0:T(8,128)S(1)} %copy-done), channel_id=1, source_target_pairs={{0,4},{4,0},{8,12},{12,8},{16,20},{20,16},{24,28},{28,24},{1,5},{5... | collective-permute-start | bytes 786440 | tf_op jit(solution)/shard_map/ppermute | solution.py:28
  3.0 5.4 %collective-permute-start.3 = (f32[264,128]{1,0:T(8,128)S(1)}, f32[264,128]{1,0:T(8,128)S(1)}, u32[]{:S(2)}, u32[]{:S(2)}) collective-permute-start(f32[264,128]{1,0:T(8,128)S(1)} %add.26), channel_id=1, source_target_pairs={{0,12},{4,16},{8,4},{12,24},{16,28},{20,0},{24,20},{28,8},{1,13},{... | collective-permute-start | bytes 405512 | tf_op jit(solution)/shard_map/ppermute | solution.py:28
  5.6 2.7 %collective-permute-start.2 = (f32[264,128]{1,0:T(8,128)S(1)}, f32[264,128]{1,0:T(8,128)S(1)}, u32[]{:S(2)}, u32[]{:S(2)}) collective-permute-start(f32[264,128]{1,0:T(8,128)S(1)} %add.26), channel_id=1, source_target_pairs={{0,4},{4,0},{8,12},{12,8},{16,20},{20,16},{24,28},{28,24},{1,5},{5... | collective-permute-start | bytes 405512 | tf_op jit(solution)/shard_map/ppermute | solution.py:28
  8.4 4.9 %copy-start.2 = (s32[3,2]{0,1:T(2,128)S(1)}, s32[3,2]{0,1:T(2,128)}, u32[]{:S(2)}) copy-start(s32[3,2]{0,1:T(2,128)} %param.5) | copy-start | bytes 76
  8.4 4.5 %collective-permute-start.6 = (f32[264,128]{1,0:T(8,128)S(1)}, f32[264,128]{1,0:T(8,128)S(1)}, u32[]{:S(2)}, u32[]{:S(2)}) collective-permute-start(f32[264,128]{1,0:T(8,128)S(1)} %add.27), channel_id=1, source_target_pairs={{0,12},{4,16},{8,4},{12,24},{16,28},{20,0},{24,20},{28,8},{1,13},{... | collective-permute-start | bytes 405512 | tf_op jit(solution)/shard_map/ppermute | solution.py:28
  10.2 2.7 %collective-permute-start.5 = (f32[264,128]{1,0:T(8,128)S(1)}, f32[264,128]{1,0:T(8,128)S(1)}, u32[]{:S(2)}, u32[]{:S(2)}) collective-permute-start(f32[264,128]{1,0:T(8,128)S(1)} %add.27), channel_id=1, source_target_pairs={{0,4},{4,0},{8,12},{12,8},{16,20},{20,16},{24,28},{28,24},{1,5},{5... | collective-permute-start | bytes 405512 | tf_op jit(solution)/shard_map/ppermute | solution.py:28
  12.9 1.4 %collective-permute-start.7 = (f32[264,128]{1,0:T(8,128)S(1)}, f32[264,128]{1,0:T(8,128)S(1)}, u32[]{:S(2)}, u32[]{:S(2)}) collective-permute-start(f32[264,128]{1,0:T(8,128)S(1)} %add.28.own_sum), channel_id=1, source_target_pairs={{0,4},{4,0},{8,12},{12,8},{16,20},{20,16},{24,28},{28,24},{1,5},{5... | collective-permute-start | bytes 405512 | tf_op jit(solution)/shard_map/ppermute | solution.py:28
  16.1 7.4 %collective-permute-start.8 = (f32[256,128]{1,0:T(8,128)S(1)}, f32[256,128]{1,0:T(8,128)S(1)}, u32[]{:S(2)}, u32[]{:S(2)}) collective-permute-start(f32[256,128]{1,0:T(8,128)S(1)} %get-tuple-element.62), channel_id=1, source_target_pairs={{0,5},{1,6},{2,7},{3,4},{4,1},{5,2},{6,3},{7,0},{8,13},{9,14},{10,... | collective-permute-start | bytes 393224 | tf_op jit(solution)/shard_map/ppermute | solution.py:22
  17.9 1.2 %collective-permute-start = (f32[128]{0:T(128)S(1)}, f32[128]{0:T(128)S(1)}, u32[]{:S(2)}, u32[]{:S(2)}) collective-permute-start(f32[128]{0:T(128)S(1)} %copy-done.1), channel_id=1, source_target_pairs={{0,4},{4,0},{8,12},{12,8},{16,20},{20,16},{24,28},{28,24},{1,5},{5... | collective-permute-start | bytes 1544 | tf_op jit(solution)/shard_map/ppermute | solution.py:28
  23.8 4.5 %collective-permute-start.10 = (f32[264,128]{1,0:T(8,128)S(1)}, f32[264,128]{1,0:T(8,128)S(1)}, u32[]{:S(2)}, u32[]{:S(2)}) collective-permute-start(f32[264,128]{1,0:T(8,128)S(1)} %shard_map.41), channel_id=1, source_target_pairs={{0,12},{4,16},{8,4},{12,24},{16,28},{20,0},{24,20},{28,8},{1,13},{... | collective-permute-start | bytes 405512 | tf_op jit(solution)/shard_map/ppermute | solution.py:28
  25.4 2.8 %collective-permute-start.9 = (f32[264,128]{1,0:T(8,128)S(1)}, f32[264,128]{1,0:T(8,128)S(1)}, u32[]{:S(2)}, u32[]{:S(2)}) collective-permute-start(f32[264,128]{1,0:T(8,128)S(1)} %shard_map.41), channel_id=1, source_target_pairs={{0,4},{4,0},{8,12},{12,8},{16,20},{20,16},{24,28},{28,24},{1,5},{5... | collective-permute-start | bytes 405512 | tf_op jit(solution)/shard_map/ppermute | solution.py:28
  25.8 2.4 %collective-permute-start.11 = (f32[256,128]{1,0:T(8,128)S(1)}, f32[256,128]{1,0:T(8,128)S(1)}, u32[]{:S(2)}, u32[]{:S(2)}) collective-permute-start(f32[256,128]{1,0:T(8,128)S(1)} %collective-permute-done.8.own_ref.refs_1_.refs_4_), channel_id=1, source_target_pairs={{0,4},{4,0},{8,12},{12,8},{16,20},{20,16},{24,28},{28,24},{1,5},{5... | collective-permute-start | bytes 393224 | tf_op jit(solution)/shard_map/ppermute | solution.py:28
  28.3 4.5 %collective-permute-start.13 = (f32[264,128]{1,0:T(8,128)S(1)}, f32[264,128]{1,0:T(8,128)S(1)}, u32[]{:S(2)}, u32[]{:S(2)}) collective-permute-start(f32[264,128]{1,0:T(8,128)S(1)} %add.29), channel_id=1, source_target_pairs={{0,12},{4,16},{8,4},{12,24},{16,28},{20,0},{24,20},{28,8},{1,13},{... | collective-permute-start | bytes 405512 | tf_op jit(solution)/shard_map/ppermute | solution.py:28
  30.0 2.8 %collective-permute-start.12 = (f32[264,128]{1,0:T(8,128)S(1)}, f32[264,128]{1,0:T(8,128)S(1)}, u32[]{:S(2)}, u32[]{:S(2)}) collective-permute-start(f32[264,128]{1,0:T(8,128)S(1)} %add.29), channel_id=1, source_target_pairs={{0,4},{4,0},{8,12},{12,8},{16,20},{20,16},{24,28},{28,24},{1,5},{5... | collective-permute-start | bytes 405512 | tf_op jit(solution)/shard_map/ppermute | solution.py:28
  32.8 1.4 %collective-permute-start.14 = (f32[264,128]{1,0:T(8,128)S(1)}, f32[264,128]{1,0:T(8,128)S(1)}, u32[]{:S(2)}, u32[]{:S(2)}) collective-permute-start(f32[264,128]{1,0:T(8,128)S(1)} %add.30.own_sum), channel_id=1, source_target_pairs={{0,4},{4,0},{8,12},{12,8},{16,20},{20,16},{24,28},{28,24},{1,5},{5... | collective-permute-start | bytes 405512 | tf_op jit(solution)/shard_map/ppermute | solution.py:28
  35.9 7.2 %collective-permute-start.15 = (f32[256,128]{1,0:T(8,128)S(1)}, f32[256,128]{1,0:T(8,128)S(1)}, u32[]{:S(2)}, u32[]{:S(2)}) collective-permute-start(f32[256,128]{1,0:T(8,128)S(1)} %get-tuple-element.75), channel_id=1, source_target_pairs={{0,5},{1,6},{2,7},{3,4},{4,1},{5,2},{6,3},{7,0},{8,13},{9,14},{10,... | collective-permute-start | bytes 393224 | tf_op jit(solution)/shard_map/ppermute | solution.py:22
  43.4 4.5 %collective-permute-start.17 = (f32[264,128]{1,0:T(8,128)S(1)}, f32[264,128]{1,0:T(8,128)S(1)}, u32[]{:S(2)}, u32[]{:S(2)}) collective-permute-start(f32[264,128]{1,0:T(8,128)S(1)} %shard_map.45), channel_id=1, source_target_pairs={{0,12},{4,16},{8,4},{12,24},{16,28},{20,0},{24,20},{28,8},{1,13},{... | collective-permute-start | bytes 405512 | tf_op jit(solution)/shard_map/ppermute | solution.py:28
  45.2 2.7 %collective-permute-start.16 = (f32[264,128]{1,0:T(8,128)S(1)}, f32[264,128]{1,0:T(8,128)S(1)}, u32[]{:S(2)}, u32[]{:S(2)}) collective-permute-start(f32[264,128]{1,0:T(8,128)S(1)} %shard_map.45), channel_id=1, source_target_pairs={{0,4},{4,0},{8,12},{12,8},{16,20},{20,16},{24,28},{28,24},{1,5},{5... | collective-permute-start | bytes 405512 | tf_op jit(solution)/shard_map/ppermute | solution.py:28
  45.6 2.4 %collective-permute-start.18 = (f32[256,128]{1,0:T(8,128)S(1)}, f32[256,128]{1,0:T(8,128)S(1)}, u32[]{:S(2)}, u32[]{:S(2)}) collective-permute-start(f32[256,128]{1,0:T(8,128)S(1)} %collective-permute-done.15.own_ref.refs_1_.refs_4_), channel_id=1, source_target_pairs={{0,4},{4,0},{8,12},{12,8},{16,20},{20,16},{24,28},{28,24},{1,5},{5... | collective-permute-start | bytes 393224 | tf_op jit(solution)/shard_map/ppermute | solution.py:28
  48.0 4.5 %collective-permute-start.20 = (f32[264,128]{1,0:T(8,128)S(1)}, f32[264,128]{1,0:T(8,128)S(1)}, u32[]{:S(2)}, u32[]{:S(2)}) collective-permute-start(f32[264,128]{1,0:T(8,128)S(1)} %add.31), channel_id=1, source_target_pairs={{0,12},{4,16},{8,4},{12,24},{16,28},{20,0},{24,20},{28,8},{1,13},{... | collective-permute-start | bytes 405512 | tf_op jit(solution)/shard_map/ppermute | solution.py:28
  49.7 2.7 %collective-permute-start.19 = (f32[264,128]{1,0:T(8,128)S(1)}, f32[264,128]{1,0:T(8,128)S(1)}, u32[]{:S(2)}, u32[]{:S(2)}) collective-permute-start(f32[264,128]{1,0:T(8,128)S(1)} %add.31), channel_id=1, source_target_pairs={{0,4},{4,0},{8,12},{12,8},{16,20},{20,16},{24,28},{28,24},{1,5},{5... | collective-permute-start | bytes 405512 | tf_op jit(solution)/shard_map/ppermute | solution.py:28
  52.5 1.4 %collective-permute-start.21 = (f32[264,128]{1,0:T(8,128)S(1)}, f32[264,128]{1,0:T(8,128)S(1)}, u32[]{:S(2)}, u32[]{:S(2)}) collective-permute-start(f32[264,128]{1,0:T(8,128)S(1)} %add.32.own_sum), channel_id=1, source_target_pairs={{0,4},{4,0},{8,12},{12,8},{16,20},{20,16},{24,28},{28,24},{1,5},{5... | collective-permute-start | bytes 405512 | tf_op jit(solution)/shard_map/ppermute | solution.py:28
  55.5 7.4 %collective-permute-start.22 = (f32[128,256]{1,0:T(8,128)S(1)}, f32[128,256]{1,0:T(8,128)S(1)}, u32[]{:S(2)}, u32[]{:S(2)}) collective-permute-start(f32[128,256]{1,0:T(8,128)S(1)} %get-tuple-element.84), channel_id=1, source_target_pairs={{0,6},{1,7},{2,4},{3,5},{4,2},{5,3},{6,0},{7,1},{8,14},{9,15},{10,... | collective-permute-start | bytes 393224 | tf_op jit(solution)/shard_map/ppermute | solution.py:22
  (2 other events, 3.8 us)

commit v14 on v13

--- a/solution.py
+++ b/solution.py
@@ -154,7 +154,7 @@
 
 
 def half_kernel(blocks, step, last, damps, own_sum, *refs):
-    *block_refs, own_coupling, left_scale, own_mixed = refs
+    *block_refs, own_coupling, own_high, own_low, upper_high, upper_low, left_scale, square, norm, own_mixed = refs
     width, half = own_coupling.shape
     upper, lower = blocks(*block_refs)
     inverse = lax.rsqrt(own_sum[width:] + EPSILON)
@@ -163,26 +163,36 @@
     left_scale[...] = jnp.broadcast_to(scaled, left_scale.shape)
     coupling = own_sum[:width] * scaled * inverse[0:1]
     own_coupling[...] = coupling
+    norm[...] = jnp.sum(coupling * coupling, axis=0, keepdims=True)
+    parts = own_high[...], own_low[...] = two_parts(coupling)
+    square[...] = product(parts, parts, 0, 0)
     taken = taken_rows(last, own_mixed.shape[0])
-    own_mixed[...] = lower[taken, :half] + product(two_parts(upper[taken]), two_parts(coupling))
-
-
-def lower_kernel(blocks, last, own_coupling, left_scale, own_mixed, other_sum, *refs):
+    upper_parts = upper_high[...], upper_low[...] = two_parts(upper[taken])
+    own_mixed[...] = lower[taken, :half] + product(upper_parts, parts)
+
+
+def lower_kernel(
+    blocks, last, own_high, own_low, upper_high, upper_low, left_scale, own_square, norm, own_mixed, other_sum, *refs
+):
     *block_refs, moved, other_coupling, scale_out = refs
-    width, half = own_coupling.shape
-    upper, lower = blocks(*block_refs)
+    width, half = own_high.shape
+    _, lower = blocks(*block_refs)
     inverse = lax.rsqrt(other_sum[width : width + 1] + EPSILON)
     coupling = halves_swapped(other_sum[:width]) * left_scale[...] * inverse
     other_coupling[...] = coupling
     other_parts = two_parts(coupling)
-    parts = [jnp.concatenate(pair, axis=1) for pair in zip(two_parts(own_coupling[...]), other_parts)]
-    square = product(parts, parts, 0, 0)
-    both = own_coupling[...] ** 2 + coupling**2
-    scale = 1.0 + jnp.sum(both, keepdims=True)
+    own_parts = own_high[...], own_low[...]
+    parts = [jnp.concatenate(pair, axis=1) for pair in zip(own_parts, other_parts)]
+    crossed = product(other_parts, own_parts, 0, 0)
+    square = jnp.concatenate(
+        [jnp.concatenate([own_square[...], crossed], axis=0), product(parts, other_parts, 0, 0)], axis=1
+    )
+    norms = norm[...] + jnp.sum(coupling * coupling, axis=0, keepdims=True)
+    scale = 1.0 + jnp.sum(norms, keepdims=True)
     scale_out[...] = jnp.broadcast_to(scale, scale_out.shape)
     rows, columns = moved.shape
     taken = taken_rows(last, rows)
-    other_mixed = lower[taken, half:] + product(two_parts(upper[taken]), other_parts)
+    other_mixed = lower[taken, half:] + product((upper_high[...], upper_low[...]), other_parts)
     mixed = jnp.concatenate([own_mixed[...], other_mixed], axis=1)
     result = times_inverse_root(mixed, square, scale, columns)
     if last:
@@ -284,7 +294,10 @@
         shape = (rows, width) if last else (2 * rows, half)
         pieces = in_vmem(
             functools.partial(half_kernel, blocks, step, last),
-            [((width, half), F32), ((width, half), F32), ((shape[0], half), F32)],
+            [((width, half), F32)]
+            + [((width, half), jnp.bfloat16)] * 2
+            + [((shape[0], width), jnp.bfloat16)] * 2
+            + [((width, half), F32), ((half, half), F32), ((1, half), F32), ((shape[0], half), F32)],
             damps,
             payload,
             *held,
@@ -292,7 +305,7 @@
         moved, other_coupling, scale = in_vmem(
             functools.partial(lower_kernel, blocks, last),
             [(shape, F32), ((width, half), F32), ((8, 128), F32)],
-            *pieces,
+            *pieces[1:],
             remote,
             *held,
         )

time: 63.8 us -> 63.7 us (level)
  no operation moved by 1% of the time
where the time goes in v14:
time: 63.7 us; the launch traced here: 63.6 us
  waiting for transfers between devices  29.6 us (46%)
  starting transfers between devices  18 us (28%)
  Pallas kernels  15.4 us (24%)
    ppermute x20, waiting for transfers between devices, swapped(): return lax.ppermute(value, 'pts', pairs)  16.9 us
    ppermute x20, starting transfers between devices, swapped(): return lax.ppermute(value, 'pts', pairs)  16.1 us
    ppermute x3, waiting for transfers between devices, column_shift(): return lax.ppermute(value, ('pts', 'cols'), pairs)  12.7 us
    pallas_call x10, Pallas kernels, in_vmem(): pl.pallas_call(kernel, out_shape=[jax.ShapeDtypeStruct(shape, dtype) for...  11 us
    pallas_call x1, Pallas kernels, body(): pl.pallas_call(functools.partial(last_upper_kernel, blocks), out_shape=ou...  2.33 us
    ppermute x3, starting transfers between devices, column_shift(): return lax.ppermute(value, ('pts', 'cols'), pairs)  1.97 us
    pallas_call x1, Pallas kernels, body(): pl.pallas_call(start_kernel, out_shape=[jax.ShapeDtypeStruct((width + 8,...  1.45 us
  transfers between devices with their start and end apart: 23, of which 14 were waited for; matrix products, arithmetic and copies ran while one was open for 0% of the time, Pallas kernels for 12%

profile of v14, /device:TPU:0, one launch (start us, length us, event | category | flops | bytes accessed | tf_op | source)
XLA Modules:
  0.0 63.6 jit_solution(16613450065165846722)
XLA Ops:
  0.0 1.5 %shard_map.37 = (f32[264,128]{1,0:T(8,128)S(1)}, f32[264,128]{1,0:T(8,128)S(1)}) custom-call(f32[128,512]{1,0:T(8,128)} %refs_3_.1, f32[1,128]{1,0:T(1,128)} %bitcast.5), custom_call_target="tpu_custom_call" | custom-call | tf_op jit(solution)/shard_map/pallas_call | solution.py:270
  2.1 0.9 %collective-permute-done.1 = f32[264,128]{1,0:T(8,128)S(1)} collective-permute-done((f32[264,128]{1,0:T(8,128)S(1)}, f32[264,128]{1,0:T(8,128)S(1)}, u32[]{:S(2)}, u32[]{:S(2)}) %collective-permute-start.1) | collective-permute-done | bytes 135200 | tf_op jit(solution)/shard_map/ppermute | solution.py:28
  3.0 2.7 %collective-permute-start.3 = (f32[264,128]{1,0:T(8,128)S(1)}, f32[264,128]{1,0:T(8,128)S(1)}, u32[]{:S(2)}, u32[]{:S(2)}) collective-permute-start(f32[264,128]{1,0:T(8,128)S(1)} %add.26), channel_id=1, source_target_pairs={{0,12},{4,16},{8,4},{12,24},{16,28},{20,0},{24,20},{28,8},{1,13},{... | collective-permute-start | bytes 405512 | tf_op jit(solution)/shard_map/ppermute | solution.py:28
  6.0 2.3 %collective-permute-done.3 = f32[264,128]{1,0:T(8,128)S(1)} collective-permute-done((f32[264,128]{1,0:T(8,128)S(1)}, f32[264,128]{1,0:T(8,128)S(1)}, u32[]{:S(2)}, u32[]{:S(2)}) %collective-permute-start.3) | collective-permute-done | bytes 135200 | tf_op jit(solution)/shard_map/ppermute | solution.py:28
  8.4 1.8 %collective-permute-start.6 = (f32[264,128]{1,0:T(8,128)S(1)}, f32[264,128]{1,0:T(8,128)S(1)}, u32[]{:S(2)}, u32[]{:S(2)}) collective-permute-start(f32[264,128]{1,0:T(8,128)S(1)} %add.27), channel_id=1, source_target_pairs={{0,12},{4,16},{8,4},{12,24},{16,28},{20,0},{24,20},{28,8},{1,13},{... | collective-permute-start | bytes 405512 | tf_op jit(solution)/shard_map/ppermute | solution.py:28
  10.6 2.3 %collective-permute-done.6 = f32[264,128]{1,0:T(8,128)S(1)} collective-permute-done((f32[264,128]{1,0:T(8,128)S(1)}, f32[264,128]{1,0:T(8,128)S(1)}, u32[]{:S(2)}, u32[]{:S(2)}) %collective-permute-start.6) | collective-permute-done | bytes 135200 | tf_op jit(solution)/shard_map/ppermute | solution.py:28
  14.3 1.7 %shard_map.39 = (f32[256,128]{1,0:T(8,128)S(1)}, f32[256,128]{1,0:T(8,128)S(1)}, f32[8,128]{1,0:T(8,128)S(1)}) custom-call(bf16[256,128]{1,0:T(8,128)(2,1)S(1)} %get-tuple-element.74.own_high, bf16[256,128]{1,0:T(8,128)(2,1)S(1)} %get-tuple-element.75.own_low, bf16[256,256]{1,0:T(8,128)(2,1)S(1)} %get-tuple-element.76.upper_high, ...), custom_call_target="tpu_custom_call" | custom-call | tf_op jit(solution)/shard_map/pallas_call | solution.py:256
  16.0 1.8 %collective-permute-start.8 = (f32[256,128]{1,0:T(8,128)S(1)}, f32[256,128]{1,0:T(8,128)S(1)}, u32[]{:S(2)}, u32[]{:S(2)}) collective-permute-start(f32[256,128]{1,0:T(8,128)S(1)} %get-tuple-element.86), channel_id=1, source_target_pairs={{0,5},{1,6},{2,7},{3,4},{4,1},{5,2},{6,3},{7,0},{8,13},{9,14},{10,... | collective-permute-start | bytes 393224 | tf_op jit(solution)/shard_map/ppermute | solution.py:22
  19.2 1.9 %shard_map.40 = (bf16[256,768]{1,0:T(8,128)(2,1)S(1)}, f32[1,256]{1,0:T(1,128)S(1)}, f32[256,256]{1,0:T(8,128)S(1)}) custom-call(f32[256,1]{1,0:T(8,128)S(1)} %copy.7.weight, f32[256,128]{1,0:T(8,128)S(1)} %get-tuple-element.73.refs_0_, f32[256,128]{1,0:T(8,128)S(1)} %get-tuple-element.82.refs_1_, f32[8,128]{1,0:T(8,128)S(1)} %get-tuple-element.83.refs_2_, ...), custom_call_target="tpu_custom_call" | custom-call | tf_op jit(solution)/shard_map/pallas_call | solution.py:256
  21.1 2.4 %collective-permute-done.8.own_ref.refs_1_.refs_4_ = f32[256,128]{1,0:T(8,128)S(1)} collective-permute-done((f32[256,128]{1,0:T(8,128)S(1)}, f32[256,128]{1,0:T(8,128)S(1)}, u32[]{:S(2)}, u32[]{:S(2)}) %collective-permute-start.8) | collective-permute-done | bytes 131104 | tf_op jit(solution)/shard_map/ppermute | solution.py:22
  23.7 1.7 %collective-permute-start.10 = (f32[264,128]{1,0:T(8,128)S(1)}, f32[264,128]{1,0:T(8,128)S(1)}, u32[]{:S(2)}, u32[]{:S(2)}) collective-permute-start(f32[264,128]{1,0:T(8,128)S(1)} %shard_map.41), channel_id=1, source_target_pairs={{0,12},{4,16},{8,4},{12,24},{16,28},{20,0},{24,20},{28,8},{1,13},{... | collective-permute-start | bytes 405512 | tf_op jit(solution)/shard_map/ppermute | solution.py:28
  25.9 2.3 %collective-permute-done.10 = f32[264,128]{1,0:T(8,128)S(1)} collective-permute-done((f32[264,128]{1,0:T(8,128)S(1)}, f32[264,128]{1,0:T(8,128)S(1)}, u32[]{:S(2)}, u32[]{:S(2)}) %collective-permute-start.10) | collective-permute-done | bytes 135200 | tf_op jit(solution)/shard_map/ppermute | solution.py:28
  28.3 1.7 %collective-permute-start.13 = (f32[264,128]{1,0:T(8,128)S(1)}, f32[264,128]{1,0:T(8,128)S(1)}, u32[]{:S(2)}, u32[]{:S(2)}) collective-permute-start(f32[264,128]{1,0:T(8,128)S(1)} %add.29), channel_id=1, source_target_pairs={{0,12},{4,16},{8,4},{12,24},{16,28},{20,0},{24,20},{28,8},{1,13},{... | collective-permute-start | bytes 405512 | tf_op jit(solution)/shard_map/ppermute | solution.py:28
  30.4 2.4 %collective-permute-done.13 = f32[264,128]{1,0:T(8,128)S(1)} collective-permute-done((f32[264,128]{1,0:T(8,128)S(1)}, f32[264,128]{1,0:T(8,128)S(1)}, u32[]{:S(2)}, u32[]{:S(2)}) %collective-permute-start.13) | collective-permute-done | bytes 135200 | tf_op jit(solution)/shard_map/ppermute | solution.py:28
  34.2 1.7 %shard_map.43 = (f32[256,128]{1,0:T(8,128)S(1)}, f32[256,128]{1,0:T(8,128)S(1)}, f32[8,128]{1,0:T(8,128)S(1)}) custom-call(bf16[256,128]{1,0:T(8,128)(2,1)S(1)} %get-tuple-element.93.own_high, bf16[256,128]{1,0:T(8,128)(2,1)S(1)} %get-tuple-element.94.own_low, bf16[256,256]{1,0:T(8,128)(2,1)S(1)} %get-tuple-element.95.upper_high, ...), custom_call_target="tpu_custom_call" | custom-call | tf_op jit(solution)/shard_map/pallas_call | solution.py:256
  35.9 1.9 %shard_map.44 = (bf16[256,768]{1,0:T(8,128)(2,1)S(1)}, f32[1,256]{1,0:T(1,128)S(1)}, f32[256,256]{1,0:T(8,128)S(1)}) custom-call(f32[256,1]{1,0:T(8,128)S(1)} %copy.7.weight, f32[256,128]{1,0:T(8,128)S(1)} %get-tuple-element.92.refs_0_, f32[256,128]{1,0:T(8,128)S(1)} %get-tuple-element.101.refs_1_, f32[8,128]{1,0:T(8,128)S(1)} %get-tuple-element.102.refs_2_, ...), custom_call_target="tpu_custom_call" | custom-call | tf_op jit(solution)/shard_map/pallas_call | solution.py:256
  37.8 5.3 %collective-permute-done.15.own_ref.refs_1_.refs_4_ = f32[256,128]{1,0:T(8,128)S(1)} collective-permute-done((f32[256,128]{1,0:T(8,128)S(1)}, f32[256,128]{1,0:T(8,128)S(1)}, u32[]{:S(2)}, u32[]{:S(2)}) %collective-permute-start.15) | collective-permute-done | bytes 131104 | tf_op jit(solution)/shard_map/ppermute | solution.py:22
  43.4 1.8 %collective-permute-start.17 = (f32[264,128]{1,0:T(8,128)S(1)}, f32[264,128]{1,0:T(8,128)S(1)}, u32[]{:S(2)}, u32[]{:S(2)}) collective-permute-start(f32[264,128]{1,0:T(8,128)S(1)} %shard_map.45), channel_id=1, source_target_pairs={{0,12},{4,16},{8,4},{12,24},{16,28},{20,0},{24,20},{28,8},{1,13},{... | collective-permute-start | bytes 405512 | tf_op jit(solution)/shard_map/ppermute | solution.py:28
  45.7 2.2 %collective-permute-done.17 = f32[264,128]{1,0:T(8,128)S(1)} collective-permute-done((f32[264,128]{1,0:T(8,128)S(1)}, f32[264,128]{1,0:T(8,128)S(1)}, u32[]{:S(2)}, u32[]{:S(2)}) %collective-permute-start.17) | collective-permute-done | bytes 135200 | tf_op jit(solution)/shard_map/ppermute | solution.py:28
  47.9 1.8 %collective-permute-start.20 = (f32[264,128]{1,0:T(8,128)S(1)}, f32[264,128]{1,0:T(8,128)S(1)}, u32[]{:S(2)}, u32[]{:S(2)}) collective-permute-start(f32[264,128]{1,0:T(8,128)S(1)} %add.31), channel_id=1, source_target_pairs={{0,12},{4,16},{8,4},{12,24},{16,28},{20,0},{24,20},{28,8},{1,13},{... | collective-permute-start | bytes 405512 | tf_op jit(solution)/shard_map/ppermute | solution.py:28
  50.1 2.3 %collective-permute-done.20 = f32[264,128]{1,0:T(8,128)S(1)} collective-permute-done((f32[264,128]{1,0:T(8,128)S(1)}, f32[264,128]{1,0:T(8,128)S(1)}, u32[]{:S(2)}, u32[]{:S(2)}) %collective-permute-start.20) | collective-permute-done | bytes 135200 | tf_op jit(solution)/shard_map/ppermute | solution.py:28
  53.9 1.6 %shard_map.47 = (f32[128,256]{1,0:T(8,128)S(1)}, f32[256,128]{1,0:T(8,128)S(1)}, f32[8,128]{1,0:T(8,128)S(1)}) custom-call(bf16[256,128]{1,0:T(8,128)(2,1)S(1)} %get-tuple-element.111.own_high, bf16[256,128]{1,0:T(8,128)(2,1)S(1)} %get-tuple-element.112.own_low, bf16[128,256]{1,0:T(8,128)(2,1)S(1)} %get-tuple-element.113.upper_high, ...), custom_call_target="tpu_custom_call" | custom-call | tf_op jit(solution)/shard_map/pallas_call | solution.py:256
  55.6 2.3 %shard_map.48.filled = f32[128,512]{1,0:T(8,128)} custom-call(f32[256,128]{1,0:T(8,128)S(1)} %get-tuple-element.120.refs_0_, f32[256,128]{1,0:T(8,128)S(1)} %get-tuple-element.121.refs_1_, f32[8,128]{1,0:T(8,128)S(1)} %get-tuple-element.122.refs_2_, f32[256,256]{1,0:T(8,128)S(1)} %get-tuple-element.109.refs_0_.refs_3_, ...), custom_call_target="tpu_custom_call" | custom-call | tf_op jit(solution)/shard_map/pallas_call | solution.py:328
  57.9 5.0 %collective-permute-done.22.lower = f32[128,256]{1,0:T(8,128)S(1)} collective-permute-done((f32[128,256]{1,0:T(8,128)S(1)}, f32[128,256]{1,0:T(8,128)S(1)}, u32[]{:S(2)}, u32[]{:S(2)}) %collective-permute-start.22) | collective-permute-done | bytes 131104 | tf_op jit(solution)/shard_map/ppermute | solution.py:22
  (52 shorter events, 10.3 us)
Async XLA Ops:
  1.5 1.5 %collective-permute-start.1 = (f32[264,128]{1,0:T(8,128)S(1)}, f32[264,128]{1,0:T(8,128)S(1)}, u32[]{:S(2)}, u32[]{:S(2)}) collective-permute-start(f32[264,128]{1,0:T(8,128)S(1)} %get-tuple-element.68), channel_id=1, source_target_pairs={{0,4},{4,0},{8,12},{12,8},{16,20},{20,16},{24,28},{28,24},{1,5},{5... | collective-permute-start | bytes 405512 | tf_op jit(solution)/shard_map/ppermute | solution.py:28
  2.0 6.4 %collective-permute-start.4 = (f32[128,512]{1,0:T(8,128)S(1)}, f32[128,512]{1,0:T(8,128)S(1)}, u32[]{:S(2)}, u32[]{:S(2)}) collective-permute-start(f32[128,512]{1,0:T(8,128)S(1)} %copy-done), channel_id=1, source_target_pairs={{0,4},{4,0},{8,12},{12,8},{16,20},{20,16},{24,28},{28,24},{1,5},{5... | collective-permute-start | bytes 786440 | tf_op jit(solution)/shard_map/ppermute | solution.py:28
  3.0 5.4 %collective-permute-start.3 = (f32[264,128]{1,0:T(8,128)S(1)}, f32[264,128]{1,0:T(8,128)S(1)}, u32[]{:S(2)}, u32[]{:S(2)}) collective-permute-start(f32[264,128]{1,0:T(8,128)S(1)} %add.26), channel_id=1, source_target_pairs={{0,12},{4,16},{8,4},{12,24},{16,28},{20,0},{24,20},{28,8},{1,13},{... | collective-permute-start | bytes 405512 | tf_op jit(solution)/shard_map/ppermute | solution.py:28
  5.6 2.7 %collective-permute-start.2 = (f32[264,128]{1,0:T(8,128)S(1)}, f32[264,128]{1,0:T(8,128)S(1)}, u32[]{:S(2)}, u32[]{:S(2)}) collective-permute-start(f32[264,128]{1,0:T(8,128)S(1)} %add.26), channel_id=1, source_target_pairs={{0,4},{4,0},{8,12},{12,8},{16,20},{20,16},{24,28},{28,24},{1,5},{5... | collective-permute-start | bytes 405512 | tf_op jit(solution)/shard_map/ppermute | solution.py:28
  8.4 4.9 %copy-start.2 = (s32[3,2]{0,1:T(2,128)S(1)}, s32[3,2]{0,1:T(2,128)}, u32[]{:S(2)}) copy-start(s32[3,2]{0,1:T(2,128)} %param.5) | copy-start | bytes 76
  8.4 4.5 %collective-permute-start.6 = (f32[264,128]{1,0:T(8,128)S(1)}, f32[264,128]{1,0:T(8,128)S(1)}, u32[]{:S(2)}, u32[]{:S(2)}) collective-permute-start(f32[264,128]{1,0:T(8,128)S(1)} %add.27), channel_id=1, source_target_pairs={{0,12},{4,16},{8,4},{12,24},{16,28},{20,0},{24,20},{28,8},{1,13},{... | collective-permute-start | bytes 405512 | tf_op jit(solution)/shard_map/ppermute | solution.py:28
  10.2 2.7 %collective-permute-start.5 = (f32[264,128]{1,0:T(8,128)S(1)}, f32[264,128]{1,0:T(8,128)S(1)}, u32[]{:S(2)}, u32[]{:S(2)}) collective-permute-start(f32[264,128]{1,0:T(8,128)S(1)} %add.27), channel_id=1, source_target_pairs={{0,4},{4,0},{8,12},{12,8},{16,20},{20,16},{24,28},{28,24},{1,5},{5... | collective-permute-start | bytes 405512 | tf_op jit(solution)/shard_map/ppermute | solution.py:28
  12.9 1.4 %collective-permute-start.7 = (f32[264,128]{1,0:T(8,128)S(1)}, f32[264,128]{1,0:T(8,128)S(1)}, u32[]{:S(2)}, u32[]{:S(2)}) collective-permute-start(f32[264,128]{1,0:T(8,128)S(1)} %add.28.own_sum), channel_id=1, source_target_pairs={{0,4},{4,0},{8,12},{12,8},{16,20},{20,16},{24,28},{28,24},{1,5},{5... | collective-permute-start | bytes 405512 | tf_op jit(solution)/shard_map/ppermute | solution.py:28
  16.0 7.4 %collective-permute-start.8 = (f32[256,128]{1,0:T(8,128)S(1)}, f32[256,128]{1,0:T(8,128)S(1)}, u32[]{:S(2)}, u32[]{:S(2)}) collective-permute-start(f32[256,128]{1,0:T(8,128)S(1)} %get-tuple-element.86), channel_id=1, source_target_pairs={{0,5},{1,6},{2,7},{3,4},{4,1},{5,2},{6,3},{7,0},{8,13},{9,14},{10,... | collective-permute-start | bytes 393224 | tf_op jit(solution)/shard_map/ppermute | solution.py:22
  17.9 1.2 %collective-permute-start = (f32[128]{0:T(128)S(1)}, f32[128]{0:T(128)S(1)}, u32[]{:S(2)}, u32[]{:S(2)}) collective-permute-start(f32[128]{0:T(128)S(1)} %copy-done.1), channel_id=1, source_target_pairs={{0,4},{4,0},{8,12},{12,8},{16,20},{20,16},{24,28},{28,24},{1,5},{5... | collective-permute-start | bytes 1544 | tf_op jit(solution)/shard_map/ppermute | solution.py:28
  23.7 4.5 %collective-permute-start.10 = (f32[264,128]{1,0:T(8,128)S(1)}, f32[264,128]{1,0:T(8,128)S(1)}, u32[]{:S(2)}, u32[]{:S(2)}) collective-permute-start(f32[264,128]{1,0:T(8,128)S(1)} %shard_map.41), channel_id=1, source_target_pairs={{0,12},{4,16},{8,4},{12,24},{16,28},{20,0},{24,20},{28,8},{1,13},{... | collective-permute-start | bytes 405512 | tf_op jit(solution)/shard_map/ppermute | solution.py:28
  25.4 2.8 %collective-permute-start.9 = (f32[264,128]{1,0:T(8,128)S(1)}, f32[264,128]{1,0:T(8,128)S(1)}, u32[]{:S(2)}, u32[]{:S(2)}) collective-permute-start(f32[264,128]{1,0:T(8,128)S(1)} %shard_map.41), channel_id=1, source_target_pairs={{0,4},{4,0},{8,12},{12,8},{16,20},{20,16},{24,28},{28,24},{1,5},{5... | collective-permute-start | bytes 405512 | tf_op jit(solution)/shard_map/ppermute | solution.py:28
  25.8 2.4 %collective-permute-start.11 = (f32[256,128]{1,0:T(8,128)S(1)}, f32[256,128]{1,0:T(8,128)S(1)}, u32[]{:S(2)}, u32[]{:S(2)}) collective-permute-start(f32[256,128]{1,0:T(8,128)S(1)} %collective-permute-done.8.own_ref.refs_1_.refs_4_), channel_id=1, source_target_pairs={{0,4},{4,0},{8,12},{12,8},{16,20},{20,16},{24,28},{28,24},{1,5},{5... | collective-permute-start | bytes 393224 | tf_op jit(solution)/shard_map/ppermute | solution.py:28
  28.3 4.5 %collective-permute-start.13 = (f32[264,128]{1,0:T(8,128)S(1)}, f32[264,128]{1,0:T(8,128)S(1)}, u32[]{:S(2)}, u32[]{:S(2)}) collective-permute-start(f32[264,128]{1,0:T(8,128)S(1)} %add.29), channel_id=1, source_target_pairs={{0,12},{4,16},{8,4},{12,24},{16,28},{20,0},{24,20},{28,8},{1,13},{... | collective-permute-start | bytes 405512 | tf_op jit(solution)/shard_map/ppermute | solution.py:28
  29.9 2.8 %collective-permute-start.12 = (f32[264,128]{1,0:T(8,128)S(1)}, f32[264,128]{1,0:T(8,128)S(1)}, u32[]{:S(2)}, u32[]{:S(2)}) collective-permute-start(f32[264,128]{1,0:T(8,128)S(1)} %add.29), channel_id=1, source_target_pairs={{0,4},{4,0},{8,12},{12,8},{16,20},{20,16},{24,28},{28,24},{1,5},{5... | collective-permute-start | bytes 405512 | tf_op jit(solution)/shard_map/ppermute | solution.py:28
  32.8 1.4 %collective-permute-start.14 = (f32[264,128]{1,0:T(8,128)S(1)}, f32[264,128]{1,0:T(8,128)S(1)}, u32[]{:S(2)}, u32[]{:S(2)}) collective-permute-start(f32[264,128]{1,0:T(8,128)S(1)} %add.30.own_sum), channel_id=1, source_target_pairs={{0,4},{4,0},{8,12},{12,8},{16,20},{20,16},{24,28},{28,24},{1,5},{5... | collective-permute-start | bytes 405512 | tf_op jit(solution)/shard_map/ppermute | solution.py:28
  35.9 7.2 %collective-permute-start.15 = (f32[256,128]{1,0:T(8,128)S(1)}, f32[256,128]{1,0:T(8,128)S(1)}, u32[]{:S(2)}, u32[]{:S(2)}) collective-permute-start(f32[256,128]{1,0:T(8,128)S(1)} %get-tuple-element.105), channel_id=1, source_target_pairs={{0,5},{1,6},{2,7},{3,4},{4,1},{5,2},{6,3},{7,0},{8,13},{9,14},{10,... | collective-permute-start | bytes 393224 | tf_op jit(solution)/shard_map/ppermute | solution.py:22
  43.4 4.5 %collective-permute-start.17 = (f32[264,128]{1,0:T(8,128)S(1)}, f32[264,128]{1,0:T(8,128)S(1)}, u32[]{:S(2)}, u32[]{:S(2)}) collective-permute-start(f32[264,128]{1,0:T(8,128)S(1)} %shard_map.45), channel_id=1, source_target_pairs={{0,12},{4,16},{8,4},{12,24},{16,28},{20,0},{24,20},{28,8},{1,13},{... | collective-permute-start | bytes 405512 | tf_op jit(solution)/shard_map/ppermute | solution.py:28
  45.2 2.7 %collective-permute-start.16 = (f32[264,128]{1,0:T(8,128)S(1)}, f32[264,128]{1,0:T(8,128)S(1)}, u32[]{:S(2)}, u32[]{:S(2)}) collective-permute-start(f32[264,128]{1,0:T(8,128)S(1)} %shard_map.45), channel_id=1, source_target_pairs={{0,4},{4,0},{8,12},{12,8},{16,20},{20,16},{24,28},{28,24},{1,5},{5... | collective-permute-start | bytes 405512 | tf_op jit(solution)/shard_map/ppermute | solution.py:28
  45.6 2.3 %collective-permute-start.18 = (f32[256,128]{1,0:T(8,128)S(1)}, f32[256,128]{1,0:T(8,128)S(1)}, u32[]{:S(2)}, u32[]{:S(2)}) collective-permute-start(f32[256,128]{1,0:T(8,128)S(1)} %collective-permute-done.15.own_ref.refs_1_.refs_4_), channel_id=1, source_target_pairs={{0,4},{4,0},{8,12},{12,8},{16,20},{20,16},{24,28},{28,24},{1,5},{5... | collective-permute-start | bytes 393224 | tf_op jit(solution)/shard_map/ppermute | solution.py:28
  47.9 4.5 %collective-permute-start.20 = (f32[264,128]{1,0:T(8,128)S(1)}, f32[264,128]{1,0:T(8,128)S(1)}, u32[]{:S(2)}, u32[]{:S(2)}) collective-permute-start(f32[264,128]{1,0:T(8,128)S(1)} %add.31), channel_id=1, source_target_pairs={{0,12},{4,16},{8,4},{12,24},{16,28},{20,0},{24,20},{28,8},{1,13},{... | collective-permute-start | bytes 405512 | tf_op jit(solution)/shard_map/ppermute | solution.py:28
  49.7 2.7 %collective-permute-start.19 = (f32[264,128]{1,0:T(8,128)S(1)}, f32[264,128]{1,0:T(8,128)S(1)}, u32[]{:S(2)}, u32[]{:S(2)}) collective-permute-start(f32[264,128]{1,0:T(8,128)S(1)} %add.31), channel_id=1, source_target_pairs={{0,4},{4,0},{8,12},{12,8},{16,20},{20,16},{24,28},{28,24},{1,5},{5... | collective-permute-start | bytes 405512 | tf_op jit(solution)/shard_map/ppermute | solution.py:28
  52.4 1.4 %collective-permute-start.21 = (f32[264,128]{1,0:T(8,128)S(1)}, f32[264,128]{1,0:T(8,128)S(1)}, u32[]{:S(2)}, u32[]{:S(2)}) collective-permute-start(f32[264,128]{1,0:T(8,128)S(1)} %add.32.own_sum), channel_id=1, source_target_pairs={{0,4},{4,0},{8,12},{12,8},{16,20},{20,16},{24,28},{28,24},{1,5},{5... | collective-permute-start | bytes 405512 | tf_op jit(solution)/shard_map/ppermute | solution.py:28
  55.5 7.4 %collective-permute-start.22 = (f32[128,256]{1,0:T(8,128)S(1)}, f32[128,256]{1,0:T(8,128)S(1)}, u32[]{:S(2)}, u32[]{:S(2)}) collective-permute-start(f32[128,256]{1,0:T(8,128)S(1)} %get-tuple-element.119), channel_id=1, source_target_pairs={{0,6},{1,7},{2,4},{3,5},{4,2},{5,3},{6,0},{7,1},{8,14},{9,15},{10,... | collective-permute-start | bytes 393224 | tf_op jit(solution)/shard_map/ppermute | solution.py:22
  (2 other events, 3.8 us)

commit v15 on v14

--- a/solution.py
+++ b/solution.py
@@ -31,16 +31,20 @@
 def chip_sum(value, beside):
     count = lax.axis_size("pts")
     bit = 2
+    own, known, needed = (value,), (), value
     while bit < count:
         if 2 * bit < count:
             for _ in range(2):
                 near = swapped(value, 1, 1)
-                value = near + swapped(value, bit ^ 1, 2 * bit ^ 1)
+                far = swapped(value, bit ^ 1, 2 * bit ^ 1)
+                own, known, needed = (near, far), (value,), far
+                value = near + far
                 value, beside = lax.optimization_barrier((value, beside))
         else:
             value = value + swapped(value, bit, bit)
+            own, known, needed = (value,), (), value
         bit *= 4
-    return value, beside
+    return own, known, needed, beside
 
 
 def two_parts(value):
@@ -66,12 +70,11 @@
     return jnp.concatenate([value[half:], value[:half]], axis=0)
 
 
-def times_inverse_root(left, square, scale, columns):
+def times_inverse_root(left_parts, square, scale, columns):
     rows = lax.broadcasted_iota(jnp.int32, square.shape, 0)
     identity = jnp.where(rows == lax.broadcasted_iota(jnp.int32, square.shape, 1), 1.0, 0.0)
     base = (identity + square) * (1.0 / scale)
     base_parts = two_parts(base)
-    left_parts = two_parts(left)
     second = product(base_parts, base_parts)
     left_base = product(left_parts, base_parts)
     first_square = two_parts(2.25 * identity - 1.5 * base + 0.25 * second)
@@ -153,8 +156,13 @@
     return slice(rows, 2 * rows) if last else slice(0, rows)
 
 
-def half_kernel(blocks, step, last, damps, own_sum, *refs):
-    *block_refs, own_coupling, own_high, own_low, upper_high, upper_low, left_scale, square, norm, own_mixed = refs
+def total(refs):
+    return sum((ref[...] for ref in refs[1:]), refs[0][...])
+
+
+def half_kernel(addends, blocks, step, last, damps, *refs):
+    *ins, own_coupling, own_high, own_low, upper_high, upper_low, left_scale, square, norm, high, low = refs
+    own_sum, block_refs = total(ins[:addends]), ins[addends:]
     width, half = own_coupling.shape
     upper, lower = blocks(*block_refs)
     inverse = lax.rsqrt(own_sum[width:] + EPSILON)
@@ -166,15 +174,16 @@
     norm[...] = jnp.sum(coupling * coupling, axis=0, keepdims=True)
     parts = own_high[...], own_low[...] = two_parts(coupling)
     square[...] = product(parts, parts, 0, 0)
-    taken = taken_rows(last, own_mixed.shape[0])
+    taken = taken_rows(last, high.shape[0])
     upper_parts = upper_high[...], upper_low[...] = two_parts(upper[taken])
-    own_mixed[...] = lower[taken, :half] + product(upper_parts, parts)
+    high[...], low[...] = two_parts(lower[taken, :half] + product(upper_parts, parts))
 
 
 def lower_kernel(
-    blocks, last, own_high, own_low, upper_high, upper_low, left_scale, own_square, norm, own_mixed, other_sum, *refs
+    addends, blocks, last, own_high, own_low, upper_high, upper_low, left_scale, own_square, norm, high, low, *refs
 ):
-    *block_refs, moved, other_coupling, scale_out = refs
+    *ins, moved, other_coupling, scale_out = refs
+    other_sum, block_refs = total(ins[:addends]), ins[addends:]
     width, half = own_high.shape
     _, lower = blocks(*block_refs)
     inverse = lax.rsqrt(other_sum[width : width + 1] + EPSILON)
@@ -193,7 +202,7 @@
     rows, columns = moved.shape
     taken = taken_rows(last, rows)
     other_mixed = lower[taken, half:] + product((upper_high[...], upper_low[...]), other_parts)
-    mixed = jnp.concatenate([own_mixed[...], other_mixed], axis=1)
+    mixed = [jnp.concatenate(pair, axis=1) for pair in zip((high[...], low[...]), two_parts(other_mixed))]
     result = times_inverse_root(mixed, square, scale, columns)
     if last:
         stored(moved, result)
@@ -207,7 +216,7 @@
     parts = two_parts(coupling)
     mixed = upper[:rows] - product(two_parts(lower[:rows]), parts, 1, 1)
     square = product(parts, parts, 1, 1)
-    return times_inverse_root(mixed, square, scale_ref[0:1, 0:1], coupling.shape[1])
+    return times_inverse_root(two_parts(mixed), square, scale_ref[0:1, 0:1], coupling.shape[1])
 
 
 def upper_kernel(blocks, weight, *refs):
@@ -288,24 +297,26 @@
     damps = lax.optimization_barrier(jnp.broadcast_to(damps[:, None], (STEPS, 128)))
     for step in range(STEPS):
         last = step + 1 == STEPS
-        payload, arriving = chip_sum(payload, arriving)
+        own, known, needed, arriving = chip_sum(payload, arriving)
         held = held + (arriving,)
-        remote = swapped(payload, 1, 1)
+        remote = swapped(needed, 1, 1)
         shape = (rows, width) if last else (2 * rows, half)
         pieces = in_vmem(
-            functools.partial(half_kernel, blocks, step, last),
+            functools.partial(half_kernel, len(own), blocks, step, last),
             [((width, half), F32)]
             + [((width, half), jnp.bfloat16)] * 2
             + [((shape[0], width), jnp.bfloat16)] * 2
-            + [((width, half), F32), ((half, half), F32), ((1, half), F32), ((shape[0], half), F32)],
+            + [((width, half), F32), ((half, half), F32), ((1, half), F32)]
+            + [((shape[0], half), jnp.bfloat16)] * 2,
             damps,
-            payload,
+            *own,
             *held,
         )
         moved, other_coupling, scale = in_vmem(
-            functools.partial(lower_kernel, blocks, last),
+            functools.partial(lower_kernel, len(known) + 1, blocks, last),
             [(shape, F32), ((width, half), F32), ((8, 128), F32)],
             *pieces[1:],
+            *known,
             remote,
             *held,
         )

time: 63.7 us -> 64.4 us (1.011)
  waiting for transfers between devices: 29.6 us -> 32.7 us
  starting transfers between devices: 18 us -> 15.6 us
    ppermute x20, waiting for transfers between devices: 16.9 us -> 19.8 us  [swapped(): return lax.ppermute(value, 'pts', pairs)]
    ppermute x20, starting transfers between devices: 16.1 us -> 13.6 us  [swapped(): return lax.ppermute(value, 'pts', pairs)]
where the time goes in v15:
time: 64.4 us; the launch traced here: 64.2 us
  waiting for transfers between devices  32.7 us (51%)
  starting transfers between devices  15.6 us (24%)
  Pallas kernels  15.4 us (24%)
    ppermute x20, waiting for transfers between devices, swapped(): return lax.ppermute(value, 'pts', pairs)  19.8 us
    ppermute x20, starting transfers between devices, swapped(): return lax.ppermute(value, 'pts', pairs)  13.6 us
    ppermute x3, waiting for transfers between devices, column_shift(): return lax.ppermute(value, ('pts', 'cols'), pairs)  12.9 us
    pallas_call x10, Pallas kernels, in_vmem(): pl.pallas_call(kernel, out_shape=[jax.ShapeDtypeStruct(shape, dtype) for...  11 us
    pallas_call x1, Pallas kernels, body(): pl.pallas_call(functools.partial(last_upper_kernel, blocks), out_shape=ou...  2.32 us
    ppermute x3, starting transfers between devices, column_shift(): return lax.ppermute(value, ('pts', 'cols'), pairs)  1.97 us
    pallas_call x1, Pallas kernels, body(): pl.pallas_call(start_kernel, out_shape=[jax.ShapeDtypeStruct((width + 8,...  1.45 us
  transfers between devices with their start and end apart: 23, of which 14 were waited for; matrix products, arithmetic and copies ran while one was open for 0% of the time, Pallas kernels for 12%

profile of v15, /device:TPU:0, one launch (start us, length us, event | category | flops | bytes accessed | tf_op | source)
XLA Modules:
  0.0 64.2 jit_solution(2232128100663313504)
XLA Ops:
  0.0 1.5 %shard_map.37 = (f32[264,128]{1,0:T(8,128)S(1)}, f32[264,128]{1,0:T(8,128)S(1)}) custom-call(f32[128,512]{1,0:T(8,128)} %refs_3_.1, f32[1,128]{1,0:T(1,128)} %bitcast.5), custom_call_target="tpu_custom_call" | custom-call | tf_op jit(solution)/shard_map/pallas_call | solution.py:279
  3.4 2.6 %collective-permute-start.3 = (f32[264,128]{1,0:T(8,128)S(1)}, f32[264,128]{1,0:T(8,128)S(1)}, u32[]{:S(2)}, u32[]{:S(2)}) collective-permute-start(f32[264,128]{1,0:T(8,128)S(1)} %add.20), channel_id=1, source_target_pairs={{0,12},{4,16},{8,4},{12,24},{16,28},{20,0},{24,20},{28,8},{1,13},{... | collective-permute-start | bytes 405512 | tf_op jit(solution)/shard_map/ppermute | solution.py:28
  6.0 2.7 %collective-permute-done.3 = f32[264,128]{1,0:T(8,128)S(1)} collective-permute-done((f32[264,128]{1,0:T(8,128)S(1)}, f32[264,128]{1,0:T(8,128)S(1)}, u32[]{:S(2)}, u32[]{:S(2)}) %collective-permute-start.3) | collective-permute-done | bytes 135200 | tf_op jit(solution)/shard_map/ppermute | solution.py:28
  8.8 1.8 %collective-permute-start.6 = (f32[264,128]{1,0:T(8,128)S(1)}, f32[264,128]{1,0:T(8,128)S(1)}, u32[]{:S(2)}, u32[]{:S(2)}) collective-permute-start(f32[264,128]{1,0:T(8,128)S(1)} %add.21.refs_0_), channel_id=1, source_target_pairs={{0,12},{4,16},{8,4},{12,24},{16,28},{20,0},{24,20},{28,8},{1,13},{... | collective-permute-start | bytes 405512 | tf_op jit(solution)/shard_map/ppermute | solution.py:28
  10.7 2.5 %collective-permute-done.6.refs_1_ = f32[264,128]{1,0:T(8,128)S(1)} collective-permute-done((f32[264,128]{1,0:T(8,128)S(1)}, f32[264,128]{1,0:T(8,128)S(1)}, u32[]{:S(2)}, u32[]{:S(2)}) %collective-permute-start.6) | collective-permute-done | bytes 135200 | tf_op jit(solution)/shard_map/ppermute | solution.py:28
  14.6 1.7 %shard_map.39 = (f32[256,128]{1,0:T(8,128)S(1)}, f32[256,128]{1,0:T(8,128)S(1)}, f32[8,128]{1,0:T(8,128)S(1)}) custom-call(bf16[256,128]{1,0:T(8,128)(2,1)S(1)} %get-tuple-element.69.own_high, bf16[256,128]{1,0:T(8,128)(2,1)S(1)} %get-tuple-element.70.own_low, bf16[256,256]{1,0:T(8,128)(2,1)S(1)} %get-tuple-element.71.upper_high, ...), custom_call_target="tpu_custom_call" | custom-call | tf_op jit(solution)/shard_map/pallas_call | solution.py:265
  16.3 1.8 %collective-permute-start.8 = (f32[256,128]{1,0:T(8,128)S(1)}, f32[256,128]{1,0:T(8,128)S(1)}, u32[]{:S(2)}, u32[]{:S(2)}) collective-permute-start(f32[256,128]{1,0:T(8,128)S(1)} %get-tuple-element.82), channel_id=1, source_target_pairs={{0,5},{1,6},{2,7},{3,4},{4,1},{5,2},{6,3},{7,0},{8,13},{9,14},{10,... | collective-permute-start | bytes 393224 | tf_op jit(solution)/shard_map/ppermute | solution.py:22
  18.3 1.0 %collective-permute-done = f32[128]{0:T(128)S(1)} collective-permute-done((f32[128]{0:T(128)S(1)}, f32[128]{0:T(128)S(1)}, u32[]{:S(2)}, u32[]{:S(2)}) %collective-permute-start) | collective-permute-done | bytes 544 | tf_op jit(solution)/shard_map/ppermute | solution.py:28
  19.4 1.9 %shard_map.40 = (bf16[256,768]{1,0:T(8,128)(2,1)S(1)}, f32[1,256]{1,0:T(1,128)S(1)}, f32[256,256]{1,0:T(8,128)S(1)}) custom-call(f32[256,1]{1,0:T(8,128)S(1)} %copy.7.weight, f32[256,128]{1,0:T(8,128)S(1)} %get-tuple-element.68.refs_0_, f32[256,128]{1,0:T(8,128)S(1)} %get-tuple-element.78.refs_1_, f32[8,128]{1,0:T(8,128)S(1)} %get-tuple-element.79.refs_2_, ...), custom_call_target="tpu_custom_call" | custom-call | tf_op jit(solution)/shard_map/pallas_call | solution.py:265
  21.3 2.6 %collective-permute-done.8.own_ref.refs_3_.refs_4_ = f32[256,128]{1,0:T(8,128)S(1)} collective-permute-done((f32[256,128]{1,0:T(8,128)S(1)}, f32[256,128]{1,0:T(8,128)S(1)}, u32[]{:S(2)}, u32[]{:S(2)}) %collective-permute-start.8) | collective-permute-done | bytes 131104 | tf_op jit(solution)/shard_map/ppermute | solution.py:22
  24.4 1.3 %collective-permute-start.10 = (f32[264,128]{1,0:T(8,128)S(1)}, f32[264,128]{1,0:T(8,128)S(1)}, u32[]{:S(2)}, u32[]{:S(2)}) collective-permute-start(f32[264,128]{1,0:T(8,128)S(1)} %shard_map.41), channel_id=1, source_target_pairs={{0,12},{4,16},{8,4},{12,24},{16,28},{20,0},{24,20},{28,8},{1,13},{... | collective-permute-start | bytes 405512 | tf_op jit(solution)/shard_map/ppermute | solution.py:28
  26.0 2.8 %collective-permute-done.10 = f32[264,128]{1,0:T(8,128)S(1)} collective-permute-done((f32[264,128]{1,0:T(8,128)S(1)}, f32[264,128]{1,0:T(8,128)S(1)}, u32[]{:S(2)}, u32[]{:S(2)}) %collective-permute-start.10) | collective-permute-done | bytes 135200 | tf_op jit(solution)/shard_map/ppermute | solution.py:28
  28.9 1.4 %collective-permute-start.13 = (f32[264,128]{1,0:T(8,128)S(1)}, f32[264,128]{1,0:T(8,128)S(1)}, u32[]{:S(2)}, u32[]{:S(2)}) collective-permute-start(f32[264,128]{1,0:T(8,128)S(1)} %add.22.refs_0_), channel_id=1, source_target_pairs={{0,12},{4,16},{8,4},{12,24},{16,28},{20,0},{24,20},{28,8},{1,13},{... | collective-permute-start | bytes 405512 | tf_op jit(solution)/shard_map/ppermute | solution.py:28
  30.6 2.8 %collective-permute-done.13.refs_1_ = f32[264,128]{1,0:T(8,128)S(1)} collective-permute-done((f32[264,128]{1,0:T(8,128)S(1)}, f32[264,128]{1,0:T(8,128)S(1)}, u32[]{:S(2)}, u32[]{:S(2)}) %collective-permute-start.13) | collective-permute-done | bytes 135200 | tf_op jit(solution)/shard_map/ppermute | solution.py:28
  34.7 1.7 %shard_map.43 = (f32[256,128]{1,0:T(8,128)S(1)}, f32[256,128]{1,0:T(8,128)S(1)}, f32[8,128]{1,0:T(8,128)S(1)}) custom-call(bf16[256,128]{1,0:T(8,128)(2,1)S(1)} %get-tuple-element.87.own_high, bf16[256,128]{1,0:T(8,128)(2,1)S(1)} %get-tuple-element.88.own_low, bf16[256,256]{1,0:T(8,128)(2,1)S(1)} %get-tuple-element.89.upper_high, ...), custom_call_target="tpu_custom_call" | custom-call | tf_op jit(solution)/shard_map/pallas_call | solution.py:265
  36.5 1.9 %shard_map.44 = (bf16[256,768]{1,0:T(8,128)(2,1)S(1)}, f32[1,256]{1,0:T(1,128)S(1)}, f32[256,256]{1,0:T(8,128)S(1)}) custom-call(f32[256,1]{1,0:T(8,128)S(1)} %copy.7.weight, f32[256,128]{1,0:T(8,128)S(1)} %get-tuple-element.86.refs_0_, f32[256,128]{1,0:T(8,128)S(1)} %get-tuple-element.96.refs_1_, f32[8,128]{1,0:T(8,128)S(1)} %get-tuple-element.97.refs_2_, ...), custom_call_target="tpu_custom_call" | custom-call | tf_op jit(solution)/shard_map/pallas_call | solution.py:265
  38.3 5.2 %collective-permute-done.15.own_ref.refs_3_.refs_4_ = f32[256,128]{1,0:T(8,128)S(1)} collective-permute-done((f32[256,128]{1,0:T(8,128)S(1)}, f32[256,128]{1,0:T(8,128)S(1)}, u32[]{:S(2)}, u32[]{:S(2)}) %collective-permute-start.15) | collective-permute-done | bytes 131104 | tf_op jit(solution)/shard_map/ppermute | solution.py:22
  44.2 1.4 %collective-permute-start.17 = (f32[264,128]{1,0:T(8,128)S(1)}, f32[264,128]{1,0:T(8,128)S(1)}, u32[]{:S(2)}, u32[]{:S(2)}) collective-permute-start(f32[264,128]{1,0:T(8,128)S(1)} %shard_map.45), channel_id=1, source_target_pairs={{0,12},{4,16},{8,4},{12,24},{16,28},{20,0},{24,20},{28,8},{1,13},{... | collective-permute-start | bytes 405512 | tf_op jit(solution)/shard_map/ppermute | solution.py:28
  45.8 2.8 %collective-permute-done.17 = f32[264,128]{1,0:T(8,128)S(1)} collective-permute-done((f32[264,128]{1,0:T(8,128)S(1)}, f32[264,128]{1,0:T(8,128)S(1)}, u32[]{:S(2)}, u32[]{:S(2)}) %collective-permute-start.17) | collective-permute-done | bytes 135200 | tf_op jit(solution)/shard_map/ppermute | solution.py:28
  48.7 1.5 %collective-permute-start.20 = (f32[264,128]{1,0:T(8,128)S(1)}, f32[264,128]{1,0:T(8,128)S(1)}, u32[]{:S(2)}, u32[]{:S(2)}) collective-permute-start(f32[264,128]{1,0:T(8,128)S(1)} %add.23.refs_0_), channel_id=1, source_target_pairs={{0,12},{4,16},{8,4},{12,24},{16,28},{20,0},{24,20},{28,8},{1,13},{... | collective-permute-start | bytes 405512 | tf_op jit(solution)/shard_map/ppermute | solution.py:28
  50.3 2.8 %collective-permute-done.20.refs_1_ = f32[264,128]{1,0:T(8,128)S(1)} collective-permute-done((f32[264,128]{1,0:T(8,128)S(1)}, f32[264,128]{1,0:T(8,128)S(1)}, u32[]{:S(2)}, u32[]{:S(2)}) %collective-permute-start.20) | collective-permute-done | bytes 135200 | tf_op jit(solution)/shard_map/ppermute | solution.py:28
  54.5 1.7 %shard_map.47 = (f32[128,256]{1,0:T(8,128)S(1)}, f32[256,128]{1,0:T(8,128)S(1)}, f32[8,128]{1,0:T(8,128)S(1)}) custom-call(bf16[256,128]{1,0:T(8,128)(2,1)S(1)} %get-tuple-element.104.own_high, bf16[256,128]{1,0:T(8,128)(2,1)S(1)} %get-tuple-element.105.own_low, bf16[128,256]{1,0:T(8,128)(2,1)S(1)} %get-tuple-element.106.upper_high, ...), custom_call_target="tpu_custom_call" | custom-call | tf_op jit(solution)/shard_map/pallas_call | solution.py:265
  56.2 2.3 %shard_map.48.filled = f32[128,512]{1,0:T(8,128)} custom-call(f32[256,128]{1,0:T(8,128)S(1)} %get-tuple-element.114.refs_0_, f32[256,128]{1,0:T(8,128)S(1)} %get-tuple-element.115.refs_1_, f32[8,128]{1,0:T(8,128)S(1)} %get-tuple-element.116.refs_2_, f32[256,256]{1,0:T(8,128)S(1)} %get-tuple-element.102.refs_2_.refs_3_, ...), custom_call_target="tpu_custom_call" | custom-call | tf_op jit(solution)/shard_map/pallas_call | solution.py:339
  58.6 5.0 %collective-permute-done.22.lower = f32[128,256]{1,0:T(8,128)S(1)} collective-permute-done((f32[128,256]{1,0:T(8,128)S(1)}, f32[128,256]{1,0:T(8,128)S(1)}, u32[]{:S(2)}, u32[]{:S(2)}) %collective-permute-start.22) | collective-permute-done | bytes 131104 | tf_op jit(solution)/shard_map/ppermute | solution.py:22
  (49 shorter events, 9.4 us)
Async XLA Ops:
  1.5 1.5 %collective-permute-start.1 = (f32[264,128]{1,0:T(8,128)S(1)}, f32[264,128]{1,0:T(8,128)S(1)}, u32[]{:S(2)}, u32[]{:S(2)}) collective-permute-start(f32[264,128]{1,0:T(8,128)S(1)} %get-tuple-element.65), channel_id=1, source_target_pairs={{0,4},{4,0},{8,12},{12,8},{16,20},{20,16},{24,28},{28,24},{1,5},{5... | collective-permute-start | bytes 405512 | tf_op jit(solution)/shard_map/ppermute | solution.py:28
  2.0 6.8 %collective-permute-start.4 = (f32[128,512]{1,0:T(8,128)S(1)}, f32[128,512]{1,0:T(8,128)S(1)}, u32[]{:S(2)}, u32[]{:S(2)}) collective-permute-start(f32[128,512]{1,0:T(8,128)S(1)} %copy-done), channel_id=1, source_target_pairs={{0,4},{4,0},{8,12},{12,8},{16,20},{20,16},{24,28},{28,24},{1,5},{5... | collective-permute-start | bytes 786440 | tf_op jit(solution)/shard_map/ppermute | solution.py:28
  3.0 10.4 %copy-start.2 = (s32[3,2]{0,1:T(2,128)S(1)}, s32[3,2]{0,1:T(2,128)}, u32[]{:S(2)}) copy-start(s32[3,2]{0,1:T(2,128)} %param.5) | copy-start | bytes 76
  3.0 3.0 %collective-permute-start.2 = (f32[264,128]{1,0:T(8,128)S(1)}, f32[264,128]{1,0:T(8,128)S(1)}, u32[]{:S(2)}, u32[]{:S(2)}) collective-permute-start(f32[264,128]{1,0:T(8,128)S(1)} %add.20), channel_id=1, source_target_pairs={{0,4},{4,0},{8,12},{12,8},{16,20},{20,16},{24,28},{28,24},{1,5},{5... | collective-permute-start | bytes 405512 | tf_op jit(solution)/shard_map/ppermute | solution.py:28
  3.4 5.3 %collective-permute-start.3 = (f32[264,128]{1,0:T(8,128)S(1)}, f32[264,128]{1,0:T(8,128)S(1)}, u32[]{:S(2)}, u32[]{:S(2)}) collective-permute-start(f32[264,128]{1,0:T(8,128)S(1)} %add.20), channel_id=1, source_target_pairs={{0,12},{4,16},{8,4},{12,24},{16,28},{20,0},{24,20},{28,8},{1,13},{... | collective-permute-start | bytes 405512 | tf_op jit(solution)/shard_map/ppermute | solution.py:28
  8.8 4.5 %collective-permute-start.6 = (f32[264,128]{1,0:T(8,128)S(1)}, f32[264,128]{1,0:T(8,128)S(1)}, u32[]{:S(2)}, u32[]{:S(2)}) collective-permute-start(f32[264,128]{1,0:T(8,128)S(1)} %add.21.refs_0_), channel_id=1, source_target_pairs={{0,12},{4,16},{8,4},{12,24},{16,28},{20,0},{24,20},{28,8},{1,13},{... | collective-permute-start | bytes 405512 | tf_op jit(solution)/shard_map/ppermute | solution.py:28
  10.6 2.9 %collective-permute-start.5 = (f32[264,128]{1,0:T(8,128)S(1)}, f32[264,128]{1,0:T(8,128)S(1)}, u32[]{:S(2)}, u32[]{:S(2)}) collective-permute-start(f32[264,128]{1,0:T(8,128)S(1)} %add.21.refs_0_), channel_id=1, source_target_pairs={{0,4},{4,0},{8,12},{12,8},{16,20},{20,16},{24,28},{28,24},{1,5},{5... | collective-permute-start | bytes 405512 | tf_op jit(solution)/shard_map/ppermute | solution.py:28
  13.3 1.4 %collective-permute-start.7 = (f32[264,128]{1,0:T(8,128)S(1)}, f32[264,128]{1,0:T(8,128)S(1)}, u32[]{:S(2)}, u32[]{:S(2)}) collective-permute-start(f32[264,128]{1,0:T(8,128)S(1)} %collective-permute-done.6.refs_1_), channel_id=1, source_target_pairs={{0,4},{4,0},{8,12},{12,8},{16,20},{20,16},{24,28},{28,24},{1,5},{5... | collective-permute-start | bytes 405512 | tf_op jit(solution)/shard_map/ppermute | solution.py:28
  16.3 7.6 %collective-permute-start.8 = (f32[256,128]{1,0:T(8,128)S(1)}, f32[256,128]{1,0:T(8,128)S(1)}, u32[]{:S(2)}, u32[]{:S(2)}) collective-permute-start(f32[256,128]{1,0:T(8,128)S(1)} %get-tuple-element.82), channel_id=1, source_target_pairs={{0,5},{1,6},{2,7},{3,4},{4,1},{5,2},{6,3},{7,0},{8,13},{9,14},{10,... | collective-permute-start | bytes 393224 | tf_op jit(solution)/shard_map/ppermute | solution.py:22
  18.2 1.1 %collective-permute-start = (f32[128]{0:T(128)S(1)}, f32[128]{0:T(128)S(1)}, u32[]{:S(2)}, u32[]{:S(2)}) collective-permute-start(f32[128]{0:T(128)S(1)} %copy-done.1), channel_id=1, source_target_pairs={{0,4},{4,0},{8,12},{12,8},{16,20},{20,16},{24,28},{28,24},{1,5},{5... | collective-permute-start | bytes 1544 | tf_op jit(solution)/shard_map/ppermute | solution.py:28
  24.2 1.8 %collective-permute-start.9 = (f32[264,128]{1,0:T(8,128)S(1)}, f32[264,128]{1,0:T(8,128)S(1)}, u32[]{:S(2)}, u32[]{:S(2)}) collective-permute-start(f32[264,128]{1,0:T(8,128)S(1)} %shard_map.41), channel_id=1, source_target_pairs={{0,4},{4,0},{8,12},{12,8},{16,20},{20,16},{24,28},{28,24},{1,5},{5... | collective-permute-start | bytes 405512 | tf_op jit(solution)/shard_map/ppermute | solution.py:28
  24.4 4.4 %collective-permute-start.10 = (f32[264,128]{1,0:T(8,128)S(1)}, f32[264,128]{1,0:T(8,128)S(1)}, u32[]{:S(2)}, u32[]{:S(2)}) collective-permute-start(f32[264,128]{1,0:T(8,128)S(1)} %shard_map.41), channel_id=1, source_target_pairs={{0,12},{4,16},{8,4},{12,24},{16,28},{20,0},{24,20},{28,8},{1,13},{... | collective-permute-start | bytes 405512 | tf_op jit(solution)/shard_map/ppermute | solution.py:28
  25.7 3.1 %collective-permute-start.11 = (f32[256,128]{1,0:T(8,128)S(1)}, f32[256,128]{1,0:T(8,128)S(1)}, u32[]{:S(2)}, u32[]{:S(2)}) collective-permute-start(f32[256,128]{1,0:T(8,128)S(1)} %collective-permute-done.8.own_ref.refs_3_.refs_4_), channel_id=1, source_target_pairs={{0,4},{4,0},{8,12},{12,8},{16,20},{20,16},{24,28},{28,24},{1,5},{5... | collective-permute-start | bytes 393224 | tf_op jit(solution)/shard_map/ppermute | solution.py:28
  28.9 4.5 %collective-permute-start.13 = (f32[264,128]{1,0:T(8,128)S(1)}, f32[264,128]{1,0:T(8,128)S(1)}, u32[]{:S(2)}, u32[]{:S(2)}) collective-permute-start(f32[264,128]{1,0:T(8,128)S(1)} %add.22.refs_0_), channel_id=1, source_target_pairs={{0,12},{4,16},{8,4},{12,24},{16,28},{20,0},{24,20},{28,8},{1,13},{... | collective-permute-start | bytes 405512 | tf_op jit(solution)/shard_map/ppermute | solution.py:28
  30.3 3.5 %collective-permute-start.12 = (f32[264,128]{1,0:T(8,128)S(1)}, f32[264,128]{1,0:T(8,128)S(1)}, u32[]{:S(2)}, u32[]{:S(2)}) collective-permute-start(f32[264,128]{1,0:T(8,128)S(1)} %add.22.refs_0_), channel_id=1, source_target_pairs={{0,4},{4,0},{8,12},{12,8},{16,20},{20,16},{24,28},{28,24},{1,5},{5... | collective-permute-start | bytes 405512 | tf_op jit(solution)/shard_map/ppermute | solution.py:28
  33.4 1.4 %collective-permute-start.14 = (f32[264,128]{1,0:T(8,128)S(1)}, f32[264,128]{1,0:T(8,128)S(1)}, u32[]{:S(2)}, u32[]{:S(2)}) collective-permute-start(f32[264,128]{1,0:T(8,128)S(1)} %collective-permute-done.13.refs_1_), channel_id=1, source_target_pairs={{0,4},{4,0},{8,12},{12,8},{16,20},{20,16},{24,28},{28,24},{1,5},{5... | collective-permute-start | bytes 405512 | tf_op jit(solution)/shard_map/ppermute | solution.py:28
  36.4 7.2 %collective-permute-start.15 = (f32[256,128]{1,0:T(8,128)S(1)}, f32[256,128]{1,0:T(8,128)S(1)}, u32[]{:S(2)}, u32[]{:S(2)}) collective-permute-start(f32[256,128]{1,0:T(8,128)S(1)} %get-tuple-element.100), channel_id=1, source_target_pairs={{0,5},{1,6},{2,7},{3,4},{4,1},{5,2},{6,3},{7,0},{8,13},{9,14},{10,... | collective-permute-start | bytes 393224 | tf_op jit(solution)/shard_map/ppermute | solution.py:22
  43.8 2.0 %collective-permute-start.16 = (f32[264,128]{1,0:T(8,128)S(1)}, f32[264,128]{1,0:T(8,128)S(1)}, u32[]{:S(2)}, u32[]{:S(2)}) collective-permute-start(f32[264,128]{1,0:T(8,128)S(1)} %shard_map.45), channel_id=1, source_target_pairs={{0,4},{4,0},{8,12},{12,8},{16,20},{20,16},{24,28},{28,24},{1,5},{5... | collective-permute-start | bytes 405512 | tf_op jit(solution)/shard_map/ppermute | solution.py:28
  44.2 4.4 %collective-permute-start.17 = (f32[264,128]{1,0:T(8,128)S(1)}, f32[264,128]{1,0:T(8,128)S(1)}, u32[]{:S(2)}, u32[]{:S(2)}) collective-permute-start(f32[264,128]{1,0:T(8,128)S(1)} %shard_map.45), channel_id=1, source_target_pairs={{0,12},{4,16},{8,4},{12,24},{16,28},{20,0},{24,20},{28,8},{1,13},{... | collective-permute-start | bytes 405512 | tf_op jit(solution)/shard_map/ppermute | solution.py:28
  45.6 3.0 %collective-permute-start.18 = (f32[256,128]{1,0:T(8,128)S(1)}, f32[256,128]{1,0:T(8,128)S(1)}, u32[]{:S(2)}, u32[]{:S(2)}) collective-permute-start(f32[256,128]{1,0:T(8,128)S(1)} %collective-permute-done.15.own_ref.refs_3_.refs_4_), channel_id=1, source_target_pairs={{0,4},{4,0},{8,12},{12,8},{16,20},{20,16},{24,28},{28,24},{1,5},{5... | collective-permute-start | bytes 393224 | tf_op jit(solution)/shard_map/ppermute | solution.py:28
  48.7 4.5 %collective-permute-start.20 = (f32[264,128]{1,0:T(8,128)S(1)}, f32[264,128]{1,0:T(8,128)S(1)}, u32[]{:S(2)}, u32[]{:S(2)}) collective-permute-start(f32[264,128]{1,0:T(8,128)S(1)} %add.23.refs_0_), channel_id=1, source_target_pairs={{0,12},{4,16},{8,4},{12,24},{16,28},{20,0},{24,20},{28,8},{1,13},{... | collective-permute-start | bytes 405512 | tf_op jit(solution)/shard_map/ppermute | solution.py:28
  50.1 3.2 %collective-permute-start.19 = (f32[264,128]{1,0:T(8,128)S(1)}, f32[264,128]{1,0:T(8,128)S(1)}, u32[]{:S(2)}, u32[]{:S(2)}) collective-permute-start(f32[264,128]{1,0:T(8,128)S(1)} %add.23.refs_0_), channel_id=1, source_target_pairs={{0,4},{4,0},{8,12},{12,8},{16,20},{20,16},{24,28},{28,24},{1,5},{5... | collective-permute-start | bytes 405512 | tf_op jit(solution)/shard_map/ppermute | solution.py:28
  53.1 1.4 %collective-permute-start.21 = (f32[264,128]{1,0:T(8,128)S(1)}, f32[264,128]{1,0:T(8,128)S(1)}, u32[]{:S(2)}, u32[]{:S(2)}) collective-permute-start(f32[264,128]{1,0:T(8,128)S(1)} %collective-permute-done.20.refs_1_), channel_id=1, source_target_pairs={{0,4},{4,0},{8,12},{12,8},{16,20},{20,16},{24,28},{28,24},{1,5},{5... | collective-permute-start | bytes 405512 | tf_op jit(solution)/shard_map/ppermute | solution.py:28
  56.2 7.4 %collective-permute-start.22 = (f32[128,256]{1,0:T(8,128)S(1)}, f32[128,256]{1,0:T(8,128)S(1)}, u32[]{:S(2)}, u32[]{:S(2)}) collective-permute-start(f32[128,256]{1,0:T(8,128)S(1)} %get-tuple-element.113), channel_id=1, source_target_pairs={{0,6},{1,7},{2,4},{3,5},{4,2},{5,3},{6,0},{7,1},{8,14},{9,15},{10,... | collective-permute-start | bytes 393224 | tf_op jit(solution)/shard_map/ppermute | solution.py:22
  (2 other events, 3.8 us)

commit v16 on v15

--- a/solution.py
+++ b/solution.py
@@ -38,7 +38,7 @@
                 near = swapped(value, 1, 1)
                 far = swapped(value, bit ^ 1, 2 * bit ^ 1)
                 own, known, needed = (near, far), (value,), far
-                value = near + far
+                value = far + near
                 value, beside = lax.optimization_barrier((value, beside))
         else:
             value = value + swapped(value, bit, bit)

time: 64.4 us -> 63.5 us (0.986)
  waiting for transfers between devices: 32.7 us -> 29.8 us
  starting transfers between devices: 15.6 us -> 17.7 us
    ppermute x20, waiting for transfers between devices: 19.8 us -> 17 us  [swapped(): return lax.ppermute(value, 'pts', pairs)]
    ppermute x20, starting transfers between devices: 13.6 us -> 15.7 us  [swapped(): return lax.ppermute(value, 'pts', pairs)]
where the time goes in v16:
time: 63.5 us; the launch traced here: 63.3 us
  waiting for transfers between devices  29.8 us (47%)
  starting transfers between devices  17.7 us (28%)
  Pallas kernels  15.4 us (24%)
    ppermute x20, waiting for transfers between devices, swapped(): return lax.ppermute(value, 'pts', pairs)  17 us
    ppermute x20, starting transfers between devices, swapped(): return lax.ppermute(value, 'pts', pairs)  15.7 us
    ppermute x3, waiting for transfers between devices, column_shift(): return lax.ppermute(value, ('pts', 'cols'), pairs)  12.8 us
    pallas_call x10, Pallas kernels, in_vmem(): pl.pallas_call(kernel, out_shape=[jax.ShapeDtypeStruct(shape, dtype) for...  11 us
    pallas_call x1, Pallas kernels, body(): pl.pallas_call(functools.partial(last_upper_kernel, blocks), out_shape=ou...  2.33 us
    ppermute x3, starting transfers between devices, column_shift(): return lax.ppermute(value, ('pts', 'cols'), pairs)  1.99 us
    pallas_call x1, Pallas kernels, body(): pl.pallas_call(start_kernel, out_shape=[jax.ShapeDtypeStruct((width + 8,...  1.45 us
  transfers between devices with their start and end apart: 23, of which 14 were waited for; matrix products, arithmetic and copies ran while one was open for 0% of the time, Pallas kernels for 12%

profile of v16, /device:TPU:0, one launch (start us, length us, event | category | flops | bytes accessed | tf_op | source)
XLA Modules:
  0.0 63.3 jit_solution(4001333289344732114)
XLA Ops:
  0.0 1.5 %shard_map.37 = (f32[264,128]{1,0:T(8,128)S(1)}, f32[264,128]{1,0:T(8,128)S(1)}) custom-call(f32[128,512]{1,0:T(8,128)} %refs_3_.1, f32[1,128]{1,0:T(1,128)} %bitcast.5), custom_call_target="tpu_custom_call" | custom-call | tf_op jit(solution)/shard_map/pallas_call | solution.py:279
  2.1 0.9 %collective-permute-done.1 = f32[264,128]{1,0:T(8,128)S(1)} collective-permute-done((f32[264,128]{1,0:T(8,128)S(1)}, f32[264,128]{1,0:T(8,128)S(1)}, u32[]{:S(2)}, u32[]{:S(2)}) %collective-permute-start.1) | collective-permute-done | bytes 135200 | tf_op jit(solution)/shard_map/ppermute | solution.py:28
  3.0 2.7 %collective-permute-start.2 = (f32[264,128]{1,0:T(8,128)S(1)}, f32[264,128]{1,0:T(8,128)S(1)}, u32[]{:S(2)}, u32[]{:S(2)}) collective-permute-start(f32[264,128]{1,0:T(8,128)S(1)} %add.20), channel_id=1, source_target_pairs={{0,12},{4,16},{8,4},{12,24},{16,28},{20,0},{24,20},{28,8},{1,13},{... | collective-permute-start | bytes 405512 | tf_op jit(solution)/shard_map/ppermute | solution.py:28
  6.0 2.3 %collective-permute-done.2 = f32[264,128]{1,0:T(8,128)S(1)} collective-permute-done((f32[264,128]{1,0:T(8,128)S(1)}, f32[264,128]{1,0:T(8,128)S(1)}, u32[]{:S(2)}, u32[]{:S(2)}) %collective-permute-start.2) | collective-permute-done | bytes 135200 | tf_op jit(solution)/shard_map/ppermute | solution.py:28
  8.4 1.8 %collective-permute-start.6 = (f32[264,128]{1,0:T(8,128)S(1)}, f32[264,128]{1,0:T(8,128)S(1)}, u32[]{:S(2)}, u32[]{:S(2)}) collective-permute-start(f32[264,128]{1,0:T(8,128)S(1)} %add.21.refs_0_), channel_id=1, source_target_pairs={{0,12},{4,16},{8,4},{12,24},{16,28},{20,0},{24,20},{28,8},{1,13},{... | collective-permute-start | bytes 405512 | tf_op jit(solution)/shard_map/ppermute | solution.py:28
  10.6 2.3 %collective-permute-done.6.refs_1_ = f32[264,128]{1,0:T(8,128)S(1)} collective-permute-done((f32[264,128]{1,0:T(8,128)S(1)}, f32[264,128]{1,0:T(8,128)S(1)}, u32[]{:S(2)}, u32[]{:S(2)}) %collective-permute-start.6) | collective-permute-done | bytes 135200 | tf_op jit(solution)/shard_map/ppermute | solution.py:28
  14.3 1.7 %shard_map.39 = (f32[256,128]{1,0:T(8,128)S(1)}, f32[256,128]{1,0:T(8,128)S(1)}, f32[8,128]{1,0:T(8,128)S(1)}) custom-call(bf16[256,128]{1,0:T(8,128)(2,1)S(1)} %get-tuple-element.69.own_high, bf16[256,128]{1,0:T(8,128)(2,1)S(1)} %get-tuple-element.70.own_low, bf16[256,256]{1,0:T(8,128)(2,1)S(1)} %get-tuple-element.71.upper_high, ...), custom_call_target="tpu_custom_call" | custom-call | tf_op jit(solution)/shard_map/pallas_call | solution.py:265
  15.9 1.9 %collective-permute-start.8 = (f32[256,128]{1,0:T(8,128)S(1)}, f32[256,128]{1,0:T(8,128)S(1)}, u32[]{:S(2)}, u32[]{:S(2)}) collective-permute-start(f32[256,128]{1,0:T(8,128)S(1)} %get-tuple-element.82), channel_id=1, source_target_pairs={{0,5},{1,6},{2,7},{3,4},{4,1},{5,2},{6,3},{7,0},{8,13},{9,14},{10,... | collective-permute-start | bytes 393224 | tf_op jit(solution)/shard_map/ppermute | solution.py:22
  19.1 1.9 %shard_map.40 = (bf16[256,768]{1,0:T(8,128)(2,1)S(1)}, f32[1,256]{1,0:T(1,128)S(1)}, f32[256,256]{1,0:T(8,128)S(1)}) custom-call(f32[256,1]{1,0:T(8,128)S(1)} %copy.7.weight, f32[256,128]{1,0:T(8,128)S(1)} %get-tuple-element.68.refs_0_, f32[256,128]{1,0:T(8,128)S(1)} %get-tuple-element.78.refs_1_, f32[8,128]{1,0:T(8,128)S(1)} %get-tuple-element.79.refs_2_, ...), custom_call_target="tpu_custom_call" | custom-call | tf_op jit(solution)/shard_map/pallas_call | solution.py:265
  21.0 2.4 %collective-permute-done.8.own_ref.refs_3_.refs_4_ = f32[256,128]{1,0:T(8,128)S(1)} collective-permute-done((f32[256,128]{1,0:T(8,128)S(1)}, f32[256,128]{1,0:T(8,128)S(1)}, u32[]{:S(2)}, u32[]{:S(2)}) %collective-permute-start.8) | collective-permute-done | bytes 131104 | tf_op jit(solution)/shard_map/ppermute | solution.py:22
  23.7 1.6 %collective-permute-start.9 = (f32[264,128]{1,0:T(8,128)S(1)}, f32[264,128]{1,0:T(8,128)S(1)}, u32[]{:S(2)}, u32[]{:S(2)}) collective-permute-start(f32[264,128]{1,0:T(8,128)S(1)} %shard_map.41), channel_id=1, source_target_pairs={{0,12},{4,16},{8,4},{12,24},{16,28},{20,0},{24,20},{28,8},{1,13},{... | collective-permute-start | bytes 405512 | tf_op jit(solution)/shard_map/ppermute | solution.py:28
  25.8 2.3 %collective-permute-done.9 = f32[264,128]{1,0:T(8,128)S(1)} collective-permute-done((f32[264,128]{1,0:T(8,128)S(1)}, f32[264,128]{1,0:T(8,128)S(1)}, u32[]{:S(2)}, u32[]{:S(2)}) %collective-permute-start.9) | collective-permute-done | bytes 135200 | tf_op jit(solution)/shard_map/ppermute | solution.py:28
  28.2 1.6 %collective-permute-start.13 = (f32[264,128]{1,0:T(8,128)S(1)}, f32[264,128]{1,0:T(8,128)S(1)}, u32[]{:S(2)}, u32[]{:S(2)}) collective-permute-start(f32[264,128]{1,0:T(8,128)S(1)} %add.22.refs_0_), channel_id=1, source_target_pairs={{0,12},{4,16},{8,4},{12,24},{16,28},{20,0},{24,20},{28,8},{1,13},{... | collective-permute-start | bytes 405512 | tf_op jit(solution)/shard_map/ppermute | solution.py:28
  30.3 2.4 %collective-permute-done.13.refs_1_ = f32[264,128]{1,0:T(8,128)S(1)} collective-permute-done((f32[264,128]{1,0:T(8,128)S(1)}, f32[264,128]{1,0:T(8,128)S(1)}, u32[]{:S(2)}, u32[]{:S(2)}) %collective-permute-start.13) | collective-permute-done | bytes 135200 | tf_op jit(solution)/shard_map/ppermute | solution.py:28
  34.0 1.7 %shard_map.43 = (f32[256,128]{1,0:T(8,128)S(1)}, f32[256,128]{1,0:T(8,128)S(1)}, f32[8,128]{1,0:T(8,128)S(1)}) custom-call(bf16[256,128]{1,0:T(8,128)(2,1)S(1)} %get-tuple-element.87.own_high, bf16[256,128]{1,0:T(8,128)(2,1)S(1)} %get-tuple-element.88.own_low, bf16[256,256]{1,0:T(8,128)(2,1)S(1)} %get-tuple-element.89.upper_high, ...), custom_call_target="tpu_custom_call" | custom-call | tf_op jit(solution)/shard_map/pallas_call | solution.py:265
  35.8 1.9 %shard_map.44 = (bf16[256,768]{1,0:T(8,128)(2,1)S(1)}, f32[1,256]{1,0:T(1,128)S(1)}, f32[256,256]{1,0:T(8,128)S(1)}) custom-call(f32[256,1]{1,0:T(8,128)S(1)} %copy.7.weight, f32[256,128]{1,0:T(8,128)S(1)} %get-tuple-element.86.refs_0_, f32[256,128]{1,0:T(8,128)S(1)} %get-tuple-element.96.refs_1_, f32[8,128]{1,0:T(8,128)S(1)} %get-tuple-element.97.refs_2_, ...), custom_call_target="tpu_custom_call" | custom-call | tf_op jit(solution)/shard_map/pallas_call | solution.py:265
  37.6 5.3 %collective-permute-done.15.own_ref.refs_3_.refs_4_ = f32[256,128]{1,0:T(8,128)S(1)} collective-permute-done((f32[256,128]{1,0:T(8,128)S(1)}, f32[256,128]{1,0:T(8,128)S(1)}, u32[]{:S(2)}, u32[]{:S(2)}) %collective-permute-start.15) | collective-permute-done | bytes 131104 | tf_op jit(solution)/shard_map/ppermute | solution.py:22
  43.2 1.7 %collective-permute-start.16 = (f32[264,128]{1,0:T(8,128)S(1)}, f32[264,128]{1,0:T(8,128)S(1)}, u32[]{:S(2)}, u32[]{:S(2)}) collective-permute-start(f32[264,128]{1,0:T(8,128)S(1)} %shard_map.45), channel_id=1, source_target_pairs={{0,12},{4,16},{8,4},{12,24},{16,28},{20,0},{24,20},{28,8},{1,13},{... | collective-permute-start | bytes 405512 | tf_op jit(solution)/shard_map/ppermute | solution.py:28
  45.5 2.2 %collective-permute-done.16 = f32[264,128]{1,0:T(8,128)S(1)} collective-permute-done((f32[264,128]{1,0:T(8,128)S(1)}, f32[264,128]{1,0:T(8,128)S(1)}, u32[]{:S(2)}, u32[]{:S(2)}) %collective-permute-start.16) | collective-permute-done | bytes 135200 | tf_op jit(solution)/shard_map/ppermute | solution.py:28
  47.8 1.7 %collective-permute-start.20 = (f32[264,128]{1,0:T(8,128)S(1)}, f32[264,128]{1,0:T(8,128)S(1)}, u32[]{:S(2)}, u32[]{:S(2)}) collective-permute-start(f32[264,128]{1,0:T(8,128)S(1)} %add.23.refs_0_), channel_id=1, source_target_pairs={{0,12},{4,16},{8,4},{12,24},{16,28},{20,0},{24,20},{28,8},{1,13},{... | collective-permute-start | bytes 405512 | tf_op jit(solution)/shard_map/ppermute | solution.py:28
  49.9 2.4 %collective-permute-done.20.refs_1_ = f32[264,128]{1,0:T(8,128)S(1)} collective-permute-done((f32[264,128]{1,0:T(8,128)S(1)}, f32[264,128]{1,0:T(8,128)S(1)}, u32[]{:S(2)}, u32[]{:S(2)}) %collective-permute-start.20) | collective-permute-done | bytes 135200 | tf_op jit(solution)/shard_map/ppermute | solution.py:28
  53.6 1.7 %shard_map.47 = (f32[128,256]{1,0:T(8,128)S(1)}, f32[256,128]{1,0:T(8,128)S(1)}, f32[8,128]{1,0:T(8,128)S(1)}) custom-call(bf16[256,128]{1,0:T(8,128)(2,1)S(1)} %get-tuple-element.104.own_high, bf16[256,128]{1,0:T(8,128)(2,1)S(1)} %get-tuple-element.105.own_low, bf16[128,256]{1,0:T(8,128)(2,1)S(1)} %get-tuple-element.106.upper_high, ...), custom_call_target="tpu_custom_call" | custom-call | tf_op jit(solution)/shard_map/pallas_call | solution.py:265
  55.3 2.3 %shard_map.48.filled = f32[128,512]{1,0:T(8,128)} custom-call(f32[256,128]{1,0:T(8,128)S(1)} %get-tuple-element.114.refs_0_, f32[256,128]{1,0:T(8,128)S(1)} %get-tuple-element.115.refs_1_, f32[8,128]{1,0:T(8,128)S(1)} %get-tuple-element.116.refs_2_, f32[256,256]{1,0:T(8,128)S(1)} %get-tuple-element.102.refs_2_.refs_3_, ...), custom_call_target="tpu_custom_call" | custom-call | tf_op jit(solution)/shard_map/pallas_call | solution.py:339
  57.7 5.0 %collective-permute-done.22.lower = f32[128,256]{1,0:T(8,128)S(1)} collective-permute-done((f32[128,256]{1,0:T(8,128)S(1)}, f32[128,256]{1,0:T(8,128)S(1)}, u32[]{:S(2)}, u32[]{:S(2)}) %collective-permute-start.22) | collective-permute-done | bytes 131104 | tf_op jit(solution)/shard_map/ppermute | solution.py:22
  (49 shorter events, 10.0 us)
Async XLA Ops:
  1.5 1.5 %collective-permute-start.1 = (f32[264,128]{1,0:T(8,128)S(1)}, f32[264,128]{1,0:T(8,128)S(1)}, u32[]{:S(2)}, u32[]{:S(2)}) collective-permute-start(f32[264,128]{1,0:T(8,128)S(1)} %get-tuple-element.65), channel_id=1, source_target_pairs={{0,4},{4,0},{8,12},{12,8},{16,20},{20,16},{24,28},{28,24},{1,5},{5... | collective-permute-start | bytes 405512 | tf_op jit(solution)/shard_map/ppermute | solution.py:28
  2.0 6.4 %collective-permute-start.4 = (f32[128,512]{1,0:T(8,128)S(1)}, f32[128,512]{1,0:T(8,128)S(1)}, u32[]{:S(2)}, u32[]{:S(2)}) collective-permute-start(f32[128,512]{1,0:T(8,128)S(1)} %copy-done), channel_id=1, source_target_pairs={{0,4},{4,0},{8,12},{12,8},{16,20},{20,16},{24,28},{28,24},{1,5},{5... | collective-permute-start | bytes 786440 | tf_op jit(solution)/shard_map/ppermute | solution.py:28
  3.0 10.3 %copy-start.2 = (s32[3,2]{0,1:T(2,128)S(1)}, s32[3,2]{0,1:T(2,128)}, u32[]{:S(2)}) copy-start(s32[3,2]{0,1:T(2,128)} %param.5) | copy-start | bytes 76
  3.0 5.4 %collective-permute-start.2 = (f32[264,128]{1,0:T(8,128)S(1)}, f32[264,128]{1,0:T(8,128)S(1)}, u32[]{:S(2)}, u32[]{:S(2)}) collective-permute-start(f32[264,128]{1,0:T(8,128)S(1)} %add.20), channel_id=1, source_target_pairs={{0,12},{4,16},{8,4},{12,24},{16,28},{20,0},{24,20},{28,8},{1,13},{... | collective-permute-start | bytes 405512 | tf_op jit(solution)/shard_map/ppermute | solution.py:28
  5.7 2.7 %collective-permute-start.3 = (f32[264,128]{1,0:T(8,128)S(1)}, f32[264,128]{1,0:T(8,128)S(1)}, u32[]{:S(2)}, u32[]{:S(2)}) collective-permute-start(f32[264,128]{1,0:T(8,128)S(1)} %add.20), channel_id=1, source_target_pairs={{0,4},{4,0},{8,12},{12,8},{16,20},{20,16},{24,28},{28,24},{1,5},{5... | collective-permute-start | bytes 405512 | tf_op jit(solution)/shard_map/ppermute | solution.py:28
  8.4 4.5 %collective-permute-start.6 = (f32[264,128]{1,0:T(8,128)S(1)}, f32[264,128]{1,0:T(8,128)S(1)}, u32[]{:S(2)}, u32[]{:S(2)}) collective-permute-start(f32[264,128]{1,0:T(8,128)S(1)} %add.21.refs_0_), channel_id=1, source_target_pairs={{0,12},{4,16},{8,4},{12,24},{16,28},{20,0},{24,20},{28,8},{1,13},{... | collective-permute-start | bytes 405512 | tf_op jit(solution)/shard_map/ppermute | solution.py:28
  10.2 3.1 %collective-permute-start.5 = (f32[264,128]{1,0:T(8,128)S(1)}, f32[264,128]{1,0:T(8,128)S(1)}, u32[]{:S(2)}, u32[]{:S(2)}) collective-permute-start(f32[264,128]{1,0:T(8,128)S(1)} %add.21.refs_0_), channel_id=1, source_target_pairs={{0,4},{4,0},{8,12},{12,8},{16,20},{20,16},{24,28},{28,24},{1,5},{5... | collective-permute-start | bytes 405512 | tf_op jit(solution)/shard_map/ppermute | solution.py:28
  12.9 1.4 %collective-permute-start.7 = (f32[264,128]{1,0:T(8,128)S(1)}, f32[264,128]{1,0:T(8,128)S(1)}, u32[]{:S(2)}, u32[]{:S(2)}) collective-permute-start(f32[264,128]{1,0:T(8,128)S(1)} %collective-permute-done.6.refs_1_), channel_id=1, source_target_pairs={{0,4},{4,0},{8,12},{12,8},{16,20},{20,16},{24,28},{28,24},{1,5},{5... | collective-permute-start | bytes 405512 | tf_op jit(solution)/shard_map/ppermute | solution.py:28
  15.9 7.5 %collective-permute-start.8 = (f32[256,128]{1,0:T(8,128)S(1)}, f32[256,128]{1,0:T(8,128)S(1)}, u32[]{:S(2)}, u32[]{:S(2)}) collective-permute-start(f32[256,128]{1,0:T(8,128)S(1)} %get-tuple-element.82), channel_id=1, source_target_pairs={{0,5},{1,6},{2,7},{3,4},{4,1},{5,2},{6,3},{7,0},{8,13},{9,14},{10,... | collective-permute-start | bytes 393224 | tf_op jit(solution)/shard_map/ppermute | solution.py:22
  17.8 1.2 %collective-permute-start = (f32[128]{0:T(128)S(1)}, f32[128]{0:T(128)S(1)}, u32[]{:S(2)}, u32[]{:S(2)}) collective-permute-start(f32[128]{0:T(128)S(1)} %copy-done.1), channel_id=1, source_target_pairs={{0,4},{4,0},{8,12},{12,8},{16,20},{20,16},{24,28},{28,24},{1,5},{5... | collective-permute-start | bytes 1544 | tf_op jit(solution)/shard_map/ppermute | solution.py:28
  23.7 4.5 %collective-permute-start.9 = (f32[264,128]{1,0:T(8,128)S(1)}, f32[264,128]{1,0:T(8,128)S(1)}, u32[]{:S(2)}, u32[]{:S(2)}) collective-permute-start(f32[264,128]{1,0:T(8,128)S(1)} %shard_map.41), channel_id=1, source_target_pairs={{0,12},{4,16},{8,4},{12,24},{16,28},{20,0},{24,20},{28,8},{1,13},{... | collective-permute-start | bytes 405512 | tf_op jit(solution)/shard_map/ppermute | solution.py:28
  25.3 2.9 %collective-permute-start.10 = (f32[264,128]{1,0:T(8,128)S(1)}, f32[264,128]{1,0:T(8,128)S(1)}, u32[]{:S(2)}, u32[]{:S(2)}) collective-permute-start(f32[264,128]{1,0:T(8,128)S(1)} %shard_map.41), channel_id=1, source_target_pairs={{0,4},{4,0},{8,12},{12,8},{16,20},{20,16},{24,28},{28,24},{1,5},{5... | collective-permute-start | bytes 405512 | tf_op jit(solution)/shard_map/ppermute | solution.py:28
  25.7 2.5 %collective-permute-start.11 = (f32[256,128]{1,0:T(8,128)S(1)}, f32[256,128]{1,0:T(8,128)S(1)}, u32[]{:S(2)}, u32[]{:S(2)}) collective-permute-start(f32[256,128]{1,0:T(8,128)S(1)} %collective-permute-done.8.own_ref.refs_3_.refs_4_), channel_id=1, source_target_pairs={{0,4},{4,0},{8,12},{12,8},{16,20},{20,16},{24,28},{28,24},{1,5},{5... | collective-permute-start | bytes 393224 | tf_op jit(solution)/shard_map/ppermute | solution.py:28
  28.2 4.5 %collective-permute-start.13 = (f32[264,128]{1,0:T(8,128)S(1)}, f32[264,128]{1,0:T(8,128)S(1)}, u32[]{:S(2)}, u32[]{:S(2)}) collective-permute-start(f32[264,128]{1,0:T(8,128)S(1)} %add.22.refs_0_), channel_id=1, source_target_pairs={{0,12},{4,16},{8,4},{12,24},{16,28},{20,0},{24,20},{28,8},{1,13},{... | collective-permute-start | bytes 405512 | tf_op jit(solution)/shard_map/ppermute | solution.py:28
  29.8 3.1 %collective-permute-start.12 = (f32[264,128]{1,0:T(8,128)S(1)}, f32[264,128]{1,0:T(8,128)S(1)}, u32[]{:S(2)}, u32[]{:S(2)}) collective-permute-start(f32[264,128]{1,0:T(8,128)S(1)} %add.22.refs_0_), channel_id=1, source_target_pairs={{0,4},{4,0},{8,12},{12,8},{16,20},{20,16},{24,28},{28,24},{1,5},{5... | collective-permute-start | bytes 405512 | tf_op jit(solution)/shard_map/ppermute | solution.py:28
  32.7 1.4 %collective-permute-start.14 = (f32[264,128]{1,0:T(8,128)S(1)}, f32[264,128]{1,0:T(8,128)S(1)}, u32[]{:S(2)}, u32[]{:S(2)}) collective-permute-start(f32[264,128]{1,0:T(8,128)S(1)} %collective-permute-done.13.refs_1_), channel_id=1, source_target_pairs={{0,4},{4,0},{8,12},{12,8},{16,20},{20,16},{24,28},{28,24},{1,5},{5... | collective-permute-start | bytes 405512 | tf_op jit(solution)/shard_map/ppermute | solution.py:28
  35.7 7.3 %collective-permute-start.15 = (f32[256,128]{1,0:T(8,128)S(1)}, f32[256,128]{1,0:T(8,128)S(1)}, u32[]{:S(2)}, u32[]{:S(2)}) collective-permute-start(f32[256,128]{1,0:T(8,128)S(1)} %get-tuple-element.100), channel_id=1, source_target_pairs={{0,5},{1,6},{2,7},{3,4},{4,1},{5,2},{6,3},{7,0},{8,13},{9,14},{10,... | collective-permute-start | bytes 393224 | tf_op jit(solution)/shard_map/ppermute | solution.py:22
  43.2 4.5 %collective-permute-start.16 = (f32[264,128]{1,0:T(8,128)S(1)}, f32[264,128]{1,0:T(8,128)S(1)}, u32[]{:S(2)}, u32[]{:S(2)}) collective-permute-start(f32[264,128]{1,0:T(8,128)S(1)} %shard_map.45), channel_id=1, source_target_pairs={{0,12},{4,16},{8,4},{12,24},{16,28},{20,0},{24,20},{28,8},{1,13},{... | collective-permute-start | bytes 405512 | tf_op jit(solution)/shard_map/ppermute | solution.py:28
  45.0 2.8 %collective-permute-start.17 = (f32[264,128]{1,0:T(8,128)S(1)}, f32[264,128]{1,0:T(8,128)S(1)}, u32[]{:S(2)}, u32[]{:S(2)}) collective-permute-start(f32[264,128]{1,0:T(8,128)S(1)} %shard_map.45), channel_id=1, source_target_pairs={{0,4},{4,0},{8,12},{12,8},{16,20},{20,16},{24,28},{28,24},{1,5},{5... | collective-permute-start | bytes 405512 | tf_op jit(solution)/shard_map/ppermute | solution.py:28
  45.4 2.4 %collective-permute-start.18 = (f32[256,128]{1,0:T(8,128)S(1)}, f32[256,128]{1,0:T(8,128)S(1)}, u32[]{:S(2)}, u32[]{:S(2)}) collective-permute-start(f32[256,128]{1,0:T(8,128)S(1)} %collective-permute-done.15.own_ref.refs_3_.refs_4_), channel_id=1, source_target_pairs={{0,4},{4,0},{8,12},{12,8},{16,20},{20,16},{24,28},{28,24},{1,5},{5... | collective-permute-start | bytes 393224 | tf_op jit(solution)/shard_map/ppermute | solution.py:28
  47.8 4.5 %collective-permute-start.20 = (f32[264,128]{1,0:T(8,128)S(1)}, f32[264,128]{1,0:T(8,128)S(1)}, u32[]{:S(2)}, u32[]{:S(2)}) collective-permute-start(f32[264,128]{1,0:T(8,128)S(1)} %add.23.refs_0_), channel_id=1, source_target_pairs={{0,12},{4,16},{8,4},{12,24},{16,28},{20,0},{24,20},{28,8},{1,13},{... | collective-permute-start | bytes 405512 | tf_op jit(solution)/shard_map/ppermute | solution.py:28
  49.5 3.1 %collective-permute-start.19 = (f32[264,128]{1,0:T(8,128)S(1)}, f32[264,128]{1,0:T(8,128)S(1)}, u32[]{:S(2)}, u32[]{:S(2)}) collective-permute-start(f32[264,128]{1,0:T(8,128)S(1)} %add.23.refs_0_), channel_id=1, source_target_pairs={{0,4},{4,0},{8,12},{12,8},{16,20},{20,16},{24,28},{28,24},{1,5},{5... | collective-permute-start | bytes 405512 | tf_op jit(solution)/shard_map/ppermute | solution.py:28
  52.3 1.4 %collective-permute-start.21 = (f32[264,128]{1,0:T(8,128)S(1)}, f32[264,128]{1,0:T(8,128)S(1)}, u32[]{:S(2)}, u32[]{:S(2)}) collective-permute-start(f32[264,128]{1,0:T(8,128)S(1)} %collective-permute-done.20.refs_1_), channel_id=1, source_target_pairs={{0,4},{4,0},{8,12},{12,8},{16,20},{20,16},{24,28},{28,24},{1,5},{5... | collective-permute-start | bytes 405512 | tf_op jit(solution)/shard_map/ppermute | solution.py:28
  55.3 7.4 %collective-permute-start.22 = (f32[128,256]{1,0:T(8,128)S(1)}, f32[128,256]{1,0:T(8,128)S(1)}, u32[]{:S(2)}, u32[]{:S(2)}) collective-permute-start(f32[128,256]{1,0:T(8,128)S(1)} %get-tuple-element.113), channel_id=1, source_target_pairs={{0,6},{1,7},{2,4},{3,5},{4,2},{5,3},{6,0},{7,1},{8,14},{9,15},{10,... | collective-permute-start | bytes 393224 | tf_op jit(solution)/shard_map/ppermute | solution.py:22
  (2 other events, 3.9 us)

commit v17 on v16

--- a/solution.py
+++ b/solution.py
@@ -70,13 +70,14 @@
     return jnp.concatenate([value[half:], value[:half]], axis=0)
 
 
-def times_inverse_root(left_parts, square, scale, columns):
+def times_inverse_root(left, left_parts, square, scale, columns):
     rows = lax.broadcasted_iota(jnp.int32, square.shape, 0)
     identity = jnp.where(rows == lax.broadcasted_iota(jnp.int32, square.shape, 1), 1.0, 0.0)
-    base = (identity + square) * (1.0 / scale)
-    base_parts = two_parts(base)
-    second = product(base_parts, base_parts)
-    left_base = product(left_parts, base_parts)
+    square_parts = two_parts(square)
+    inverse = 1.0 / scale
+    base = (identity + square) * inverse
+    second = (identity + 2.0 * square + product(square_parts, square_parts)) * (inverse * inverse)
+    left_base = (left + product(left_parts, square_parts)) * inverse
     first_square = two_parts(2.25 * identity - 1.5 * base + 0.25 * second)
     cubic = product(two_parts(1.5 * base - 0.5 * second), first_square)
     both = two_parts(2.25 * identity - 0.75 * base - 0.5 * cubic)
@@ -202,8 +203,9 @@
     rows, columns = moved.shape
     taken = taken_rows(last, rows)
     other_mixed = lower[taken, half:] + product((upper_high[...], upper_low[...]), other_parts)
-    mixed = [jnp.concatenate(pair, axis=1) for pair in zip((high[...], low[...]), two_parts(other_mixed))]
-    result = times_inverse_root(mixed, square, scale, columns)
+    mixed_parts = [jnp.concatenate(pair, axis=1) for pair in zip((high[...], low[...]), two_parts(other_mixed))]
+    mixed = jnp.concatenate([high[...].astype(F32) + low[...].astype(F32), other_mixed], axis=1)
+    result = times_inverse_root(mixed, mixed_parts, square, scale, columns)
     if last:
         stored(moved, result)
     else:
@@ -216,7 +218,7 @@
     parts = two_parts(coupling)
     mixed = upper[:rows] - product(two_parts(lower[:rows]), parts, 1, 1)
     square = product(parts, parts, 1, 1)
-    return times_inverse_root(two_parts(mixed), square, scale_ref[0:1, 0:1], coupling.shape[1])
+    return times_inverse_root(mixed, two_parts(mixed), square, scale_ref[0:1, 0:1], coupling.shape[1])
 
 
 def upper_kernel(blocks, weight, *refs):
@@ -276,13 +278,12 @@
     width = columns // 2
     half = width // 2
     whole = (2 * rows, width)
-    own_part, other_part = pl.pallas_call(
+    own_part, other_part, near = pl.pallas_call(
         start_kernel,
-        out_shape=[jax.ShapeDtypeStruct((width + 8, half), F32)] * 2,
+        out_shape=[jax.ShapeDtypeStruct((width + 8, half), F32)] * 2 + [jax.ShapeDtypeStruct(snapshot.shape, F32)],
         in_specs=[pl.BlockSpec(memory_space=pltpu.HBM)] * 2,
-        out_specs=[ON_CHIP] * 2,
+        out_specs=[ON_CHIP] * 3,
         scratch_shapes=[
-            pltpu.VMEM((rows, columns), F32),
             pltpu.VMEM((1, rows), F32),
             pltpu.SemaphoreType.DMA(()),
             pltpu.SemaphoreType.DMA(()),
@@ -292,7 +293,7 @@
     own_part, other_part, damping = lax.optimization_barrier((own_part, other_part, damping))
     payload = own_part + swapped(other_part, 1, 1)
     weight = jnp.concatenate([weights, swapped(weights, 1, 1)])[:, None]
-    blocks, held, arriving = start_blocks, (snapshot,), swapped(snapshot, 1, 1)
+    blocks, held, arriving = start_blocks, (near,), swapped(near, 1, 1)
     damps = damping[:, 0].astype(F32) / (damping[:, 0] + damping[:, 1]).astype(F32)
     damps = lax.optimization_barrier(jnp.broadcast_to(damps[:, None], (STEPS, 128)))
     for step in range(STEPS):

time: 63.5 us -> 63.8 us (level)
  no operation moved by 1% of the time
where the time goes in v17:
time: 63.8 us; the launch traced here: 63.7 us
  waiting for transfers between devices  29.8 us (47%)
  starting transfers between devices  17.7 us (28%)
  Pallas kernels  15.5 us (24%)
    ppermute x20, waiting for transfers between devices, swapped(): return lax.ppermute(value, 'pts', pairs)  17.1 us
    ppermute x20, starting transfers between devices, swapped(): return lax.ppermute(value, 'pts', pairs)  15.8 us
    ppermute x3, waiting for transfers between devices, column_shift(): return lax.ppermute(value, ('pts', 'cols'), pairs)  12.7 us
    pallas_call x10, Pallas kernels, in_vmem(): pl.pallas_call(kernel, out_shape=[jax.ShapeDtypeStruct(shape, dtype) for...  11.1 us
    pallas_call x1, Pallas kernels, body(): pl.pallas_call(functools.partial(last_upper_kernel, blocks), out_shape=ou...  2.33 us
    ppermute x3, starting transfers between devices, column_shift(): return lax.ppermute(value, ('pts', 'cols'), pairs)  1.98 us
    pallas_call x1, Pallas kernels, body(): pl.pallas_call(start_kernel, out_shape=[jax.ShapeDtypeStruct((width + 8,...  1.38 us
  transfers between devices with their start and end apart: 23, of which 14 were waited for; matrix products, arithmetic and copies ran while one was open for 0% of the time, Pallas kernels for 12%

profile of v17, /device:TPU:0, one launch (start us, length us, event | category | flops | bytes accessed | tf_op | source)
XLA Modules:
  0.0 63.7 jit_solution(6448070929396550807)
XLA Ops:
  0.0 1.4 %shard_map.37 = (f32[264,128]{1,0:T(8,128)S(1)}, f32[264,128]{1,0:T(8,128)S(1)}, f32[128,512]{1,0:T(8,128)S(1)}) custom-call(f32[128,512]{1,0:T(8,128)} %near_ref.1, f32[1,128]{1,0:T(1,128)} %bitcast.5), custom_call_target="tpu_custom_call" | custom-call | tf_op jit(solution)/shard_map/pallas_call | solution.py:281
  2.0 0.9 %collective-permute-done.1 = f32[264,128]{1,0:T(8,128)S(1)} collective-permute-done((f32[264,128]{1,0:T(8,128)S(1)}, f32[264,128]{1,0:T(8,128)S(1)}, u32[]{:S(2)}, u32[]{:S(2)}) %collective-permute-start.1) | collective-permute-done | bytes 135200 | tf_op jit(solution)/shard_map/ppermute | solution.py:28
  2.9 2.7 %collective-permute-start.2 = (f32[264,128]{1,0:T(8,128)S(1)}, f32[264,128]{1,0:T(8,128)S(1)}, u32[]{:S(2)}, u32[]{:S(2)}) collective-permute-start(f32[264,128]{1,0:T(8,128)S(1)} %add.20), channel_id=1, source_target_pairs={{0,12},{4,16},{8,4},{12,24},{16,28},{20,0},{24,20},{28,8},{1,13},{... | collective-permute-start | bytes 405512 | tf_op jit(solution)/shard_map/ppermute | solution.py:28
  6.0 2.3 %collective-permute-done.2 = f32[264,128]{1,0:T(8,128)S(1)} collective-permute-done((f32[264,128]{1,0:T(8,128)S(1)}, f32[264,128]{1,0:T(8,128)S(1)}, u32[]{:S(2)}, u32[]{:S(2)}) %collective-permute-start.2) | collective-permute-done | bytes 135200 | tf_op jit(solution)/shard_map/ppermute | solution.py:28
  8.3 1.8 %collective-permute-start.6 = (f32[264,128]{1,0:T(8,128)S(1)}, f32[264,128]{1,0:T(8,128)S(1)}, u32[]{:S(2)}, u32[]{:S(2)}) collective-permute-start(f32[264,128]{1,0:T(8,128)S(1)} %add.21.refs_0_), channel_id=1, source_target_pairs={{0,12},{4,16},{8,4},{12,24},{16,28},{20,0},{24,20},{28,8},{1,13},{... | collective-permute-start | bytes 405512 | tf_op jit(solution)/shard_map/ppermute | solution.py:28
  10.5 2.3 %collective-permute-done.6.refs_1_ = f32[264,128]{1,0:T(8,128)S(1)} collective-permute-done((f32[264,128]{1,0:T(8,128)S(1)}, f32[264,128]{1,0:T(8,128)S(1)}, u32[]{:S(2)}, u32[]{:S(2)}) %collective-permute-start.6) | collective-permute-done | bytes 135200 | tf_op jit(solution)/shard_map/ppermute | solution.py:28
  14.2 1.7 %shard_map.39 = (f32[256,128]{1,0:T(8,128)S(1)}, f32[256,128]{1,0:T(8,128)S(1)}, f32[8,128]{1,0:T(8,128)S(1)}) custom-call(bf16[256,128]{1,0:T(8,128)(2,1)S(1)} %get-tuple-element.71.own_high, bf16[256,128]{1,0:T(8,128)(2,1)S(1)} %get-tuple-element.72.own_low, bf16[256,256]{1,0:T(8,128)(2,1)S(1)} %get-tuple-element.73.upper_high, ...), custom_call_target="tpu_custom_call" | custom-call | tf_op jit(solution)/shard_map/pallas_call | solution.py:267
  15.9 1.9 %collective-permute-start.8 = (f32[256,128]{1,0:T(8,128)S(1)}, f32[256,128]{1,0:T(8,128)S(1)}, u32[]{:S(2)}, u32[]{:S(2)}) collective-permute-start(f32[256,128]{1,0:T(8,128)S(1)} %get-tuple-element.84), channel_id=1, source_target_pairs={{0,5},{1,6},{2,7},{3,4},{4,1},{5,2},{6,3},{7,0},{8,13},{9,14},{10,... | collective-permute-start | bytes 393224 | tf_op jit(solution)/shard_map/ppermute | solution.py:22
  19.1 1.9 %shard_map.40 = (bf16[256,768]{1,0:T(8,128)(2,1)S(1)}, f32[1,256]{1,0:T(1,128)S(1)}, f32[256,256]{1,0:T(8,128)S(1)}) custom-call(f32[256,1]{1,0:T(8,128)S(1)} %copy.7.weight, f32[256,128]{1,0:T(8,128)S(1)} %get-tuple-element.70.refs_0_, f32[256,128]{1,0:T(8,128)S(1)} %get-tuple-element.80.refs_1_, f32[8,128]{1,0:T(8,128)S(1)} %get-tuple-element.81.refs_2_, ...), custom_call_target="tpu_custom_call" | custom-call | tf_op jit(solution)/shard_map/pallas_call | solution.py:267
  21.0 2.4 %collective-permute-done.8.own_ref.refs_3_.refs_4_ = f32[256,128]{1,0:T(8,128)S(1)} collective-permute-done((f32[256,128]{1,0:T(8,128)S(1)}, f32[256,128]{1,0:T(8,128)S(1)}, u32[]{:S(2)}, u32[]{:S(2)}) %collective-permute-start.8) | collective-permute-done | bytes 131104 | tf_op jit(solution)/shard_map/ppermute | solution.py:22
  23.6 1.6 %collective-permute-start.9 = (f32[264,128]{1,0:T(8,128)S(1)}, f32[264,128]{1,0:T(8,128)S(1)}, u32[]{:S(2)}, u32[]{:S(2)}) collective-permute-start(f32[264,128]{1,0:T(8,128)S(1)} %shard_map.41), channel_id=1, source_target_pairs={{0,12},{4,16},{8,4},{12,24},{16,28},{20,0},{24,20},{28,8},{1,13},{... | collective-permute-start | bytes 405512 | tf_op jit(solution)/shard_map/ppermute | solution.py:28
  25.8 2.3 %collective-permute-done.9 = f32[264,128]{1,0:T(8,128)S(1)} collective-permute-done((f32[264,128]{1,0:T(8,128)S(1)}, f32[264,128]{1,0:T(8,128)S(1)}, u32[]{:S(2)}, u32[]{:S(2)}) %collective-permute-start.9) | collective-permute-done | bytes 135200 | tf_op jit(solution)/shard_map/ppermute | solution.py:28
  28.1 1.6 %collective-permute-start.13 = (f32[264,128]{1,0:T(8,128)S(1)}, f32[264,128]{1,0:T(8,128)S(1)}, u32[]{:S(2)}, u32[]{:S(2)}) collective-permute-start(f32[264,128]{1,0:T(8,128)S(1)} %add.22.refs_0_), channel_id=1, source_target_pairs={{0,12},{4,16},{8,4},{12,24},{16,28},{20,0},{24,20},{28,8},{1,13},{... | collective-permute-start | bytes 405512 | tf_op jit(solution)/shard_map/ppermute | solution.py:28
  30.2 2.4 %collective-permute-done.13.refs_1_ = f32[264,128]{1,0:T(8,128)S(1)} collective-permute-done((f32[264,128]{1,0:T(8,128)S(1)}, f32[264,128]{1,0:T(8,128)S(1)}, u32[]{:S(2)}, u32[]{:S(2)}) %collective-permute-start.13) | collective-permute-done | bytes 135200 | tf_op jit(solution)/shard_map/ppermute | solution.py:28
  34.0 1.7 %shard_map.43 = (f32[256,128]{1,0:T(8,128)S(1)}, f32[256,128]{1,0:T(8,128)S(1)}, f32[8,128]{1,0:T(8,128)S(1)}) custom-call(bf16[256,128]{1,0:T(8,128)(2,1)S(1)} %get-tuple-element.89.own_high, bf16[256,128]{1,0:T(8,128)(2,1)S(1)} %get-tuple-element.90.own_low, bf16[256,256]{1,0:T(8,128)(2,1)S(1)} %get-tuple-element.91.upper_high, ...), custom_call_target="tpu_custom_call" | custom-call | tf_op jit(solution)/shard_map/pallas_call | solution.py:267
  35.7 1.9 %shard_map.44 = (bf16[256,768]{1,0:T(8,128)(2,1)S(1)}, f32[1,256]{1,0:T(1,128)S(1)}, f32[256,256]{1,0:T(8,128)S(1)}) custom-call(f32[256,1]{1,0:T(8,128)S(1)} %copy.7.weight, f32[256,128]{1,0:T(8,128)S(1)} %get-tuple-element.88.refs_0_, f32[256,128]{1,0:T(8,128)S(1)} %get-tuple-element.98.refs_1_, f32[8,128]{1,0:T(8,128)S(1)} %get-tuple-element.99.refs_2_, ...), custom_call_target="tpu_custom_call" | custom-call | tf_op jit(solution)/shard_map/pallas_call | solution.py:267
  37.7 5.3 %collective-permute-done.15.own_ref.refs_3_.refs_4_ = f32[256,128]{1,0:T(8,128)S(1)} collective-permute-done((f32[256,128]{1,0:T(8,128)S(1)}, f32[256,128]{1,0:T(8,128)S(1)}, u32[]{:S(2)}, u32[]{:S(2)}) %collective-permute-start.15) | collective-permute-done | bytes 131104 | tf_op jit(solution)/shard_map/ppermute | solution.py:22
  43.2 1.7 %collective-permute-start.16 = (f32[264,128]{1,0:T(8,128)S(1)}, f32[264,128]{1,0:T(8,128)S(1)}, u32[]{:S(2)}, u32[]{:S(2)}) collective-permute-start(f32[264,128]{1,0:T(8,128)S(1)} %shard_map.45), channel_id=1, source_target_pairs={{0,12},{4,16},{8,4},{12,24},{16,28},{20,0},{24,20},{28,8},{1,13},{... | collective-permute-start | bytes 405512 | tf_op jit(solution)/shard_map/ppermute | solution.py:28
  45.4 2.3 %collective-permute-done.16 = f32[264,128]{1,0:T(8,128)S(1)} collective-permute-done((f32[264,128]{1,0:T(8,128)S(1)}, f32[264,128]{1,0:T(8,128)S(1)}, u32[]{:S(2)}, u32[]{:S(2)}) %collective-permute-start.16) | collective-permute-done | bytes 135200 | tf_op jit(solution)/shard_map/ppermute | solution.py:28
  47.7 1.9 %collective-permute-start.20 = (f32[264,128]{1,0:T(8,128)S(1)}, f32[264,128]{1,0:T(8,128)S(1)}, u32[]{:S(2)}, u32[]{:S(2)}) collective-permute-start(f32[264,128]{1,0:T(8,128)S(1)} %add.23.refs_0_), channel_id=1, source_target_pairs={{0,12},{4,16},{8,4},{12,24},{16,28},{20,0},{24,20},{28,8},{1,13},{... | collective-permute-start | bytes 405512 | tf_op jit(solution)/shard_map/ppermute | solution.py:28
  50.1 2.3 %collective-permute-done.20.refs_1_ = f32[264,128]{1,0:T(8,128)S(1)} collective-permute-done((f32[264,128]{1,0:T(8,128)S(1)}, f32[264,128]{1,0:T(8,128)S(1)}, u32[]{:S(2)}, u32[]{:S(2)}) %collective-permute-start.20) | collective-permute-done | bytes 135200 | tf_op jit(solution)/shard_map/ppermute | solution.py:28
  53.7 1.7 %shard_map.47 = (f32[128,256]{1,0:T(8,128)S(1)}, f32[256,128]{1,0:T(8,128)S(1)}, f32[8,128]{1,0:T(8,128)S(1)}) custom-call(bf16[256,128]{1,0:T(8,128)(2,1)S(1)} %get-tuple-element.106.own_high, bf16[256,128]{1,0:T(8,128)(2,1)S(1)} %get-tuple-element.107.own_low, bf16[128,256]{1,0:T(8,128)(2,1)S(1)} %get-tuple-element.108.upper_high, ...), custom_call_target="tpu_custom_call" | custom-call | tf_op jit(solution)/shard_map/pallas_call | solution.py:267
  55.5 2.3 %shard_map.48.filled = f32[128,512]{1,0:T(8,128)} custom-call(f32[256,128]{1,0:T(8,128)S(1)} %get-tuple-element.116.refs_0_, f32[256,128]{1,0:T(8,128)S(1)} %get-tuple-element.117.refs_1_, f32[8,128]{1,0:T(8,128)S(1)} %get-tuple-element.118.refs_2_, f32[256,256]{1,0:T(8,128)S(1)} %get-tuple-element.104.refs_2_.refs_3_, ...), custom_call_target="tpu_custom_call" | custom-call | tf_op jit(solution)/shard_map/pallas_call | solution.py:340
  57.8 5.0 %collective-permute-done.22.lower = f32[128,256]{1,0:T(8,128)S(1)} collective-permute-done((f32[128,256]{1,0:T(8,128)S(1)}, f32[128,256]{1,0:T(8,128)S(1)}, u32[]{:S(2)}, u32[]{:S(2)}) %collective-permute-start.22) | collective-permute-done | bytes 131104 | tf_op jit(solution)/shard_map/ppermute | solution.py:22
  (47 shorter events, 10.1 us)
Async XLA Ops:
  1.4 1.5 %collective-permute-start.1 = (f32[264,128]{1,0:T(8,128)S(1)}, f32[264,128]{1,0:T(8,128)S(1)}, u32[]{:S(2)}, u32[]{:S(2)}) collective-permute-start(f32[264,128]{1,0:T(8,128)S(1)} %get-tuple-element.66), channel_id=1, source_target_pairs={{0,4},{4,0},{8,12},{12,8},{16,20},{20,16},{24,28},{28,24},{1,5},{5... | collective-permute-start | bytes 405512 | tf_op jit(solution)/shard_map/ppermute | solution.py:28
  1.9 6.4 %collective-permute-start.4 = (f32[128,512]{1,0:T(8,128)S(1)}, f32[128,512]{1,0:T(8,128)S(1)}, u32[]{:S(2)}, u32[]{:S(2)}) collective-permute-start(f32[128,512]{1,0:T(8,128)S(1)} %get-tuple-element.67.refs_2_.refs_3_), channel_id=1, source_target_pairs={{0,4},{4,0},{8,12},{12,8},{16,20},{20,16},{24,28},{28,24},{1,5},{5... | collective-permute-start | bytes 786440 | tf_op jit(solution)/shard_map/ppermute | solution.py:28
  2.9 10.3 %copy-start.1 = (s32[3,2]{0,1:T(2,128)S(1)}, s32[3,2]{0,1:T(2,128)}, u32[]{:S(2)}) copy-start(s32[3,2]{0,1:T(2,128)} %param.5) | copy-start | bytes 76
  2.9 5.4 %collective-permute-start.2 = (f32[264,128]{1,0:T(8,128)S(1)}, f32[264,128]{1,0:T(8,128)S(1)}, u32[]{:S(2)}, u32[]{:S(2)}) collective-permute-start(f32[264,128]{1,0:T(8,128)S(1)} %add.20), channel_id=1, source_target_pairs={{0,12},{4,16},{8,4},{12,24},{16,28},{20,0},{24,20},{28,8},{1,13},{... | collective-permute-start | bytes 405512 | tf_op jit(solution)/shard_map/ppermute | solution.py:28
  5.6 2.7 %collective-permute-start.3 = (f32[264,128]{1,0:T(8,128)S(1)}, f32[264,128]{1,0:T(8,128)S(1)}, u32[]{:S(2)}, u32[]{:S(2)}) collective-permute-start(f32[264,128]{1,0:T(8,128)S(1)} %add.20), channel_id=1, source_target_pairs={{0,4},{4,0},{8,12},{12,8},{16,20},{20,16},{24,28},{28,24},{1,5},{5... | collective-permute-start | bytes 405512 | tf_op jit(solution)/shard_map/ppermute | solution.py:28
  8.3 4.5 %collective-permute-start.6 = (f32[264,128]{1,0:T(8,128)S(1)}, f32[264,128]{1,0:T(8,128)S(1)}, u32[]{:S(2)}, u32[]{:S(2)}) collective-permute-start(f32[264,128]{1,0:T(8,128)S(1)} %add.21.refs_0_), channel_id=1, source_target_pairs={{0,12},{4,16},{8,4},{12,24},{16,28},{20,0},{24,20},{28,8},{1,13},{... | collective-permute-start | bytes 405512 | tf_op jit(solution)/shard_map/ppermute | solution.py:28
  10.1 3.1 %collective-permute-start.5 = (f32[264,128]{1,0:T(8,128)S(1)}, f32[264,128]{1,0:T(8,128)S(1)}, u32[]{:S(2)}, u32[]{:S(2)}) collective-permute-start(f32[264,128]{1,0:T(8,128)S(1)} %add.21.refs_0_), channel_id=1, source_target_pairs={{0,4},{4,0},{8,12},{12,8},{16,20},{20,16},{24,28},{28,24},{1,5},{5... | collective-permute-start | bytes 405512 | tf_op jit(solution)/shard_map/ppermute | solution.py:28
  12.8 1.4 %collective-permute-start.7 = (f32[264,128]{1,0:T(8,128)S(1)}, f32[264,128]{1,0:T(8,128)S(1)}, u32[]{:S(2)}, u32[]{:S(2)}) collective-permute-start(f32[264,128]{1,0:T(8,128)S(1)} %collective-permute-done.6.refs_1_), channel_id=1, source_target_pairs={{0,4},{4,0},{8,12},{12,8},{16,20},{20,16},{24,28},{28,24},{1,5},{5... | collective-permute-start | bytes 405512 | tf_op jit(solution)/shard_map/ppermute | solution.py:28
  15.9 7.5 %collective-permute-start.8 = (f32[256,128]{1,0:T(8,128)S(1)}, f32[256,128]{1,0:T(8,128)S(1)}, u32[]{:S(2)}, u32[]{:S(2)}) collective-permute-start(f32[256,128]{1,0:T(8,128)S(1)} %get-tuple-element.84), channel_id=1, source_target_pairs={{0,5},{1,6},{2,7},{3,4},{4,1},{5,2},{6,3},{7,0},{8,13},{9,14},{10,... | collective-permute-start | bytes 393224 | tf_op jit(solution)/shard_map/ppermute | solution.py:22
  17.7 1.2 %collective-permute-start = (f32[128]{0:T(128)S(1)}, f32[128]{0:T(128)S(1)}, u32[]{:S(2)}, u32[]{:S(2)}) collective-permute-start(f32[128]{0:T(128)S(1)} %copy-done), channel_id=1, source_target_pairs={{0,4},{4,0},{8,12},{12,8},{16,20},{20,16},{24,28},{28,24},{1,5},{5... | collective-permute-start | bytes 1544 | tf_op jit(solution)/shard_map/ppermute | solution.py:28
  23.6 4.5 %collective-permute-start.9 = (f32[264,128]{1,0:T(8,128)S(1)}, f32[264,128]{1,0:T(8,128)S(1)}, u32[]{:S(2)}, u32[]{:S(2)}) collective-permute-start(f32[264,128]{1,0:T(8,128)S(1)} %shard_map.41), channel_id=1, source_target_pairs={{0,12},{4,16},{8,4},{12,24},{16,28},{20,0},{24,20},{28,8},{1,13},{... | collective-permute-start | bytes 405512 | tf_op jit(solution)/shard_map/ppermute | solution.py:28
  25.2 2.9 %collective-permute-start.10 = (f32[264,128]{1,0:T(8,128)S(1)}, f32[264,128]{1,0:T(8,128)S(1)}, u32[]{:S(2)}, u32[]{:S(2)}) collective-permute-start(f32[264,128]{1,0:T(8,128)S(1)} %shard_map.41), channel_id=1, source_target_pairs={{0,4},{4,0},{8,12},{12,8},{16,20},{20,16},{24,28},{28,24},{1,5},{5... | collective-permute-start | bytes 405512 | tf_op jit(solution)/shard_map/ppermute | solution.py:28
  25.7 2.4 %collective-permute-start.11 = (f32[256,128]{1,0:T(8,128)S(1)}, f32[256,128]{1,0:T(8,128)S(1)}, u32[]{:S(2)}, u32[]{:S(2)}) collective-permute-start(f32[256,128]{1,0:T(8,128)S(1)} %collective-permute-done.8.own_ref.refs_3_.refs_4_), channel_id=1, source_target_pairs={{0,4},{4,0},{8,12},{12,8},{16,20},{20,16},{24,28},{28,24},{1,5},{5... | collective-permute-start | bytes 393224 | tf_op jit(solution)/shard_map/ppermute | solution.py:28
  28.1 4.5 %collective-permute-start.13 = (f32[264,128]{1,0:T(8,128)S(1)}, f32[264,128]{1,0:T(8,128)S(1)}, u32[]{:S(2)}, u32[]{:S(2)}) collective-permute-start(f32[264,128]{1,0:T(8,128)S(1)} %add.22.refs_0_), channel_id=1, source_target_pairs={{0,12},{4,16},{8,4},{12,24},{16,28},{20,0},{24,20},{28,8},{1,13},{... | collective-permute-start | bytes 405512 | tf_op jit(solution)/shard_map/ppermute | solution.py:28
  29.8 3.2 %collective-permute-start.12 = (f32[264,128]{1,0:T(8,128)S(1)}, f32[264,128]{1,0:T(8,128)S(1)}, u32[]{:S(2)}, u32[]{:S(2)}) collective-permute-start(f32[264,128]{1,0:T(8,128)S(1)} %add.22.refs_0_), channel_id=1, source_target_pairs={{0,4},{4,0},{8,12},{12,8},{16,20},{20,16},{24,28},{28,24},{1,5},{5... | collective-permute-start | bytes 405512 | tf_op jit(solution)/shard_map/ppermute | solution.py:28
  32.6 1.4 %collective-permute-start.14 = (f32[264,128]{1,0:T(8,128)S(1)}, f32[264,128]{1,0:T(8,128)S(1)}, u32[]{:S(2)}, u32[]{:S(2)}) collective-permute-start(f32[264,128]{1,0:T(8,128)S(1)} %collective-permute-done.13.refs_1_), channel_id=1, source_target_pairs={{0,4},{4,0},{8,12},{12,8},{16,20},{20,16},{24,28},{28,24},{1,5},{5... | collective-permute-start | bytes 405512 | tf_op jit(solution)/shard_map/ppermute | solution.py:28
  35.7 7.2 %collective-permute-start.15 = (f32[256,128]{1,0:T(8,128)S(1)}, f32[256,128]{1,0:T(8,128)S(1)}, u32[]{:S(2)}, u32[]{:S(2)}) collective-permute-start(f32[256,128]{1,0:T(8,128)S(1)} %get-tuple-element.102), channel_id=1, source_target_pairs={{0,5},{1,6},{2,7},{3,4},{4,1},{5,2},{6,3},{7,0},{8,13},{9,14},{10,... | collective-permute-start | bytes 393224 | tf_op jit(solution)/shard_map/ppermute | solution.py:22
  43.2 4.5 %collective-permute-start.16 = (f32[264,128]{1,0:T(8,128)S(1)}, f32[264,128]{1,0:T(8,128)S(1)}, u32[]{:S(2)}, u32[]{:S(2)}) collective-permute-start(f32[264,128]{1,0:T(8,128)S(1)} %shard_map.45), channel_id=1, source_target_pairs={{0,12},{4,16},{8,4},{12,24},{16,28},{20,0},{24,20},{28,8},{1,13},{... | collective-permute-start | bytes 405512 | tf_op jit(solution)/shard_map/ppermute | solution.py:28
  44.9 2.8 %collective-permute-start.17 = (f32[264,128]{1,0:T(8,128)S(1)}, f32[264,128]{1,0:T(8,128)S(1)}, u32[]{:S(2)}, u32[]{:S(2)}) collective-permute-start(f32[264,128]{1,0:T(8,128)S(1)} %shard_map.45), channel_id=1, source_target_pairs={{0,4},{4,0},{8,12},{12,8},{16,20},{20,16},{24,28},{28,24},{1,5},{5... | collective-permute-start | bytes 405512 | tf_op jit(solution)/shard_map/ppermute | solution.py:28
  45.3 2.4 %collective-permute-start.18 = (f32[256,128]{1,0:T(8,128)S(1)}, f32[256,128]{1,0:T(8,128)S(1)}, u32[]{:S(2)}, u32[]{:S(2)}) collective-permute-start(f32[256,128]{1,0:T(8,128)S(1)} %collective-permute-done.15.own_ref.refs_3_.refs_4_), channel_id=1, source_target_pairs={{0,4},{4,0},{8,12},{12,8},{16,20},{20,16},{24,28},{28,24},{1,5},{5... | collective-permute-start | bytes 393224 | tf_op jit(solution)/shard_map/ppermute | solution.py:28
  47.7 4.7 %collective-permute-start.20 = (f32[264,128]{1,0:T(8,128)S(1)}, f32[264,128]{1,0:T(8,128)S(1)}, u32[]{:S(2)}, u32[]{:S(2)}) collective-permute-start(f32[264,128]{1,0:T(8,128)S(1)} %add.23.refs_0_), channel_id=1, source_target_pairs={{0,12},{4,16},{8,4},{12,24},{16,28},{20,0},{24,20},{28,8},{1,13},{... | collective-permute-start | bytes 405512 | tf_op jit(solution)/shard_map/ppermute | solution.py:28
  49.6 3.0 %collective-permute-start.19 = (f32[264,128]{1,0:T(8,128)S(1)}, f32[264,128]{1,0:T(8,128)S(1)}, u32[]{:S(2)}, u32[]{:S(2)}) collective-permute-start(f32[264,128]{1,0:T(8,128)S(1)} %add.23.refs_0_), channel_id=1, source_target_pairs={{0,4},{4,0},{8,12},{12,8},{16,20},{20,16},{24,28},{28,24},{1,5},{5... | collective-permute-start | bytes 405512 | tf_op jit(solution)/shard_map/ppermute | solution.py:28
  52.4 1.4 %collective-permute-start.21 = (f32[264,128]{1,0:T(8,128)S(1)}, f32[264,128]{1,0:T(8,128)S(1)}, u32[]{:S(2)}, u32[]{:S(2)}) collective-permute-start(f32[264,128]{1,0:T(8,128)S(1)} %collective-permute-done.20.refs_1_), channel_id=1, source_target_pairs={{0,4},{4,0},{8,12},{12,8},{16,20},{20,16},{24,28},{28,24},{1,5},{5... | collective-permute-start | bytes 405512 | tf_op jit(solution)/shard_map/ppermute | solution.py:28
  55.4 7.5 %collective-permute-start.22 = (f32[128,256]{1,0:T(8,128)S(1)}, f32[128,256]{1,0:T(8,128)S(1)}, u32[]{:S(2)}, u32[]{:S(2)}) collective-permute-start(f32[128,256]{1,0:T(8,128)S(1)} %get-tuple-element.115), channel_id=1, source_target_pairs={{0,6},{1,7},{2,4},{3,5},{4,2},{5,3},{6,0},{7,1},{8,14},{9,15},{10,... | collective-permute-start | bytes 393224 | tf_op jit(solution)/shard_map/ppermute | solution.py:22
  (1 other events, 1.9 us)

commit v18 on v16

--- a/solution.py
+++ b/solution.py
@@ -276,13 +276,12 @@
     width = columns // 2
     half = width // 2
     whole = (2 * rows, width)
-    own_part, other_part = pl.pallas_call(
+    own_part, other_part, near = pl.pallas_call(
         start_kernel,
-        out_shape=[jax.ShapeDtypeStruct((width + 8, half), F32)] * 2,
+        out_shape=[jax.ShapeDtypeStruct((width + 8, half), F32)] * 2 + [jax.ShapeDtypeStruct(snapshot.shape, F32)],
         in_specs=[pl.BlockSpec(memory_space=pltpu.HBM)] * 2,
-        out_specs=[ON_CHIP] * 2,
+        out_specs=[ON_CHIP] * 3,
         scratch_shapes=[
-            pltpu.VMEM((rows, columns), F32),
             pltpu.VMEM((1, rows), F32),
             pltpu.SemaphoreType.DMA(()),
             pltpu.SemaphoreType.DMA(()),
@@ -292,7 +291,7 @@
     own_part, other_part, damping = lax.optimization_barrier((own_part, other_part, damping))
     payload = own_part + swapped(other_part, 1, 1)
     weight = jnp.concatenate([weights, swapped(weights, 1, 1)])[:, None]
-    blocks, held, arriving = start_blocks, (snapshot,), swapped(snapshot, 1, 1)
+    blocks, held, arriving = start_blocks, (near,), swapped(near, 1, 1)
     damps = damping[:, 0].astype(F32) / (damping[:, 0] + damping[:, 1]).astype(F32)
     damps = lax.optimization_barrier(jnp.broadcast_to(damps[:, None], (STEPS, 128)))
     for step in range(STEPS):

time: 63.5 us -> 63.4 us (level)
  no operation moved by 1% of the time
where the time goes in v18:
time: 63.4 us; the launch traced here: 63.3 us
  waiting for transfers between devices  29.7 us (47%)
  starting transfers between devices  17.7 us (28%)
  Pallas kernels  15.4 us (24%)
    ppermute x20, waiting for transfers between devices, swapped(): return lax.ppermute(value, 'pts', pairs)  16.9 us
    ppermute x20, starting transfers between devices, swapped(): return lax.ppermute(value, 'pts', pairs)  15.8 us
    ppermute x3, waiting for transfers between devices, column_shift(): return lax.ppermute(value, ('pts', 'cols'), pairs)  12.8 us
    pallas_call x10, Pallas kernels, in_vmem(): pl.pallas_call(kernel, out_shape=[jax.ShapeDtypeStruct(shape, dtype) for...  11 us
    pallas_call x1, Pallas kernels, body(): pl.pallas_call(functools.partial(last_upper_kernel, blocks), out_shape=ou...  2.32 us
    ppermute x3, starting transfers between devices, column_shift(): return lax.ppermute(value, ('pts', 'cols'), pairs)  1.98 us
    pallas_call x1, Pallas kernels, body(): pl.pallas_call(start_kernel, out_shape=[jax.ShapeDtypeStruct((width + 8,...  1.38 us
  transfers between devices with their start and end apart: 23, of which 14 were waited for; matrix products, arithmetic and copies ran while one was open for 0% of the time, Pallas kernels for 12%

profile of v18, /device:TPU:0, one launch (start us, length us, event | category | flops | bytes accessed | tf_op | source)
XLA Modules:
  0.0 63.3 jit_solution(2761982143867971784)
XLA Ops:
  0.0 1.4 %shard_map.37 = (f32[264,128]{1,0:T(8,128)S(1)}, f32[264,128]{1,0:T(8,128)S(1)}, f32[128,512]{1,0:T(8,128)S(1)}) custom-call(f32[128,512]{1,0:T(8,128)} %near_ref.1, f32[1,128]{1,0:T(1,128)} %bitcast.5), custom_call_target="tpu_custom_call" | custom-call | tf_op jit(solution)/shard_map/pallas_call | solution.py:279
  2.0 0.9 %collective-permute-done.1 = f32[264,128]{1,0:T(8,128)S(1)} collective-permute-done((f32[264,128]{1,0:T(8,128)S(1)}, f32[264,128]{1,0:T(8,128)S(1)}, u32[]{:S(2)}, u32[]{:S(2)}) %collective-permute-start.1) | collective-permute-done | bytes 135200 | tf_op jit(solution)/shard_map/ppermute | solution.py:28
  2.9 2.7 %collective-permute-start.2 = (f32[264,128]{1,0:T(8,128)S(1)}, f32[264,128]{1,0:T(8,128)S(1)}, u32[]{:S(2)}, u32[]{:S(2)}) collective-permute-start(f32[264,128]{1,0:T(8,128)S(1)} %add.20), channel_id=1, source_target_pairs={{0,12},{4,16},{8,4},{12,24},{16,28},{20,0},{24,20},{28,8},{1,13},{... | collective-permute-start | bytes 405512 | tf_op jit(solution)/shard_map/ppermute | solution.py:28
  6.0 2.3 %collective-permute-done.2 = f32[264,128]{1,0:T(8,128)S(1)} collective-permute-done((f32[264,128]{1,0:T(8,128)S(1)}, f32[264,128]{1,0:T(8,128)S(1)}, u32[]{:S(2)}, u32[]{:S(2)}) %collective-permute-start.2) | collective-permute-done | bytes 135200 | tf_op jit(solution)/shard_map/ppermute | solution.py:28
  8.3 1.8 %collective-permute-start.6 = (f32[264,128]{1,0:T(8,128)S(1)}, f32[264,128]{1,0:T(8,128)S(1)}, u32[]{:S(2)}, u32[]{:S(2)}) collective-permute-start(f32[264,128]{1,0:T(8,128)S(1)} %add.21.refs_0_), channel_id=1, source_target_pairs={{0,12},{4,16},{8,4},{12,24},{16,28},{20,0},{24,20},{28,8},{1,13},{... | collective-permute-start | bytes 405512 | tf_op jit(solution)/shard_map/ppermute | solution.py:28
  10.5 2.3 %collective-permute-done.6.refs_1_ = f32[264,128]{1,0:T(8,128)S(1)} collective-permute-done((f32[264,128]{1,0:T(8,128)S(1)}, f32[264,128]{1,0:T(8,128)S(1)}, u32[]{:S(2)}, u32[]{:S(2)}) %collective-permute-start.6) | collective-permute-done | bytes 135200 | tf_op jit(solution)/shard_map/ppermute | solution.py:28
  14.2 1.7 %shard_map.39 = (f32[256,128]{1,0:T(8,128)S(1)}, f32[256,128]{1,0:T(8,128)S(1)}, f32[8,128]{1,0:T(8,128)S(1)}) custom-call(bf16[256,128]{1,0:T(8,128)(2,1)S(1)} %get-tuple-element.71.own_high, bf16[256,128]{1,0:T(8,128)(2,1)S(1)} %get-tuple-element.72.own_low, bf16[256,256]{1,0:T(8,128)(2,1)S(1)} %get-tuple-element.73.upper_high, ...), custom_call_target="tpu_custom_call" | custom-call | tf_op jit(solution)/shard_map/pallas_call | solution.py:265
  15.9 1.9 %collective-permute-start.8 = (f32[256,128]{1,0:T(8,128)S(1)}, f32[256,128]{1,0:T(8,128)S(1)}, u32[]{:S(2)}, u32[]{:S(2)}) collective-permute-start(f32[256,128]{1,0:T(8,128)S(1)} %get-tuple-element.84), channel_id=1, source_target_pairs={{0,5},{1,6},{2,7},{3,4},{4,1},{5,2},{6,3},{7,0},{8,13},{9,14},{10,... | collective-permute-start | bytes 393224 | tf_op jit(solution)/shard_map/ppermute | solution.py:22
  19.1 1.9 %shard_map.40 = (bf16[256,768]{1,0:T(8,128)(2,1)S(1)}, f32[1,256]{1,0:T(1,128)S(1)}, f32[256,256]{1,0:T(8,128)S(1)}) custom-call(f32[256,1]{1,0:T(8,128)S(1)} %copy.7.weight, f32[256,128]{1,0:T(8,128)S(1)} %get-tuple-element.70.refs_0_, f32[256,128]{1,0:T(8,128)S(1)} %get-tuple-element.80.refs_1_, f32[8,128]{1,0:T(8,128)S(1)} %get-tuple-element.81.refs_2_, ...), custom_call_target="tpu_custom_call" | custom-call | tf_op jit(solution)/shard_map/pallas_call | solution.py:265
  20.9 2.4 %collective-permute-done.8.own_ref.refs_3_.refs_4_ = f32[256,128]{1,0:T(8,128)S(1)} collective-permute-done((f32[256,128]{1,0:T(8,128)S(1)}, f32[256,128]{1,0:T(8,128)S(1)}, u32[]{:S(2)}, u32[]{:S(2)}) %collective-permute-start.8) | collective-permute-done | bytes 131104 | tf_op jit(solution)/shard_map/ppermute | solution.py:22
  23.6 1.6 %collective-permute-start.9 = (f32[264,128]{1,0:T(8,128)S(1)}, f32[264,128]{1,0:T(8,128)S(1)}, u32[]{:S(2)}, u32[]{:S(2)}) collective-permute-start(f32[264,128]{1,0:T(8,128)S(1)} %shard_map.41), channel_id=1, source_target_pairs={{0,12},{4,16},{8,4},{12,24},{16,28},{20,0},{24,20},{28,8},{1,13},{... | collective-permute-start | bytes 405512 | tf_op jit(solution)/shard_map/ppermute | solution.py:28
  25.8 2.3 %collective-permute-done.9 = f32[264,128]{1,0:T(8,128)S(1)} collective-permute-done((f32[264,128]{1,0:T(8,128)S(1)}, f32[264,128]{1,0:T(8,128)S(1)}, u32[]{:S(2)}, u32[]{:S(2)}) %collective-permute-start.9) | collective-permute-done | bytes 135200 | tf_op jit(solution)/shard_map/ppermute | solution.py:28
  28.1 1.6 %collective-permute-start.13 = (f32[264,128]{1,0:T(8,128)S(1)}, f32[264,128]{1,0:T(8,128)S(1)}, u32[]{:S(2)}, u32[]{:S(2)}) collective-permute-start(f32[264,128]{1,0:T(8,128)S(1)} %add.22.refs_0_), channel_id=1, source_target_pairs={{0,12},{4,16},{8,4},{12,24},{16,28},{20,0},{24,20},{28,8},{1,13},{... | collective-permute-start | bytes 405512 | tf_op jit(solution)/shard_map/ppermute | solution.py:28
  30.2 2.4 %collective-permute-done.13.refs_1_ = f32[264,128]{1,0:T(8,128)S(1)} collective-permute-done((f32[264,128]{1,0:T(8,128)S(1)}, f32[264,128]{1,0:T(8,128)S(1)}, u32[]{:S(2)}, u32[]{:S(2)}) %collective-permute-start.13) | collective-permute-done | bytes 135200 | tf_op jit(solution)/shard_map/ppermute | solution.py:28
  34.0 1.7 %shard_map.43 = (f32[256,128]{1,0:T(8,128)S(1)}, f32[256,128]{1,0:T(8,128)S(1)}, f32[8,128]{1,0:T(8,128)S(1)}) custom-call(bf16[256,128]{1,0:T(8,128)(2,1)S(1)} %get-tuple-element.89.own_high, bf16[256,128]{1,0:T(8,128)(2,1)S(1)} %get-tuple-element.90.own_low, bf16[256,256]{1,0:T(8,128)(2,1)S(1)} %get-tuple-element.91.upper_high, ...), custom_call_target="tpu_custom_call" | custom-call | tf_op jit(solution)/shard_map/pallas_call | solution.py:265
  35.7 1.9 %shard_map.44 = (bf16[256,768]{1,0:T(8,128)(2,1)S(1)}, f32[1,256]{1,0:T(1,128)S(1)}, f32[256,256]{1,0:T(8,128)S(1)}) custom-call(f32[256,1]{1,0:T(8,128)S(1)} %copy.7.weight, f32[256,128]{1,0:T(8,128)S(1)} %get-tuple-element.88.refs_0_, f32[256,128]{1,0:T(8,128)S(1)} %get-tuple-element.98.refs_1_, f32[8,128]{1,0:T(8,128)S(1)} %get-tuple-element.99.refs_2_, ...), custom_call_target="tpu_custom_call" | custom-call | tf_op jit(solution)/shard_map/pallas_call | solution.py:265
  37.6 5.3 %collective-permute-done.15.own_ref.refs_3_.refs_4_ = f32[256,128]{1,0:T(8,128)S(1)} collective-permute-done((f32[256,128]{1,0:T(8,128)S(1)}, f32[256,128]{1,0:T(8,128)S(1)}, u32[]{:S(2)}, u32[]{:S(2)}) %collective-permute-start.15) | collective-permute-done | bytes 131104 | tf_op jit(solution)/shard_map/ppermute | solution.py:22
  43.1 1.8 %collective-permute-start.16 = (f32[264,128]{1,0:T(8,128)S(1)}, f32[264,128]{1,0:T(8,128)S(1)}, u32[]{:S(2)}, u32[]{:S(2)}) collective-permute-start(f32[264,128]{1,0:T(8,128)S(1)} %shard_map.45), channel_id=1, source_target_pairs={{0,12},{4,16},{8,4},{12,24},{16,28},{20,0},{24,20},{28,8},{1,13},{... | collective-permute-start | bytes 405512 | tf_op jit(solution)/shard_map/ppermute | solution.py:28
  45.4 2.2 %collective-permute-done.16 = f32[264,128]{1,0:T(8,128)S(1)} collective-permute-done((f32[264,128]{1,0:T(8,128)S(1)}, f32[264,128]{1,0:T(8,128)S(1)}, u32[]{:S(2)}, u32[]{:S(2)}) %collective-permute-start.16) | collective-permute-done | bytes 135200 | tf_op jit(solution)/shard_map/ppermute | solution.py:28
  47.7 1.8 %collective-permute-start.20 = (f32[264,128]{1,0:T(8,128)S(1)}, f32[264,128]{1,0:T(8,128)S(1)}, u32[]{:S(2)}, u32[]{:S(2)}) collective-permute-start(f32[264,128]{1,0:T(8,128)S(1)} %add.23.refs_0_), channel_id=1, source_target_pairs={{0,12},{4,16},{8,4},{12,24},{16,28},{20,0},{24,20},{28,8},{1,13},{... | collective-permute-start | bytes 405512 | tf_op jit(solution)/shard_map/ppermute | solution.py:28
  49.8 2.3 %collective-permute-done.20.refs_1_ = f32[264,128]{1,0:T(8,128)S(1)} collective-permute-done((f32[264,128]{1,0:T(8,128)S(1)}, f32[264,128]{1,0:T(8,128)S(1)}, u32[]{:S(2)}, u32[]{:S(2)}) %collective-permute-start.20) | collective-permute-done | bytes 135200 | tf_op jit(solution)/shard_map/ppermute | solution.py:28
  53.5 1.6 %shard_map.47 = (f32[128,256]{1,0:T(8,128)S(1)}, f32[256,128]{1,0:T(8,128)S(1)}, f32[8,128]{1,0:T(8,128)S(1)}) custom-call(bf16[256,128]{1,0:T(8,128)(2,1)S(1)} %get-tuple-element.106.own_high, bf16[256,128]{1,0:T(8,128)(2,1)S(1)} %get-tuple-element.107.own_low, bf16[128,256]{1,0:T(8,128)(2,1)S(1)} %get-tuple-element.108.upper_high, ...), custom_call_target="tpu_custom_call" | custom-call | tf_op jit(solution)/shard_map/pallas_call | solution.py:265
  55.2 2.3 %shard_map.48.filled = f32[128,512]{1,0:T(8,128)} custom-call(f32[256,128]{1,0:T(8,128)S(1)} %get-tuple-element.116.refs_0_, f32[256,128]{1,0:T(8,128)S(1)} %get-tuple-element.117.refs_1_, f32[8,128]{1,0:T(8,128)S(1)} %get-tuple-element.118.refs_2_, f32[256,256]{1,0:T(8,128)S(1)} %get-tuple-element.104.refs_2_.refs_3_, ...), custom_call_target="tpu_custom_call" | custom-call | tf_op jit(solution)/shard_map/pallas_call | solution.py:338
  57.6 5.0 %collective-permute-done.22.lower = f32[128,256]{1,0:T(8,128)S(1)} collective-permute-done((f32[128,256]{1,0:T(8,128)S(1)}, f32[128,256]{1,0:T(8,128)S(1)}, u32[]{:S(2)}, u32[]{:S(2)}) %collective-permute-start.22) | collective-permute-done | bytes 131104 | tf_op jit(solution)/shard_map/ppermute | solution.py:22
  (47 shorter events, 10.0 us)
Async XLA Ops:
  1.4 1.5 %collective-permute-start.1 = (f32[264,128]{1,0:T(8,128)S(1)}, f32[264,128]{1,0:T(8,128)S(1)}, u32[]{:S(2)}, u32[]{:S(2)}) collective-permute-start(f32[264,128]{1,0:T(8,128)S(1)} %get-tuple-element.66), channel_id=1, source_target_pairs={{0,4},{4,0},{8,12},{12,8},{16,20},{20,16},{24,28},{28,24},{1,5},{5... | collective-permute-start | bytes 405512 | tf_op jit(solution)/shard_map/ppermute | solution.py:28
  1.9 6.4 %collective-permute-start.4 = (f32[128,512]{1,0:T(8,128)S(1)}, f32[128,512]{1,0:T(8,128)S(1)}, u32[]{:S(2)}, u32[]{:S(2)}) collective-permute-start(f32[128,512]{1,0:T(8,128)S(1)} %get-tuple-element.67.refs_2_.refs_3_), channel_id=1, source_target_pairs={{0,4},{4,0},{8,12},{12,8},{16,20},{20,16},{24,28},{28,24},{1,5},{5... | collective-permute-start | bytes 786440 | tf_op jit(solution)/shard_map/ppermute | solution.py:28
  2.9 10.3 %copy-start.1 = (s32[3,2]{0,1:T(2,128)S(1)}, s32[3,2]{0,1:T(2,128)}, u32[]{:S(2)}) copy-start(s32[3,2]{0,1:T(2,128)} %param.5) | copy-start | bytes 76
  2.9 5.4 %collective-permute-start.2 = (f32[264,128]{1,0:T(8,128)S(1)}, f32[264,128]{1,0:T(8,128)S(1)}, u32[]{:S(2)}, u32[]{:S(2)}) collective-permute-start(f32[264,128]{1,0:T(8,128)S(1)} %add.20), channel_id=1, source_target_pairs={{0,12},{4,16},{8,4},{12,24},{16,28},{20,0},{24,20},{28,8},{1,13},{... | collective-permute-start | bytes 405512 | tf_op jit(solution)/shard_map/ppermute | solution.py:28
  5.6 2.7 %collective-permute-start.3 = (f32[264,128]{1,0:T(8,128)S(1)}, f32[264,128]{1,0:T(8,128)S(1)}, u32[]{:S(2)}, u32[]{:S(2)}) collective-permute-start(f32[264,128]{1,0:T(8,128)S(1)} %add.20), channel_id=1, source_target_pairs={{0,4},{4,0},{8,12},{12,8},{16,20},{20,16},{24,28},{28,24},{1,5},{5... | collective-permute-start | bytes 405512 | tf_op jit(solution)/shard_map/ppermute | solution.py:28
  8.3 4.5 %collective-permute-start.6 = (f32[264,128]{1,0:T(8,128)S(1)}, f32[264,128]{1,0:T(8,128)S(1)}, u32[]{:S(2)}, u32[]{:S(2)}) collective-permute-start(f32[264,128]{1,0:T(8,128)S(1)} %add.21.refs_0_), channel_id=1, source_target_pairs={{0,12},{4,16},{8,4},{12,24},{16,28},{20,0},{24,20},{28,8},{1,13},{... | collective-permute-start | bytes 405512 | tf_op jit(solution)/shard_map/ppermute | solution.py:28
  10.1 3.1 %collective-permute-start.5 = (f32[264,128]{1,0:T(8,128)S(1)}, f32[264,128]{1,0:T(8,128)S(1)}, u32[]{:S(2)}, u32[]{:S(2)}) collective-permute-start(f32[264,128]{1,0:T(8,128)S(1)} %add.21.refs_0_), channel_id=1, source_target_pairs={{0,4},{4,0},{8,12},{12,8},{16,20},{20,16},{24,28},{28,24},{1,5},{5... | collective-permute-start | bytes 405512 | tf_op jit(solution)/shard_map/ppermute | solution.py:28
  12.8 1.4 %collective-permute-start.7 = (f32[264,128]{1,0:T(8,128)S(1)}, f32[264,128]{1,0:T(8,128)S(1)}, u32[]{:S(2)}, u32[]{:S(2)}) collective-permute-start(f32[264,128]{1,0:T(8,128)S(1)} %collective-permute-done.6.refs_1_), channel_id=1, source_target_pairs={{0,4},{4,0},{8,12},{12,8},{16,20},{20,16},{24,28},{28,24},{1,5},{5... | collective-permute-start | bytes 405512 | tf_op jit(solution)/shard_map/ppermute | solution.py:28
  15.9 7.5 %collective-permute-start.8 = (f32[256,128]{1,0:T(8,128)S(1)}, f32[256,128]{1,0:T(8,128)S(1)}, u32[]{:S(2)}, u32[]{:S(2)}) collective-permute-start(f32[256,128]{1,0:T(8,128)S(1)} %get-tuple-element.84), channel_id=1, source_target_pairs={{0,5},{1,6},{2,7},{3,4},{4,1},{5,2},{6,3},{7,0},{8,13},{9,14},{10,... | collective-permute-start | bytes 393224 | tf_op jit(solution)/shard_map/ppermute | solution.py:22
  17.7 1.2 %collective-permute-start = (f32[128]{0:T(128)S(1)}, f32[128]{0:T(128)S(1)}, u32[]{:S(2)}, u32[]{:S(2)}) collective-permute-start(f32[128]{0:T(128)S(1)} %copy-done), channel_id=1, source_target_pairs={{0,4},{4,0},{8,12},{12,8},{16,20},{20,16},{24,28},{28,24},{1,5},{5... | collective-permute-start | bytes 1544 | tf_op jit(solution)/shard_map/ppermute | solution.py:28
  23.6 4.5 %collective-permute-start.9 = (f32[264,128]{1,0:T(8,128)S(1)}, f32[264,128]{1,0:T(8,128)S(1)}, u32[]{:S(2)}, u32[]{:S(2)}) collective-permute-start(f32[264,128]{1,0:T(8,128)S(1)} %shard_map.41), channel_id=1, source_target_pairs={{0,12},{4,16},{8,4},{12,24},{16,28},{20,0},{24,20},{28,8},{1,13},{... | collective-permute-start | bytes 405512 | tf_op jit(solution)/shard_map/ppermute | solution.py:28
  25.2 2.8 %collective-permute-start.10 = (f32[264,128]{1,0:T(8,128)S(1)}, f32[264,128]{1,0:T(8,128)S(1)}, u32[]{:S(2)}, u32[]{:S(2)}) collective-permute-start(f32[264,128]{1,0:T(8,128)S(1)} %shard_map.41), channel_id=1, source_target_pairs={{0,4},{4,0},{8,12},{12,8},{16,20},{20,16},{24,28},{28,24},{1,5},{5... | collective-permute-start | bytes 405512 | tf_op jit(solution)/shard_map/ppermute | solution.py:28
  25.7 2.4 %collective-permute-start.11 = (f32[256,128]{1,0:T(8,128)S(1)}, f32[256,128]{1,0:T(8,128)S(1)}, u32[]{:S(2)}, u32[]{:S(2)}) collective-permute-start(f32[256,128]{1,0:T(8,128)S(1)} %collective-permute-done.8.own_ref.refs_3_.refs_4_), channel_id=1, source_target_pairs={{0,4},{4,0},{8,12},{12,8},{16,20},{20,16},{24,28},{28,24},{1,5},{5... | collective-permute-start | bytes 393224 | tf_op jit(solution)/shard_map/ppermute | solution.py:28
  28.1 4.5 %collective-permute-start.13 = (f32[264,128]{1,0:T(8,128)S(1)}, f32[264,128]{1,0:T(8,128)S(1)}, u32[]{:S(2)}, u32[]{:S(2)}) collective-permute-start(f32[264,128]{1,0:T(8,128)S(1)} %add.22.refs_0_), channel_id=1, source_target_pairs={{0,12},{4,16},{8,4},{12,24},{16,28},{20,0},{24,20},{28,8},{1,13},{... | collective-permute-start | bytes 405512 | tf_op jit(solution)/shard_map/ppermute | solution.py:28
  29.8 3.1 %collective-permute-start.12 = (f32[264,128]{1,0:T(8,128)S(1)}, f32[264,128]{1,0:T(8,128)S(1)}, u32[]{:S(2)}, u32[]{:S(2)}) collective-permute-start(f32[264,128]{1,0:T(8,128)S(1)} %add.22.refs_0_), channel_id=1, source_target_pairs={{0,4},{4,0},{8,12},{12,8},{16,20},{20,16},{24,28},{28,24},{1,5},{5... | collective-permute-start | bytes 405512 | tf_op jit(solution)/shard_map/ppermute | solution.py:28
  32.6 1.4 %collective-permute-start.14 = (f32[264,128]{1,0:T(8,128)S(1)}, f32[264,128]{1,0:T(8,128)S(1)}, u32[]{:S(2)}, u32[]{:S(2)}) collective-permute-start(f32[264,128]{1,0:T(8,128)S(1)} %collective-permute-done.13.refs_1_), channel_id=1, source_target_pairs={{0,4},{4,0},{8,12},{12,8},{16,20},{20,16},{24,28},{28,24},{1,5},{5... | collective-permute-start | bytes 405512 | tf_op jit(solution)/shard_map/ppermute | solution.py:28
  35.6 7.2 %collective-permute-start.15 = (f32[256,128]{1,0:T(8,128)S(1)}, f32[256,128]{1,0:T(8,128)S(1)}, u32[]{:S(2)}, u32[]{:S(2)}) collective-permute-start(f32[256,128]{1,0:T(8,128)S(1)} %get-tuple-element.102), channel_id=1, source_target_pairs={{0,5},{1,6},{2,7},{3,4},{4,1},{5,2},{6,3},{7,0},{8,13},{9,14},{10,... | collective-permute-start | bytes 393224 | tf_op jit(solution)/shard_map/ppermute | solution.py:22
  43.1 4.5 %collective-permute-start.16 = (f32[264,128]{1,0:T(8,128)S(1)}, f32[264,128]{1,0:T(8,128)S(1)}, u32[]{:S(2)}, u32[]{:S(2)}) collective-permute-start(f32[264,128]{1,0:T(8,128)S(1)} %shard_map.45), channel_id=1, source_target_pairs={{0,12},{4,16},{8,4},{12,24},{16,28},{20,0},{24,20},{28,8},{1,13},{... | collective-permute-start | bytes 405512 | tf_op jit(solution)/shard_map/ppermute | solution.py:28
  44.9 2.7 %collective-permute-start.17 = (f32[264,128]{1,0:T(8,128)S(1)}, f32[264,128]{1,0:T(8,128)S(1)}, u32[]{:S(2)}, u32[]{:S(2)}) collective-permute-start(f32[264,128]{1,0:T(8,128)S(1)} %shard_map.45), channel_id=1, source_target_pairs={{0,4},{4,0},{8,12},{12,8},{16,20},{20,16},{24,28},{28,24},{1,5},{5... | collective-permute-start | bytes 405512 | tf_op jit(solution)/shard_map/ppermute | solution.py:28
  45.3 2.4 %collective-permute-start.18 = (f32[256,128]{1,0:T(8,128)S(1)}, f32[256,128]{1,0:T(8,128)S(1)}, u32[]{:S(2)}, u32[]{:S(2)}) collective-permute-start(f32[256,128]{1,0:T(8,128)S(1)} %collective-permute-done.15.own_ref.refs_3_.refs_4_), channel_id=1, source_target_pairs={{0,4},{4,0},{8,12},{12,8},{16,20},{20,16},{24,28},{28,24},{1,5},{5... | collective-permute-start | bytes 393224 | tf_op jit(solution)/shard_map/ppermute | solution.py:28
  47.7 4.5 %collective-permute-start.20 = (f32[264,128]{1,0:T(8,128)S(1)}, f32[264,128]{1,0:T(8,128)S(1)}, u32[]{:S(2)}, u32[]{:S(2)}) collective-permute-start(f32[264,128]{1,0:T(8,128)S(1)} %add.23.refs_0_), channel_id=1, source_target_pairs={{0,12},{4,16},{8,4},{12,24},{16,28},{20,0},{24,20},{28,8},{1,13},{... | collective-permute-start | bytes 405512 | tf_op jit(solution)/shard_map/ppermute | solution.py:28
  49.4 3.1 %collective-permute-start.19 = (f32[264,128]{1,0:T(8,128)S(1)}, f32[264,128]{1,0:T(8,128)S(1)}, u32[]{:S(2)}, u32[]{:S(2)}) collective-permute-start(f32[264,128]{1,0:T(8,128)S(1)} %add.23.refs_0_), channel_id=1, source_target_pairs={{0,4},{4,0},{8,12},{12,8},{16,20},{20,16},{24,28},{28,24},{1,5},{5... | collective-permute-start | bytes 405512 | tf_op jit(solution)/shard_map/ppermute | solution.py:28
  52.2 1.4 %collective-permute-start.21 = (f32[264,128]{1,0:T(8,128)S(1)}, f32[264,128]{1,0:T(8,128)S(1)}, u32[]{:S(2)}, u32[]{:S(2)}) collective-permute-start(f32[264,128]{1,0:T(8,128)S(1)} %collective-permute-done.20.refs_1_), channel_id=1, source_target_pairs={{0,4},{4,0},{8,12},{12,8},{16,20},{20,16},{24,28},{28,24},{1,5},{5... | collective-permute-start | bytes 405512 | tf_op jit(solution)/shard_map/ppermute | solution.py:28
  55.2 7.5 %collective-permute-start.22 = (f32[128,256]{1,0:T(8,128)S(1)}, f32[128,256]{1,0:T(8,128)S(1)}, u32[]{:S(2)}, u32[]{:S(2)}) collective-permute-start(f32[128,256]{1,0:T(8,128)S(1)} %get-tuple-element.115), channel_id=1, source_target_pairs={{0,6},{1,7},{2,4},{3,5},{4,2},{5,3},{6,0},{7,1},{8,14},{9,15},{10,... | collective-permute-start | bytes 393224 | tf_op jit(solution)/shard_map/ppermute | solution.py:22
  (1 other events, 1.9 us)

commit v19 on v18

--- a/solution.py
+++ b/solution.py
@@ -126,30 +126,37 @@
     return jnp.where(rows == 0, norm_lower, uppers)
 
 
-def start_kernel(near_ref, weight_ref, own_part, other_part, near, weight, near_sent, weight_sent):
+def start_kernel(near_ref, weight_ref, own_part, other_part, near, weight, weight_sent, *near_sent):
+    rows = near.shape[0] // len(near_sent)
+    pieces = [pl.ds(index * rows, rows) for index in range(len(near_sent))]
+    weight_copy = pltpu.make_async_copy(weight_ref, weight, weight_sent)
+    weight_copy.start()
     copies = [
-        pltpu.make_async_copy(near_ref, near, near_sent),
-        pltpu.make_async_copy(weight_ref, weight, weight_sent),
+        pltpu.make_async_copy(near_ref.at[piece], near.at[piece], sent) for piece, sent in zip(pieces, near_sent)
     ]
     for copy in copies:
         copy.start()
-    for copy in copies:
-        copy.wait()
+    weight_copy.wait()
     width = near.shape[1] // 2
     half = width // 2
     own, other = own_half(half)
-    point_weight = jnp.broadcast_to(weight[...], (8, weight.shape[1])).T[:, 0:1]
-    upper_own, upper_other = near[:, pl.ds(own, half)], near[:, pl.ds(other, half)]
-    upper_parts = two_parts(jnp.concatenate([upper_own, upper_other], axis=1))
-    orders = ((upper_own, upper_other), (upper_other, upper_own))
-    for start, order, out in zip((own, other), orders, (own_part, other_part)):
-        lower = near[:, pl.ds(width + start, half)]
-        weighted = point_weight * lower
-        gram = product(upper_parts, two_parts(weighted), 0, 0)
-        out[:width] = gram if out is own_part else halves_swapped(gram)
-        norm_lower = jnp.sum(weighted * lower, axis=0, keepdims=True)
-        uppers = [jnp.sum(point_weight * value * value, axis=0, keepdims=True) for value in order]
-        out[width:] = norm_rows(norm_lower, *uppers)
+    point_weights = jnp.broadcast_to(weight[...], (8, weight.shape[1])).T[:, 0:1]
+    grams, norms = [0.0, 0.0], [0.0, 0.0, 0.0, 0.0]
+    for index, (piece, copy) in enumerate(zip(pieces, copies)):
+        copy.wait()
+        point_weight = point_weights[index * rows : (index + 1) * rows]
+        uppers = near[piece, pl.ds(own, half)], near[piece, pl.ds(other, half)]
+        upper_parts = two_parts(jnp.concatenate(uppers, axis=1))
+        for place, start in enumerate((own, other)):
+            lower = near[piece, pl.ds(width + start, half)]
+            weighted = point_weight * lower
+            grams[place] += product(upper_parts, two_parts(weighted), 0, 0)
+            norms[place] += jnp.sum(weighted * lower, axis=0, keepdims=True)
+            norms[2 + place] += jnp.sum(point_weight * uppers[place] * uppers[place], axis=0, keepdims=True)
+    own_part[:width] = grams[0]
+    own_part[width:] = norm_rows(norms[0], norms[2], norms[3])
+    other_part[:width] = halves_swapped(grams[1])
+    other_part[width:] = norm_rows(norms[1], norms[3], norms[2])
 
 
 def taken_rows(last, rows):
@@ -283,6 +290,7 @@
         out_specs=[ON_CHIP] * 3,
         scratch_shapes=[
             pltpu.VMEM((1, rows), F32),
+            pltpu.SemaphoreType.DMA(()),
             pltpu.SemaphoreType.DMA(()),
             pltpu.SemaphoreType.DMA(()),
         ],

time: 63.4 us -> 63.4 us (level)
  no operation moved by 1% of the time
where the time goes in v19:
time: 63.4 us; the launch traced here: 63.3 us
  waiting for transfers between devices  29.6 us (47%)
  starting transfers between devices  17.8 us (28%)
  Pallas kernels  15.4 us (24%)
    ppermute x20, waiting for transfers between devices, swapped(): return lax.ppermute(value, 'pts', pairs)  16.9 us
    ppermute x20, starting transfers between devices, swapped(): return lax.ppermute(value, 'pts', pairs)  15.8 us
    ppermute x3, waiting for transfers between devices, column_shift(): return lax.ppermute(value, ('pts', 'cols'), pairs)  12.7 us
    pallas_call x10, Pallas kernels, in_vmem(): pl.pallas_call(kernel, out_shape=[jax.ShapeDtypeStruct(shape, dtype) for...  11 us
    pallas_call x1, Pallas kernels, body(): pl.pallas_call(functools.partial(last_upper_kernel, blocks), out_shape=ou...  2.33 us
    ppermute x3, starting transfers between devices, column_shift(): return lax.ppermute(value, ('pts', 'cols'), pairs)  1.99 us
    pallas_call x1, Pallas kernels, body(): pl.pallas_call(start_kernel, out_shape=[jax.ShapeDtypeStruct((width + 8,...  1.4 us
  transfers between devices with their start and end apart: 23, of which 14 were waited for; matrix products, arithmetic and copies ran while one was open for 0% of the time, Pallas kernels for 12%

profile of v19, /device:TPU:0, one launch (start us, length us, event | category | flops | bytes accessed | tf_op | source)
XLA Modules:
  0.0 63.3 jit_solution(15301628721875938313)
XLA Ops:
  0.0 1.4 %shard_map.37 = (f32[264,128]{1,0:T(8,128)S(1)}, f32[264,128]{1,0:T(8,128)S(1)}, f32[128,512]{1,0:T(8,128)S(1)}) custom-call(f32[128,512]{1,0:T(8,128)} %near_ref.1, f32[1,128]{1,0:T(1,128)} %bitcast.5), custom_call_target="tpu_custom_call" | custom-call | tf_op jit(solution)/shard_map/pallas_call | solution.py:286
  2.0 0.9 %collective-permute-done.1 = f32[264,128]{1,0:T(8,128)S(1)} collective-permute-done((f32[264,128]{1,0:T(8,128)S(1)}, f32[264,128]{1,0:T(8,128)S(1)}, u32[]{:S(2)}, u32[]{:S(2)}) %collective-permute-start.1) | collective-permute-done | bytes 135200 | tf_op jit(solution)/shard_map/ppermute | solution.py:28
  2.9 2.7 %collective-permute-start.2 = (f32[264,128]{1,0:T(8,128)S(1)}, f32[264,128]{1,0:T(8,128)S(1)}, u32[]{:S(2)}, u32[]{:S(2)}) collective-permute-start(f32[264,128]{1,0:T(8,128)S(1)} %add.20), channel_id=1, source_target_pairs={{0,12},{4,16},{8,4},{12,24},{16,28},{20,0},{24,20},{28,8},{1,13},{... | collective-permute-start | bytes 405512 | tf_op jit(solution)/shard_map/ppermute | solution.py:28
  6.0 2.3 %collective-permute-done.2 = f32[264,128]{1,0:T(8,128)S(1)} collective-permute-done((f32[264,128]{1,0:T(8,128)S(1)}, f32[264,128]{1,0:T(8,128)S(1)}, u32[]{:S(2)}, u32[]{:S(2)}) %collective-permute-start.2) | collective-permute-done | bytes 135200 | tf_op jit(solution)/shard_map/ppermute | solution.py:28
  8.4 1.8 %collective-permute-start.6 = (f32[264,128]{1,0:T(8,128)S(1)}, f32[264,128]{1,0:T(8,128)S(1)}, u32[]{:S(2)}, u32[]{:S(2)}) collective-permute-start(f32[264,128]{1,0:T(8,128)S(1)} %add.21.refs_0_), channel_id=1, source_target_pairs={{0,12},{4,16},{8,4},{12,24},{16,28},{20,0},{24,20},{28,8},{1,13},{... | collective-permute-start | bytes 405512 | tf_op jit(solution)/shard_map/ppermute | solution.py:28
  10.5 2.3 %collective-permute-done.6.refs_1_ = f32[264,128]{1,0:T(8,128)S(1)} collective-permute-done((f32[264,128]{1,0:T(8,128)S(1)}, f32[264,128]{1,0:T(8,128)S(1)}, u32[]{:S(2)}, u32[]{:S(2)}) %collective-permute-start.6) | collective-permute-done | bytes 135200 | tf_op jit(solution)/shard_map/ppermute | solution.py:28
  14.2 1.7 %shard_map.39 = (f32[256,128]{1,0:T(8,128)S(1)}, f32[256,128]{1,0:T(8,128)S(1)}, f32[8,128]{1,0:T(8,128)S(1)}) custom-call(bf16[256,128]{1,0:T(8,128)(2,1)S(1)} %get-tuple-element.71.own_high, bf16[256,128]{1,0:T(8,128)(2,1)S(1)} %get-tuple-element.72.own_low, bf16[256,256]{1,0:T(8,128)(2,1)S(1)} %get-tuple-element.73.upper_high, ...), custom_call_target="tpu_custom_call" | custom-call | tf_op jit(solution)/shard_map/pallas_call | solution.py:272
  15.9 1.9 %collective-permute-start.8 = (f32[256,128]{1,0:T(8,128)S(1)}, f32[256,128]{1,0:T(8,128)S(1)}, u32[]{:S(2)}, u32[]{:S(2)}) collective-permute-start(f32[256,128]{1,0:T(8,128)S(1)} %get-tuple-element.84), channel_id=1, source_target_pairs={{0,5},{1,6},{2,7},{3,4},{4,1},{5,2},{6,3},{7,0},{8,13},{9,14},{10,... | collective-permute-start | bytes 393224 | tf_op jit(solution)/shard_map/ppermute | solution.py:22
  19.1 1.9 %shard_map.40 = (bf16[256,768]{1,0:T(8,128)(2,1)S(1)}, f32[1,256]{1,0:T(1,128)S(1)}, f32[256,256]{1,0:T(8,128)S(1)}) custom-call(f32[256,1]{1,0:T(8,128)S(1)} %copy.7.weight, f32[256,128]{1,0:T(8,128)S(1)} %get-tuple-element.70.refs_0_, f32[256,128]{1,0:T(8,128)S(1)} %get-tuple-element.80.refs_1_, f32[8,128]{1,0:T(8,128)S(1)} %get-tuple-element.81.refs_2_, ...), custom_call_target="tpu_custom_call" | custom-call | tf_op jit(solution)/shard_map/pallas_call | solution.py:272
  21.0 2.4 %collective-permute-done.8.own_ref.refs_3_.refs_4_ = f32[256,128]{1,0:T(8,128)S(1)} collective-permute-done((f32[256,128]{1,0:T(8,128)S(1)}, f32[256,128]{1,0:T(8,128)S(1)}, u32[]{:S(2)}, u32[]{:S(2)}) %collective-permute-start.8) | collective-permute-done | bytes 131104 | tf_op jit(solution)/shard_map/ppermute | solution.py:22
  23.6 1.7 %collective-permute-start.9 = (f32[264,128]{1,0:T(8,128)S(1)}, f32[264,128]{1,0:T(8,128)S(1)}, u32[]{:S(2)}, u32[]{:S(2)}) collective-permute-start(f32[264,128]{1,0:T(8,128)S(1)} %shard_map.41), channel_id=1, source_target_pairs={{0,12},{4,16},{8,4},{12,24},{16,28},{20,0},{24,20},{28,8},{1,13},{... | collective-permute-start | bytes 405512 | tf_op jit(solution)/shard_map/ppermute | solution.py:28
  25.8 2.3 %collective-permute-done.9 = f32[264,128]{1,0:T(8,128)S(1)} collective-permute-done((f32[264,128]{1,0:T(8,128)S(1)}, f32[264,128]{1,0:T(8,128)S(1)}, u32[]{:S(2)}, u32[]{:S(2)}) %collective-permute-start.9) | collective-permute-done | bytes 135200 | tf_op jit(solution)/shard_map/ppermute | solution.py:28
  28.1 1.7 %collective-permute-start.13 = (f32[264,128]{1,0:T(8,128)S(1)}, f32[264,128]{1,0:T(8,128)S(1)}, u32[]{:S(2)}, u32[]{:S(2)}) collective-permute-start(f32[264,128]{1,0:T(8,128)S(1)} %add.22.refs_0_), channel_id=1, source_target_pairs={{0,12},{4,16},{8,4},{12,24},{16,28},{20,0},{24,20},{28,8},{1,13},{... | collective-permute-start | bytes 405512 | tf_op jit(solution)/shard_map/ppermute | solution.py:28
  30.2 2.4 %collective-permute-done.13.refs_1_ = f32[264,128]{1,0:T(8,128)S(1)} collective-permute-done((f32[264,128]{1,0:T(8,128)S(1)}, f32[264,128]{1,0:T(8,128)S(1)}, u32[]{:S(2)}, u32[]{:S(2)}) %collective-permute-start.13) | collective-permute-done | bytes 135200 | tf_op jit(solution)/shard_map/ppermute | solution.py:28
  34.0 1.7 %shard_map.43 = (f32[256,128]{1,0:T(8,128)S(1)}, f32[256,128]{1,0:T(8,128)S(1)}, f32[8,128]{1,0:T(8,128)S(1)}) custom-call(bf16[256,128]{1,0:T(8,128)(2,1)S(1)} %get-tuple-element.89.own_high, bf16[256,128]{1,0:T(8,128)(2,1)S(1)} %get-tuple-element.90.own_low, bf16[256,256]{1,0:T(8,128)(2,1)S(1)} %get-tuple-element.91.upper_high, ...), custom_call_target="tpu_custom_call" | custom-call | tf_op jit(solution)/shard_map/pallas_call | solution.py:272
  35.7 1.9 %shard_map.44 = (bf16[256,768]{1,0:T(8,128)(2,1)S(1)}, f32[1,256]{1,0:T(1,128)S(1)}, f32[256,256]{1,0:T(8,128)S(1)}) custom-call(f32[256,1]{1,0:T(8,128)S(1)} %copy.7.weight, f32[256,128]{1,0:T(8,128)S(1)} %get-tuple-element.88.refs_0_, f32[256,128]{1,0:T(8,128)S(1)} %get-tuple-element.98.refs_1_, f32[8,128]{1,0:T(8,128)S(1)} %get-tuple-element.99.refs_2_, ...), custom_call_target="tpu_custom_call" | custom-call | tf_op jit(solution)/shard_map/pallas_call | solution.py:272
  37.6 5.3 %collective-permute-done.15.own_ref.refs_3_.refs_4_ = f32[256,128]{1,0:T(8,128)S(1)} collective-permute-done((f32[256,128]{1,0:T(8,128)S(1)}, f32[256,128]{1,0:T(8,128)S(1)}, u32[]{:S(2)}, u32[]{:S(2)}) %collective-permute-start.15) | collective-permute-done | bytes 131104 | tf_op jit(solution)/shard_map/ppermute | solution.py:22
  43.2 1.8 %collective-permute-start.16 = (f32[264,128]{1,0:T(8,128)S(1)}, f32[264,128]{1,0:T(8,128)S(1)}, u32[]{:S(2)}, u32[]{:S(2)}) collective-permute-start(f32[264,128]{1,0:T(8,128)S(1)} %shard_map.45), channel_id=1, source_target_pairs={{0,12},{4,16},{8,4},{12,24},{16,28},{20,0},{24,20},{28,8},{1,13},{... | collective-permute-start | bytes 405512 | tf_op jit(solution)/shard_map/ppermute | solution.py:28
  45.4 2.2 %collective-permute-done.16 = f32[264,128]{1,0:T(8,128)S(1)} collective-permute-done((f32[264,128]{1,0:T(8,128)S(1)}, f32[264,128]{1,0:T(8,128)S(1)}, u32[]{:S(2)}, u32[]{:S(2)}) %collective-permute-start.16) | collective-permute-done | bytes 135200 | tf_op jit(solution)/shard_map/ppermute | solution.py:28
  47.7 1.8 %collective-permute-start.20 = (f32[264,128]{1,0:T(8,128)S(1)}, f32[264,128]{1,0:T(8,128)S(1)}, u32[]{:S(2)}, u32[]{:S(2)}) collective-permute-start(f32[264,128]{1,0:T(8,128)S(1)} %add.23.refs_0_), channel_id=1, source_target_pairs={{0,12},{4,16},{8,4},{12,24},{16,28},{20,0},{24,20},{28,8},{1,13},{... | collective-permute-start | bytes 405512 | tf_op jit(solution)/shard_map/ppermute | solution.py:28
  49.8 2.3 %collective-permute-done.20.refs_1_ = f32[264,128]{1,0:T(8,128)S(1)} collective-permute-done((f32[264,128]{1,0:T(8,128)S(1)}, f32[264,128]{1,0:T(8,128)S(1)}, u32[]{:S(2)}, u32[]{:S(2)}) %collective-permute-start.20) | collective-permute-done | bytes 135200 | tf_op jit(solution)/shard_map/ppermute | solution.py:28
  53.5 1.7 %shard_map.47 = (f32[128,256]{1,0:T(8,128)S(1)}, f32[256,128]{1,0:T(8,128)S(1)}, f32[8,128]{1,0:T(8,128)S(1)}) custom-call(bf16[256,128]{1,0:T(8,128)(2,1)S(1)} %get-tuple-element.106.own_high, bf16[256,128]{1,0:T(8,128)(2,1)S(1)} %get-tuple-element.107.own_low, bf16[128,256]{1,0:T(8,128)(2,1)S(1)} %get-tuple-element.108.upper_high, ...), custom_call_target="tpu_custom_call" | custom-call | tf_op jit(solution)/shard_map/pallas_call | solution.py:272
  55.3 2.3 %shard_map.48.filled = f32[128,512]{1,0:T(8,128)} custom-call(f32[256,128]{1,0:T(8,128)S(1)} %get-tuple-element.116.refs_0_, f32[256,128]{1,0:T(8,128)S(1)} %get-tuple-element.117.refs_1_, f32[8,128]{1,0:T(8,128)S(1)} %get-tuple-element.118.refs_2_, f32[256,256]{1,0:T(8,128)S(1)} %get-tuple-element.104.refs_2_.refs_3_, ...), custom_call_target="tpu_custom_call" | custom-call | tf_op jit(solution)/shard_map/pallas_call | solution.py:346
  57.6 5.0 %collective-permute-done.22.lower = f32[128,256]{1,0:T(8,128)S(1)} collective-permute-done((f32[128,256]{1,0:T(8,128)S(1)}, f32[128,256]{1,0:T(8,128)S(1)}, u32[]{:S(2)}, u32[]{:S(2)}) %collective-permute-start.22) | collective-permute-done | bytes 131104 | tf_op jit(solution)/shard_map/ppermute | solution.py:22
  (47 shorter events, 10.0 us)
Async XLA Ops:
  1.4 1.5 %collective-permute-start.1 = (f32[264,128]{1,0:T(8,128)S(1)}, f32[264,128]{1,0:T(8,128)S(1)}, u32[]{:S(2)}, u32[]{:S(2)}) collective-permute-start(f32[264,128]{1,0:T(8,128)S(1)} %get-tuple-element.66), channel_id=1, source_target_pairs={{0,4},{4,0},{8,12},{12,8},{16,20},{20,16},{24,28},{28,24},{1,5},{5... | collective-permute-start | bytes 405512 | tf_op jit(solution)/shard_map/ppermute | solution.py:28
  1.9 6.4 %collective-permute-start.4 = (f32[128,512]{1,0:T(8,128)S(1)}, f32[128,512]{1,0:T(8,128)S(1)}, u32[]{:S(2)}, u32[]{:S(2)}) collective-permute-start(f32[128,512]{1,0:T(8,128)S(1)} %get-tuple-element.67.refs_2_.refs_3_), channel_id=1, source_target_pairs={{0,4},{4,0},{8,12},{12,8},{16,20},{20,16},{24,28},{28,24},{1,5},{5... | collective-permute-start | bytes 786440 | tf_op jit(solution)/shard_map/ppermute | solution.py:28
  2.9 10.3 %copy-start.1 = (s32[3,2]{0,1:T(2,128)S(1)}, s32[3,2]{0,1:T(2,128)}, u32[]{:S(2)}) copy-start(s32[3,2]{0,1:T(2,128)} %param.5) | copy-start | bytes 76
  2.9 5.4 %collective-permute-start.2 = (f32[264,128]{1,0:T(8,128)S(1)}, f32[264,128]{1,0:T(8,128)S(1)}, u32[]{:S(2)}, u32[]{:S(2)}) collective-permute-start(f32[264,128]{1,0:T(8,128)S(1)} %add.20), channel_id=1, source_target_pairs={{0,12},{4,16},{8,4},{12,24},{16,28},{20,0},{24,20},{28,8},{1,13},{... | collective-permute-start | bytes 405512 | tf_op jit(solution)/shard_map/ppermute | solution.py:28
  5.6 2.7 %collective-permute-start.3 = (f32[264,128]{1,0:T(8,128)S(1)}, f32[264,128]{1,0:T(8,128)S(1)}, u32[]{:S(2)}, u32[]{:S(2)}) collective-permute-start(f32[264,128]{1,0:T(8,128)S(1)} %add.20), channel_id=1, source_target_pairs={{0,4},{4,0},{8,12},{12,8},{16,20},{20,16},{24,28},{28,24},{1,5},{5... | collective-permute-start | bytes 405512 | tf_op jit(solution)/shard_map/ppermute | solution.py:28
  8.4 4.5 %collective-permute-start.6 = (f32[264,128]{1,0:T(8,128)S(1)}, f32[264,128]{1,0:T(8,128)S(1)}, u32[]{:S(2)}, u32[]{:S(2)}) collective-permute-start(f32[264,128]{1,0:T(8,128)S(1)} %add.21.refs_0_), channel_id=1, source_target_pairs={{0,12},{4,16},{8,4},{12,24},{16,28},{20,0},{24,20},{28,8},{1,13},{... | collective-permute-start | bytes 405512 | tf_op jit(solution)/shard_map/ppermute | solution.py:28
  10.1 3.1 %collective-permute-start.5 = (f32[264,128]{1,0:T(8,128)S(1)}, f32[264,128]{1,0:T(8,128)S(1)}, u32[]{:S(2)}, u32[]{:S(2)}) collective-permute-start(f32[264,128]{1,0:T(8,128)S(1)} %add.21.refs_0_), channel_id=1, source_target_pairs={{0,4},{4,0},{8,12},{12,8},{16,20},{20,16},{24,28},{28,24},{1,5},{5... | collective-permute-start | bytes 405512 | tf_op jit(solution)/shard_map/ppermute | solution.py:28
  12.9 1.4 %collective-permute-start.7 = (f32[264,128]{1,0:T(8,128)S(1)}, f32[264,128]{1,0:T(8,128)S(1)}, u32[]{:S(2)}, u32[]{:S(2)}) collective-permute-start(f32[264,128]{1,0:T(8,128)S(1)} %collective-permute-done.6.refs_1_), channel_id=1, source_target_pairs={{0,4},{4,0},{8,12},{12,8},{16,20},{20,16},{24,28},{28,24},{1,5},{5... | collective-permute-start | bytes 405512 | tf_op jit(solution)/shard_map/ppermute | solution.py:28
  15.9 7.4 %collective-permute-start.8 = (f32[256,128]{1,0:T(8,128)S(1)}, f32[256,128]{1,0:T(8,128)S(1)}, u32[]{:S(2)}, u32[]{:S(2)}) collective-permute-start(f32[256,128]{1,0:T(8,128)S(1)} %get-tuple-element.84), channel_id=1, source_target_pairs={{0,5},{1,6},{2,7},{3,4},{4,1},{5,2},{6,3},{7,0},{8,13},{9,14},{10,... | collective-permute-start | bytes 393224 | tf_op jit(solution)/shard_map/ppermute | solution.py:22
  17.8 1.2 %collective-permute-start = (f32[128]{0:T(128)S(1)}, f32[128]{0:T(128)S(1)}, u32[]{:S(2)}, u32[]{:S(2)}) collective-permute-start(f32[128]{0:T(128)S(1)} %copy-done), channel_id=1, source_target_pairs={{0,4},{4,0},{8,12},{12,8},{16,20},{20,16},{24,28},{28,24},{1,5},{5... | collective-permute-start | bytes 1544 | tf_op jit(solution)/shard_map/ppermute | solution.py:28
  23.6 4.5 %collective-permute-start.9 = (f32[264,128]{1,0:T(8,128)S(1)}, f32[264,128]{1,0:T(8,128)S(1)}, u32[]{:S(2)}, u32[]{:S(2)}) collective-permute-start(f32[264,128]{1,0:T(8,128)S(1)} %shard_map.41), channel_id=1, source_target_pairs={{0,12},{4,16},{8,4},{12,24},{16,28},{20,0},{24,20},{28,8},{1,13},{... | collective-permute-start | bytes 405512 | tf_op jit(solution)/shard_map/ppermute | solution.py:28
  25.3 2.8 %collective-permute-start.10 = (f32[264,128]{1,0:T(8,128)S(1)}, f32[264,128]{1,0:T(8,128)S(1)}, u32[]{:S(2)}, u32[]{:S(2)}) collective-permute-start(f32[264,128]{1,0:T(8,128)S(1)} %shard_map.41), channel_id=1, source_target_pairs={{0,4},{4,0},{8,12},{12,8},{16,20},{20,16},{24,28},{28,24},{1,5},{5... | collective-permute-start | bytes 405512 | tf_op jit(solution)/shard_map/ppermute | solution.py:28
  25.7 2.4 %collective-permute-start.11 = (f32[256,128]{1,0:T(8,128)S(1)}, f32[256,128]{1,0:T(8,128)S(1)}, u32[]{:S(2)}, u32[]{:S(2)}) collective-permute-start(f32[256,128]{1,0:T(8,128)S(1)} %collective-permute-done.8.own_ref.refs_3_.refs_4_), channel_id=1, source_target_pairs={{0,4},{4,0},{8,12},{12,8},{16,20},{20,16},{24,28},{28,24},{1,5},{5... | collective-permute-start | bytes 393224 | tf_op jit(solution)/shard_map/ppermute | solution.py:28
  28.1 4.5 %collective-permute-start.13 = (f32[264,128]{1,0:T(8,128)S(1)}, f32[264,128]{1,0:T(8,128)S(1)}, u32[]{:S(2)}, u32[]{:S(2)}) collective-permute-start(f32[264,128]{1,0:T(8,128)S(1)} %add.22.refs_0_), channel_id=1, source_target_pairs={{0,12},{4,16},{8,4},{12,24},{16,28},{20,0},{24,20},{28,8},{1,13},{... | collective-permute-start | bytes 405512 | tf_op jit(solution)/shard_map/ppermute | solution.py:28
  29.8 3.1 %collective-permute-start.12 = (f32[264,128]{1,0:T(8,128)S(1)}, f32[264,128]{1,0:T(8,128)S(1)}, u32[]{:S(2)}, u32[]{:S(2)}) collective-permute-start(f32[264,128]{1,0:T(8,128)S(1)} %add.22.refs_0_), channel_id=1, source_target_pairs={{0,4},{4,0},{8,12},{12,8},{16,20},{20,16},{24,28},{28,24},{1,5},{5... | collective-permute-start | bytes 405512 | tf_op jit(solution)/shard_map/ppermute | solution.py:28
  32.6 1.4 %collective-permute-start.14 = (f32[264,128]{1,0:T(8,128)S(1)}, f32[264,128]{1,0:T(8,128)S(1)}, u32[]{:S(2)}, u32[]{:S(2)}) collective-permute-start(f32[264,128]{1,0:T(8,128)S(1)} %collective-permute-done.13.refs_1_), channel_id=1, source_target_pairs={{0,4},{4,0},{8,12},{12,8},{16,20},{20,16},{24,28},{28,24},{1,5},{5... | collective-permute-start | bytes 405512 | tf_op jit(solution)/shard_map/ppermute | solution.py:28
  35.6 7.2 %collective-permute-start.15 = (f32[256,128]{1,0:T(8,128)S(1)}, f32[256,128]{1,0:T(8,128)S(1)}, u32[]{:S(2)}, u32[]{:S(2)}) collective-permute-start(f32[256,128]{1,0:T(8,128)S(1)} %get-tuple-element.102), channel_id=1, source_target_pairs={{0,5},{1,6},{2,7},{3,4},{4,1},{5,2},{6,3},{7,0},{8,13},{9,14},{10,... | collective-permute-start | bytes 393224 | tf_op jit(solution)/shard_map/ppermute | solution.py:22
  43.2 4.5 %collective-permute-start.16 = (f32[264,128]{1,0:T(8,128)S(1)}, f32[264,128]{1,0:T(8,128)S(1)}, u32[]{:S(2)}, u32[]{:S(2)}) collective-permute-start(f32[264,128]{1,0:T(8,128)S(1)} %shard_map.45), channel_id=1, source_target_pairs={{0,12},{4,16},{8,4},{12,24},{16,28},{20,0},{24,20},{28,8},{1,13},{... | collective-permute-start | bytes 405512 | tf_op jit(solution)/shard_map/ppermute | solution.py:28
  44.9 2.7 %collective-permute-start.17 = (f32[264,128]{1,0:T(8,128)S(1)}, f32[264,128]{1,0:T(8,128)S(1)}, u32[]{:S(2)}, u32[]{:S(2)}) collective-permute-start(f32[264,128]{1,0:T(8,128)S(1)} %shard_map.45), channel_id=1, source_target_pairs={{0,4},{4,0},{8,12},{12,8},{16,20},{20,16},{24,28},{28,24},{1,5},{5... | collective-permute-start | bytes 405512 | tf_op jit(solution)/shard_map/ppermute | solution.py:28
  45.3 2.4 %collective-permute-start.18 = (f32[256,128]{1,0:T(8,128)S(1)}, f32[256,128]{1,0:T(8,128)S(1)}, u32[]{:S(2)}, u32[]{:S(2)}) collective-permute-start(f32[256,128]{1,0:T(8,128)S(1)} %collective-permute-done.15.own_ref.refs_3_.refs_4_), channel_id=1, source_target_pairs={{0,4},{4,0},{8,12},{12,8},{16,20},{20,16},{24,28},{28,24},{1,5},{5... | collective-permute-start | bytes 393224 | tf_op jit(solution)/shard_map/ppermute | solution.py:28
  47.7 4.5 %collective-permute-start.20 = (f32[264,128]{1,0:T(8,128)S(1)}, f32[264,128]{1,0:T(8,128)S(1)}, u32[]{:S(2)}, u32[]{:S(2)}) collective-permute-start(f32[264,128]{1,0:T(8,128)S(1)} %add.23.refs_0_), channel_id=1, source_target_pairs={{0,12},{4,16},{8,4},{12,24},{16,28},{20,0},{24,20},{28,8},{1,13},{... | collective-permute-start | bytes 405512 | tf_op jit(solution)/shard_map/ppermute | solution.py:28
  49.4 3.1 %collective-permute-start.19 = (f32[264,128]{1,0:T(8,128)S(1)}, f32[264,128]{1,0:T(8,128)S(1)}, u32[]{:S(2)}, u32[]{:S(2)}) collective-permute-start(f32[264,128]{1,0:T(8,128)S(1)} %add.23.refs_0_), channel_id=1, source_target_pairs={{0,4},{4,0},{8,12},{12,8},{16,20},{20,16},{24,28},{28,24},{1,5},{5... | collective-permute-start | bytes 405512 | tf_op jit(solution)/shard_map/ppermute | solution.py:28
  52.2 1.4 %collective-permute-start.21 = (f32[264,128]{1,0:T(8,128)S(1)}, f32[264,128]{1,0:T(8,128)S(1)}, u32[]{:S(2)}, u32[]{:S(2)}) collective-permute-start(f32[264,128]{1,0:T(8,128)S(1)} %collective-permute-done.20.refs_1_), channel_id=1, source_target_pairs={{0,4},{4,0},{8,12},{12,8},{16,20},{20,16},{24,28},{28,24},{1,5},{5... | collective-permute-start | bytes 405512 | tf_op jit(solution)/shard_map/ppermute | solution.py:28
  55.2 7.4 %collective-permute-start.22 = (f32[128,256]{1,0:T(8,128)S(1)}, f32[128,256]{1,0:T(8,128)S(1)}, u32[]{:S(2)}, u32[]{:S(2)}) collective-permute-start(f32[128,256]{1,0:T(8,128)S(1)} %get-tuple-element.115), channel_id=1, source_target_pairs={{0,6},{1,7},{2,4},{3,5},{4,2},{5,3},{6,0},{7,1},{8,14},{9,15},{10,... | collective-permute-start | bytes 393224 | tf_op jit(solution)/shard_map/ppermute | solution.py:22
  (1 other events, 1.9 us)

commit v20 on v18

--- a/solution.py
+++ b/solution.py
@@ -36,7 +36,7 @@
         if 2 * bit < count:
             for _ in range(2):
                 near = swapped(value, 1, 1)
-                far = swapped(value, bit ^ 1, 2 * bit ^ 1)
+                far = swapped(value, 2 * bit ^ 1, bit ^ 1)
                 own, known, needed = (near, far), (value,), far
                 value = far + near
                 value, beside = lax.optimization_barrier((value, beside))

time: 63.4 us -> 63.4 us (level)
  no operation moved by 1% of the time
where the time goes in v20:
time: 63.4 us; the launch traced here: 63.3 us
  waiting for transfers between devices  29.6 us (47%)
  starting transfers between devices  17.8 us (28%)
  Pallas kernels  15.4 us (24%)
    ppermute x20, waiting for transfers between devices, swapped(): return lax.ppermute(value, 'pts', pairs)  16.9 us
    ppermute x20, starting transfers between devices, swapped(): return lax.ppermute(value, 'pts', pairs)  15.8 us
    ppermute x3, waiting for transfers between devices, column_shift(): return lax.ppermute(value, ('pts', 'cols'), pairs)  12.8 us
    pallas_call x10, Pallas kernels, in_vmem(): pl.pallas_call(kernel, out_shape=[jax.ShapeDtypeStruct(shape, dtype) for...  11 us
    pallas_call x1, Pallas kernels, body(): pl.pallas_call(functools.partial(last_upper_kernel, blocks), out_shape=ou...  2.32 us
    ppermute x3, starting transfers between devices, column_shift(): return lax.ppermute(value, ('pts', 'cols'), pairs)  1.98 us
    pallas_call x1, Pallas kernels, body(): pl.pallas_call(start_kernel, out_shape=[jax.ShapeDtypeStruct((width + 8,...  1.38 us
  transfers between devices with their start and end apart: 23, of which 14 were waited for; matrix products, arithmetic and copies ran while one was open for 0% of the time, Pallas kernels for 12%

profile of v20, /device:TPU:0, one launch (start us, length us, event | category | flops | bytes accessed | tf_op | source)
XLA Modules:
  0.0 63.3 jit_solution(17097620955339719767)
XLA Ops:
  0.0 1.4 %shard_map.37 = (f32[264,128]{1,0:T(8,128)S(1)}, f32[264,128]{1,0:T(8,128)S(1)}, f32[128,512]{1,0:T(8,128)S(1)}) custom-call(f32[128,512]{1,0:T(8,128)} %near_ref.1, f32[1,128]{1,0:T(1,128)} %bitcast.5), custom_call_target="tpu_custom_call" | custom-call | tf_op jit(solution)/shard_map/pallas_call | solution.py:279
  2.0 0.9 %collective-permute-done.1 = f32[264,128]{1,0:T(8,128)S(1)} collective-permute-done((f32[264,128]{1,0:T(8,128)S(1)}, f32[264,128]{1,0:T(8,128)S(1)}, u32[]{:S(2)}, u32[]{:S(2)}) %collective-permute-start.1) | collective-permute-done | bytes 135200 | tf_op jit(solution)/shard_map/ppermute | solution.py:28
  2.9 2.7 %collective-permute-start.2 = (f32[264,128]{1,0:T(8,128)S(1)}, f32[264,128]{1,0:T(8,128)S(1)}, u32[]{:S(2)}, u32[]{:S(2)}) collective-permute-start(f32[264,128]{1,0:T(8,128)S(1)} %add.20), channel_id=1, source_target_pairs={{0,20},{4,8},{8,28},{12,0},{16,4},{20,24},{24,12},{28,16},{1,21},{... | collective-permute-start | bytes 405512 | tf_op jit(solution)/shard_map/ppermute | solution.py:28
  5.9 2.3 %collective-permute-done.2 = f32[264,128]{1,0:T(8,128)S(1)} collective-permute-done((f32[264,128]{1,0:T(8,128)S(1)}, f32[264,128]{1,0:T(8,128)S(1)}, u32[]{:S(2)}, u32[]{:S(2)}) %collective-permute-start.2) | collective-permute-done | bytes 135200 | tf_op jit(solution)/shard_map/ppermute | solution.py:28
  8.3 1.8 %collective-permute-start.6 = (f32[264,128]{1,0:T(8,128)S(1)}, f32[264,128]{1,0:T(8,128)S(1)}, u32[]{:S(2)}, u32[]{:S(2)}) collective-permute-start(f32[264,128]{1,0:T(8,128)S(1)} %add.21.refs_0_), channel_id=1, source_target_pairs={{0,20},{4,8},{8,28},{12,0},{16,4},{20,24},{24,12},{28,16},{1,21},{... | collective-permute-start | bytes 405512 | tf_op jit(solution)/shard_map/ppermute | solution.py:28
  10.5 2.3 %collective-permute-done.6.refs_1_ = f32[264,128]{1,0:T(8,128)S(1)} collective-permute-done((f32[264,128]{1,0:T(8,128)S(1)}, f32[264,128]{1,0:T(8,128)S(1)}, u32[]{:S(2)}, u32[]{:S(2)}) %collective-permute-start.6) | collective-permute-done | bytes 135200 | tf_op jit(solution)/shard_map/ppermute | solution.py:28
  14.2 1.7 %shard_map.39 = (f32[256,128]{1,0:T(8,128)S(1)}, f32[256,128]{1,0:T(8,128)S(1)}, f32[8,128]{1,0:T(8,128)S(1)}) custom-call(bf16[256,128]{1,0:T(8,128)(2,1)S(1)} %get-tuple-element.71.own_high, bf16[256,128]{1,0:T(8,128)(2,1)S(1)} %get-tuple-element.72.own_low, bf16[256,256]{1,0:T(8,128)(2,1)S(1)} %get-tuple-element.73.upper_high, ...), custom_call_target="tpu_custom_call" | custom-call | tf_op jit(solution)/shard_map/pallas_call | solution.py:265
  15.9 1.8 %collective-permute-start.8 = (f32[256,128]{1,0:T(8,128)S(1)}, f32[256,128]{1,0:T(8,128)S(1)}, u32[]{:S(2)}, u32[]{:S(2)}) collective-permute-start(f32[256,128]{1,0:T(8,128)S(1)} %get-tuple-element.84), channel_id=1, source_target_pairs={{0,5},{1,6},{2,7},{3,4},{4,1},{5,2},{6,3},{7,0},{8,13},{9,14},{10,... | collective-permute-start | bytes 393224 | tf_op jit(solution)/shard_map/ppermute | solution.py:22
  19.1 1.9 %shard_map.40 = (bf16[256,768]{1,0:T(8,128)(2,1)S(1)}, f32[1,256]{1,0:T(1,128)S(1)}, f32[256,256]{1,0:T(8,128)S(1)}) custom-call(f32[256,1]{1,0:T(8,128)S(1)} %copy.7.weight, f32[256,128]{1,0:T(8,128)S(1)} %get-tuple-element.70.refs_0_, f32[256,128]{1,0:T(8,128)S(1)} %get-tuple-element.80.refs_1_, f32[8,128]{1,0:T(8,128)S(1)} %get-tuple-element.81.refs_2_, ...), custom_call_target="tpu_custom_call" | custom-call | tf_op jit(solution)/shard_map/pallas_call | solution.py:265
  20.9 2.4 %collective-permute-done.8.own_ref.refs_3_.refs_4_ = f32[256,128]{1,0:T(8,128)S(1)} collective-permute-done((f32[256,128]{1,0:T(8,128)S(1)}, f32[256,128]{1,0:T(8,128)S(1)}, u32[]{:S(2)}, u32[]{:S(2)}) %collective-permute-start.8) | collective-permute-done | bytes 131104 | tf_op jit(solution)/shard_map/ppermute | solution.py:22
  23.6 1.7 %collective-permute-start.9 = (f32[264,128]{1,0:T(8,128)S(1)}, f32[264,128]{1,0:T(8,128)S(1)}, u32[]{:S(2)}, u32[]{:S(2)}) collective-permute-start(f32[264,128]{1,0:T(8,128)S(1)} %shard_map.41), channel_id=1, source_target_pairs={{0,20},{4,8},{8,28},{12,0},{16,4},{20,24},{24,12},{28,16},{1,21},{... | collective-permute-start | bytes 405512 | tf_op jit(solution)/shard_map/ppermute | solution.py:28
  25.8 2.3 %collective-permute-done.9 = f32[264,128]{1,0:T(8,128)S(1)} collective-permute-done((f32[264,128]{1,0:T(8,128)S(1)}, f32[264,128]{1,0:T(8,128)S(1)}, u32[]{:S(2)}, u32[]{:S(2)}) %collective-permute-start.9) | collective-permute-done | bytes 135200 | tf_op jit(solution)/shard_map/ppermute | solution.py:28
  28.1 1.7 %collective-permute-start.13 = (f32[264,128]{1,0:T(8,128)S(1)}, f32[264,128]{1,0:T(8,128)S(1)}, u32[]{:S(2)}, u32[]{:S(2)}) collective-permute-start(f32[264,128]{1,0:T(8,128)S(1)} %add.22.refs_0_), channel_id=1, source_target_pairs={{0,20},{4,8},{8,28},{12,0},{16,4},{20,24},{24,12},{28,16},{1,21},{... | collective-permute-start | bytes 405512 | tf_op jit(solution)/shard_map/ppermute | solution.py:28
  30.2 2.4 %collective-permute-done.13.refs_1_ = f32[264,128]{1,0:T(8,128)S(1)} collective-permute-done((f32[264,128]{1,0:T(8,128)S(1)}, f32[264,128]{1,0:T(8,128)S(1)}, u32[]{:S(2)}, u32[]{:S(2)}) %collective-permute-start.13) | collective-permute-done | bytes 135200 | tf_op jit(solution)/shard_map/ppermute | solution.py:28
  34.0 1.7 %shard_map.43 = (f32[256,128]{1,0:T(8,128)S(1)}, f32[256,128]{1,0:T(8,128)S(1)}, f32[8,128]{1,0:T(8,128)S(1)}) custom-call(bf16[256,128]{1,0:T(8,128)(2,1)S(1)} %get-tuple-element.89.own_high, bf16[256,128]{1,0:T(8,128)(2,1)S(1)} %get-tuple-element.90.own_low, bf16[256,256]{1,0:T(8,128)(2,1)S(1)} %get-tuple-element.91.upper_high, ...), custom_call_target="tpu_custom_call" | custom-call | tf_op jit(solution)/shard_map/pallas_call | solution.py:265
  35.7 1.9 %shard_map.44 = (bf16[256,768]{1,0:T(8,128)(2,1)S(1)}, f32[1,256]{1,0:T(1,128)S(1)}, f32[256,256]{1,0:T(8,128)S(1)}) custom-call(f32[256,1]{1,0:T(8,128)S(1)} %copy.7.weight, f32[256,128]{1,0:T(8,128)S(1)} %get-tuple-element.88.refs_0_, f32[256,128]{1,0:T(8,128)S(1)} %get-tuple-element.98.refs_1_, f32[8,128]{1,0:T(8,128)S(1)} %get-tuple-element.99.refs_2_, ...), custom_call_target="tpu_custom_call" | custom-call | tf_op jit(solution)/shard_map/pallas_call | solution.py:265
  37.6 5.3 %collective-permute-done.15.own_ref.refs_3_.refs_4_ = f32[256,128]{1,0:T(8,128)S(1)} collective-permute-done((f32[256,128]{1,0:T(8,128)S(1)}, f32[256,128]{1,0:T(8,128)S(1)}, u32[]{:S(2)}, u32[]{:S(2)}) %collective-permute-start.15) | collective-permute-done | bytes 131104 | tf_op jit(solution)/shard_map/ppermute | solution.py:22
  43.1 1.8 %collective-permute-start.16 = (f32[264,128]{1,0:T(8,128)S(1)}, f32[264,128]{1,0:T(8,128)S(1)}, u32[]{:S(2)}, u32[]{:S(2)}) collective-permute-start(f32[264,128]{1,0:T(8,128)S(1)} %shard_map.45), channel_id=1, source_target_pairs={{0,20},{4,8},{8,28},{12,0},{16,4},{20,24},{24,12},{28,16},{1,21},{... | collective-permute-start | bytes 405512 | tf_op jit(solution)/shard_map/ppermute | solution.py:28
  45.4 2.2 %collective-permute-done.16 = f32[264,128]{1,0:T(8,128)S(1)} collective-permute-done((f32[264,128]{1,0:T(8,128)S(1)}, f32[264,128]{1,0:T(8,128)S(1)}, u32[]{:S(2)}, u32[]{:S(2)}) %collective-permute-start.16) | collective-permute-done | bytes 135200 | tf_op jit(solution)/shard_map/ppermute | solution.py:28
  47.7 1.8 %collective-permute-start.20 = (f32[264,128]{1,0:T(8,128)S(1)}, f32[264,128]{1,0:T(8,128)S(1)}, u32[]{:S(2)}, u32[]{:S(2)}) collective-permute-start(f32[264,128]{1,0:T(8,128)S(1)} %add.23.refs_0_), channel_id=1, source_target_pairs={{0,20},{4,8},{8,28},{12,0},{16,4},{20,24},{24,12},{28,16},{1,21},{... | collective-permute-start | bytes 405512 | tf_op jit(solution)/shard_map/ppermute | solution.py:28
  49.8 2.4 %collective-permute-done.20.refs_1_ = f32[264,128]{1,0:T(8,128)S(1)} collective-permute-done((f32[264,128]{1,0:T(8,128)S(1)}, f32[264,128]{1,0:T(8,128)S(1)}, u32[]{:S(2)}, u32[]{:S(2)}) %collective-permute-start.20) | collective-permute-done | bytes 135200 | tf_op jit(solution)/shard_map/ppermute | solution.py:28
  53.5 1.6 %shard_map.47 = (f32[128,256]{1,0:T(8,128)S(1)}, f32[256,128]{1,0:T(8,128)S(1)}, f32[8,128]{1,0:T(8,128)S(1)}) custom-call(bf16[256,128]{1,0:T(8,128)(2,1)S(1)} %get-tuple-element.106.own_high, bf16[256,128]{1,0:T(8,128)(2,1)S(1)} %get-tuple-element.107.own_low, bf16[128,256]{1,0:T(8,128)(2,1)S(1)} %get-tuple-element.108.upper_high, ...), custom_call_target="tpu_custom_call" | custom-call | tf_op jit(solution)/shard_map/pallas_call | solution.py:265
  55.2 2.3 %shard_map.48.filled = f32[128,512]{1,0:T(8,128)} custom-call(f32[256,128]{1,0:T(8,128)S(1)} %get-tuple-element.116.refs_0_, f32[256,128]{1,0:T(8,128)S(1)} %get-tuple-element.117.refs_1_, f32[8,128]{1,0:T(8,128)S(1)} %get-tuple-element.118.refs_2_, f32[256,256]{1,0:T(8,128)S(1)} %get-tuple-element.104.refs_2_.refs_3_, ...), custom_call_target="tpu_custom_call" | custom-call | tf_op jit(solution)/shard_map/pallas_call | solution.py:338
  57.6 5.0 %collective-permute-done.22.lower = f32[128,256]{1,0:T(8,128)S(1)} collective-permute-done((f32[128,256]{1,0:T(8,128)S(1)}, f32[128,256]{1,0:T(8,128)S(1)}, u32[]{:S(2)}, u32[]{:S(2)}) %collective-permute-start.22) | collective-permute-done | bytes 131104 | tf_op jit(solution)/shard_map/ppermute | solution.py:22
  (47 shorter events, 9.8 us)
Async XLA Ops:
  1.4 1.5 %collective-permute-start.1 = (f32[264,128]{1,0:T(8,128)S(1)}, f32[264,128]{1,0:T(8,128)S(1)}, u32[]{:S(2)}, u32[]{:S(2)}) collective-permute-start(f32[264,128]{1,0:T(8,128)S(1)} %get-tuple-element.66), channel_id=1, source_target_pairs={{0,4},{4,0},{8,12},{12,8},{16,20},{20,16},{24,28},{28,24},{1,5},{5... | collective-permute-start | bytes 405512 | tf_op jit(solution)/shard_map/ppermute | solution.py:28
  1.9 6.4 %collective-permute-start.4 = (f32[128,512]{1,0:T(8,128)S(1)}, f32[128,512]{1,0:T(8,128)S(1)}, u32[]{:S(2)}, u32[]{:S(2)}) collective-permute-start(f32[128,512]{1,0:T(8,128)S(1)} %get-tuple-element.67.refs_2_.refs_3_), channel_id=1, source_target_pairs={{0,4},{4,0},{8,12},{12,8},{16,20},{20,16},{24,28},{28,24},{1,5},{5... | collective-permute-start | bytes 786440 | tf_op jit(solution)/shard_map/ppermute | solution.py:28
  2.9 10.3 %copy-start.1 = (s32[3,2]{0,1:T(2,128)S(1)}, s32[3,2]{0,1:T(2,128)}, u32[]{:S(2)}) copy-start(s32[3,2]{0,1:T(2,128)} %param.5) | copy-start | bytes 76
  2.9 5.3 %collective-permute-start.2 = (f32[264,128]{1,0:T(8,128)S(1)}, f32[264,128]{1,0:T(8,128)S(1)}, u32[]{:S(2)}, u32[]{:S(2)}) collective-permute-start(f32[264,128]{1,0:T(8,128)S(1)} %add.20), channel_id=1, source_target_pairs={{0,20},{4,8},{8,28},{12,0},{16,4},{20,24},{24,12},{28,16},{1,21},{... | collective-permute-start | bytes 405512 | tf_op jit(solution)/shard_map/ppermute | solution.py:28
  5.6 2.7 %collective-permute-start.3 = (f32[264,128]{1,0:T(8,128)S(1)}, f32[264,128]{1,0:T(8,128)S(1)}, u32[]{:S(2)}, u32[]{:S(2)}) collective-permute-start(f32[264,128]{1,0:T(8,128)S(1)} %add.20), channel_id=1, source_target_pairs={{0,4},{4,0},{8,12},{12,8},{16,20},{20,16},{24,28},{28,24},{1,5},{5... | collective-permute-start | bytes 405512 | tf_op jit(solution)/shard_map/ppermute | solution.py:28
  8.3 4.5 %collective-permute-start.6 = (f32[264,128]{1,0:T(8,128)S(1)}, f32[264,128]{1,0:T(8,128)S(1)}, u32[]{:S(2)}, u32[]{:S(2)}) collective-permute-start(f32[264,128]{1,0:T(8,128)S(1)} %add.21.refs_0_), channel_id=1, source_target_pairs={{0,20},{4,8},{8,28},{12,0},{16,4},{20,24},{24,12},{28,16},{1,21},{... | collective-permute-start | bytes 405512 | tf_op jit(solution)/shard_map/ppermute | solution.py:28
  10.1 3.1 %collective-permute-start.5 = (f32[264,128]{1,0:T(8,128)S(1)}, f32[264,128]{1,0:T(8,128)S(1)}, u32[]{:S(2)}, u32[]{:S(2)}) collective-permute-start(f32[264,128]{1,0:T(8,128)S(1)} %add.21.refs_0_), channel_id=1, source_target_pairs={{0,4},{4,0},{8,12},{12,8},{16,20},{20,16},{24,28},{28,24},{1,5},{5... | collective-permute-start | bytes 405512 | tf_op jit(solution)/shard_map/ppermute | solution.py:28
  12.8 1.4 %collective-permute-start.7 = (f32[264,128]{1,0:T(8,128)S(1)}, f32[264,128]{1,0:T(8,128)S(1)}, u32[]{:S(2)}, u32[]{:S(2)}) collective-permute-start(f32[264,128]{1,0:T(8,128)S(1)} %collective-permute-done.6.refs_1_), channel_id=1, source_target_pairs={{0,4},{4,0},{8,12},{12,8},{16,20},{20,16},{24,28},{28,24},{1,5},{5... | collective-permute-start | bytes 405512 | tf_op jit(solution)/shard_map/ppermute | solution.py:28
  15.9 7.5 %collective-permute-start.8 = (f32[256,128]{1,0:T(8,128)S(1)}, f32[256,128]{1,0:T(8,128)S(1)}, u32[]{:S(2)}, u32[]{:S(2)}) collective-permute-start(f32[256,128]{1,0:T(8,128)S(1)} %get-tuple-element.84), channel_id=1, source_target_pairs={{0,5},{1,6},{2,7},{3,4},{4,1},{5,2},{6,3},{7,0},{8,13},{9,14},{10,... | collective-permute-start | bytes 393224 | tf_op jit(solution)/shard_map/ppermute | solution.py:22
  17.7 1.2 %collective-permute-start = (f32[128]{0:T(128)S(1)}, f32[128]{0:T(128)S(1)}, u32[]{:S(2)}, u32[]{:S(2)}) collective-permute-start(f32[128]{0:T(128)S(1)} %copy-done), channel_id=1, source_target_pairs={{0,4},{4,0},{8,12},{12,8},{16,20},{20,16},{24,28},{28,24},{1,5},{5... | collective-permute-start | bytes 1544 | tf_op jit(solution)/shard_map/ppermute | solution.py:28
  23.6 4.5 %collective-permute-start.9 = (f32[264,128]{1,0:T(8,128)S(1)}, f32[264,128]{1,0:T(8,128)S(1)}, u32[]{:S(2)}, u32[]{:S(2)}) collective-permute-start(f32[264,128]{1,0:T(8,128)S(1)} %shard_map.41), channel_id=1, source_target_pairs={{0,20},{4,8},{8,28},{12,0},{16,4},{20,24},{24,12},{28,16},{1,21},{... | collective-permute-start | bytes 405512 | tf_op jit(solution)/shard_map/ppermute | solution.py:28
  25.3 2.8 %collective-permute-start.10 = (f32[264,128]{1,0:T(8,128)S(1)}, f32[264,128]{1,0:T(8,128)S(1)}, u32[]{:S(2)}, u32[]{:S(2)}) collective-permute-start(f32[264,128]{1,0:T(8,128)S(1)} %shard_map.41), channel_id=1, source_target_pairs={{0,4},{4,0},{8,12},{12,8},{16,20},{20,16},{24,28},{28,24},{1,5},{5... | collective-permute-start | bytes 405512 | tf_op jit(solution)/shard_map/ppermute | solution.py:28
  25.6 2.5 %collective-permute-start.11 = (f32[256,128]{1,0:T(8,128)S(1)}, f32[256,128]{1,0:T(8,128)S(1)}, u32[]{:S(2)}, u32[]{:S(2)}) collective-permute-start(f32[256,128]{1,0:T(8,128)S(1)} %collective-permute-done.8.own_ref.refs_3_.refs_4_), channel_id=1, source_target_pairs={{0,4},{4,0},{8,12},{12,8},{16,20},{20,16},{24,28},{28,24},{1,5},{5... | collective-permute-start | bytes 393224 | tf_op jit(solution)/shard_map/ppermute | solution.py:28
  28.1 4.5 %collective-permute-start.13 = (f32[264,128]{1,0:T(8,128)S(1)}, f32[264,128]{1,0:T(8,128)S(1)}, u32[]{:S(2)}, u32[]{:S(2)}) collective-permute-start(f32[264,128]{1,0:T(8,128)S(1)} %add.22.refs_0_), channel_id=1, source_target_pairs={{0,20},{4,8},{8,28},{12,0},{16,4},{20,24},{24,12},{28,16},{1,21},{... | collective-permute-start | bytes 405512 | tf_op jit(solution)/shard_map/ppermute | solution.py:28
  29.8 3.1 %collective-permute-start.12 = (f32[264,128]{1,0:T(8,128)S(1)}, f32[264,128]{1,0:T(8,128)S(1)}, u32[]{:S(2)}, u32[]{:S(2)}) collective-permute-start(f32[264,128]{1,0:T(8,128)S(1)} %add.22.refs_0_), channel_id=1, source_target_pairs={{0,4},{4,0},{8,12},{12,8},{16,20},{20,16},{24,28},{28,24},{1,5},{5... | collective-permute-start | bytes 405512 | tf_op jit(solution)/shard_map/ppermute | solution.py:28
  32.6 1.4 %collective-permute-start.14 = (f32[264,128]{1,0:T(8,128)S(1)}, f32[264,128]{1,0:T(8,128)S(1)}, u32[]{:S(2)}, u32[]{:S(2)}) collective-permute-start(f32[264,128]{1,0:T(8,128)S(1)} %collective-permute-done.13.refs_1_), channel_id=1, source_target_pairs={{0,4},{4,0},{8,12},{12,8},{16,20},{20,16},{24,28},{28,24},{1,5},{5... | collective-permute-start | bytes 405512 | tf_op jit(solution)/shard_map/ppermute | solution.py:28
  35.6 7.2 %collective-permute-start.15 = (f32[256,128]{1,0:T(8,128)S(1)}, f32[256,128]{1,0:T(8,128)S(1)}, u32[]{:S(2)}, u32[]{:S(2)}) collective-permute-start(f32[256,128]{1,0:T(8,128)S(1)} %get-tuple-element.102), channel_id=1, source_target_pairs={{0,5},{1,6},{2,7},{3,4},{4,1},{5,2},{6,3},{7,0},{8,13},{9,14},{10,... | collective-permute-start | bytes 393224 | tf_op jit(solution)/shard_map/ppermute | solution.py:22
  43.1 4.5 %collective-permute-start.16 = (f32[264,128]{1,0:T(8,128)S(1)}, f32[264,128]{1,0:T(8,128)S(1)}, u32[]{:S(2)}, u32[]{:S(2)}) collective-permute-start(f32[264,128]{1,0:T(8,128)S(1)} %shard_map.45), channel_id=1, source_target_pairs={{0,20},{4,8},{8,28},{12,0},{16,4},{20,24},{24,12},{28,16},{1,21},{... | collective-permute-start | bytes 405512 | tf_op jit(solution)/shard_map/ppermute | solution.py:28
  44.9 2.7 %collective-permute-start.17 = (f32[264,128]{1,0:T(8,128)S(1)}, f32[264,128]{1,0:T(8,128)S(1)}, u32[]{:S(2)}, u32[]{:S(2)}) collective-permute-start(f32[264,128]{1,0:T(8,128)S(1)} %shard_map.45), channel_id=1, source_target_pairs={{0,4},{4,0},{8,12},{12,8},{16,20},{20,16},{24,28},{28,24},{1,5},{5... | collective-permute-start | bytes 405512 | tf_op jit(solution)/shard_map/ppermute | solution.py:28
  45.3 2.4 %collective-permute-start.18 = (f32[256,128]{1,0:T(8,128)S(1)}, f32[256,128]{1,0:T(8,128)S(1)}, u32[]{:S(2)}, u32[]{:S(2)}) collective-permute-start(f32[256,128]{1,0:T(8,128)S(1)} %collective-permute-done.15.own_ref.refs_3_.refs_4_), channel_id=1, source_target_pairs={{0,4},{4,0},{8,12},{12,8},{16,20},{20,16},{24,28},{28,24},{1,5},{5... | collective-permute-start | bytes 393224 | tf_op jit(solution)/shard_map/ppermute | solution.py:28
  47.7 4.5 %collective-permute-start.20 = (f32[264,128]{1,0:T(8,128)S(1)}, f32[264,128]{1,0:T(8,128)S(1)}, u32[]{:S(2)}, u32[]{:S(2)}) collective-permute-start(f32[264,128]{1,0:T(8,128)S(1)} %add.23.refs_0_), channel_id=1, source_target_pairs={{0,20},{4,8},{8,28},{12,0},{16,4},{20,24},{24,12},{28,16},{1,21},{... | collective-permute-start | bytes 405512 | tf_op jit(solution)/shard_map/ppermute | solution.py:28
  49.5 3.1 %collective-permute-start.19 = (f32[264,128]{1,0:T(8,128)S(1)}, f32[264,128]{1,0:T(8,128)S(1)}, u32[]{:S(2)}, u32[]{:S(2)}) collective-permute-start(f32[264,128]{1,0:T(8,128)S(1)} %add.23.refs_0_), channel_id=1, source_target_pairs={{0,4},{4,0},{8,12},{12,8},{16,20},{20,16},{24,28},{28,24},{1,5},{5... | collective-permute-start | bytes 405512 | tf_op jit(solution)/shard_map/ppermute | solution.py:28
  52.2 1.4 %collective-permute-start.21 = (f32[264,128]{1,0:T(8,128)S(1)}, f32[264,128]{1,0:T(8,128)S(1)}, u32[]{:S(2)}, u32[]{:S(2)}) collective-permute-start(f32[264,128]{1,0:T(8,128)S(1)} %collective-permute-done.20.refs_1_), channel_id=1, source_target_pairs={{0,4},{4,0},{8,12},{12,8},{16,20},{20,16},{24,28},{28,24},{1,5},{5... | collective-permute-start | bytes 405512 | tf_op jit(solution)/shard_map/ppermute | solution.py:28
  55.2 7.5 %collective-permute-start.22 = (f32[128,256]{1,0:T(8,128)S(1)}, f32[128,256]{1,0:T(8,128)S(1)}, u32[]{:S(2)}, u32[]{:S(2)}) collective-permute-start(f32[128,256]{1,0:T(8,128)S(1)} %get-tuple-element.115), channel_id=1, source_target_pairs={{0,6},{1,7},{2,4},{3,5},{4,2},{5,3},{6,0},{7,1},{8,14},{9,15},{10,... | collective-permute-start | bytes 393224 | tf_op jit(solution)/shard_map/ppermute | solution.py:22
  (1 other events, 1.9 us)

commit v21 on v20

--- a/solution.py
+++ b/solution.py
@@ -85,7 +85,8 @@
     left_cubic = product(two_parts(left_base), both)
     left_both = product(left_parts, both_first)
     left_last = product(two_parts(left_cubic), two_parts(both_square))
-    return (1.5 * left_both - 0.5 * left_last) * lax.rsqrt(scale)
+    root = lax.rsqrt(scale)
+    return left_both * (1.5 * root) - left_last * (0.5 * root)
 
 
 def joined(own, other):

time: 63.4 us -> 63.4 us (level)
  no operation moved by 1% of the time
where the time goes in v21:
time: 63.4 us; the launch traced here: 63.3 us
  waiting for transfers between devices  29.6 us (47%)
  starting transfers between devices  17.8 us (28%)
  Pallas kernels  15.4 us (24%)
    ppermute x20, waiting for transfers between devices, swapped(): return lax.ppermute(value, 'pts', pairs)  16.9 us
    ppermute x20, starting transfers between devices, swapped(): return lax.ppermute(value, 'pts', pairs)  15.8 us
    ppermute x3, waiting for transfers between devices, column_shift(): return lax.ppermute(value, ('pts', 'cols'), pairs)  12.8 us
    pallas_call x10, Pallas kernels, in_vmem(): pl.pallas_call(kernel, out_shape=[jax.ShapeDtypeStruct(shape, dtype) for...  11 us
    pallas_call x1, Pallas kernels, body(): pl.pallas_call(functools.partial(last_upper_kernel, blocks), out_shape=ou...  2.33 us
    ppermute x3, starting transfers between devices, column_shift(): return lax.ppermute(value, ('pts', 'cols'), pairs)  1.98 us
    pallas_call x1, Pallas kernels, body(): pl.pallas_call(start_kernel, out_shape=[jax.ShapeDtypeStruct((width + 8,...  1.38 us
  transfers between devices with their start and end apart: 23, of which 14 were waited for; matrix products, arithmetic and copies ran while one was open for 0% of the time, Pallas kernels for 12%

profile of v21, /device:TPU:0, one launch (start us, length us, event | category | flops | bytes accessed | tf_op | source)
XLA Modules:
  0.0 63.3 jit_solution(11358985637411854114)
XLA Ops:
  0.0 1.4 %shard_map.37 = (f32[264,128]{1,0:T(8,128)S(1)}, f32[264,128]{1,0:T(8,128)S(1)}, f32[128,512]{1,0:T(8,128)S(1)}) custom-call(f32[128,512]{1,0:T(8,128)} %near_ref.1, f32[1,128]{1,0:T(1,128)} %bitcast.5), custom_call_target="tpu_custom_call" | custom-call | tf_op jit(solution)/shard_map/pallas_call | solution.py:280
  2.0 0.9 %collective-permute-done.1 = f32[264,128]{1,0:T(8,128)S(1)} collective-permute-done((f32[264,128]{1,0:T(8,128)S(1)}, f32[264,128]{1,0:T(8,128)S(1)}, u32[]{:S(2)}, u32[]{:S(2)}) %collective-permute-start.1) | collective-permute-done | bytes 135200 | tf_op jit(solution)/shard_map/ppermute | solution.py:28
  2.9 2.7 %collective-permute-start.2 = (f32[264,128]{1,0:T(8,128)S(1)}, f32[264,128]{1,0:T(8,128)S(1)}, u32[]{:S(2)}, u32[]{:S(2)}) collective-permute-start(f32[264,128]{1,0:T(8,128)S(1)} %add.20), channel_id=1, source_target_pairs={{0,20},{4,8},{8,28},{12,0},{16,4},{20,24},{24,12},{28,16},{1,21},{... | collective-permute-start | bytes 405512 | tf_op jit(solution)/shard_map/ppermute | solution.py:28
  5.9 2.3 %collective-permute-done.2 = f32[264,128]{1,0:T(8,128)S(1)} collective-permute-done((f32[264,128]{1,0:T(8,128)S(1)}, f32[264,128]{1,0:T(8,128)S(1)}, u32[]{:S(2)}, u32[]{:S(2)}) %collective-permute-start.2) | collective-permute-done | bytes 135200 | tf_op jit(solution)/shard_map/ppermute | solution.py:28
  8.3 1.8 %collective-permute-start.6 = (f32[264,128]{1,0:T(8,128)S(1)}, f32[264,128]{1,0:T(8,128)S(1)}, u32[]{:S(2)}, u32[]{:S(2)}) collective-permute-start(f32[264,128]{1,0:T(8,128)S(1)} %add.21.refs_0_), channel_id=1, source_target_pairs={{0,20},{4,8},{8,28},{12,0},{16,4},{20,24},{24,12},{28,16},{1,21},{... | collective-permute-start | bytes 405512 | tf_op jit(solution)/shard_map/ppermute | solution.py:28
  10.5 2.3 %collective-permute-done.6.refs_1_ = f32[264,128]{1,0:T(8,128)S(1)} collective-permute-done((f32[264,128]{1,0:T(8,128)S(1)}, f32[264,128]{1,0:T(8,128)S(1)}, u32[]{:S(2)}, u32[]{:S(2)}) %collective-permute-start.6) | collective-permute-done | bytes 135200 | tf_op jit(solution)/shard_map/ppermute | solution.py:28
  14.2 1.7 %shard_map.39 = (f32[256,128]{1,0:T(8,128)S(1)}, f32[256,128]{1,0:T(8,128)S(1)}, f32[8,128]{1,0:T(8,128)S(1)}) custom-call(bf16[256,128]{1,0:T(8,128)(2,1)S(1)} %get-tuple-element.71.own_high, bf16[256,128]{1,0:T(8,128)(2,1)S(1)} %get-tuple-element.72.own_low, bf16[256,256]{1,0:T(8,128)(2,1)S(1)} %get-tuple-element.73.upper_high, ...), custom_call_target="tpu_custom_call" | custom-call | tf_op jit(solution)/shard_map/pallas_call | solution.py:266
  15.9 1.8 %collective-permute-start.8 = (f32[256,128]{1,0:T(8,128)S(1)}, f32[256,128]{1,0:T(8,128)S(1)}, u32[]{:S(2)}, u32[]{:S(2)}) collective-permute-start(f32[256,128]{1,0:T(8,128)S(1)} %get-tuple-element.84), channel_id=1, source_target_pairs={{0,5},{1,6},{2,7},{3,4},{4,1},{5,2},{6,3},{7,0},{8,13},{9,14},{10,... | collective-permute-start | bytes 393224 | tf_op jit(solution)/shard_map/ppermute | solution.py:22
  19.1 1.9 %shard_map.40 = (bf16[256,768]{1,0:T(8,128)(2,1)S(1)}, f32[1,256]{1,0:T(1,128)S(1)}, f32[256,256]{1,0:T(8,128)S(1)}) custom-call(f32[256,1]{1,0:T(8,128)S(1)} %copy.7.weight, f32[256,128]{1,0:T(8,128)S(1)} %get-tuple-element.70.refs_0_, f32[256,128]{1,0:T(8,128)S(1)} %get-tuple-element.80.refs_1_, f32[8,128]{1,0:T(8,128)S(1)} %get-tuple-element.81.refs_2_, ...), custom_call_target="tpu_custom_call" | custom-call | tf_op jit(solution)/shard_map/pallas_call | solution.py:266
  20.9 2.4 %collective-permute-done.8.own_ref.refs_3_.refs_4_ = f32[256,128]{1,0:T(8,128)S(1)} collective-permute-done((f32[256,128]{1,0:T(8,128)S(1)}, f32[256,128]{1,0:T(8,128)S(1)}, u32[]{:S(2)}, u32[]{:S(2)}) %collective-permute-start.8) | collective-permute-done | bytes 131104 | tf_op jit(solution)/shard_map/ppermute | solution.py:22
  23.6 1.7 %collective-permute-start.9 = (f32[264,128]{1,0:T(8,128)S(1)}, f32[264,128]{1,0:T(8,128)S(1)}, u32[]{:S(2)}, u32[]{:S(2)}) collective-permute-start(f32[264,128]{1,0:T(8,128)S(1)} %shard_map.41), channel_id=1, source_target_pairs={{0,20},{4,8},{8,28},{12,0},{16,4},{20,24},{24,12},{28,16},{1,21},{... | collective-permute-start | bytes 405512 | tf_op jit(solution)/shard_map/ppermute | solution.py:28
  25.8 2.3 %collective-permute-done.9 = f32[264,128]{1,0:T(8,128)S(1)} collective-permute-done((f32[264,128]{1,0:T(8,128)S(1)}, f32[264,128]{1,0:T(8,128)S(1)}, u32[]{:S(2)}, u32[]{:S(2)}) %collective-permute-start.9) | collective-permute-done | bytes 135200 | tf_op jit(solution)/shard_map/ppermute | solution.py:28
  28.1 1.7 %collective-permute-start.13 = (f32[264,128]{1,0:T(8,128)S(1)}, f32[264,128]{1,0:T(8,128)S(1)}, u32[]{:S(2)}, u32[]{:S(2)}) collective-permute-start(f32[264,128]{1,0:T(8,128)S(1)} %add.22.refs_0_), channel_id=1, source_target_pairs={{0,20},{4,8},{8,28},{12,0},{16,4},{20,24},{24,12},{28,16},{1,21},{... | collective-permute-start | bytes 405512 | tf_op jit(solution)/shard_map/ppermute | solution.py:28
  30.2 2.4 %collective-permute-done.13.refs_1_ = f32[264,128]{1,0:T(8,128)S(1)} collective-permute-done((f32[264,128]{1,0:T(8,128)S(1)}, f32[264,128]{1,0:T(8,128)S(1)}, u32[]{:S(2)}, u32[]{:S(2)}) %collective-permute-start.13) | collective-permute-done | bytes 135200 | tf_op jit(solution)/shard_map/ppermute | solution.py:28
  34.0 1.7 %shard_map.43 = (f32[256,128]{1,0:T(8,128)S(1)}, f32[256,128]{1,0:T(8,128)S(1)}, f32[8,128]{1,0:T(8,128)S(1)}) custom-call(bf16[256,128]{1,0:T(8,128)(2,1)S(1)} %get-tuple-element.89.own_high, bf16[256,128]{1,0:T(8,128)(2,1)S(1)} %get-tuple-element.90.own_low, bf16[256,256]{1,0:T(8,128)(2,1)S(1)} %get-tuple-element.91.upper_high, ...), custom_call_target="tpu_custom_call" | custom-call | tf_op jit(solution)/shard_map/pallas_call | solution.py:266
  35.7 1.9 %shard_map.44 = (bf16[256,768]{1,0:T(8,128)(2,1)S(1)}, f32[1,256]{1,0:T(1,128)S(1)}, f32[256,256]{1,0:T(8,128)S(1)}) custom-call(f32[256,1]{1,0:T(8,128)S(1)} %copy.7.weight, f32[256,128]{1,0:T(8,128)S(1)} %get-tuple-element.88.refs_0_, f32[256,128]{1,0:T(8,128)S(1)} %get-tuple-element.98.refs_1_, f32[8,128]{1,0:T(8,128)S(1)} %get-tuple-element.99.refs_2_, ...), custom_call_target="tpu_custom_call" | custom-call | tf_op jit(solution)/shard_map/pallas_call | solution.py:266
  37.6 5.3 %collective-permute-done.15.own_ref.refs_3_.refs_4_ = f32[256,128]{1,0:T(8,128)S(1)} collective-permute-done((f32[256,128]{1,0:T(8,128)S(1)}, f32[256,128]{1,0:T(8,128)S(1)}, u32[]{:S(2)}, u32[]{:S(2)}) %collective-permute-start.15) | collective-permute-done | bytes 131104 | tf_op jit(solution)/shard_map/ppermute | solution.py:22
  43.1 1.8 %collective-permute-start.16 = (f32[264,128]{1,0:T(8,128)S(1)}, f32[264,128]{1,0:T(8,128)S(1)}, u32[]{:S(2)}, u32[]{:S(2)}) collective-permute-start(f32[264,128]{1,0:T(8,128)S(1)} %shard_map.45), channel_id=1, source_target_pairs={{0,20},{4,8},{8,28},{12,0},{16,4},{20,24},{24,12},{28,16},{1,21},{... | collective-permute-start | bytes 405512 | tf_op jit(solution)/shard_map/ppermute | solution.py:28
  45.4 2.2 %collective-permute-done.16 = f32[264,128]{1,0:T(8,128)S(1)} collective-permute-done((f32[264,128]{1,0:T(8,128)S(1)}, f32[264,128]{1,0:T(8,128)S(1)}, u32[]{:S(2)}, u32[]{:S(2)}) %collective-permute-start.16) | collective-permute-done | bytes 135200 | tf_op jit(solution)/shard_map/ppermute | solution.py:28
  47.7 1.8 %collective-permute-start.20 = (f32[264,128]{1,0:T(8,128)S(1)}, f32[264,128]{1,0:T(8,128)S(1)}, u32[]{:S(2)}, u32[]{:S(2)}) collective-permute-start(f32[264,128]{1,0:T(8,128)S(1)} %add.23.refs_0_), channel_id=1, source_target_pairs={{0,20},{4,8},{8,28},{12,0},{16,4},{20,24},{24,12},{28,16},{1,21},{... | collective-permute-start | bytes 405512 | tf_op jit(solution)/shard_map/ppermute | solution.py:28
  49.8 2.4 %collective-permute-done.20.refs_1_ = f32[264,128]{1,0:T(8,128)S(1)} collective-permute-done((f32[264,128]{1,0:T(8,128)S(1)}, f32[264,128]{1,0:T(8,128)S(1)}, u32[]{:S(2)}, u32[]{:S(2)}) %collective-permute-start.20) | collective-permute-done | bytes 135200 | tf_op jit(solution)/shard_map/ppermute | solution.py:28
  53.5 1.7 %shard_map.47 = (f32[128,256]{1,0:T(8,128)S(1)}, f32[256,128]{1,0:T(8,128)S(1)}, f32[8,128]{1,0:T(8,128)S(1)}) custom-call(bf16[256,128]{1,0:T(8,128)(2,1)S(1)} %get-tuple-element.106.own_high, bf16[256,128]{1,0:T(8,128)(2,1)S(1)} %get-tuple-element.107.own_low, bf16[128,256]{1,0:T(8,128)(2,1)S(1)} %get-tuple-element.108.upper_high, ...), custom_call_target="tpu_custom_call" | custom-call | tf_op jit(solution)/shard_map/pallas_call | solution.py:266
  55.2 2.3 %shard_map.48.filled = f32[128,512]{1,0:T(8,128)} custom-call(f32[256,128]{1,0:T(8,128)S(1)} %get-tuple-element.116.refs_0_, f32[256,128]{1,0:T(8,128)S(1)} %get-tuple-element.117.refs_1_, f32[8,128]{1,0:T(8,128)S(1)} %get-tuple-element.118.refs_2_, f32[256,256]{1,0:T(8,128)S(1)} %get-tuple-element.104.refs_2_.refs_3_, ...), custom_call_target="tpu_custom_call" | custom-call | tf_op jit(solution)/shard_map/pallas_call | solution.py:339
  57.6 5.0 %collective-permute-done.22.lower = f32[128,256]{1,0:T(8,128)S(1)} collective-permute-done((f32[128,256]{1,0:T(8,128)S(1)}, f32[128,256]{1,0:T(8,128)S(1)}, u32[]{:S(2)}, u32[]{:S(2)}) %collective-permute-start.22) | collective-permute-done | bytes 131104 | tf_op jit(solution)/shard_map/ppermute | solution.py:22
  (47 shorter events, 9.8 us)
Async XLA Ops:
  1.4 1.5 %collective-permute-start.1 = (f32[264,128]{1,0:T(8,128)S(1)}, f32[264,128]{1,0:T(8,128)S(1)}, u32[]{:S(2)}, u32[]{:S(2)}) collective-permute-start(f32[264,128]{1,0:T(8,128)S(1)} %get-tuple-element.66), channel_id=1, source_target_pairs={{0,4},{4,0},{8,12},{12,8},{16,20},{20,16},{24,28},{28,24},{1,5},{5... | collective-permute-start | bytes 405512 | tf_op jit(solution)/shard_map/ppermute | solution.py:28
  1.9 6.4 %collective-permute-start.4 = (f32[128,512]{1,0:T(8,128)S(1)}, f32[128,512]{1,0:T(8,128)S(1)}, u32[]{:S(2)}, u32[]{:S(2)}) collective-permute-start(f32[128,512]{1,0:T(8,128)S(1)} %get-tuple-element.67.refs_2_.refs_3_), channel_id=1, source_target_pairs={{0,4},{4,0},{8,12},{12,8},{16,20},{20,16},{24,28},{28,24},{1,5},{5... | collective-permute-start | bytes 786440 | tf_op jit(solution)/shard_map/ppermute | solution.py:28
  2.9 10.3 %copy-start.1 = (s32[3,2]{0,1:T(2,128)S(1)}, s32[3,2]{0,1:T(2,128)}, u32[]{:S(2)}) copy-start(s32[3,2]{0,1:T(2,128)} %param.5) | copy-start | bytes 76
  2.9 5.3 %collective-permute-start.2 = (f32[264,128]{1,0:T(8,128)S(1)}, f32[264,128]{1,0:T(8,128)S(1)}, u32[]{:S(2)}, u32[]{:S(2)}) collective-permute-start(f32[264,128]{1,0:T(8,128)S(1)} %add.20), channel_id=1, source_target_pairs={{0,20},{4,8},{8,28},{12,0},{16,4},{20,24},{24,12},{28,16},{1,21},{... | collective-permute-start | bytes 405512 | tf_op jit(solution)/shard_map/ppermute | solution.py:28
  5.6 2.7 %collective-permute-start.3 = (f32[264,128]{1,0:T(8,128)S(1)}, f32[264,128]{1,0:T(8,128)S(1)}, u32[]{:S(2)}, u32[]{:S(2)}) collective-permute-start(f32[264,128]{1,0:T(8,128)S(1)} %add.20), channel_id=1, source_target_pairs={{0,4},{4,0},{8,12},{12,8},{16,20},{20,16},{24,28},{28,24},{1,5},{5... | collective-permute-start | bytes 405512 | tf_op jit(solution)/shard_map/ppermute | solution.py:28
  8.3 4.5 %collective-permute-start.6 = (f32[264,128]{1,0:T(8,128)S(1)}, f32[264,128]{1,0:T(8,128)S(1)}, u32[]{:S(2)}, u32[]{:S(2)}) collective-permute-start(f32[264,128]{1,0:T(8,128)S(1)} %add.21.refs_0_), channel_id=1, source_target_pairs={{0,20},{4,8},{8,28},{12,0},{16,4},{20,24},{24,12},{28,16},{1,21},{... | collective-permute-start | bytes 405512 | tf_op jit(solution)/shard_map/ppermute | solution.py:28
  10.1 3.1 %collective-permute-start.5 = (f32[264,128]{1,0:T(8,128)S(1)}, f32[264,128]{1,0:T(8,128)S(1)}, u32[]{:S(2)}, u32[]{:S(2)}) collective-permute-start(f32[264,128]{1,0:T(8,128)S(1)} %add.21.refs_0_), channel_id=1, source_target_pairs={{0,4},{4,0},{8,12},{12,8},{16,20},{20,16},{24,28},{28,24},{1,5},{5... | collective-permute-start | bytes 405512 | tf_op jit(solution)/shard_map/ppermute | solution.py:28
  12.8 1.4 %collective-permute-start.7 = (f32[264,128]{1,0:T(8,128)S(1)}, f32[264,128]{1,0:T(8,128)S(1)}, u32[]{:S(2)}, u32[]{:S(2)}) collective-permute-start(f32[264,128]{1,0:T(8,128)S(1)} %collective-permute-done.6.refs_1_), channel_id=1, source_target_pairs={{0,4},{4,0},{8,12},{12,8},{16,20},{20,16},{24,28},{28,24},{1,5},{5... | collective-permute-start | bytes 405512 | tf_op jit(solution)/shard_map/ppermute | solution.py:28
  15.9 7.5 %collective-permute-start.8 = (f32[256,128]{1,0:T(8,128)S(1)}, f32[256,128]{1,0:T(8,128)S(1)}, u32[]{:S(2)}, u32[]{:S(2)}) collective-permute-start(f32[256,128]{1,0:T(8,128)S(1)} %get-tuple-element.84), channel_id=1, source_target_pairs={{0,5},{1,6},{2,7},{3,4},{4,1},{5,2},{6,3},{7,0},{8,13},{9,14},{10,... | collective-permute-start | bytes 393224 | tf_op jit(solution)/shard_map/ppermute | solution.py:22
  17.7 1.2 %collective-permute-start = (f32[128]{0:T(128)S(1)}, f32[128]{0:T(128)S(1)}, u32[]{:S(2)}, u32[]{:S(2)}) collective-permute-start(f32[128]{0:T(128)S(1)} %copy-done), channel_id=1, source_target_pairs={{0,4},{4,0},{8,12},{12,8},{16,20},{20,16},{24,28},{28,24},{1,5},{5... | collective-permute-start | bytes 1544 | tf_op jit(solution)/shard_map/ppermute | solution.py:28
  23.6 4.5 %collective-permute-start.9 = (f32[264,128]{1,0:T(8,128)S(1)}, f32[264,128]{1,0:T(8,128)S(1)}, u32[]{:S(2)}, u32[]{:S(2)}) collective-permute-start(f32[264,128]{1,0:T(8,128)S(1)} %shard_map.41), channel_id=1, source_target_pairs={{0,20},{4,8},{8,28},{12,0},{16,4},{20,24},{24,12},{28,16},{1,21},{... | collective-permute-start | bytes 405512 | tf_op jit(solution)/shard_map/ppermute | solution.py:28
  25.3 2.8 %collective-permute-start.10 = (f32[264,128]{1,0:T(8,128)S(1)}, f32[264,128]{1,0:T(8,128)S(1)}, u32[]{:S(2)}, u32[]{:S(2)}) collective-permute-start(f32[264,128]{1,0:T(8,128)S(1)} %shard_map.41), channel_id=1, source_target_pairs={{0,4},{4,0},{8,12},{12,8},{16,20},{20,16},{24,28},{28,24},{1,5},{5... | collective-permute-start | bytes 405512 | tf_op jit(solution)/shard_map/ppermute | solution.py:28
  25.6 2.5 %collective-permute-start.11 = (f32[256,128]{1,0:T(8,128)S(1)}, f32[256,128]{1,0:T(8,128)S(1)}, u32[]{:S(2)}, u32[]{:S(2)}) collective-permute-start(f32[256,128]{1,0:T(8,128)S(1)} %collective-permute-done.8.own_ref.refs_3_.refs_4_), channel_id=1, source_target_pairs={{0,4},{4,0},{8,12},{12,8},{16,20},{20,16},{24,28},{28,24},{1,5},{5... | collective-permute-start | bytes 393224 | tf_op jit(solution)/shard_map/ppermute | solution.py:28
  28.1 4.5 %collective-permute-start.13 = (f32[264,128]{1,0:T(8,128)S(1)}, f32[264,128]{1,0:T(8,128)S(1)}, u32[]{:S(2)}, u32[]{:S(2)}) collective-permute-start(f32[264,128]{1,0:T(8,128)S(1)} %add.22.refs_0_), channel_id=1, source_target_pairs={{0,20},{4,8},{8,28},{12,0},{16,4},{20,24},{24,12},{28,16},{1,21},{... | collective-permute-start | bytes 405512 | tf_op jit(solution)/shard_map/ppermute | solution.py:28
  29.8 3.1 %collective-permute-start.12 = (f32[264,128]{1,0:T(8,128)S(1)}, f32[264,128]{1,0:T(8,128)S(1)}, u32[]{:S(2)}, u32[]{:S(2)}) collective-permute-start(f32[264,128]{1,0:T(8,128)S(1)} %add.22.refs_0_), channel_id=1, source_target_pairs={{0,4},{4,0},{8,12},{12,8},{16,20},{20,16},{24,28},{28,24},{1,5},{5... | collective-permute-start | bytes 405512 | tf_op jit(solution)/shard_map/ppermute | solution.py:28
  32.6 1.4 %collective-permute-start.14 = (f32[264,128]{1,0:T(8,128)S(1)}, f32[264,128]{1,0:T(8,128)S(1)}, u32[]{:S(2)}, u32[]{:S(2)}) collective-permute-start(f32[264,128]{1,0:T(8,128)S(1)} %collective-permute-done.13.refs_1_), channel_id=1, source_target_pairs={{0,4},{4,0},{8,12},{12,8},{16,20},{20,16},{24,28},{28,24},{1,5},{5... | collective-permute-start | bytes 405512 | tf_op jit(solution)/shard_map/ppermute | solution.py:28
  35.6 7.2 %collective-permute-start.15 = (f32[256,128]{1,0:T(8,128)S(1)}, f32[256,128]{1,0:T(8,128)S(1)}, u32[]{:S(2)}, u32[]{:S(2)}) collective-permute-start(f32[256,128]{1,0:T(8,128)S(1)} %get-tuple-element.102), channel_id=1, source_target_pairs={{0,5},{1,6},{2,7},{3,4},{4,1},{5,2},{6,3},{7,0},{8,13},{9,14},{10,... | collective-permute-start | bytes 393224 | tf_op jit(solution)/shard_map/ppermute | solution.py:22
  43.1 4.5 %collective-permute-start.16 = (f32[264,128]{1,0:T(8,128)S(1)}, f32[264,128]{1,0:T(8,128)S(1)}, u32[]{:S(2)}, u32[]{:S(2)}) collective-permute-start(f32[264,128]{1,0:T(8,128)S(1)} %shard_map.45), channel_id=1, source_target_pairs={{0,20},{4,8},{8,28},{12,0},{16,4},{20,24},{24,12},{28,16},{1,21},{... | collective-permute-start | bytes 405512 | tf_op jit(solution)/shard_map/ppermute | solution.py:28
  44.9 2.7 %collective-permute-start.17 = (f32[264,128]{1,0:T(8,128)S(1)}, f32[264,128]{1,0:T(8,128)S(1)}, u32[]{:S(2)}, u32[]{:S(2)}) collective-permute-start(f32[264,128]{1,0:T(8,128)S(1)} %shard_map.45), channel_id=1, source_target_pairs={{0,4},{4,0},{8,12},{12,8},{16,20},{20,16},{24,28},{28,24},{1,5},{5... | collective-permute-start | bytes 405512 | tf_op jit(solution)/shard_map/ppermute | solution.py:28
  45.3 2.4 %collective-permute-start.18 = (f32[256,128]{1,0:T(8,128)S(1)}, f32[256,128]{1,0:T(8,128)S(1)}, u32[]{:S(2)}, u32[]{:S(2)}) collective-permute-start(f32[256,128]{1,0:T(8,128)S(1)} %collective-permute-done.15.own_ref.refs_3_.refs_4_), channel_id=1, source_target_pairs={{0,4},{4,0},{8,12},{12,8},{16,20},{20,16},{24,28},{28,24},{1,5},{5... | collective-permute-start | bytes 393224 | tf_op jit(solution)/shard_map/ppermute | solution.py:28
  47.7 4.5 %collective-permute-start.20 = (f32[264,128]{1,0:T(8,128)S(1)}, f32[264,128]{1,0:T(8,128)S(1)}, u32[]{:S(2)}, u32[]{:S(2)}) collective-permute-start(f32[264,128]{1,0:T(8,128)S(1)} %add.23.refs_0_), channel_id=1, source_target_pairs={{0,20},{4,8},{8,28},{12,0},{16,4},{20,24},{24,12},{28,16},{1,21},{... | collective-permute-start | bytes 405512 | tf_op jit(solution)/shard_map/ppermute | solution.py:28
  49.5 3.1 %collective-permute-start.19 = (f32[264,128]{1,0:T(8,128)S(1)}, f32[264,128]{1,0:T(8,128)S(1)}, u32[]{:S(2)}, u32[]{:S(2)}) collective-permute-start(f32[264,128]{1,0:T(8,128)S(1)} %add.23.refs_0_), channel_id=1, source_target_pairs={{0,4},{4,0},{8,12},{12,8},{16,20},{20,16},{24,28},{28,24},{1,5},{5... | collective-permute-start | bytes 405512 | tf_op jit(solution)/shard_map/ppermute | solution.py:28
  52.2 1.4 %collective-permute-start.21 = (f32[264,128]{1,0:T(8,128)S(1)}, f32[264,128]{1,0:T(8,128)S(1)}, u32[]{:S(2)}, u32[]{:S(2)}) collective-permute-start(f32[264,128]{1,0:T(8,128)S(1)} %collective-permute-done.20.refs_1_), channel_id=1, source_target_pairs={{0,4},{4,0},{8,12},{12,8},{16,20},{20,16},{24,28},{28,24},{1,5},{5... | collective-permute-start | bytes 405512 | tf_op jit(solution)/shard_map/ppermute | solution.py:28
  55.2 7.5 %collective-permute-start.22 = (f32[128,256]{1,0:T(8,128)S(1)}, f32[128,256]{1,0:T(8,128)S(1)}, u32[]{:S(2)}, u32[]{:S(2)}) collective-permute-start(f32[128,256]{1,0:T(8,128)S(1)} %get-tuple-element.115), channel_id=1, source_target_pairs={{0,6},{1,7},{2,4},{3,5},{4,2},{5,3},{6,0},{7,1},{8,14},{9,15},{10,... | collective-permute-start | bytes 393224 | tf_op jit(solution)/shard_map/ppermute | solution.py:22
  (1 other events, 1.9 us)

commit v22 on v21

--- a/solution.py
+++ b/solution.py
@@ -78,8 +78,8 @@
     second = product(base_parts, base_parts)
     left_base = product(left_parts, base_parts)
     first_square = two_parts(2.25 * identity - 1.5 * base + 0.25 * second)
-    cubic = product(two_parts(1.5 * base - 0.5 * second), first_square)
-    both = two_parts(2.25 * identity - 0.75 * base - 0.5 * cubic)
+    cubic = product(two_parts(0.25 * second - 0.75 * base), first_square)
+    both = two_parts((2.25 * identity - 0.75 * base) + cubic)
     both_first = first_columns(both, columns)
     both_square = product(both, both_first)
     left_cubic = product(two_parts(left_base), both)

time: 63.4 us -> 63.4 us (level)
  no operation moved by 1% of the time
where the time goes in v22:
time: 63.4 us; the launch traced here: 63.2 us
  waiting for transfers between devices  29.7 us (47%)
  starting transfers between devices  17.7 us (28%)
  Pallas kernels  15.4 us (24%)
    ppermute x20, waiting for transfers between devices, swapped(): return lax.ppermute(value, 'pts', pairs)  17 us
    ppermute x20, starting transfers between devices, swapped(): return lax.ppermute(value, 'pts', pairs)  15.7 us
    ppermute x3, waiting for transfers between devices, column_shift(): return lax.ppermute(value, ('pts', 'cols'), pairs)  12.7 us
    pallas_call x10, Pallas kernels, in_vmem(): pl.pallas_call(kernel, out_shape=[jax.ShapeDtypeStruct(shape, dtype) for...  11 us
    pallas_call x1, Pallas kernels, body(): pl.pallas_call(functools.partial(last_upper_kernel, blocks), out_shape=ou...  2.33 us
    ppermute x3, starting transfers between devices, column_shift(): return lax.ppermute(value, ('pts', 'cols'), pairs)  1.97 us
    pallas_call x1, Pallas kernels, body(): pl.pallas_call(start_kernel, out_shape=[jax.ShapeDtypeStruct((width + 8,...  1.38 us
  transfers between devices with their start and end apart: 23, of which 14 were waited for; matrix products, arithmetic and copies ran while one was open for 0% of the time, Pallas kernels for 12%

profile of v22, /device:TPU:0, one launch (start us, length us, event | category | flops | bytes accessed | tf_op | source)
XLA Modules:
  0.0 63.2 jit_solution(13009055431983110853)
XLA Ops:
  0.0 1.4 %shard_map.37 = (f32[264,128]{1,0:T(8,128)S(1)}, f32[264,128]{1,0:T(8,128)S(1)}, f32[128,512]{1,0:T(8,128)S(1)}) custom-call(f32[128,512]{1,0:T(8,128)} %near_ref.1, f32[1,128]{1,0:T(1,128)} %bitcast.5), custom_call_target="tpu_custom_call" | custom-call | tf_op jit(solution)/shard_map/pallas_call | solution.py:280
  2.0 0.9 %collective-permute-done.1 = f32[264,128]{1,0:T(8,128)S(1)} collective-permute-done((f32[264,128]{1,0:T(8,128)S(1)}, f32[264,128]{1,0:T(8,128)S(1)}, u32[]{:S(2)}, u32[]{:S(2)}) %collective-permute-start.1) | collective-permute-done | bytes 135200 | tf_op jit(solution)/shard_map/ppermute | solution.py:28
  2.9 2.7 %collective-permute-start.2 = (f32[264,128]{1,0:T(8,128)S(1)}, f32[264,128]{1,0:T(8,128)S(1)}, u32[]{:S(2)}, u32[]{:S(2)}) collective-permute-start(f32[264,128]{1,0:T(8,128)S(1)} %add.20), channel_id=1, source_target_pairs={{0,20},{4,8},{8,28},{12,0},{16,4},{20,24},{24,12},{28,16},{1,21},{... | collective-permute-start | bytes 405512 | tf_op jit(solution)/shard_map/ppermute | solution.py:28
  5.9 2.3 %collective-permute-done.2 = f32[264,128]{1,0:T(8,128)S(1)} collective-permute-done((f32[264,128]{1,0:T(8,128)S(1)}, f32[264,128]{1,0:T(8,128)S(1)}, u32[]{:S(2)}, u32[]{:S(2)}) %collective-permute-start.2) | collective-permute-done | bytes 135200 | tf_op jit(solution)/shard_map/ppermute | solution.py:28
  8.3 1.8 %collective-permute-start.6 = (f32[264,128]{1,0:T(8,128)S(1)}, f32[264,128]{1,0:T(8,128)S(1)}, u32[]{:S(2)}, u32[]{:S(2)}) collective-permute-start(f32[264,128]{1,0:T(8,128)S(1)} %add.21.refs_0_), channel_id=1, source_target_pairs={{0,20},{4,8},{8,28},{12,0},{16,4},{20,24},{24,12},{28,16},{1,21},{... | collective-permute-start | bytes 405512 | tf_op jit(solution)/shard_map/ppermute | solution.py:28
  10.5 2.3 %collective-permute-done.6.refs_1_ = f32[264,128]{1,0:T(8,128)S(1)} collective-permute-done((f32[264,128]{1,0:T(8,128)S(1)}, f32[264,128]{1,0:T(8,128)S(1)}, u32[]{:S(2)}, u32[]{:S(2)}) %collective-permute-start.6) | collective-permute-done | bytes 135200 | tf_op jit(solution)/shard_map/ppermute | solution.py:28
  14.2 1.7 %shard_map.39 = (f32[256,128]{1,0:T(8,128)S(1)}, f32[256,128]{1,0:T(8,128)S(1)}, f32[8,128]{1,0:T(8,128)S(1)}) custom-call(bf16[256,128]{1,0:T(8,128)(2,1)S(1)} %get-tuple-element.71.own_high, bf16[256,128]{1,0:T(8,128)(2,1)S(1)} %get-tuple-element.72.own_low, bf16[256,256]{1,0:T(8,128)(2,1)S(1)} %get-tuple-element.73.upper_high, ...), custom_call_target="tpu_custom_call" | custom-call | tf_op jit(solution)/shard_map/pallas_call | solution.py:266
  15.9 1.8 %collective-permute-start.8 = (f32[256,128]{1,0:T(8,128)S(1)}, f32[256,128]{1,0:T(8,128)S(1)}, u32[]{:S(2)}, u32[]{:S(2)}) collective-permute-start(f32[256,128]{1,0:T(8,128)S(1)} %get-tuple-element.84), channel_id=1, source_target_pairs={{0,5},{1,6},{2,7},{3,4},{4,1},{5,2},{6,3},{7,0},{8,13},{9,14},{10,... | collective-permute-start | bytes 393224 | tf_op jit(solution)/shard_map/ppermute | solution.py:22
  19.0 1.9 %shard_map.40 = (bf16[256,768]{1,0:T(8,128)(2,1)S(1)}, f32[1,256]{1,0:T(1,128)S(1)}, f32[256,256]{1,0:T(8,128)S(1)}) custom-call(f32[256,1]{1,0:T(8,128)S(1)} %copy.7.weight, f32[256,128]{1,0:T(8,128)S(1)} %get-tuple-element.70.refs_0_, f32[256,128]{1,0:T(8,128)S(1)} %get-tuple-element.80.refs_1_, f32[8,128]{1,0:T(8,128)S(1)} %get-tuple-element.81.refs_2_, ...), custom_call_target="tpu_custom_call" | custom-call | tf_op jit(solution)/shard_map/pallas_call | solution.py:266
  20.9 2.4 %collective-permute-done.8.own_ref.refs_3_.refs_4_ = f32[256,128]{1,0:T(8,128)S(1)} collective-permute-done((f32[256,128]{1,0:T(8,128)S(1)}, f32[256,128]{1,0:T(8,128)S(1)}, u32[]{:S(2)}, u32[]{:S(2)}) %collective-permute-start.8) | collective-permute-done | bytes 131104 | tf_op jit(solution)/shard_map/ppermute | solution.py:22
  23.6 1.7 %collective-permute-start.9 = (f32[264,128]{1,0:T(8,128)S(1)}, f32[264,128]{1,0:T(8,128)S(1)}, u32[]{:S(2)}, u32[]{:S(2)}) collective-permute-start(f32[264,128]{1,0:T(8,128)S(1)} %shard_map.41), channel_id=1, source_target_pairs={{0,20},{4,8},{8,28},{12,0},{16,4},{20,24},{24,12},{28,16},{1,21},{... | collective-permute-start | bytes 405512 | tf_op jit(solution)/shard_map/ppermute | solution.py:28
  25.8 2.3 %collective-permute-done.9 = f32[264,128]{1,0:T(8,128)S(1)} collective-permute-done((f32[264,128]{1,0:T(8,128)S(1)}, f32[264,128]{1,0:T(8,128)S(1)}, u32[]{:S(2)}, u32[]{:S(2)}) %collective-permute-start.9) | collective-permute-done | bytes 135200 | tf_op jit(solution)/shard_map/ppermute | solution.py:28
  28.1 1.7 %collective-permute-start.13 = (f32[264,128]{1,0:T(8,128)S(1)}, f32[264,128]{1,0:T(8,128)S(1)}, u32[]{:S(2)}, u32[]{:S(2)}) collective-permute-start(f32[264,128]{1,0:T(8,128)S(1)} %add.22.refs_0_), channel_id=1, source_target_pairs={{0,20},{4,8},{8,28},{12,0},{16,4},{20,24},{24,12},{28,16},{1,21},{... | collective-permute-start | bytes 405512 | tf_op jit(solution)/shard_map/ppermute | solution.py:28
  30.2 2.4 %collective-permute-done.13.refs_1_ = f32[264,128]{1,0:T(8,128)S(1)} collective-permute-done((f32[264,128]{1,0:T(8,128)S(1)}, f32[264,128]{1,0:T(8,128)S(1)}, u32[]{:S(2)}, u32[]{:S(2)}) %collective-permute-start.13) | collective-permute-done | bytes 135200 | tf_op jit(solution)/shard_map/ppermute | solution.py:28
  34.0 1.7 %shard_map.43 = (f32[256,128]{1,0:T(8,128)S(1)}, f32[256,128]{1,0:T(8,128)S(1)}, f32[8,128]{1,0:T(8,128)S(1)}) custom-call(bf16[256,128]{1,0:T(8,128)(2,1)S(1)} %get-tuple-element.89.own_high, bf16[256,128]{1,0:T(8,128)(2,1)S(1)} %get-tuple-element.90.own_low, bf16[256,256]{1,0:T(8,128)(2,1)S(1)} %get-tuple-element.91.upper_high, ...), custom_call_target="tpu_custom_call" | custom-call | tf_op jit(solution)/shard_map/pallas_call | solution.py:266
  35.7 1.9 %shard_map.44 = (bf16[256,768]{1,0:T(8,128)(2,1)S(1)}, f32[1,256]{1,0:T(1,128)S(1)}, f32[256,256]{1,0:T(8,128)S(1)}) custom-call(f32[256,1]{1,0:T(8,128)S(1)} %copy.7.weight, f32[256,128]{1,0:T(8,128)S(1)} %get-tuple-element.88.refs_0_, f32[256,128]{1,0:T(8,128)S(1)} %get-tuple-element.98.refs_1_, f32[8,128]{1,0:T(8,128)S(1)} %get-tuple-element.99.refs_2_, ...), custom_call_target="tpu_custom_call" | custom-call | tf_op jit(solution)/shard_map/pallas_call | solution.py:266
  37.6 5.3 %collective-permute-done.15.own_ref.refs_3_.refs_4_ = f32[256,128]{1,0:T(8,128)S(1)} collective-permute-done((f32[256,128]{1,0:T(8,128)S(1)}, f32[256,128]{1,0:T(8,128)S(1)}, u32[]{:S(2)}, u32[]{:S(2)}) %collective-permute-start.15) | collective-permute-done | bytes 131104 | tf_op jit(solution)/shard_map/ppermute | solution.py:22
  43.2 1.8 %collective-permute-start.16 = (f32[264,128]{1,0:T(8,128)S(1)}, f32[264,128]{1,0:T(8,128)S(1)}, u32[]{:S(2)}, u32[]{:S(2)}) collective-permute-start(f32[264,128]{1,0:T(8,128)S(1)} %shard_map.45), channel_id=1, source_target_pairs={{0,20},{4,8},{8,28},{12,0},{16,4},{20,24},{24,12},{28,16},{1,21},{... | collective-permute-start | bytes 405512 | tf_op jit(solution)/shard_map/ppermute | solution.py:28
  45.4 2.2 %collective-permute-done.16 = f32[264,128]{1,0:T(8,128)S(1)} collective-permute-done((f32[264,128]{1,0:T(8,128)S(1)}, f32[264,128]{1,0:T(8,128)S(1)}, u32[]{:S(2)}, u32[]{:S(2)}) %collective-permute-start.16) | collective-permute-done | bytes 135200 | tf_op jit(solution)/shard_map/ppermute | solution.py:28
  47.7 1.8 %collective-permute-start.20 = (f32[264,128]{1,0:T(8,128)S(1)}, f32[264,128]{1,0:T(8,128)S(1)}, u32[]{:S(2)}, u32[]{:S(2)}) collective-permute-start(f32[264,128]{1,0:T(8,128)S(1)} %add.23.refs_0_), channel_id=1, source_target_pairs={{0,20},{4,8},{8,28},{12,0},{16,4},{20,24},{24,12},{28,16},{1,21},{... | collective-permute-start | bytes 405512 | tf_op jit(solution)/shard_map/ppermute | solution.py:28
  49.8 2.4 %collective-permute-done.20.refs_1_ = f32[264,128]{1,0:T(8,128)S(1)} collective-permute-done((f32[264,128]{1,0:T(8,128)S(1)}, f32[264,128]{1,0:T(8,128)S(1)}, u32[]{:S(2)}, u32[]{:S(2)}) %collective-permute-start.20) | collective-permute-done | bytes 135200 | tf_op jit(solution)/shard_map/ppermute | solution.py:28
  53.5 1.6 %shard_map.47 = (f32[128,256]{1,0:T(8,128)S(1)}, f32[256,128]{1,0:T(8,128)S(1)}, f32[8,128]{1,0:T(8,128)S(1)}) custom-call(bf16[256,128]{1,0:T(8,128)(2,1)S(1)} %get-tuple-element.106.own_high, bf16[256,128]{1,0:T(8,128)(2,1)S(1)} %get-tuple-element.107.own_low, bf16[128,256]{1,0:T(8,128)(2,1)S(1)} %get-tuple-element.108.upper_high, ...), custom_call_target="tpu_custom_call" | custom-call | tf_op jit(solution)/shard_map/pallas_call | solution.py:266
  55.2 2.3 %shard_map.48.filled = f32[128,512]{1,0:T(8,128)} custom-call(f32[256,128]{1,0:T(8,128)S(1)} %get-tuple-element.116.refs_0_, f32[256,128]{1,0:T(8,128)S(1)} %get-tuple-element.117.refs_1_, f32[8,128]{1,0:T(8,128)S(1)} %get-tuple-element.118.refs_2_, f32[256,256]{1,0:T(8,128)S(1)} %get-tuple-element.104.refs_2_.refs_3_, ...), custom_call_target="tpu_custom_call" | custom-call | tf_op jit(solution)/shard_map/pallas_call | solution.py:339
  57.6 5.0 %collective-permute-done.22.lower = f32[128,256]{1,0:T(8,128)S(1)} collective-permute-done((f32[128,256]{1,0:T(8,128)S(1)}, f32[128,256]{1,0:T(8,128)S(1)}, u32[]{:S(2)}, u32[]{:S(2)}) %collective-permute-start.22) | collective-permute-done | bytes 131104 | tf_op jit(solution)/shard_map/ppermute | solution.py:22
  (47 shorter events, 9.8 us)
Async XLA Ops:
  1.4 1.5 %collective-permute-start.1 = (f32[264,128]{1,0:T(8,128)S(1)}, f32[264,128]{1,0:T(8,128)S(1)}, u32[]{:S(2)}, u32[]{:S(2)}) collective-permute-start(f32[264,128]{1,0:T(8,128)S(1)} %get-tuple-element.66), channel_id=1, source_target_pairs={{0,4},{4,0},{8,12},{12,8},{16,20},{20,16},{24,28},{28,24},{1,5},{5... | collective-permute-start | bytes 405512 | tf_op jit(solution)/shard_map/ppermute | solution.py:28
  1.9 6.4 %collective-permute-start.4 = (f32[128,512]{1,0:T(8,128)S(1)}, f32[128,512]{1,0:T(8,128)S(1)}, u32[]{:S(2)}, u32[]{:S(2)}) collective-permute-start(f32[128,512]{1,0:T(8,128)S(1)} %get-tuple-element.67.refs_2_.refs_3_), channel_id=1, source_target_pairs={{0,4},{4,0},{8,12},{12,8},{16,20},{20,16},{24,28},{28,24},{1,5},{5... | collective-permute-start | bytes 786440 | tf_op jit(solution)/shard_map/ppermute | solution.py:28
  2.9 10.3 %copy-start.1 = (s32[3,2]{0,1:T(2,128)S(1)}, s32[3,2]{0,1:T(2,128)}, u32[]{:S(2)}) copy-start(s32[3,2]{0,1:T(2,128)} %param.5) | copy-start | bytes 76
  2.9 5.3 %collective-permute-start.2 = (f32[264,128]{1,0:T(8,128)S(1)}, f32[264,128]{1,0:T(8,128)S(1)}, u32[]{:S(2)}, u32[]{:S(2)}) collective-permute-start(f32[264,128]{1,0:T(8,128)S(1)} %add.20), channel_id=1, source_target_pairs={{0,20},{4,8},{8,28},{12,0},{16,4},{20,24},{24,12},{28,16},{1,21},{... | collective-permute-start | bytes 405512 | tf_op jit(solution)/shard_map/ppermute | solution.py:28
  5.6 2.7 %collective-permute-start.3 = (f32[264,128]{1,0:T(8,128)S(1)}, f32[264,128]{1,0:T(8,128)S(1)}, u32[]{:S(2)}, u32[]{:S(2)}) collective-permute-start(f32[264,128]{1,0:T(8,128)S(1)} %add.20), channel_id=1, source_target_pairs={{0,4},{4,0},{8,12},{12,8},{16,20},{20,16},{24,28},{28,24},{1,5},{5... | collective-permute-start | bytes 405512 | tf_op jit(solution)/shard_map/ppermute | solution.py:28
  8.3 4.5 %collective-permute-start.6 = (f32[264,128]{1,0:T(8,128)S(1)}, f32[264,128]{1,0:T(8,128)S(1)}, u32[]{:S(2)}, u32[]{:S(2)}) collective-permute-start(f32[264,128]{1,0:T(8,128)S(1)} %add.21.refs_0_), channel_id=1, source_target_pairs={{0,20},{4,8},{8,28},{12,0},{16,4},{20,24},{24,12},{28,16},{1,21},{... | collective-permute-start | bytes 405512 | tf_op jit(solution)/shard_map/ppermute | solution.py:28
  10.1 3.1 %collective-permute-start.5 = (f32[264,128]{1,0:T(8,128)S(1)}, f32[264,128]{1,0:T(8,128)S(1)}, u32[]{:S(2)}, u32[]{:S(2)}) collective-permute-start(f32[264,128]{1,0:T(8,128)S(1)} %add.21.refs_0_), channel_id=1, source_target_pairs={{0,4},{4,0},{8,12},{12,8},{16,20},{20,16},{24,28},{28,24},{1,5},{5... | collective-permute-start | bytes 405512 | tf_op jit(solution)/shard_map/ppermute | solution.py:28
  12.8 1.4 %collective-permute-start.7 = (f32[264,128]{1,0:T(8,128)S(1)}, f32[264,128]{1,0:T(8,128)S(1)}, u32[]{:S(2)}, u32[]{:S(2)}) collective-permute-start(f32[264,128]{1,0:T(8,128)S(1)} %collective-permute-done.6.refs_1_), channel_id=1, source_target_pairs={{0,4},{4,0},{8,12},{12,8},{16,20},{20,16},{24,28},{28,24},{1,5},{5... | collective-permute-start | bytes 405512 | tf_op jit(solution)/shard_map/ppermute | solution.py:28
  15.9 7.4 %collective-permute-start.8 = (f32[256,128]{1,0:T(8,128)S(1)}, f32[256,128]{1,0:T(8,128)S(1)}, u32[]{:S(2)}, u32[]{:S(2)}) collective-permute-start(f32[256,128]{1,0:T(8,128)S(1)} %get-tuple-element.84), channel_id=1, source_target_pairs={{0,5},{1,6},{2,7},{3,4},{4,1},{5,2},{6,3},{7,0},{8,13},{9,14},{10,... | collective-permute-start | bytes 393224 | tf_op jit(solution)/shard_map/ppermute | solution.py:22
  17.7 1.2 %collective-permute-start = (f32[128]{0:T(128)S(1)}, f32[128]{0:T(128)S(1)}, u32[]{:S(2)}, u32[]{:S(2)}) collective-permute-start(f32[128]{0:T(128)S(1)} %copy-done), channel_id=1, source_target_pairs={{0,4},{4,0},{8,12},{12,8},{16,20},{20,16},{24,28},{28,24},{1,5},{5... | collective-permute-start | bytes 1544 | tf_op jit(solution)/shard_map/ppermute | solution.py:28
  23.6 4.5 %collective-permute-start.9 = (f32[264,128]{1,0:T(8,128)S(1)}, f32[264,128]{1,0:T(8,128)S(1)}, u32[]{:S(2)}, u32[]{:S(2)}) collective-permute-start(f32[264,128]{1,0:T(8,128)S(1)} %shard_map.41), channel_id=1, source_target_pairs={{0,20},{4,8},{8,28},{12,0},{16,4},{20,24},{24,12},{28,16},{1,21},{... | collective-permute-start | bytes 405512 | tf_op jit(solution)/shard_map/ppermute | solution.py:28
  25.3 2.8 %collective-permute-start.10 = (f32[264,128]{1,0:T(8,128)S(1)}, f32[264,128]{1,0:T(8,128)S(1)}, u32[]{:S(2)}, u32[]{:S(2)}) collective-permute-start(f32[264,128]{1,0:T(8,128)S(1)} %shard_map.41), channel_id=1, source_target_pairs={{0,4},{4,0},{8,12},{12,8},{16,20},{20,16},{24,28},{28,24},{1,5},{5... | collective-permute-start | bytes 405512 | tf_op jit(solution)/shard_map/ppermute | solution.py:28
  25.6 2.5 %collective-permute-start.11 = (f32[256,128]{1,0:T(8,128)S(1)}, f32[256,128]{1,0:T(8,128)S(1)}, u32[]{:S(2)}, u32[]{:S(2)}) collective-permute-start(f32[256,128]{1,0:T(8,128)S(1)} %collective-permute-done.8.own_ref.refs_3_.refs_4_), channel_id=1, source_target_pairs={{0,4},{4,0},{8,12},{12,8},{16,20},{20,16},{24,28},{28,24},{1,5},{5... | collective-permute-start | bytes 393224 | tf_op jit(solution)/shard_map/ppermute | solution.py:28
  28.1 4.5 %collective-permute-start.13 = (f32[264,128]{1,0:T(8,128)S(1)}, f32[264,128]{1,0:T(8,128)S(1)}, u32[]{:S(2)}, u32[]{:S(2)}) collective-permute-start(f32[264,128]{1,0:T(8,128)S(1)} %add.22.refs_0_), channel_id=1, source_target_pairs={{0,20},{4,8},{8,28},{12,0},{16,4},{20,24},{24,12},{28,16},{1,21},{... | collective-permute-start | bytes 405512 | tf_op jit(solution)/shard_map/ppermute | solution.py:28
  29.8 3.1 %collective-permute-start.12 = (f32[264,128]{1,0:T(8,128)S(1)}, f32[264,128]{1,0:T(8,128)S(1)}, u32[]{:S(2)}, u32[]{:S(2)}) collective-permute-start(f32[264,128]{1,0:T(8,128)S(1)} %add.22.refs_0_), channel_id=1, source_target_pairs={{0,4},{4,0},{8,12},{12,8},{16,20},{20,16},{24,28},{28,24},{1,5},{5... | collective-permute-start | bytes 405512 | tf_op jit(solution)/shard_map/ppermute | solution.py:28
  32.6 1.4 %collective-permute-start.14 = (f32[264,128]{1,0:T(8,128)S(1)}, f32[264,128]{1,0:T(8,128)S(1)}, u32[]{:S(2)}, u32[]{:S(2)}) collective-permute-start(f32[264,128]{1,0:T(8,128)S(1)} %collective-permute-done.13.refs_1_), channel_id=1, source_target_pairs={{0,4},{4,0},{8,12},{12,8},{16,20},{20,16},{24,28},{28,24},{1,5},{5... | collective-permute-start | bytes 405512 | tf_op jit(solution)/shard_map/ppermute | solution.py:28
  35.6 7.3 %collective-permute-start.15 = (f32[256,128]{1,0:T(8,128)S(1)}, f32[256,128]{1,0:T(8,128)S(1)}, u32[]{:S(2)}, u32[]{:S(2)}) collective-permute-start(f32[256,128]{1,0:T(8,128)S(1)} %get-tuple-element.102), channel_id=1, source_target_pairs={{0,5},{1,6},{2,7},{3,4},{4,1},{5,2},{6,3},{7,0},{8,13},{9,14},{10,... | collective-permute-start | bytes 393224 | tf_op jit(solution)/shard_map/ppermute | solution.py:22
  43.2 4.5 %collective-permute-start.16 = (f32[264,128]{1,0:T(8,128)S(1)}, f32[264,128]{1,0:T(8,128)S(1)}, u32[]{:S(2)}, u32[]{:S(2)}) collective-permute-start(f32[264,128]{1,0:T(8,128)S(1)} %shard_map.45), channel_id=1, source_target_pairs={{0,20},{4,8},{8,28},{12,0},{16,4},{20,24},{24,12},{28,16},{1,21},{... | collective-permute-start | bytes 405512 | tf_op jit(solution)/shard_map/ppermute | solution.py:28
  44.9 2.7 %collective-permute-start.17 = (f32[264,128]{1,0:T(8,128)S(1)}, f32[264,128]{1,0:T(8,128)S(1)}, u32[]{:S(2)}, u32[]{:S(2)}) collective-permute-start(f32[264,128]{1,0:T(8,128)S(1)} %shard_map.45), channel_id=1, source_target_pairs={{0,4},{4,0},{8,12},{12,8},{16,20},{20,16},{24,28},{28,24},{1,5},{5... | collective-permute-start | bytes 405512 | tf_op jit(solution)/shard_map/ppermute | solution.py:28
  45.2 2.4 %collective-permute-start.18 = (f32[256,128]{1,0:T(8,128)S(1)}, f32[256,128]{1,0:T(8,128)S(1)}, u32[]{:S(2)}, u32[]{:S(2)}) collective-permute-start(f32[256,128]{1,0:T(8,128)S(1)} %collective-permute-done.15.own_ref.refs_3_.refs_4_), channel_id=1, source_target_pairs={{0,4},{4,0},{8,12},{12,8},{16,20},{20,16},{24,28},{28,24},{1,5},{5... | collective-permute-start | bytes 393224 | tf_op jit(solution)/shard_map/ppermute | solution.py:28
  47.7 4.5 %collective-permute-start.20 = (f32[264,128]{1,0:T(8,128)S(1)}, f32[264,128]{1,0:T(8,128)S(1)}, u32[]{:S(2)}, u32[]{:S(2)}) collective-permute-start(f32[264,128]{1,0:T(8,128)S(1)} %add.23.refs_0_), channel_id=1, source_target_pairs={{0,20},{4,8},{8,28},{12,0},{16,4},{20,24},{24,12},{28,16},{1,21},{... | collective-permute-start | bytes 405512 | tf_op jit(solution)/shard_map/ppermute | solution.py:28
  49.4 3.1 %collective-permute-start.19 = (f32[264,128]{1,0:T(8,128)S(1)}, f32[264,128]{1,0:T(8,128)S(1)}, u32[]{:S(2)}, u32[]{:S(2)}) collective-permute-start(f32[264,128]{1,0:T(8,128)S(1)} %add.23.refs_0_), channel_id=1, source_target_pairs={{0,4},{4,0},{8,12},{12,8},{16,20},{20,16},{24,28},{28,24},{1,5},{5... | collective-permute-start | bytes 405512 | tf_op jit(solution)/shard_map/ppermute | solution.py:28
  52.2 1.4 %collective-permute-start.21 = (f32[264,128]{1,0:T(8,128)S(1)}, f32[264,128]{1,0:T(8,128)S(1)}, u32[]{:S(2)}, u32[]{:S(2)}) collective-permute-start(f32[264,128]{1,0:T(8,128)S(1)} %collective-permute-done.20.refs_1_), channel_id=1, source_target_pairs={{0,4},{4,0},{8,12},{12,8},{16,20},{20,16},{24,28},{28,24},{1,5},{5... | collective-permute-start | bytes 405512 | tf_op jit(solution)/shard_map/ppermute | solution.py:28
  55.2 7.4 %collective-permute-start.22 = (f32[128,256]{1,0:T(8,128)S(1)}, f32[128,256]{1,0:T(8,128)S(1)}, u32[]{:S(2)}, u32[]{:S(2)}) collective-permute-start(f32[128,256]{1,0:T(8,128)S(1)} %get-tuple-element.115), channel_id=1, source_target_pairs={{0,6},{1,7},{2,4},{3,5},{4,2},{5,3},{6,0},{7,1},{8,14},{9,15},{10,... | collective-permute-start | bytes 393224 | tf_op jit(solution)/shard_map/ppermute | solution.py:22
  (1 other events, 1.9 us)
